TPU v7x, 32 devices: a whole 2x2x4 slice. The times are simulated.
32 devices in a mesh: dp: 8 (over y, x, core), fsdp: 4 (over z).
Axes of the slice: x: 2, y: 2, z: 4, core: 2. Of those that a mesh axis runs over, the one named last changes fastest.
Arguments:
- tokens: bfloat16 [8192, 1024], P(('dp', 'fsdp')), may hold values from -6 to 6
- lengths: int32 [8, 4], P('dp'), may hold values from 0 to 1024, as said below
- packing: int32 [8, 1024], P('dp'), may hold values from 0 to 1023, each once within a row
- w_query: bfloat16 [1024, 1024], P(('dp', 'fsdp')), may hold values from -0.1875 to 0.1875
- w_key: bfloat16 [1024, 1024], P(('dp', 'fsdp')), may hold values from -0.1875 to 0.1875
- w_value: bfloat16 [1024, 1024], P(('dp', 'fsdp')), may hold values from -0.1875 to 0.1875
- w_gate: bfloat16 [1024, 1024], P(('dp', 'fsdp')), may hold values from -0.1875 to 0.1875
- w_beta: bfloat16 [1024, 8], P(('dp', 'fsdp')), may hold values from -0.1875 to 0.1875
- conv_taps: bfloat16 [3, 4, 1024], P(None, None, ('dp', 'fsdp')), may hold values from -3 to 3
- w_out: bfloat16 [1024, 1024], P(('dp', 'fsdp')), may hold values from -0.3125 to 0.3125
- gain_mix: bfloat16 [1024], P(('dp', 'fsdp')), may hold values from 0.5 to 1.5
- gain_head: bfloat16 [128], P(('dp', 'fsdp')), may hold values from 0.5 to 1.5
- gain_ffn: bfloat16 [1024], P(('dp', 'fsdp')), may hold values from 0.5 to 1.5
- w_ffn_gate: bfloat16 [1024, 2816], P(('dp', 'fsdp')), may hold values from -0.1875 to 0.1875
- w_ffn_up: bfloat16 [1024, 2816], P(('dp', 'fsdp')), may hold values from -0.1875 to 0.1875
- w_ffn_down: bfloat16 [2816, 1024], P(('dp', 'fsdp')), may hold values from -0.1875 to 0.1875
- cotangent: bfloat16 [8192, 1024], P(('dp', 'fsdp')), may hold values from -6 to 6
Outputs:
- layer_out: bfloat16 [8192, 1024], P(('dp', 'fsdp'))
- grad_tokens: float32 [8192, 1024], P(('dp', 'fsdp'))
- grad_w_query: float32 [1024, 1024], P(('dp', 'fsdp'))
- grad_w_key: float32 [1024, 1024], P(('dp', 'fsdp'))
- grad_w_value: float32 [1024, 1024], P(('dp', 'fsdp'))
- grad_w_gate: float32 [1024, 1024], P(('dp', 'fsdp'))
- grad_w_beta: float32 [1024, 8], P(('dp', 'fsdp'))
- grad_conv_taps: float32 [3, 4, 1024], P(None, None, ('dp', 'fsdp'))
- grad_w_out: float32 [1024, 1024], P(('dp', 'fsdp'))
- grad_gain_mix: float32 [1024], P(('dp', 'fsdp'))
- grad_gain_head: float32 [128], P(('dp', 'fsdp'))
- grad_gain_ffn: float32 [1024], P(('dp', 'fsdp'))
- grad_w_ffn_gate: float32 [1024, 2816], P(('dp', 'fsdp'))
- grad_w_ffn_up: float32 [1024, 2816], P(('dp', 'fsdp'))
- grad_w_ffn_down: float32 [2816, 1024], P(('dp', 'fsdp'))
Inputs may be any that keep to these rules, and one draw needn't show every extreme that they name: `lengths`: each row sums to 1024; its nonzero entries come first; in every draw some group holds a single sequence of 1024 tokens. `packing`: each row lists every arrival index of its group once.
All inputs are finite; a program needn't handle non-finite values.
Results may differ from a plain program's by a relative error of at most 0.014.
Values may be sent and summed in bfloat16 or wider, within the bound.
No kernel may reach another device: no remote copies, remote signals or barrier semaphores. Data moves between devices by JAX's collectives and lax.ppermute only.
A program may use at most 192 MiB of HBM per device.

v0:
```python
import jax
import jax.numpy as jnp
from jax import lax
from jax.sharding import PartitionSpec as P

BLOCK = 64


norm_eps = 1e-05
unit_eps = 1e-06


def rms_scale(values, gain):
    return values * lax.rsqrt(jnp.mean(values * values, axis=-1, keepdims=True) + norm_eps) * gain


def gated_norm(mixed_rows, gate_proj, gain):
    count, width = mixed_rows.shape
    split = mixed_rows.reshape(count, width // gain.shape[0], gain.shape[0])
    normed = split * lax.rsqrt(jnp.mean(split * split, axis=-1, keepdims=True) + norm_eps) * gain
    return normed.reshape(count, width) * jax.nn.silu(gate_proj)


def swiglu(gate_proj, up_proj):
    return jax.nn.silu(gate_proj) * up_proj


def sequence_layout(lengths_row, total):
    ends = jnp.cumsum(lengths_row)
    index = jnp.arange(total, dtype=jnp.int32)
    before = index[:, None] >= ends[None, :]
    segment = jnp.sum(before.astype(jnp.int32), axis=1)
    start = jnp.sum(jnp.where(before, lengths_row[None, :], 0), axis=1)
    return (segment, index - start)


def short_conv(values, taps, position):
    width = taps.shape[0]
    total = values.shape[0]
    result = taps[width - 1] * values
    for offset in range(1, width):
        moved = jnp.pad(values, ((offset, 0), (0, 0)))[:total]
        result = result + jnp.where(
            (position >= offset)[:, None], taps[width - 1 - offset] * moved, 0.0
        )
    return result


def block_step(state, query, keys, values, beta, segment, previous):
    high = lax.Precision.HIGHEST
    size = segment.shape[0]
    same = segment[:, None] == segment[None, :]
    places = jnp.arange(size)
    strict = (places[:, None] > places[None, :]) & same
    inclusive = (places[:, None] >= places[None, :]) & same
    carried = (segment == previous).astype(jnp.float32)
    keys_dot = jnp.einsum("hcd,hed->hce", keys, keys, precision=high)
    system = jnp.eye(size, dtype=jnp.float32) + jnp.where(strict, beta[:, :, None] * keys_dot, 0.0)
    right_side = jnp.concatenate(
        [beta[..., None] * values, (beta * carried)[..., None] * keys], axis=-1
    )
    solved = jax.scipy.linalg.solve_triangular(system, right_side, lower=True, unit_diagonal=True)
    value_width = values.shape[-1]
    update = solved[..., :value_width] - jnp.einsum(
        "hcd,hde->hce", solved[..., value_width:], state, precision=high
    )
    scores = jnp.where(inclusive, jnp.einsum("hcd,hed->hce", query, keys, precision=high), 0.0)
    output = carried[:, None] * jnp.einsum("hcd,hde->hce", query, state, precision=high)
    output = output + jnp.einsum("hce,hed->hcd", scores, update, precision=high)
    last_seq = (segment == segment[-1]).astype(jnp.float32)
    new_state = carried[-1] * state + jnp.einsum(
        "hcd,hce->hde", keys * last_seq[:, None], update, precision=high
    )
    return (new_state, output)


def delta_blocks(query, keys, values, beta, segment):
    total, heads, width = query.shape
    count = total // BLOCK

    def blocks(array):
        return jnp.swapaxes(array.reshape(count, BLOCK, heads, -1), 1, 2)

    beta_blocks = jnp.swapaxes(beta.reshape(count, BLOCK, heads), 1, 2)
    seg_blocks = segment.reshape(count, BLOCK)
    previous = jnp.concatenate([jnp.full((1,), -1, jnp.int32), seg_blocks[:-1, -1]])
    state = jnp.zeros((heads, width, values.shape[-1]), jnp.float32)

    def advance(carry, block):
        return block_step(carry, block[0], block[1], block[2], block[3], block[4], block[5])

    _, outputs = lax.scan(
        jax.checkpoint(advance),
        state,
        (blocks(query), blocks(keys), blocks(values), beta_blocks, seg_blocks, previous),
    )
    return jnp.swapaxes(outputs, 1, 2).reshape(total, heads, -1)


def head_mixer(query_raw, key_raw, value_raw, beta_raw, taps, packing_row, lengths_row):
    total, width = query_raw.shape
    heads = beta_raw.shape[1]
    segment, position = sequence_layout(lengths_row, total)

    def prepare(raw_rows, tap_rows):
        return jax.nn.silu(short_conv(raw_rows[packing_row], tap_rows, position)).reshape(
            total, heads, width // heads
        )

    query = prepare(query_raw, taps[0])
    query = query * lax.rsqrt(jnp.sum(query * query, axis=-1, keepdims=True) + unit_eps)
    keys = prepare(key_raw, taps[1])
    keys = keys * lax.rsqrt(jnp.sum(keys * keys, axis=-1, keepdims=True) + unit_eps)
    values = prepare(value_raw, taps[2])
    beta = jax.nn.sigmoid(beta_raw[packing_row])
    output = delta_blocks(query, keys, values, beta, segment).reshape(total, width)
    return jnp.zeros_like(output).at[packing_row].set(output)


def project(left, right):
    return jnp.dot(left, right, preferred_element_type=jnp.float32)


def project_back(left, right):
    return lax.dot_general(
        left, right, (((1,), (1,)), ((), ())), preferred_element_type=jnp.float32
    )


def weight_grad(left, right):
    return lax.dot_general(
        left, right, (((0,), (0,)), ((), ())), preferred_element_type=jnp.float32
    )


def per_device(
    tokens,
    lengths,
    packing,
    w_query,
    w_key,
    w_value,
    w_gate,
    w_beta,
    conv_taps,
    w_out,
    gain_mix,
    gain_head,
    gain_ffn,
    w_ffn_gate,
    w_ffn_up,
    w_ffn_down,
    cotangent,
):
    lengths_row = lengths[0]
    packing_row = packing[0]
    mixer_set = (
        lax.all_gather(w_query, ("dp", "fsdp"), axis=0, tiled=True),
        lax.all_gather(w_key, ("dp", "fsdp"), axis=0, tiled=True),
        lax.all_gather(w_value, ("dp", "fsdp"), axis=0, tiled=True),
        lax.all_gather(w_gate, ("dp", "fsdp"), axis=0, tiled=True),
        lax.all_gather(w_beta, ("dp", "fsdp"), axis=0, tiled=True),
        lax.all_gather(w_out, ("dp", "fsdp"), axis=0, tiled=True),
        lax.all_gather(conv_taps, ("dp", "fsdp"), axis=2, tiled=True),
        lax.all_gather(gain_mix, ("dp", "fsdp"), axis=0, tiled=True),
        lax.all_gather(gain_head, ("dp", "fsdp"), axis=0, tiled=True),
    )
    (
        full_query,
        full_key,
        full_value,
        full_gate,
        full_beta,
        full_out,
        full_taps,
        full_gmix,
        full_ghead,
    ) = mixer_set
    inputs_f = tokens.astype(jnp.float32)
    hidden, norm_mix_back = jax.vjp(rms_scale, inputs_f, full_gmix.astype(jnp.float32))
    hidden_b = hidden.astype(jnp.bfloat16)
    query_raw = project(hidden_b, full_query).astype(jnp.bfloat16)
    key_raw = project(hidden_b, full_key).astype(jnp.bfloat16)
    value_raw = project(hidden_b, full_value).astype(jnp.bfloat16)
    beta_raw = project(hidden_b, full_beta).astype(jnp.bfloat16)
    gate_proj = project(hidden_b, full_gate)
    query_heads, key_heads, value_heads, beta_heads = (
        lax.all_to_all(query_raw, "fsdp", split_axis=1, concat_axis=0, tiled=True),
        lax.all_to_all(key_raw, "fsdp", split_axis=1, concat_axis=0, tiled=True),
        lax.all_to_all(value_raw, "fsdp", split_axis=1, concat_axis=0, tiled=True),
        lax.all_to_all(beta_raw, "fsdp", split_axis=1, concat_axis=0, tiled=True),
    )
    span = query_heads.shape[1]
    first_col = lax.axis_index("fsdp") * span
    local_taps = lax.dynamic_slice_in_dim(full_taps, first_col, span, 2).astype(jnp.float32)

    def local_mixer(query_in, key_in, value_in, beta_in, taps_in):
        return head_mixer(query_in, key_in, value_in, beta_in, taps_in, packing_row, lengths_row)

    mixed_heads, mixer_back = jax.vjp(
        local_mixer,
        query_heads.astype(jnp.float32),
        key_heads.astype(jnp.float32),
        value_heads.astype(jnp.float32),
        beta_heads.astype(jnp.float32),
        local_taps,
    )
    mixed = lax.all_to_all(
        mixed_heads.astype(jnp.bfloat16), "fsdp", split_axis=0, concat_axis=1, tiled=True
    )
    normed, gated_back = jax.vjp(
        gated_norm, mixed.astype(jnp.float32), gate_proj, full_ghead.astype(jnp.float32)
    )
    normed_b = normed.astype(jnp.bfloat16)
    middle = inputs_f + project(normed_b, full_out)
    ffn_set = (
        lax.all_gather(w_ffn_gate, ("dp", "fsdp"), axis=0, tiled=True),
        lax.all_gather(w_ffn_up, ("dp", "fsdp"), axis=0, tiled=True),
        lax.all_gather(w_ffn_down, ("dp", "fsdp"), axis=0, tiled=True),
        lax.all_gather(gain_ffn, ("dp", "fsdp"), axis=0, tiled=True),
    )
    full_fgate, full_fup, full_fdown, full_gffn = ffn_set
    ffn_in, norm_ffn_back = jax.vjp(rms_scale, middle, full_gffn.astype(jnp.float32))
    ffn_in_b = ffn_in.astype(jnp.bfloat16)
    gate_ffn = project(ffn_in_b, full_fgate)
    up_ffn = project(ffn_in_b, full_fup)
    active, active_back = jax.vjp(swiglu, gate_ffn, up_ffn)
    active_b = active.astype(jnp.bfloat16)
    layer_out = (middle + project(active_b, full_fdown)).astype(jnp.bfloat16)
    full_fgate, full_fup, full_fdown = (
        lax.all_gather(w_ffn_gate, ("dp", "fsdp"), axis=0, tiled=True),
        lax.all_gather(w_ffn_up, ("dp", "fsdp"), axis=0, tiled=True),
        lax.all_gather(w_ffn_down, ("dp", "fsdp"), axis=0, tiled=True),
    )
    grad_fdown = lax.psum_scatter(
        weight_grad(active_b, cotangent), ("dp", "fsdp"), scatter_dimension=0, tiled=True
    )
    d_active = project_back(cotangent, full_fdown)
    d_fgate, d_fup = active_back(d_active)
    d_fgate_b = d_fgate.astype(jnp.bfloat16)
    d_fup_b = d_fup.astype(jnp.bfloat16)
    d_ffn_in = project_back(d_fgate_b, full_fgate) + project_back(d_fup_b, full_fup)
    d_middle_norm, d_gffn = norm_ffn_back(d_ffn_in)
    ffn_terms = (weight_grad(ffn_in_b, d_fgate_b), weight_grad(ffn_in_b, d_fup_b), d_gffn)
    grad_fgate, grad_fup, grad_gffn = (
        lax.psum_scatter(ffn_terms[0], ("dp", "fsdp"), scatter_dimension=0, tiled=True),
        lax.psum_scatter(ffn_terms[1], ("dp", "fsdp"), scatter_dimension=0, tiled=True),
        lax.psum_scatter(ffn_terms[2], ("dp", "fsdp"), scatter_dimension=0, tiled=True),
    )
    d_middle = cotangent.astype(jnp.float32) + d_middle_norm
    d_branch = d_middle.astype(jnp.bfloat16)
    full_query, full_key, full_value, full_gate, full_beta, full_out = (
        lax.all_gather(w_query, ("dp", "fsdp"), axis=0, tiled=True),
        lax.all_gather(w_key, ("dp", "fsdp"), axis=0, tiled=True),
        lax.all_gather(w_value, ("dp", "fsdp"), axis=0, tiled=True),
        lax.all_gather(w_gate, ("dp", "fsdp"), axis=0, tiled=True),
        lax.all_gather(w_beta, ("dp", "fsdp"), axis=0, tiled=True),
        lax.all_gather(w_out, ("dp", "fsdp"), axis=0, tiled=True),
    )
    grad_wout = lax.psum_scatter(
        weight_grad(normed_b, d_branch), ("dp", "fsdp"), scatter_dimension=0, tiled=True
    )
    d_normed = project_back(d_branch, full_out)
    d_mixed, d_gate_proj, d_ghead = gated_back(d_normed)
    d_mixed_heads = lax.all_to_all(
        d_mixed.astype(jnp.bfloat16), "fsdp", split_axis=1, concat_axis=0, tiled=True
    )
    d_query_h, d_key_h, d_value_h, d_beta_h, d_taps = mixer_back(d_mixed_heads.astype(jnp.float32))
    d_query_raw, d_key_raw, d_value_raw, d_beta_raw = (
        lax.all_to_all(
            d_query_h.astype(jnp.bfloat16), "fsdp", split_axis=0, concat_axis=1, tiled=True
        ),
        lax.all_to_all(
            d_key_h.astype(jnp.bfloat16), "fsdp", split_axis=0, concat_axis=1, tiled=True
        ),
        lax.all_to_all(
            d_value_h.astype(jnp.bfloat16), "fsdp", split_axis=0, concat_axis=1, tiled=True
        ),
        lax.all_to_all(
            d_beta_h.astype(jnp.bfloat16), "fsdp", split_axis=0, concat_axis=1, tiled=True
        ),
    )
    d_gate_b = d_gate_proj.astype(jnp.bfloat16)
    d_hidden = project_back(d_query_raw, full_query) + project_back(d_key_raw, full_key)
    d_hidden = d_hidden + project_back(d_value_raw, full_value) + project_back(d_gate_b, full_gate)
    d_hidden = d_hidden + project_back(d_beta_raw, full_beta)
    d_inputs_norm, d_gmix = norm_mix_back(d_hidden)
    grad_tokens = d_middle + d_inputs_norm
    taps_term = lax.dynamic_update_slice_in_dim(
        jnp.zeros(full_taps.shape, jnp.float32), d_taps, first_col, 2
    )
    mixer_grads = (
        lax.psum_scatter(
            weight_grad(hidden_b, d_query_raw), ("dp", "fsdp"), scatter_dimension=0, tiled=True
        ),
        lax.psum_scatter(
            weight_grad(hidden_b, d_key_raw), ("dp", "fsdp"), scatter_dimension=0, tiled=True
        ),
        lax.psum_scatter(
            weight_grad(hidden_b, d_value_raw), ("dp", "fsdp"), scatter_dimension=0, tiled=True
        ),
        lax.psum_scatter(
            weight_grad(hidden_b, d_gate_b), ("dp", "fsdp"), scatter_dimension=0, tiled=True
        ),
        lax.psum_scatter(
            weight_grad(hidden_b, d_beta_raw), ("dp", "fsdp"), scatter_dimension=0, tiled=True
        ),
        lax.psum_scatter(taps_term, ("dp", "fsdp"), scatter_dimension=2, tiled=True),
        lax.psum_scatter(d_gmix, ("dp", "fsdp"), scatter_dimension=0, tiled=True),
        lax.psum_scatter(d_ghead, ("dp", "fsdp"), scatter_dimension=0, tiled=True),
    )
    grad_query, grad_key, grad_value, grad_wgate, grad_wbeta, grad_taps, grad_gmix, grad_ghead = (
        mixer_grads
    )
    return (
        layer_out,
        grad_tokens,
        grad_query,
        grad_key,
        grad_value,
        grad_wgate,
        grad_wbeta,
        grad_taps,
        grad_wout,
        grad_gmix,
        grad_ghead,
        grad_gffn,
        grad_fgate,
        grad_fup,
        grad_fdown,
    )


def solution(mesh):
    in_specs = (
        P(("dp", "fsdp"), None),
        P("dp", None),
        P("dp", None),
        P(("dp", "fsdp"), None),
        P(("dp", "fsdp"), None),
        P(("dp", "fsdp"), None),
        P(("dp", "fsdp"), None),
        P(("dp", "fsdp"), None),
        P(None, None, ("dp", "fsdp")),
        P(("dp", "fsdp"), None),
        P(("dp", "fsdp")),
        P(("dp", "fsdp")),
        P(("dp", "fsdp")),
        P(("dp", "fsdp"), None),
        P(("dp", "fsdp"), None),
        P(("dp", "fsdp"), None),
        P(("dp", "fsdp"), None),
    )
    out_specs = (
        P(("dp", "fsdp"), None),
        P(("dp", "fsdp"), None),
        P(("dp", "fsdp"), None),
        P(("dp", "fsdp"), None),
        P(("dp", "fsdp"), None),
        P(("dp", "fsdp"), None),
        P(("dp", "fsdp"), None),
        P(None, None, ("dp", "fsdp")),
        P(("dp", "fsdp"), None),
        P(("dp", "fsdp")),
        P(("dp", "fsdp")),
        P(("dp", "fsdp")),
        P(("dp", "fsdp"), None),
        P(("dp", "fsdp"), None),
        P(("dp", "fsdp"), None),
    )
    return jax.shard_map(
        per_device, mesh=mesh, in_specs=in_specs, out_specs=out_specs, check_vma=False
    )
```

profile of v0, /device:TPU:9, one launch (start us, length us, event | category | flops | bytes accessed | tf_op | source)
XLA Modules:
  0.0 2970.7 jit_solution(13384407699068714305)
XLA Ops:
  14.5 39.9 %all-reduce.42 = (bf16[128]{0:T(256)(128)(2,1)S(1)}, bf16[1024]{0:T(1024)(128)(2,1)S(1)}, bf16[1024]{0:T(1024)(128)(2,1)S(1)}) all-reduce(bf16[128]{0:T(256)(128)(2,1)S(1)} %dynamic-update-slice.1, bf16[1024]{0:T(1024)(128)(2,1)S(1)} %dynamic-update-slice, ...), channel_id=1, replica_groups=mesh['dp'=8,'fsdp'=4] {'dp','fsdp'}, use_global_device_ids=true, to_apply=%add.36 | all-reduce | flops 2176 | bytes 8704
  54.4 60.9 %all-gather = bf16[32,32,8]{1,2,0:T(8,128)(2,1)S(1)} all-gather(bf16[1,32,8]{1,2,0:T(8,128)(2,1)} %bitcast.561), channel_id=1, replica_groups=mesh['dp'=8,'fsdp'=4] {'dp','fsdp'}, dimensions={0}, use_global_device_ids=true | all-gather | bytes 16896 | tf_op jit(solution)/shard_map/all_gather | solution.py:162
  133.7 75.8 %all_gather.48 = bf16[3,4,1024]{1,0,2:T(4,128)(2,1)S(1)} all-gather(bf16[3,4,32]{1,0,2:T(4,128)(2,1)S(1)} %copy.388), channel_id=1, replica_groups=mesh['dp'=8,'fsdp'=4] {'dp','fsdp'}, dimensions={2}, use_global_device_ids=true | all-gather | bytes 25344 | tf_op jit(solution)/shard_map/all_gather | solution.py:164
  209.6 12.4 slice_reduce_fusion.3
  225.2 22.0 all-to-all-start.3
  314.2 353.9 %while.40 = (s32[]{:T(128)}, f32[2,128,128]{2,1,0:T(8,128)S(1)}, f32[16,2,64,128]{3,2,1,0:T(8,128)}, f32[16,2,128,128]{3,2,1,0:T(8,128)}, s32[16,64]{1,0:T(8,128...) while((s32[]{:T(128)}, f32[2,128,128]{2,1,0:T(8,128)S(1)}, ...), condition=%wide.region_8.10_spmd.clone, body=%wide.region_7.9_spmd.clone.sunk | while | flops 138830400 | bytes 2394550 | solution.py:92
  317.4 9.9 custom-call.37
  339.6 9.8 custom-call.37
  361.7 9.8 custom-call.37
  383.8 9.8 custom-call.37
  405.9 9.9 custom-call.37
  428.1 9.8 custom-call.37
  450.2 9.8 custom-call.37
  472.3 9.8 custom-call.37
  494.4 9.8 custom-call.37
  516.5 9.8 custom-call.37
  538.7 9.8 custom-call.37
  560.8 9.8 custom-call.37
  582.9 9.8 custom-call.37
  605.0 9.8 custom-call.37
  627.1 9.8 custom-call.37
  649.2 9.8 custom-call.37
  671.3 8.2 scatter_custom_fusion.1
  686.5 7.2 all-to-all-done.4
  716.3 8.3 multiply_convert_fusion
  770.8 383.9 %while.41 = (s32[]{:T(128)}, f32[2,128,128]{2,1,0:T(8,128)S(1)}, f32[16,2,64,128]{3,2,1,0:T(8,128)S(1)}, f32[16,2,64,128]{3,2,1,0:T(8,128)}, f32[16,2,64,128]{3,...) while((s32[]{:T(128)}, f32[2,128,128]{2,1,0:T(8,128)S(1)}, ...), condition=%wide.region_18.20_spmd.clone, body=%wide.region_14.19_spmd.clone.sunk | while | flops 359342528 | bytes 6606115 | solution.py:92
  774.7 9.8 custom-call.38
  798.7 9.8 custom-call.38
  822.7 9.8 custom-call.38
  846.7 9.8 custom-call.38
  870.7 9.8 custom-call.38
  894.7 9.8 custom-call.38
  918.6 9.8 custom-call.38
  942.6 9.8 custom-call.38
  966.6 9.8 custom-call.38
  990.6 9.8 custom-call.38
  1014.6 9.8 custom-call.38
  1038.6 9.8 custom-call.38
  1062.6 9.8 custom-call.38
  1086.6 9.8 custom-call.38
  1110.6 9.8 custom-call.38
  1134.6 9.8 custom-call.38
  1165.3 7.0 scatter_custom_fusion.5
  1185.2 6.2 multiply_reduce_fusion.8
  1211.2 7.8 scatter_custom_fusion.4
  1221.3 13.2 all_to_all.154
  1237.3 7.7 scatter_custom_fusion.3
  1246.5 12.6 all_to_all.155
  1264.0 7.5 scatter_custom_fusion.2
  1272.9 12.0 all_to_all.156
  1288.9 7.4 fusion.189
  1296.5 7.3 fusion.190
  1304.9 7.3 fusion.191
  1318.9 7.9 reduce-scatter.31.cloned.1.call-done
  1328.3 131.2 %reduce-scatter.33.cloned.1.call-done = f32[32,12]{1,0:T(8,128)} async-done(((f32[1024,12]{1,0:T(8,128)}), f32[32,12]{1,0:T(8,128)}) %reduce-scatter.33.cloned.1.call-update) | async-done | bytes 1552
  1468.4 48.5 %all-reduce.41 = (f32[1024]{0:T(1024)S(1)}, f32[128]{0:T(128)S(1)}, f32[1024]{0:T(1024)S(1)}) all-reduce(f32[1024]{0:T(1024)S(1)} %get-tuple-element.563, f32[128]{0:T(128)S(1)} %bitcast_reduce_fusion, f32[1024]{0:T(1024)S(1)} %copy-done.57), channel_id=9, replica_groups=mesh['dp'=8,'fsdp'=4] {'dp','fsdp'}, use_global_device_ids=true, to_apply=%region_46.48.clone | all-reduce | flops 2176 | bytes 17408
  1519.9 89.1 %reduce-scatter.23.cloned.1.call-done = f32[32,1024]{1,0:T(8,128)} async-done(((f32[1024,1024]{1,0:T(8,128)}), f32[32,1024]{1,0:T(8,128)}) %reduce-scatter.23.cloned.1.call-update) | async-done | bytes 131088 | tf_op jit(solution)/shard_map/reduce_scatter | solution.py:260
  1609.0 149.7 %reduce-scatter.21.cloned.1.call-done = f32[32,1024]{1,0:T(8,128)} async-done(((f32[1024,1024]{1,0:T(8,128)}), f32[32,1024]{1,0:T(8,128)}) %reduce-scatter.21.cloned.1.call-update) | async-done | bytes 131088 | tf_op jit(solution)/shard_map/reduce_scatter | solution.py:302
  1758.7 148.1 %reduce-scatter.19.cloned.1.call-done = f32[32,1024]{1,0:T(8,128)} async-done(((f32[1024,1024]{1,0:T(8,128)}), f32[32,1024]{1,0:T(8,128)}) %reduce-scatter.19.cloned.1.call-update) | async-done | bytes 131088 | tf_op jit(solution)/shard_map/reduce_scatter | solution.py:299
  1906.8 149.7 %reduce-scatter.17.cloned.1.call-done = f32[32,1024]{1,0:T(8,128)} async-done(((f32[1024,1024]{1,0:T(8,128)}), f32[32,1024]{1,0:T(8,128)}) %reduce-scatter.17.cloned.1.call-update) | async-done | bytes 131088 | tf_op jit(solution)/shard_map/reduce_scatter | solution.py:296
  2056.5 148.9 %reduce-scatter.15.cloned.1.call-done = f32[32,1024]{1,0:T(8,128)} async-done(((f32[1024,1024]{1,0:T(8,128)}), f32[32,1024]{1,0:T(8,128)}) %reduce-scatter.15.cloned.1.call-update) | async-done | bytes 131088 | tf_op jit(solution)/shard_map/reduce_scatter | solution.py:293
  2205.4 255.8 %reduce-scatter.25.cloned.1.call-done = f32[32,2816]{1,0:T(8,128)} async-done(((f32[1024,2816]{1,0:T(8,128)}), f32[32,2816]{1,0:T(8,128)}) %reduce-scatter.25.cloned.1.call-update) | async-done | bytes 360464 | tf_op jit(solution)/shard_map/reduce_scatter | solution.py:246
  2461.3 251.2 %reduce-scatter.27.cloned.1.call-done = f32[32,2816]{1,0:T(8,128)} async-done(((f32[1024,2816]{1,0:T(8,128)}), f32[32,2816]{1,0:T(8,128)}) %reduce-scatter.27.cloned.1.call-update) | async-done | bytes 360464 | tf_op jit(solution)/shard_map/reduce_scatter | solution.py:247
  2712.5 251.2 %reduce-scatter.29.cloned.1.call-done = f32[88,1024]{1,0:T(8,128)} async-done(((f32[2816,1024]{1,0:T(8,128)}), f32[88,1024]{1,0:T(8,128)}) %reduce-scatter.29.cloned.1.call-update) | async-done | bytes 360464 | tf_op jit(solution)/shard_map/reduce_scatter | solution.py:235
  (1317 shorter events, 672.4 us)
Async XLA Ops:
  7.2 118.8 %copy-start = (bf16[256,1024]{1,0:T(8,128)(2,1)S(1)}, bf16[256,1024]{1,0:T(8,128)(2,1)}, u32[]{:S(2)}) copy-start(bf16[256,1024]{1,0:T(8,128)(2,1)} %param.23) | copy-start | bytes 1572868
  7.2 118.0 %copy-start.51 = (s32[1,1024]{1,0:T(1,128)S(1)}, s32[1,1024]{1,0:T(1,128)}, u32[]{:S(2)}) copy-start(s32[1,1024]{1,0:T(1,128)} %param.25) | copy-start | bytes 12292
  7.2 118.1 %copy-start.58 = (bf16[3,4,32]{2,1,0:T(4,128)(2,1)S(1)}, bf16[3,4,32]{2,1,0:T(4,128)(2,1)}, u32[]{:S(2)}) copy-start(bf16[3,4,32]{2,1,0:T(4,128)(2,1)} %param.31) | copy-start | bytes 2308
  7.2 118.2 %copy-start.59 = (s32[1,4]{1,0:T(1,128)S(1)}, s32[1,4]{1,0:T(1,128)}, u32[]{:S(2)}) copy-start(s32[1,4]{1,0:T(1,128)} %param.24) | copy-start | bytes 52
  7.2 118.8 %all-gather.12.cloned.1.call-start = ((), (), s32[]{:S(2)}) async-start(), calls=%async_computation.21 | async-start | bytes 2162688 | tf_op jit(solution)/shard_map/all_gather | solution.py:160
  8.0 214.1 %all-gather.14.cloned.1.call-start = ((), (), s32[]{:S(2)}) async-start(), calls=%async_computation.22 | async-start | bytes 2162688 | tf_op jit(solution)/shard_map/all_gather | solution.py:158
  8.7 252.3 %all-gather.10.cloned.1.call-start = ((), (), s32[]{:S(2)}) async-start(), calls=%async_computation.20 | async-start | bytes 2162688 | tf_op jit(solution)/shard_map/all_gather | solution.py:159
  9.4 686.1 %all-gather.16.cloned.1.call-start = ((), (), s32[]{:S(2)}) async-start(), calls=%async_computation.23 | async-start | bytes 2162688 | tf_op jit(solution)/shard_map/all_gather | solution.py:161
  10.0 690.6 %all-gather.18.cloned.1.call-start = ((), (), s32[]{:S(2)}) async-start(), calls=%async_computation.24 | async-start | bytes 2162688 | tf_op jit(solution)/shard_map/all_gather | solution.py:163
  10.6 693.8 %all-gather.20.cloned.1.call-start = ((), (), s32[]{:S(2)}) async-start(), calls=%async_computation.25 | async-start | bytes 5947392 | tf_op jit(solution)/shard_map/all_gather | solution.py:217
  11.2 699.3 %all-gather.22.cloned.1.call-start = ((), (), s32[]{:S(2)}) async-start(), calls=%async_computation.26 | async-start | bytes 5947392 | tf_op jit(solution)/shard_map/all_gather | solution.py:218
  115.4 13.0 copy-start.49
  118.6 10.6 all-to-all-start.1
  124.5 591.8 %all-gather.24.cloned.1.call-start = ((), (), s32[]{:S(2)}) async-start(), calls=%async_computation.27 | async-start | bytes 5947392 | tf_op jit(solution)/shard_map/all_gather | solution.py:219
  129.2 96.0 %all-to-all-start.2 = ((bf16[256,4,256]{2,0,1:T(8,128)(2,1)}), bf16[256,4,256]{2,0,1:T(8,128)(2,1)S(1)}, u32[]{:S(2)}, u32[]{:S(2)}) async-start(bf16[256,4,256]{2,0,1:T(8,128)(2,1)} %bitcast.371), calls=%async_computation.2 | async-start | bytes 1048576 | tf_op jit(solution)/shard_map/all_to_all | solution.py:190
  222.0 56.1 %copy-start.52 = (f32[256]{0:T(256)}, f32[256]{0:T(256)S(1)}, u32[]{:S(2)}) copy-start(f32[256]{0:T(256)S(1)} %get-tuple-element.571) | copy-start | bytes 3076
  225.2 42.5 %all-to-all-start.3 = ((bf16[256,4,256]{2,0,1:T(8,128)(2,1)}), bf16[256,4,256]{2,0,1:T(8,128)(2,1)}, u32[]{:S(2)}, u32[]{:S(2)}) async-start(bf16[256,4,256]{2,0,1:T(8,128)(2,1)} %bitcast.370), calls=%async_computation.3 | async-start | bytes 1048576 | tf_op jit(solution)/shard_map/all_to_all | solution.py:188
  267.7 20.9 all-to-all-start
  668.1 11.4 copy-start.61
  681.6 12.1 all-to-all-start.4
  704.3 6.2 copy-start.19
  724.7 5.4 copy-start.48
  724.7 5.4 copy-start.47
  724.7 5.4 copy-start.11
  724.7 5.7 copy-start.60
  733.2 4.9 copy-start.14
  745.2 5.8 copy-start.7
  746.1 12.6 all-to-all-start.5
  788.1 6.8 copy-start.63
  812.1 6.8 copy-start.63
  836.1 6.8 copy-start.63
  860.0 6.7 copy-start.63
  884.0 6.7 copy-start.63
  908.0 6.8 copy-start.63
  932.0 6.7 copy-start.63
  956.0 6.7 copy-start.63
  980.0 6.8 copy-start.63
  1004.0 6.8 copy-start.63
  1028.0 6.8 copy-start.63
  1052.0 6.7 copy-start.63
  1076.0 6.8 copy-start.63
  1100.0 6.8 copy-start.63
  1124.0 6.8 copy-start.63
  1148.0 6.8 copy-start.63
  1172.3 10.3 copy-start.39
  1172.3 11.5 copy-start.38
  1174.2 17.2 all-to-all-start.9
  1179.0 147.9 %reduce-scatter.31.cloned.1.call-start = ((), (), s32[]{:S(2)}) async-start(), calls=%async_computation.36 | async-start | bytes 540672
  1179.0 6.1 copy-start.21
  1179.0 6.1 copy-start.24
  1180.2 4.9 copy-start.1
  1180.2 4.9 copy-start.4
  1192.7 266.8 %reduce-scatter.33.cloned.1.call-start = ((), (), s32[]{:S(2)}) async-start(), calls=%async_computation.37 | async-start | bytes 540672
  1198.1 410.9 %reduce-scatter.23.cloned.1.call-start = ((), (), s32[]{:S(2)}) async-start(), calls=%async_computation.32 | async-start | bytes 4325376 | tf_op jit(solution)/shard_map/reduce_scatter | solution.py:260
  1201.0 557.7 %reduce-scatter.21.cloned.1.call-start = ((), (), s32[]{:S(2)}) async-start(), calls=%async_computation.31 | async-start | bytes 4325376 | tf_op jit(solution)/shard_map/reduce_scatter | solution.py:302
  1204.9 701.9 %reduce-scatter.19.cloned.1.call-start = ((), (), s32[]{:S(2)}) async-start(), calls=%async_computation.30 | async-start | bytes 4325376 | tf_op jit(solution)/shard_map/reduce_scatter | solution.py:299
  1237.3 819.2 %reduce-scatter.17.cloned.1.call-start = ((), (), s32[]{:S(2)}) async-start(), calls=%async_computation.29 | async-start | bytes 4325376 | tf_op jit(solution)/shard_map/reduce_scatter | solution.py:296
  1262.8 942.7 %reduce-scatter.15.cloned.1.call-start = ((), (), s32[]{:S(2)}) async-start(), calls=%async_computation.28 | async-start | bytes 4325376 | tf_op jit(solution)/shard_map/reduce_scatter | solution.py:293
  1287.9 1173.4 %reduce-scatter.25.cloned.1.call-start = ((), (), s32[]{:S(2)}) async-start(), calls=%async_computation.33 | async-start | bytes 11894784 | tf_op jit(solution)/shard_map/reduce_scatter | solution.py:246
  1296.3 1416.1 %reduce-scatter.27.cloned.1.call-start = ((), (), s32[]{:S(2)}) async-start(), calls=%async_computation.34 | async-start | bytes 11894784 | tf_op jit(solution)/shard_map/reduce_scatter | solution.py:247
  1303.9 1659.8 %reduce-scatter.29.cloned.1.call-start = ((), (), s32[]{:S(2)}) async-start(), calls=%async_computation.35 | async-start | bytes 11894784 | tf_op jit(solution)/shard_map/reduce_scatter | solution.py:235
  1318.9 144.6 %copy-start.18 = (bf16[4,256,256]{1,2,0:T(8,128)(2,1)S(1)}, bf16[4,256,256]{1,2,0:T(8,128)(2,1)}, u32[]{:S(2)}) copy-start(bf16[4,256,256]{1,2,0:T(8,128)(2,1)} %copy-done.17) | copy-start | bytes 1572868
  1467.7 50.9 %copy-start.55 = (f32[256]{0:T(256)S(1)}, f32[256]{0:T(256)}, u32[]{:S(2)}) copy-start(f32[256]{0:T(256)} %copy-done.54) | copy-start | bytes 3076
  1467.7 50.9 %copy-start.16 = (f32[256,1024]{1,0:T(8,128)S(1)}, f32[256,1024]{1,0:T(8,128)}, u32[]{:S(2)}) copy-start(f32[256,1024]{1,0:T(8,128)} %copy-done.14) | copy-start | bytes 3145732
  (41 other events, 79.7 us)
Sparse Core Ops, SparseCore 0:
  11.0 57.2 all-gather.11
  71.2 55.3 all-gather.13
  129.5 57.1 all-gather.9
  189.5 55.5 all-gather.15
  247.9 58.5 all-gather.17
  309.2 68.1 all-gather.19
  380.2 67.5 all-gather.21
  450.6 67.3 all-gather.23
  1192.8 134.0 reduce-scatter.30
  1329.1 130.3 reduce-scatter.32
  1462.3 146.6 reduce-scatter.22
  1611.7 146.9 reduce-scatter.20
  1761.5 145.1 reduce-scatter.18
  1909.5 146.9 reduce-scatter.16
  2059.2 146.1 reduce-scatter.14
  2208.2 253.0 reduce-scatter.24
  2464.0 248.3 reduce-scatter.26
  2715.2 248.4 reduce-scatter.28
where the time goes:
time: 2980 us; the launch traced here: 2970 us
  waiting for transfers between devices  1600 us (54%)
  other arithmetic  502 us (17%)
  matrix products  313 us (11%)
  blocking collectives  263 us (9%)
  local copies, waits for them, and re-layouts  220 us (7%)
  starting transfers between devices  52.4 us (2%)
    another operation x128, other arithmetic, block_step(): jax.scipy.linalg.solve_triangular(system, right_side, lower=True, unit_di...  318 us
    reduce_scatter x1, waiting for transfers between devices, per_device(): lax.psum_scatter(ffn_terms[0], ('dp', 'fsdp'), scatter_dimension=0, tiled...  256 us
    reduce_scatter x1, waiting for transfers between devices, per_device(): lax.psum_scatter(weight_grad(active_b, cotangent), ('dp', 'fsdp'), scatte...  251 us
    reduce_scatter x1, waiting for transfers between devices, per_device(): lax.psum_scatter(ffn_terms[1], ('dp', 'fsdp'), scatter_dimension=0, tiled...  251 us
    reduce_scatter x1, waiting for transfers between devices, per_device(): lax.psum_scatter(weight_grad(hidden_b, d_key_raw), ('dp', 'fsdp'), scatte...  150 us
    reduce_scatter x1, waiting for transfers between devices, per_device(): lax.psum_scatter(weight_grad(hidden_b, d_gate_b), ('dp', 'fsdp'), scatter...  150 us
    reduce_scatter x1, waiting for transfers between devices, per_device(): lax.psum_scatter(weight_grad(hidden_b, d_query_raw), ('dp', 'fsdp'), scat...  149 us
    reduce_scatter x1, waiting for transfers between devices, per_device(): lax.psum_scatter(weight_grad(hidden_b, d_value_raw), ('dp', 'fsdp'), scat...  148 us
  transfers between devices with their start and end apart: 25, of which 12 were waited for; matrix products, arithmetic and copies ran while one was open for 19% of the time, Pallas kernels for 0%

commit v1 on v0

v1 whole, which is shorter than its diff:
```python
import functools

import jax
import jax.numpy as jnp
from jax import lax
from jax.experimental import pallas as pl
from jax.experimental.pallas import tpu as pltpu
from jax.sharding import PartitionSpec as P

CHUNK = 128
HALO = 8
norm_eps = 1e-05
unit_eps = 1e-06
NARROW = jnp.bfloat16
WIDE = jnp.float32


def halves(value):
    top = value.astype(NARROW)
    return top, (value - top.astype(WIDE)).astype(NARROW)


def product(left, right, left_dim=1, right_dim=0):
    dims = (((left_dim,), (right_dim,)), ((), ()))

    def one(a, b):
        return lax.dot_general(a, b, dims, preferred_element_type=WIDE)

    if PASSES == 1:
        return one(left[0], right[0])
    return one(left[0], right[0]) + (one(left[0], right[1]) + one(left[1], right[0]))


PASSES = 3


def turned(value):
    return halves(value.T)


def chunk_masks(seg_col, seg_row, before, after):
    size = seg_col.shape[0]
    down = lax.broadcasted_iota(jnp.int32, (size, size), 0)
    across = lax.broadcasted_iota(jnp.int32, (size, size), 1)
    same = seg_col == seg_row
    strict = same & (down > across)
    inclusive = same & (down >= across)
    carried = jnp.where(seg_col == before, 1.0, 0.0).astype(WIDE)
    last = jnp.where(seg_col == after, 1.0, 0.0).astype(WIDE)
    return strict, inclusive, carried, last


def unit_lower_inverse(system):
    size = system.shape[0]
    down = lax.broadcasted_iota(jnp.int32, (size, size), 0)
    across = lax.broadcasted_iota(jnp.int32, (size, size), 1)
    gap = down ^ across
    result = jnp.where(down == across, 1.0, 0.0) - jnp.where((gap == 1) & (down > across), system, 0.0)
    step = 2
    while step < size:
        part = halves(jnp.where((gap >= step) & (gap < 2 * step) & (down > across), system, 0.0))
        done = halves(result)
        result = result - product(done, halves(product(part, done)))
        step *= 2
    return result


def conv_rows(pad_ref, taps, pos, start, column, width):
    window = pad_ref[pl.ds(start, CHUNK + HALO), pl.ds(column, width)]
    count = taps.shape[0]
    result = taps[count - 1 : count] * window[HALO : HALO + CHUNK]
    moved = []
    for offset in range(1, count):
        rows = jnp.where(pos >= offset, window[HALO - offset : HALO - offset + CHUNK], 0.0)
        moved.append(rows)
        result = result + taps[count - 1 - offset : count - offset] * rows
    return result, window[HALO : HALO + CHUNK], moved


def fill_padded(raw_ref, pad_ref, width):
    pad_ref[0:HALO, :] = jnp.zeros((HALO, width), WIDE)
    total = raw_ref.shape[0]

    def copy(index, _):
        start = pl.multiple_of(index * CHUNK, CHUNK)
        pad_ref[pl.ds(start + HALO, CHUNK), :] = raw_ref[pl.ds(start, CHUNK), 0:width].astype(WIDE)
        return 0

    lax.fori_loop(0, total // CHUNK, copy, 0)


def forward_kernel(heads, width, raw_ref, taps_ref, segcol_ref, poscol_ref, segrow_ref, edges_ref,
                   out_ref, q_ref, k_ref, inv_ref, score_ref, dots_ref, upd_ref, state_ref, move_ref,
                   pad_ref, v_ref, base_ref, w_ref):
    total = raw_ref.shape[0]
    count = total // CHUNK
    span = heads * width
    fill_padded(raw_ref, pad_ref, 3 * span)

    def first(index, _):
        start = pl.multiple_of(index * CHUNK, CHUNK)
        rows = pl.ds(start, CHUNK)
        pos = poscol_ref[rows, :]
        before, after = edges_ref[index, 0], edges_ref[index, 1]
        strict, inclusive, carried, last = chunk_masks(
            segcol_ref[rows, :], segrow_ref[pl.ds(index, 1), :], before, after)
        keep = jnp.where(before == after, 1.0, 0.0).astype(WIDE)
        for head in range(heads):
            cols = pl.ds(head * width, width)
            parts = []
            for which in range(3):
                column = which * span + head * width
                value = conv_rows(pad_ref, taps_ref[which, :, head * width:(head + 1) * width], pos,
                                  start, column, width)[0]
                parts.append(value * jax.nn.sigmoid(value))
            query, key, value = parts
            query = query * lax.rsqrt(jnp.sum(query * query, axis=-1, keepdims=True) + unit_eps)
            key = key * lax.rsqrt(jnp.sum(key * key, axis=-1, keepdims=True) + unit_eps)
            q_ref[rows, cols] = query
            k_ref[rows, cols] = key
            beta = jax.nn.sigmoid(raw_ref[rows, 3 * span + head:3 * span + head + 1].astype(WIDE))
            key_h, query_h = halves(key), halves(query)
            dots = product(key_h, key_h, 1, 1)
            score = jnp.where(inclusive, product(query_h, key_h, 1, 1), 0.0)
            inverse = unit_lower_inverse(jnp.where(strict, beta * dots, 0.0))
            inv_h = halves(inverse)
            base = product(inv_h, halves(beta * value))
            carry = product(inv_h, halves((beta * carried) * key))
            tail = turned(last * key)
            eye = jnp.where(lax.broadcasted_iota(jnp.int32, (width, width), 0)
                            == lax.broadcasted_iota(jnp.int32, (width, width), 1), keep, 0.0)
            at = index * heads + head
            dots_ref[at] = dots
            score_ref[at] = score
            inv_ref[at] = inverse
            base_ref[rows, cols] = base
            w_ref[rows, cols] = carry
            move_ref[at] = eye - product(tail, halves(carry))
            state_ref[at] = product(tail, halves(base))
        return 0

    lax.fori_loop(0, count, first, 0)

    def second(index, states):
        result = []
        for head in range(heads):
            at = index * heads + head
            added = state_ref[at]
            state_ref[at] = states[head]
            result.append(product(halves(move_ref[at]), halves(states[head])) + added)
        return tuple(result)

    lax.fori_loop(0, count, second, tuple(jnp.zeros((width, width), WIDE) for _ in range(heads)))

    def third(index, _):
        rows = pl.ds(pl.multiple_of(index * CHUNK, CHUNK), CHUNK)
        carried = jnp.where(segcol_ref[rows, :] == edges_ref[index, 0], 1.0, 0.0).astype(WIDE)
        for head in range(heads):
            cols = pl.ds(head * width, width)
            at = index * heads + head
            state = halves(state_ref[at])
            update = base_ref[rows, cols] - product(halves(w_ref[rows, cols]), state)
            upd_ref[rows, cols] = update
            out = carried * product(halves(q_ref[rows, cols]), state)
            out = out + product(halves(score_ref[at]), halves(update))
            out_ref[rows, cols] = out.astype(out_ref.dtype)
        return 0

    lax.fori_loop(0, count, third, 0)


def backward_kernel(heads, width, raw_ref, taps_ref, segcol_ref, poscol_ref, segrow_ref, edges_ref,
                    q_ref, k_ref, inv_ref, score_ref, dots_ref, upd_ref, state_ref, move_ref, dout_ref,
                    draw_ref, dtaps_ref,
                    pad_ref, grad_ref, pdo_ref, dconv_ref):
    total = raw_ref.shape[0]
    count = total // CHUNK
    span = heads * width
    fill_padded(raw_ref, pad_ref, 3 * span)

    def beta_of(rows, head):
        return jax.nn.sigmoid(raw_ref[rows, 3 * span + head:3 * span + head + 1].astype(WIDE))

    def first(index, _):
        rows = pl.ds(pl.multiple_of(index * CHUNK, CHUNK), CHUNK)
        carried = jnp.where(segcol_ref[rows, :] == edges_ref[index, 0], 1.0, 0.0).astype(WIDE)
        for head in range(heads):
            cols = pl.ds(head * width, width)
            at = index * heads + head
            dout = (dout_ref[rows, cols],)
            dout = (dout[0], jnp.zeros_like(dout[0]))
            score_t = turned(score_ref[at])
            back = product_exact(score_t, dout[0])
            pdo_ref[rows, cols] = back
            inv_t = turned(inv_ref[at])
            back = product(inv_t, halves(back))
            query_t = turned(carried * q_ref[rows, cols])
            key_t = turned((beta_of(rows, head) * carried) * k_ref[rows, cols])
            grad_ref[at] = product_exact(query_t, dout[0]) - product(key_t, halves(back))
        return 0

    lax.fori_loop(0, count, first, 0)

    def second(step, grads):
        index = count - 1 - step
        result = []
        for head in range(heads):
            at = index * heads + head
            added = grad_ref[at]
            grad_ref[at] = grads[head]
            result.append(product(turned(move_ref[at]), halves(grads[head])) + added)
        return tuple(result)

    lax.fori_loop(0, count, second, tuple(jnp.zeros((width, width), WIDE) for _ in range(heads)))
    dconv_ref[total:total + HALO, :] = jnp.zeros((HALO, 3 * span), WIDE)

    def third(index, tap_sums):
        start = pl.multiple_of(index * CHUNK, CHUNK)
        rows = pl.ds(start, CHUNK)
        pos = poscol_ref[rows, :]
        strict, inclusive, carried, last = chunk_masks(
            segcol_ref[rows, :], segrow_ref[pl.ds(index, 1), :], edges_ref[index, 0], edges_ref[index, 1])
        new_sums = []
        dbetas = []
        for head in range(heads):
            cols = pl.ds(head * width, width)
            at = index * heads + head
            beta = beta_of(rows, head)
            query, key, update = q_ref[rows, cols], k_ref[rows, cols], upd_ref[rows, cols]
            query_h, key_h, update_h = halves(query), halves(key), halves(update)
            dout = dout_ref[rows, cols]
            state, grad = halves(state_ref[at]), halves(grad_ref[at])
            convs = []
            for which in range(3):
                column = which * span + head * width
                convs.append(conv_rows(pad_ref, taps_ref[which, :, head * width:(head + 1) * width], pos,
                                       start, column, width))
            gates = [jax.nn.sigmoid(c[0]) for c in convs]
            value = convs[2][0] * gates[2]
            dupdate = pdo_ref[rows, cols] + last * product(key_h, grad)
            dright = product(turned(inv_ref[at]), halves(dupdate))
            dright_h = halves(dright)
            dscore = jnp.where(inclusive, product_exact(update_h, dout, 1, 1, flip=True), 0.0)
            dsystem = jnp.where(strict, product(dright_h, update_h, 1, 1), 0.0)
            dscore_h = halves(dscore)
            dquery = carried * product_exact(state, dout, 1, 1, flip=True) + product(dscore_h, key_h)
            weighted = beta * dsystem
            scaled = beta * carried
            dkey = product(turned(dscore), query_h) + last * product(update_h, grad, 1, 1)
            dkey = dkey - product(halves(weighted + weighted.T), key_h)
            dkey = dkey - scaled * product(dright_h, state, 1, 1)
            dvalue = beta * dright
            seen = carried * product(key_h, state)
            dbeta = jnp.sum(dright * (value - seen), axis=-1, keepdims=True) - jnp.sum(
                dsystem * dots_ref[at], axis=-1, keepdims=True)
            dbetas.append(dbeta * beta * (1.0 - beta))
            sides = []
            for grads, unit, conv, gate in ((dquery, query, convs[0][0], gates[0]), (dkey, key, convs[1][0], gates[1])):
                plain = conv * gate
                inv_norm = lax.rsqrt(jnp.sum(plain * plain, axis=-1, keepdims=True) + unit_eps)
                sides.append(inv_norm * (grads - unit * jnp.sum(unit * grads, axis=-1, keepdims=True)))
            sides.append(dvalue)
            for which in range(3):
                conv, plain, moved = convs[which]
                gate = gates[which]
                dconv = sides[which] * gate * (1.0 + conv * (1.0 - gate))
                column = which * span + head * width
                dconv_ref[rows, pl.ds(column, width)] = dconv
                sums = [jnp.sum(dconv * plain, axis=0, keepdims=True)]
                for shifted in moved:
                    sums.append(jnp.sum(dconv * shifted, axis=0, keepdims=True))
                new_sums.append(jnp.concatenate(sums[::-1], axis=0))
        lane = lax.broadcasted_iota(jnp.int32, (CHUNK, draw_ref.shape[1] - 3 * span), 1)
        packed = jnp.zeros(lane.shape, WIDE)
        for head in range(heads):
            packed = jnp.where(lane == head, dbetas[head], packed)
        draw_ref[rows, pl.ds(3 * span, lane.shape[1])] = packed.astype(draw_ref.dtype)
        return tuple(old + new for old, new in zip(tap_sums, new_sums))

    zero = tuple(jnp.zeros((taps_ref.shape[1], width), WIDE) for _ in range(3 * heads))
    sums = lax.fori_loop(0, count, third, zero)
    for head in range(heads):
        for which in range(3):
            dtaps_ref[which, :, head * width:(head + 1) * width] = sums[head * 3 + which]
    taps_count = taps_ref.shape[1]

    def fourth(index, _):
        start = pl.multiple_of(index * CHUNK, CHUNK)
        pos_window = poscol_ref[pl.ds(start, CHUNK + HALO), :]
        for which in range(3):
            columns = pl.ds(which * span, span)
            window = dconv_ref[pl.ds(start, CHUNK + HALO), columns]
            result = taps_ref[which, taps_count - 1:taps_count, :] * window[0:CHUNK]
            for offset in range(1, taps_count):
                part = jnp.where(pos_window >= offset, window, 0.0)[offset:offset + CHUNK]
                result = result + taps_ref[which, taps_count - 1 - offset:taps_count - offset, :] * part
            draw_ref[pl.ds(start, CHUNK), columns] = result.astype(draw_ref.dtype)
        return 0

    lax.fori_loop(0, count, fourth, 0)


def product_exact(left, exact, left_dim=1, right_dim=0, flip=False):
    def one(a):
        if flip:
            return lax.dot_general(exact, a, (((right_dim,), (left_dim,)), ((), ())), preferred_element_type=WIDE)
        return lax.dot_general(a, exact, (((left_dim,), (right_dim,)), ((), ())), preferred_element_type=WIDE)

    if PASSES == 1:
        return one(left[0])
    return one(left[0]) + one(left[1])


def cost(flops, size):
    return pl.CostEstimate(flops=flops, bytes_accessed=size, transcendentals=0)


def delta_forward(raw, taps, segcol, poscol, segrow, edges, heads, width):
    total, lanes = raw.shape
    count = total // CHUNK
    span = heads * width
    vm = pl.BlockSpec(memory_space=pltpu.VMEM)
    sm = pl.BlockSpec(memory_space=pltpu.SMEM)
    rows = jax.ShapeDtypeStruct((total, span), WIDE)
    square = jax.ShapeDtypeStruct((count * heads, CHUNK, CHUNK), WIDE)
    state = jax.ShapeDtypeStruct((count * heads, width, width), WIDE)
    return pl.pallas_call(
        lambda *refs: forward_kernel(heads, width, *refs),
        out_shape=(jax.ShapeDtypeStruct((total, span), NARROW), rows, rows, square, square, square, rows, state, state),
        in_specs=[vm, vm, vm, vm, vm, sm],
        out_specs=(vm,) * 9,
        scratch_shapes=[
            pltpu.VMEM((total + HALO, 3 * span), WIDE),
            pltpu.VMEM((8, 128), WIDE),
            pltpu.VMEM((total, span), WIDE),
            pltpu.VMEM((total, span), WIDE),
        ],
        compiler_params=pltpu.CompilerParams(vmem_limit_bytes=48 << 20),
        cost_estimate=cost(40_000_000_000, 4 << 20),
        name="delta_forward",
    )(raw, taps, segcol, poscol, segrow, edges)


def delta_backward(raw, taps, segcol, poscol, segrow, edges, kept, dout, heads, width):
    total, lanes = raw.shape
    count = total // CHUNK
    span = heads * width
    vm = pl.BlockSpec(memory_space=pltpu.VMEM)
    sm = pl.BlockSpec(memory_space=pltpu.SMEM)
    poscol = jnp.pad(poscol, ((0, HALO), (0, 0)))
    return pl.pallas_call(
        lambda *refs: backward_kernel(heads, width, *refs),
        out_shape=(jax.ShapeDtypeStruct((total, lanes), NARROW), jax.ShapeDtypeStruct(taps.shape, WIDE)),
        in_specs=[vm, vm, vm, vm, vm, sm] + [vm] * 9,
        out_specs=(vm, vm),
        scratch_shapes=[
            pltpu.VMEM((total + HALO, 3 * span), WIDE),
            pltpu.VMEM((count * heads, width, width), WIDE),
            pltpu.VMEM((total, span), WIDE),
            pltpu.VMEM((total + HALO, 3 * span), WIDE),
        ],
        compiler_params=pltpu.CompilerParams(vmem_limit_bytes=48 << 20),
        cost_estimate=cost(60_000_000_000, 4 << 20),
        name="delta_backward",
    )(raw, taps, segcol, poscol, segrow, edges, *kept, dout)


def rms_scale(values, gain):
    return values * lax.rsqrt(jnp.mean(values * values, axis=-1, keepdims=True) + norm_eps) * gain


def gated_norm(mixed_rows, gate_proj, gain):
    count, width = mixed_rows.shape
    split = mixed_rows.reshape(count, width // gain.shape[0], gain.shape[0])
    normed = split * lax.rsqrt(jnp.mean(split * split, axis=-1, keepdims=True) + norm_eps) * gain
    return normed.reshape(count, width) * jax.nn.silu(gate_proj)


def swiglu(gate_proj, up_proj):
    return jax.nn.silu(gate_proj) * up_proj


def sequence_layout(lengths_row, total):
    ends = jnp.cumsum(lengths_row)
    index = jnp.arange(total, dtype=jnp.int32)
    before = index[:, None] >= ends[None, :]
    segment = jnp.sum(before.astype(jnp.int32), axis=1)
    start = jnp.sum(jnp.where(before, lengths_row[None, :], 0), axis=1)
    return (segment, index - start)


def project(left, right):
    return jnp.dot(left, right, preferred_element_type=WIDE)


def project_back(left, right):
    return lax.dot_general(left, right, (((1,), (1,)), ((), ())), preferred_element_type=WIDE)


def weight_grad(left, right):
    return lax.dot_general(left, right, (((0,), (0,)), ((), ())), preferred_element_type=WIDE)


def flip(value, bit, n_dp):
    return lax.ppermute(value, "dp", [(i, i ^ bit) for i in range(n_dp)])


def shift(value, by, n_fs):
    return lax.ppermute(value, "fsdp", [(i, (i + by) % n_fs) for i in range(n_fs)])


def gather_line(shard, z, n_fs):
    rows = shard.shape[0]
    whole = jnp.zeros((n_fs * rows,) + shard.shape[1:], shard.dtype)
    whole = lax.dynamic_update_slice_in_dim(whole, shard, z * rows, 0)
    for by in range(1, n_fs):
        place = lax.rem(z + n_fs - by, n_fs) * rows
        whole = lax.dynamic_update_slice_in_dim(whole, shift(shard, by, n_fs), place, 0)
    return whole


def gather_cube(piece, order, n_dp):
    pieces = {0: piece}
    for bit in order:
        for key in list(pieces):
            pieces[key ^ bit] = flip(pieces[key], bit, n_dp)
    return pieces


def in_order(pieces, me, columns=slice(None)):
    rows = pieces[0].shape[0]
    whole = None
    for key, piece in pieces.items():
        part = piece[:, columns]
        if whole is None:
            whole = jnp.zeros((len(pieces) * rows, part.shape[1]), part.dtype)
        whole = lax.dynamic_update_slice_in_dim(whole, part, (me ^ key) * rows, 0)
    return whole


def exchange_rows(value, z, n_fs):
    rows = value.shape[0] // n_fs
    total = lax.dynamic_slice_in_dim(value, z * rows, rows, 0)
    for by in range(1, n_fs):
        block = lax.dynamic_slice_in_dim(value, lax.rem(z + by, n_fs) * rows, rows, 0)
        total = total + shift(block.astype(NARROW), by, n_fs).astype(WIDE)
    return total


def scatter_cube(left, right, order, me, n_dp):
    keys = sorted(range(n_dp), key=lambda key: tuple((key & bit) != 0 for bit in order))
    arrived = []
    keep = n_dp
    rows = left.shape[2]

    def term(lo, hi):
        blocks = [lax.dynamic_index_in_dim(left, me ^ key, 0, keepdims=False) for key in keys[lo:hi]]
        stacked = jnp.concatenate(blocks, axis=1) if len(blocks) > 1 else blocks[0]
        value = weight_grad(stacked, right)
        for earlier in arrived:
            value = value + earlier[lo * rows : hi * rows].astype(WIDE)
        return value

    for bit in order:
        keep //= 2
        arrived.append(flip(term(keep, 2 * keep).astype(NARROW), bit, n_dp))
    return term(0, 1)


def column_blocks(value, count):
    tokens = value.shape[0]
    return jnp.swapaxes(value.reshape(tokens, count, -1), 0, 1)


def per_device(
    n_dp,
    n_fs,
    tokens,
    lengths,
    packing,
    w_query,
    w_key,
    w_value,
    w_gate,
    w_beta,
    conv_taps,
    w_out,
    gain_mix,
    gain_head,
    gain_ffn,
    w_ffn_gate,
    w_ffn_up,
    w_ffn_down,
    cotangent,
):
    me = lax.axis_index("dp")
    z = lax.axis_index("fsdp")
    bits = [1 << k for k in range(n_dp.bit_length() - 1)]
    first_order = bits[:1] + bits[1:]
    second_order = bits[:1] + bits[1:][::-1]
    packing_row = packing[0]
    lengths_row = lengths[0]
    own_rows, features = tokens.shape
    total = own_rows * n_fs
    rows = w_query.shape[0]
    heads_all = w_beta.shape[1]
    heads = heads_all // n_fs
    span = features // n_fs
    width = span // heads
    hidden_ffn = w_ffn_gate.shape[1]
    head_rows = gain_head.shape[0]
    n_taps = conv_taps.shape[1]

    def by_owner(matrix):
        return jnp.swapaxes(matrix.reshape(rows, n_fs, -1), 0, 1)

    small = jnp.concatenate(
        [
            gain_mix[:, None],
            gain_ffn[:, None],
            conv_taps.reshape(3 * n_taps, rows).T,
            jnp.pad(gain_head, (0, rows - head_rows))[:, None],
        ],
        axis=1,
    )
    n_small = small.shape[1]
    side = jnp.concatenate(
        [by_owner(w_beta), jnp.broadcast_to(small[None], (n_fs, rows, n_small))], axis=2
    )
    side = jnp.pad(side, ((0, 0), (0, 0), (0, 128 - heads - n_small)))
    packet = jnp.concatenate([by_owner(w_query), by_owner(w_key), by_owner(w_value), side], axis=2)
    packet = lax.all_to_all(packet, "fsdp", split_axis=0, concat_axis=0, tiled=True)
    packet = packet.reshape(n_fs * rows, 3 * span + 128)
    w_in = in_order(gather_cube(packet, first_order[::-1], n_dp), me)
    side_rows = w_in[:, 3 * span :].astype(WIDE).T
    full_gmix = side_rows[heads]
    full_gffn = side_rows[heads + 1]
    local_taps = lax.dynamic_slice_in_dim(
        side_rows[heads + 2 : heads + 2 + 3 * n_taps], z * span, span, 1
    ).reshape(3, n_taps, span)
    full_ghead = side_rows[heads + 2 + 3 * n_taps].reshape(-1, rows)[:, :head_rows].reshape(-1)

    tokens_near = jnp.concatenate([tokens] + [shift(tokens, by, n_fs) for by in range(1, n_fs)], axis=0)
    near_index = lax.rem(z + n_fs - packing_row // own_rows, n_fs) * own_rows + lax.rem(packing_row, own_rows)
    places = jnp.arange(total, dtype=jnp.int32)
    pick_near = (near_index[:, None] == places[None, :]).astype(NARROW)
    pick = (packing_row[:, None] == places[None, :]).astype(NARROW)
    packed = project(pick_near, tokens_near)
    packed_unit = packed * lax.rsqrt(jnp.mean(packed * packed, axis=-1, keepdims=True) + norm_eps)
    hidden_p = (packed_unit * full_gmix).astype(NARROW)
    raw = project(hidden_p, w_in).astype(NARROW)

    segment, position = sequence_layout(lengths_row, total)
    seg_rows = segment.reshape(-1, CHUNK)
    ends = seg_rows[:, -1]
    edges = jnp.stack([jnp.concatenate([jnp.full((1,), -1, jnp.int32), ends[:-1]]), ends], axis=1)
    layout = (segment[:, None], position[:, None], seg_rows, edges)
    forward = delta_forward(raw, local_taps, *layout, heads, width)
    mixed_packed, kept = forward[0], forward[1:]

    pair = gather_cube(
        gather_line(jnp.concatenate([w_gate, w_out], axis=1), z, n_fs), second_order[::-1], n_dp
    )
    full_gate = in_order(pair, me, slice(0, features))
    full_out = in_order(pair, me, slice(features, None))
    full_both = in_order(
        gather_cube(
            gather_line(jnp.concatenate([w_ffn_gate, w_ffn_up], axis=1), z, n_fs),
            first_order[::-1],
            n_dp,
        ),
        me,
    )
    full_down = in_order(gather_cube(gather_line(w_ffn_down, z, n_fs), second_order[::-1], n_dp), me)

    inputs_f = tokens.astype(WIDE)
    hidden, norm_mix_back = jax.vjp(rms_scale, inputs_f, full_gmix)
    hidden_b = hidden.astype(NARROW)
    gate_proj = project(hidden_b, full_gate)
    mixed_arrived = weight_grad(pick, mixed_packed).astype(NARROW)
    mixed = lax.all_to_all(mixed_arrived, "fsdp", split_axis=0, concat_axis=1, tiled=True)
    normed, gated_back = jax.vjp(gated_norm, mixed.astype(WIDE), gate_proj, full_ghead)
    normed_b = normed.astype(NARROW)
    middle = inputs_f + project(normed_b, full_out)
    ffn_in, norm_ffn_back = jax.vjp(rms_scale, middle, full_gffn)
    ffn_in_b = ffn_in.astype(NARROW)
    both = project(ffn_in_b, full_both)
    active, active_back = jax.vjp(swiglu, both[:, :hidden_ffn], both[:, hidden_ffn:])
    active_b = active.astype(NARROW)
    layer_out = (middle + project(active_b, full_down)).astype(NARROW)

    active_blocks = jnp.swapaxes(active_b.T.reshape(n_dp, hidden_ffn // n_dp, own_rows), 1, 2)
    sum_down = scatter_cube(active_blocks, cotangent, second_order, me, n_dp)
    grad_fdown = exchange_rows(sum_down, z, n_fs)
    d_active = project_back(cotangent, full_down)
    d_fgate, d_fup = active_back(d_active)
    d_both = jnp.concatenate([d_fgate.astype(NARROW), d_fup.astype(NARROW)], axis=1)
    d_ffn_in = project_back(d_both, full_both)
    d_middle_norm, d_gffn = norm_ffn_back(d_ffn_in)
    d_middle = cotangent.astype(WIDE) + d_middle_norm
    d_branch = d_middle.astype(NARROW)
    d_normed = project_back(d_branch, full_out)
    d_mixed, d_gate_proj, d_ghead = gated_back(d_normed)
    d_gate_b = d_gate_proj.astype(NARROW)
    d_mixed_arrived = lax.all_to_all(
        d_mixed.astype(NARROW), "fsdp", split_axis=1, concat_axis=0, tiled=True
    )
    d_mixed_packed = project(pick, d_mixed_arrived).astype(NARROW)
    sum_both = scatter_cube(column_blocks(ffn_in_b, n_dp), d_both, first_order, me, n_dp)
    grad_both = exchange_rows(sum_both, z, n_fs)
    sum_out = scatter_cube(column_blocks(normed_b, n_dp), d_branch, second_order, me, n_dp)
    grad_wout = exchange_rows(sum_out, z, n_fs)
    sum_gate = scatter_cube(column_blocks(hidden_b, n_dp), d_gate_b, second_order, me, n_dp)
    grad_wgate = exchange_rows(sum_gate, z, n_fs)

    d_raw, d_taps = delta_backward(raw, local_taps, *layout, kept, d_mixed_packed, heads, width)
    d_hidden_packed = project_back(d_raw, w_in)
    d_hidden_group = weight_grad(pick, d_hidden_packed.astype(NARROW))
    d_hidden_gate = project_back(d_gate_b, full_gate)
    d_hidden = exchange_rows(d_hidden_group, z, n_fs) + d_hidden_gate
    d_inputs_norm, _ = norm_mix_back(d_hidden)
    grad_tokens = d_middle + d_inputs_norm
    own_unit = inputs_f * lax.rsqrt(jnp.mean(inputs_f * inputs_f, axis=-1, keepdims=True) + norm_eps)
    d_gmix = jnp.sum(d_hidden_packed * packed_unit, axis=0) + jnp.sum(d_hidden_gate * own_unit, axis=0)

    grad_in = weight_grad(hidden_p, d_raw)
    taps_rows = lax.dynamic_update_slice_in_dim(
        jnp.zeros((3 * n_taps, features), WIDE), d_taps.reshape(3 * n_taps, span), z * span, 1
    )
    ghead_row = jnp.pad(d_ghead.reshape(-1, head_rows), ((0, 0), (0, rows - head_rows))).reshape(1, features)
    small_rows = jnp.concatenate([d_gmix[None], d_gffn[None], taps_rows, ghead_row], axis=0)
    small_grads = jnp.pad(small_rows.T, ((0, 0), (heads, 128 - heads - n_small)))
    grad_in = jnp.concatenate([grad_in[:, : 3 * span], grad_in[:, 3 * span :] + small_grads], axis=1)
    part = grad_in.reshape(n_dp, n_fs * rows, 3 * span + 128)
    keys = sorted(range(n_dp), key=lambda key: tuple((key & bit) != 0 for bit in first_order))
    part = jnp.stack([lax.dynamic_index_in_dim(part, me ^ key, 0, keepdims=False) for key in keys])
    for bit in first_order:
        keep = part.shape[0] // 2
        part = part[:keep] + flip(part[keep:].astype(NARROW), bit, n_dp).astype(WIDE)
    part = part.reshape(n_fs, rows, 3 * span + 128)
    part = lax.all_to_all(part, "fsdp", split_axis=0, concat_axis=0, tiled=True)

    def columns_of(which):
        return jnp.swapaxes(part[:, :, which * span : (which + 1) * span], 0, 1).reshape(rows, features)

    grad_beta = jnp.swapaxes(part[:, :, 3 * span : 3 * span + heads], 0, 1).reshape(rows, heads_all)
    small_sum = jnp.sum(part[:, :, 3 * span + heads : 3 * span + heads + n_small], axis=0)
    grad_taps = small_sum[:, 2 : 2 + 3 * n_taps].T.reshape(3, n_taps, rows)
    return (
        layer_out,
        grad_tokens,
        columns_of(0),
        columns_of(1),
        columns_of(2),
        grad_wgate,
        grad_beta,
        grad_taps,
        grad_wout,
        small_sum[:, 0],
        small_sum[:head_rows, 2 + 3 * n_taps],
        small_sum[:, 1],
        grad_both[:, :hidden_ffn],
        grad_both[:, hidden_ffn:],
        grad_fdown,
    )


def solution(mesh):
    both = ("dp", "fsdp")
    rows = P(both, None)
    group = P("dp", None)
    taps = P(None, None, both)
    line = P(both)
    in_specs = (rows, group, group) + (rows,) * 5 + (taps, rows, line, line, line) + (rows,) * 4
    out_specs = (rows,) * 7 + (taps, rows, line, line, line) + (rows,) * 3
    return jax.shard_map(
        functools.partial(per_device, mesh.shape["dp"], mesh.shape["fsdp"]),
        mesh=mesh,
        in_specs=in_specs,
        out_specs=out_specs,
        check_vma=False,
    )
```

time: 2980 us -> 700 us (0.23)
  waiting for transfers between devices: 1600 us -> 276 us
  other arithmetic: 502 us -> 25.5 us
  blocking collectives: 263 us -> 0 us
  matrix products: 313 us -> 101 us
  local copies, waits for them, and re-layouts: 220 us -> 134 us
  Pallas kernels: 0 us -> 83.5 us
    reduce_scatter x8 -> x0, waiting for transfers between devices: 1440 us -> none  [the longest x1 256 us: per_device(): lax.psum_scatter(ffn_terms[0], ('dp', 'fsdp'), scatter_dimension=0, tiled...]
    another operation x145 -> x4, other arithmetic: 318 us -> 0.47 us  [the longest x128 318 us: block_step(): jax.scipy.linalg.solve_triangular(system, right_side, lower=True, unit_di...]
    ppermute x0 -> x70, waiting for transfers between devices: none -> 265 us  [the longest x43 134 us: flip(): return lax.ppermute(value, 'dp', [(i, i ^ bit) for i in range(n_dp)])]
    dot_general x361 -> x7, matrix products: 232 us -> 29.1 us  [project(): return jnp.dot(left, right, preferred_element_type=WIDE)]
    unnamed x20 -> x0, waiting for transfers between devices: 144 us -> none
    all_gather x2 -> x0, blocking collectives: 137 us -> none  [the longest x1 75.8 us: per_device(): lax.all_gather(conv_taps, ('dp', 'fsdp'), axis=2, tiled=True)]
    unnamed x2 -> x0, blocking collectives: 88.4 us -> none
    pallas_call x0 -> x2, Pallas kernels: none -> 83.5 us  [the longest x1 52.6 us: delta_forward(): pl.pallas_call(lambda *refs: forward_kernel(heads, width, *refs), out_sha...]
  transfers between devices with their start and end apart: 25 -> 74, of which waited for: 12 -> 28; matrix products, arithmetic and copies ran while one was open for 19% -> 26% of each run, Pallas kernels for 0% -> 8%
where the time goes in v1:
time: 700 us; the launch traced here: 694 us
  waiting for transfers between devices  276 us (39%)
  local copies, waits for them, and re-layouts  134 us (19%)
  matrix products  101 us (14%)
  Pallas kernels  83.5 us (12%)
  starting transfers between devices  71.1 us (10%)
  other arithmetic  25.5 us (4%)
    ppermute x43, waiting for transfers between devices, flip(): return lax.ppermute(value, 'dp', [(i, i ^ bit) for i in range(n_dp)])  134 us
    ppermute x27, waiting for transfers between devices, shift(): lax.ppermute(value, 'fsdp', [(i, (i + by) % n_fs) for i in range(n_fs)])  131 us
    pallas_call x1, Pallas kernels, delta_forward(): pl.pallas_call(lambda *refs: forward_kernel(heads, width, *refs), out_sha...  52.6 us
    dynamic_update_slice x33, local copies, waits for them, and re-layouts, in_order(): whole = lax.dynamic_update_slice_in_dim(whole, part, (me ^ key) * rows, 0)  44.9 us
    dot_general x19, matrix products, weight_grad(): lax.dot_general(left, right, (((0,), (0,)), ((), ())), preferred_element_...  43 us
    ppermute x43, starting transfers between devices, flip(): return lax.ppermute(value, 'dp', [(i, i ^ bit) for i in range(n_dp)])  32 us
    pallas_call x1, Pallas kernels, delta_backward(): pl.pallas_call(lambda *refs: backward_kernel(heads, width, *refs), out_sh...  30.9 us
    dot_general x7, matrix products, project(): return jnp.dot(left, right, preferred_element_type=WIDE)  29.1 us
  transfers between devices with their start and end apart: 74, of which 28 were waited for; matrix products, arithmetic and copies ran while one was open for 26% of the time, Pallas kernels for 8%

profile of v1, /device:TPU:9, one launch (start us, length us, event | category | flops | bytes accessed | tf_op | source)
XLA Modules:
  0.0 694.0 jit_solution(16798239237557132182)
XLA Ops:
  9.3 3.1 collective-permute-start.11
  20.0 3.4 all-to-all-start
  28.7 17.9 %collective-permute-done.10 = bf16[32,2048]{1,0:T(8,128)(2,1)} collective-permute-done((bf16[32,2048]{1,0:T(8,128)(2,1)S(1)}, bf16[32,2048]{1,0:T(8,128)(2,1)}, u32[]{:S(2)}, u32[]{:S(2)}) %collective-permute-start.10) | collective-permute-done | bytes 131104 | tf_op jit(solution)/shard_map/ppermute | solution.py:409
  49.9 3.9 collective-permute-done.12
  59.1 6.3 collective-permute-done.31
  65.4 4.3 collective-permute-done.32
  69.7 3.2 broadcast_in_dim.89
  83.9 5.0 broadcast_in_dim.87
  88.9 2.6 constant_dynamic-update-slice_fusion.20
  91.7 20.4 %collective-permute-done.1 = bf16[256,1024]{1,0:T(8,128)(2,1)} collective-permute-done((bf16[256,1024]{1,0:T(8,128)(2,1)S(1)}, bf16[256,1024]{1,0:T(8,128)(2,1)}, u32[]{:S(2)}, u32[]{:S(2)}) %collective-permute-start.1) | collective-permute-done | bytes 524320 | tf_op jit(solution)/shard_map/ppermute | solution.py:409
  115.6 5.6 multiply_reduce_fusion.1
  134.8 9.8 %collective-permute-done.5 = bf16[128,896]{1,0:T(8,128)(2,1)S(1)} collective-permute-done((bf16[128,896]{1,0:T(8,128)(2,1)}, bf16[128,896]{1,0:T(8,128)(2,1)S(1)}, u32[]{:S(2)}, u32[]{:S(2)}) %collective-permute-start.5) | collective-permute-done | bytes 229408 | tf_op jit(solution)/shard_map/ppermute | solution.py:405
  158.8 6.4 convolution_convert_fusion.2.refs_0_
  165.2 52.6 %delta_forward.1 = (bf16[1024,256]{1,0:T(8,128)(2,1)S(1)}, f32[1024,256]{1,0:T(8,128)S(1)}, f32[1024,256]{1,0:T(8,128)S(1)}, f32[16,128,128]{2,1,0:T(8,128)S(1)}...) custom-call(bf16[1024,896]{1,0:T(8,128)(2,1)} %convolution_convert_f, ...), custom_call_target="tpu_custom_call" | custom-call | flops 40000000000 | bytes 4194304 | tf_op jit(solution)/shard_map/delta_forward/pallas_call | solution.py:327
  222.1 5.7 all-to-all-start.1
  237.1 11.4 %collective-permute-done.35 = bf16[352,1024]{1,0:T(8,128)(2,1)} collective-permute-done((bf16[352,1024]{1,0:T(8,128)(2,1)}, bf16[352,1024]{1,0:T(8,128)(2,1)}, u32[]{:S(2)}, u32[]{:S(2)}) %collective-permute-start.35) | collective-permute-done | bytes 720928 | tf_op jit(solution)/shard_map/ppermute | solution.py:405
  258.7 2.6 constant_dynamic-update-slice_fusion.19
  261.2 19.9 %collective-permute-done.24 = bf16[128,5632]{1,0:T(8,128)(2,1)} collective-permute-done((bf16[128,5632]{1,0:T(8,128)(2,1)}, bf16[128,5632]{1,0:T(8,128)(2,1)}, u32[]{:S(2)}, u32[]{:S(2)}) %collective-permute-start.24) | collective-permute-done | bytes 1441824 | tf_op jit(solution)/shard_map/ppermute | solution.py:405
  281.1 3.0 collective-permute-start.28
  284.2 2.6 constant_dynamic-update-slice_fusion.18
  289.8 4.4 multiply_convert_fusion.4
  294.1 3.4 multiply_reduce_fusion.6
  297.5 2.4 constant_dynamic-update-slice_fusion.1
  300.0 12.0 %collective-permute-done.25 = bf16[128,5632]{1,0:T(8,128)(2,1)} collective-permute-done((bf16[128,5632]{1,0:T(8,128)(2,1)}, bf16[128,5632]{1,0:T(8,128)(2,1)}, u32[]{:S(2)}, u32[]{:S(2)}) %collective-permute-start.25) | collective-permute-done | bytes 1441824 | tf_op jit(solution)/shard_map/ppermute | solution.py:405
  320.0 3.2 fusion.130
  324.2 8.7 %fusion.6 = (bf16[256,2816]{1,0:T(8,128)(2,1)S(1)}, bf16[256,2816]{1,0:T(8,128)(2,1)}, bf16[256,2816]{1,0:T(8,128)(2,1)}) fusion(f32[256,5632]{1,0:T(8,128)S(1)} %fusion.130, bf16[2816,1024]{1,0:T(8,128)(2,1)} %constant_dynamic-update-slice_fusion.1, bf16[256,1024]{1,0:T(8,128)(2,1)S(1)} %copy-done.29), kind=kOutput, calls=%fused_computation.17 | convolution fusion | flops 1487929344 | bytes 16384000 | tf_op jit(solution)/shard_map/dot_general | solution.py:397
  333.0 7.3 %multiply_reduce_fusion.3 = (f32[1024]{0:T(1024)S(1)}, f32[256]{0:T(256)S(1)}, f32[256,1024]{1,0:T(8,128)S(1)}) fusion(f32[256,1024]{1,0:T(8,128)S(1)} %get-tuple-element.150, f32[256]{0:T(256)S(1)} %fusion.119, f32[1024]{0:T(1024)S(1)} %bitcast.276, bf16[1024,5632]{1,0:T(8,128)(2,1)} %copy-done.7, bf16[256,2816]{1,0:T(8,128)(2,1)} %get-tuple-element.64, ...), kind=kOutput, calls=%fused_computation.75 | convolution fusion | flops 2960128768 | bytes 16525312 | tf_op jit(solution)/shard_map/dot_general | solution.py:397
  342.8 4.6 multiply_reduce_fusion.2
  347.4 2.5 copy.380
  351.9 2.5 fusion.28
  355.3 4.5 all-to-all-start.2
  359.9 11.3 %all-to-all-done.2 = bf16[256,4,256]{2,0,1:T(8,128)(2,1)S(1)} async-done(((bf16[256,4,256]{2,0,1:T(8,128)(2,1)}), bf16[256,4,256]{2,0,1:T(8,128)(2,1)S(1)}, u32[]{:S(2)}, u32[]{:S(2)}) %all-to-all-start.2) | async-done | bytes 524320 | tf_op jit(solution)/shard_map/all_to_all | solution.py:605
  375.7 30.9 %delta_backward.1 = (bf16[1024,896]{1,0:T(8,128)(2,1)}, f32[3,4,256]{2,1,0:T(4,128)S(1)}) custom-call(bf16[1024,896]{1,0:T(8,128)(2,1)} %convolution_convert_fusion.2.refs_0_, f32[3,4,256]{2,1,0:T(4,128)S(1)} %reshape.330.refs_1_, s32[1024,1]{1,0:T(8,128)S(1)} %copy.326.refs_2_, s32[1032,1]{1,0:T(8,128)S(1)} %pad.22.refs_3_, s32[8,128]{1,0:T(8,128)S(1)} %bitcast.240, ...), custom_call_target="tpu_custom_call" | custom-call | flops 60000002048 | bytes 4194304 | tf_op jit(solution)/shard_map/delta_backward/pallas_call | solution.py:351
  406.7 3.9 multiply_reduce_fusion
  410.6 2.6 fusion
  417.6 3.9 collective-permute-start.41
  421.9 8.9 %collective-permute-done.40 = bf16[256,1024]{1,0:T(8,128)(2,1)S(1)} collective-permute-done((bf16[256,1024]{1,0:T(8,128)(2,1)}, bf16[256,1024]{1,0:T(8,128)(2,1)S(1)}, u32[]{:S(2)}, u32[]{:S(2)}) %collective-permute-start.40) | collective-permute-done | bytes 524320 | tf_op jit(solution)/shard_map/ppermute | solution.py:409
  430.8 30.9 %collective-permute-done.41 = bf16[256,1024]{1,0:T(8,128)(2,1)S(1)} collective-permute-done((bf16[256,1024]{1,0:T(8,128)(2,1)}, bf16[256,1024]{1,0:T(8,128)(2,1)S(1)}, u32[]{:S(2)}, u32[]{:S(2)}) %collective-permute-start.41) | collective-permute-done | bytes 524320 | tf_op jit(solution)/shard_map/ppermute | solution.py:409
  461.7 4.4 collective-permute-done.42
  466.1 4.3 fusion.26
  472.2 3.1 constant_dynamic-slice_fusion.7
  475.5 4.2 convolution_convert_fusion
  484.5 2.5 convolution_convert_fusion.1
  487.2 2.7 fusion.74
  489.9 5.3 fusion.20
  507.2 5.3 copy.381
  520.9 4.5 add_convert_fusion
  534.1 3.1 add_convert_fusion.1
  537.4 3.5 collective-permute-done.53
  543.4 8.8 %collective-permute-done.47 = bf16[256,1024]{1,0:T(8,128)(2,1)S(1)} collective-permute-done((bf16[256,1024]{1,0:T(8,128)(2,1)S(1)}, bf16[256,1024]{1,0:T(8,128)(2,1)S(1)}, u32[]{:S(2)}, u32[]{:S(2)}) %collective-permute-start.47) | collective-permute-done | bytes 524320 | tf_op jit(solution)/shard_map/ppermute | solution.py:405
  554.6 2.4 collective-permute-done.45
  557.9 3.5 all-to-all-start.3
  561.4 38.8 %collective-permute-done.54 = bf16[128,1024]{1,0:T(8,128)(2,1)} collective-permute-done((bf16[128,1024]{1,0:T(8,128)(2,1)}, bf16[128,1024]{1,0:T(8,128)(2,1)}, u32[]{:S(2)}, u32[]{:S(2)}) %collective-permute-start.54) | collective-permute-done | bytes 262176 | tf_op jit(solution)/shard_map/ppermute | solution.py:405
  601.8 4.0 collective-permute-done.48
  611.0 2.9 collective-permute-done.50
  616.2 3.7 add_convert_fusion.2
  621.3 2.7 add_convert_fusion.3
  624.4 15.8 %collective-permute-done.66 = bf16[352,1024]{1,0:T(8,128)(2,1)} collective-permute-done((bf16[352,1024]{1,0:T(8,128)(2,1)}, bf16[352,1024]{1,0:T(8,128)(2,1)}, u32[]{:S(2)}, u32[]{:S(2)}) %collective-permute-start.66) | collective-permute-done | bytes 720928 | tf_op jit(solution)/shard_map/ppermute | solution.py:405
  640.2 2.4 convert_add_fusion.2
  645.8 6.0 collective-permute-done.60
  651.8 2.9 convert_add_fusion
  663.7 10.7 %collective-permute-done.69 = bf16[88,1024]{1,0:T(8,128)(2,1)} collective-permute-done((bf16[88,1024]{1,0:T(8,128)(2,1)S(1)}, bf16[88,1024]{1,0:T(8,128)(2,1)}, u32[]{:S(2)}, u32[]{:S(2)}) %collective-permute-start.69) | collective-permute-done | bytes 180256 | tf_op jit(solution)/shard_map/ppermute | solution.py:409
  676.4 11.5 %collective-permute-done.62 = bf16[32,5632]{1,0:T(8,128)(2,1)S(1)} collective-permute-done((bf16[32,5632]{1,0:T(8,128)(2,1)S(1)}, bf16[32,5632]{1,0:T(8,128)(2,1)S(1)}, u32[]{:S(2)}, u32[]{:S(2)}) %collective-permute-start.62) | collective-permute-done | bytes 360480 | tf_op jit(solution)/shard_map/ppermute | solution.py:409
  687.9 3.4 collective-permute-done.63
  (471 shorter events, 191.0 us)
Async XLA Ops:
  3.9 71.7 %collective-permute-start.20 = (bf16[32,5632]{1,0:T(8,128)(2,1)}, bf16[32,5632]{1,0:T(8,128)(2,1)}, u32[]{:S(2)}, u32[]{:S(2)}) collective-permute-start(bf16[32,5632]{1,0:T(8,128)(2,1)} %constant_dynamic-update-slice_fusion.39), channel_id=1, source_target_pairs={{0,1},{1,2},{2,3},{3,0},{4,5},{5,6},{6,7},{7,4},{8,9},{9,10},{10,1... | collective-permute-start | bytes 1081352 | tf_op jit(solution)/shard_map/ppermute | solution.py:409
  5.2 72.8 %collective-permute-start.21 = (bf16[32,5632]{1,0:T(8,128)(2,1)}, bf16[32,5632]{1,0:T(8,128)(2,1)}, u32[]{:S(2)}, u32[]{:S(2)}) collective-permute-start(bf16[32,5632]{1,0:T(8,128)(2,1)} %constant_dynamic-update-slice_fusion.39), channel_id=1, source_target_pairs={{0,2},{1,3},{2,0},{3,1},{4,6},{5,7},{6,4},{7,5},{8,10},{9,11},{10,... | collective-permute-start | bytes 1081352 | tf_op jit(solution)/shard_map/ppermute | solution.py:409
  6.2 74.8 %collective-permute-start.22 = (bf16[32,5632]{1,0:T(8,128)(2,1)}, bf16[32,5632]{1,0:T(8,128)(2,1)}, u32[]{:S(2)}, u32[]{:S(2)}) collective-permute-start(bf16[32,5632]{1,0:T(8,128)(2,1)} %constant_dynamic-update-slice_fusion.39), channel_id=1, source_target_pairs={{0,3},{1,0},{2,1},{3,2},{4,7},{5,4},{6,5},{7,6},{8,11},{9,8},{10,9... | collective-permute-start | bytes 1081352 | tf_op jit(solution)/shard_map/ppermute | solution.py:409
  9.3 37.2 %collective-permute-start.10 = (bf16[32,2048]{1,0:T(8,128)(2,1)S(1)}, bf16[32,2048]{1,0:T(8,128)(2,1)}, u32[]{:S(2)}, u32[]{:S(2)}) collective-permute-start(bf16[32,2048]{1,0:T(8,128)(2,1)S(1)} %constant_dynamic-update-slice_fusion.37), channel_id=1, source_target_pairs={{0,1},{1,2},{2,3},{3,0},{4,5},{5,6},{6,7},{7,4},{8,9},{9,10},{10,1... | collective-permute-start | bytes 393224 | tf_op jit(solution)/shard_map/ppermute | solution.py:409
  9.3 40.0 %collective-permute-start.11 = (bf16[32,2048]{1,0:T(8,128)(2,1)S(1)}, bf16[32,2048]{1,0:T(8,128)(2,1)S(1)}, u32[]{:S(2)}, u32[]{:S(2)}) collective-permute-start(bf16[32,2048]{1,0:T(8,128)(2,1)S(1)} %constant_dynamic-update-slice_fusion.37), channel_id=1, source_target_pairs={{0,2},{1,3},{2,0},{3,1},{4,6},{5,7},{6,4},{7,5},{8,10},{9,11},{10,... | collective-permute-start | bytes 393224 | tf_op jit(solution)/shard_map/ppermute | solution.py:409
  20.0 53.8 %all-to-all-start = ((bf16[4,32,896]{2,1,0:T(8,128)(2,1)}), bf16[4,32,896]{2,1,0:T(8,128)(2,1)S(1)}, u32[]{:S(2)}, u32[]{:S(2)}) async-start(bf16[4,32,896]{2,1,0:T(8,128)(2,1)} %copy.315), calls=%async_computation | async-start | bytes 458752 | tf_op jit(solution)/shard_map/all_to_all | solution.py:532
  49.4 9.2 %collective-permute-start.30 = (bf16[88,1024]{1,0:T(8,128)(2,1)S(1)}, bf16[88,1024]{1,0:T(8,128)(2,1)S(1)}, u32[]{:S(2)}, u32[]{:S(2)}) collective-permute-start(bf16[88,1024]{1,0:T(8,128)(2,1)S(1)} %copy-done.65), channel_id=1, source_target_pairs={{0,1},{1,2},{2,3},{3,0},{4,5},{5,6},{6,7},{7,4},{8,9},{9,10},{10,1... | collective-permute-start | bytes 540680 | tf_op jit(solution)/shard_map/ppermute | solution.py:409
  53.8 11.6 %collective-permute-start.31 = (bf16[88,1024]{1,0:T(8,128)(2,1)S(1)}, bf16[88,1024]{1,0:T(8,128)(2,1)S(1)}, u32[]{:S(2)}, u32[]{:S(2)}) collective-permute-start(bf16[88,1024]{1,0:T(8,128)(2,1)S(1)} %copy-done.65), channel_id=1, source_target_pairs={{0,2},{1,3},{2,0},{3,1},{4,6},{5,7},{6,4},{7,5},{8,10},{9,11},{10,... | collective-permute-start | bytes 540680 | tf_op jit(solution)/shard_map/ppermute | solution.py:409
  58.6 11.1 %collective-permute-start.32 = (bf16[88,1024]{1,0:T(8,128)(2,1)S(1)}, bf16[88,1024]{1,0:T(8,128)(2,1)S(1)}, u32[]{:S(2)}, u32[]{:S(2)}) collective-permute-start(bf16[88,1024]{1,0:T(8,128)(2,1)S(1)} %copy-done.65), channel_id=1, source_target_pairs={{0,3},{1,0},{2,1},{3,2},{4,7},{5,4},{6,5},{7,6},{8,11},{9,8},{10,9... | collective-permute-start | bytes 540680 | tf_op jit(solution)/shard_map/ppermute | solution.py:409
  65.3 26.1 %collective-permute-start = (bf16[256,1024]{1,0:T(8,128)(2,1)S(1)}, bf16[256,1024]{1,0:T(8,128)(2,1)}, u32[]{:S(2)}, u32[]{:S(2)}) collective-permute-start(bf16[256,1024]{1,0:T(8,128)(2,1)S(1)} %copy-done.14), channel_id=1, source_target_pairs={{0,1},{1,2},{2,3},{3,0},{4,5},{5,6},{6,7},{7,4},{8,9},{9,10},{10,1... | collective-permute-start | bytes 1572872 | tf_op jit(solution)/shard_map/ppermute | solution.py:409
  69.7 42.4 %collective-permute-start.1 = (bf16[256,1024]{1,0:T(8,128)(2,1)S(1)}, bf16[256,1024]{1,0:T(8,128)(2,1)}, u32[]{:S(2)}, u32[]{:S(2)}) collective-permute-start(bf16[256,1024]{1,0:T(8,128)(2,1)S(1)} %copy-done.14), channel_id=1, source_target_pairs={{0,2},{1,3},{2,0},{3,1},{4,6},{5,7},{6,4},{7,5},{8,10},{9,11},{10,... | collective-permute-start | bytes 1572872 | tf_op jit(solution)/shard_map/ppermute | solution.py:409
  75.6 39.4 %collective-permute-start.2 = (bf16[256,1024]{1,0:T(8,128)(2,1)S(1)}, bf16[256,1024]{1,0:T(8,128)(2,1)S(1)}, u32[]{:S(2)}, u32[]{:S(2)}) collective-permute-start(bf16[256,1024]{1,0:T(8,128)(2,1)S(1)} %copy-done.14), channel_id=1, source_target_pairs={{0,3},{1,0},{2,1},{3,2},{4,7},{5,4},{6,5},{7,6},{8,11},{9,8},{10,9... | collective-permute-start | bytes 1572872 | tf_op jit(solution)/shard_map/ppermute | solution.py:409
  78.0 52.2 %collective-permute-start.13 = (bf16[128,2048]{1,0:T(8,128)(2,1)S(1)}, bf16[128,2048]{1,0:T(8,128)(2,1)}, u32[]{:S(2)}, u32[]{:S(2)}) collective-permute-start(bf16[128,2048]{1,0:T(8,128)(2,1)S(1)} %constant_dynamic-update-slice_fusion.25), channel_id=1, source_target_pairs={{0,8},{4,12},{8,0},{12,4},{16,24},{20,28},{24,16},{28,20},{1,9},{5... | collective-permute-start | bytes 1572872 | tf_op jit(solution)/shard_map/ppermute | solution.py:405
  80.9 51.9 %collective-permute-start.14 = (bf16[128,2048]{1,0:T(8,128)(2,1)S(1)}, bf16[128,2048]{1,0:T(8,128)(2,1)}, u32[]{:S(2)}, u32[]{:S(2)}) collective-permute-start(bf16[128,2048]{1,0:T(8,128)(2,1)S(1)} %constant_dynamic-update-slice_fusion.25), channel_id=1, source_target_pairs={{0,16},{4,20},{8,24},{12,28},{16,0},{20,4},{24,8},{28,12},{1,17},{... | collective-permute-start | bytes 1572872 | tf_op jit(solution)/shard_map/ppermute | solution.py:405
  91.5 29.7 %collective-permute-start.3 = (bf16[128,896]{1,0:T(8,128)(2,1)S(1)}, bf16[128,896]{1,0:T(8,128)(2,1)S(1)}, u32[]{:S(2)}, u32[]{:S(2)}) collective-permute-start(bf16[128,896]{1,0:T(8,128)(2,1)S(1)} %bitcast.261), channel_id=1, source_target_pairs={{0,16},{4,20},{8,24},{12,28},{16,0},{20,4},{24,8},{28,12},{1,17},{... | collective-permute-start | bytes 688136 | tf_op jit(solution)/shard_map/ppermute | solution.py:405
  112.1 12.1 %collective-permute-start.4 = (bf16[128,896]{1,0:T(8,128)(2,1)S(1)}, bf16[128,896]{1,0:T(8,128)(2,1)S(1)}, u32[]{:S(2)}, u32[]{:S(2)}) collective-permute-start(bf16[128,896]{1,0:T(8,128)(2,1)S(1)} %bitcast.262), channel_id=1, source_target_pairs={{0,8},{4,12},{8,0},{12,4},{16,24},{20,28},{24,16},{28,20},{1,9},{5... | collective-permute-start | bytes 688136 | tf_op jit(solution)/shard_map/ppermute | solution.py:405
  115.0 12.2 %collective-permute-start.6 = (bf16[128,896]{1,0:T(8,128)(2,1)S(1)}, bf16[128,896]{1,0:T(8,128)(2,1)}, u32[]{:S(2)}, u32[]{:S(2)}) collective-permute-start(bf16[128,896]{1,0:T(8,128)(2,1)S(1)} %bitcast.263), channel_id=1, source_target_pairs={{0,4},{4,0},{8,12},{12,8},{16,20},{20,16},{24,28},{28,24},{1,5},{5... | collective-permute-start | bytes 688136 | tf_op jit(solution)/shard_map/ppermute | solution.py:405
  121.9 29.7 %collective-permute-start.33 = (bf16[352,1024]{1,0:T(8,128)(2,1)S(1)}, bf16[352,1024]{1,0:T(8,128)(2,1)}, u32[]{:S(2)}, u32[]{:S(2)}) collective-permute-start(bf16[352,1024]{1,0:T(8,128)(2,1)S(1)} %constant_dynamic-update-slice_fusion.9), channel_id=1, source_target_pairs={{0,8},{4,12},{8,0},{12,4},{16,24},{20,28},{24,16},{28,20},{1,9},{5... | collective-permute-start | bytes 2162696 | tf_op jit(solution)/shard_map/ppermute | solution.py:405
  124.9 29.1 %collective-permute-start.34 = (bf16[352,1024]{1,0:T(8,128)(2,1)S(1)}, bf16[352,1024]{1,0:T(8,128)(2,1)}, u32[]{:S(2)}, u32[]{:S(2)}) collective-permute-start(bf16[352,1024]{1,0:T(8,128)(2,1)S(1)} %constant_dynamic-update-slice_fusion.9), channel_id=1, source_target_pairs={{0,16},{4,20},{8,24},{12,28},{16,0},{20,4},{24,8},{28,12},{1,17},{... | collective-permute-start | bytes 2162696 | tf_op jit(solution)/shard_map/ppermute | solution.py:405
  127.3 17.3 %collective-permute-start.5 = (bf16[128,896]{1,0:T(8,128)(2,1)}, bf16[128,896]{1,0:T(8,128)(2,1)S(1)}, u32[]{:S(2)}, u32[]{:S(2)}) collective-permute-start(bf16[128,896]{1,0:T(8,128)(2,1)} %copy-done.64), channel_id=1, source_target_pairs={{0,8},{4,12},{8,0},{12,4},{16,24},{20,28},{24,16},{28,20},{1,9},{5... | collective-permute-start | bytes 688136 | tf_op jit(solution)/shard_map/ppermute | solution.py:405
  130.2 15.4 %collective-permute-start.7 = (bf16[128,896]{1,0:T(8,128)(2,1)}, bf16[128,896]{1,0:T(8,128)(2,1)S(1)}, u32[]{:S(2)}, u32[]{:S(2)}) collective-permute-start(bf16[128,896]{1,0:T(8,128)(2,1)} %copy-done.64), channel_id=1, source_target_pairs={{0,4},{4,0},{8,12},{12,8},{16,20},{20,16},{24,28},{28,24},{1,5},{5... | collective-permute-start | bytes 688136 | tf_op jit(solution)/shard_map/ppermute | solution.py:405
  132.8 13.4 %collective-permute-start.8 = (bf16[128,896]{1,0:T(8,128)(2,1)}, bf16[128,896]{1,0:T(8,128)(2,1)}, u32[]{:S(2)}, u32[]{:S(2)}) collective-permute-start(bf16[128,896]{1,0:T(8,128)(2,1)} %copy-done.63), channel_id=1, source_target_pairs={{0,4},{4,0},{8,12},{12,8},{16,20},{20,16},{24,28},{28,24},{1,5},{5... | collective-permute-start | bytes 688136 | tf_op jit(solution)/shard_map/ppermute | solution.py:405
  144.6 85.9 %collective-permute-start.16 = (bf16[128,2048]{1,0:T(8,128)(2,1)S(1)}, bf16[128,2048]{1,0:T(8,128)(2,1)}, u32[]{:S(2)}, u32[]{:S(2)}) collective-permute-start(bf16[128,2048]{1,0:T(8,128)(2,1)S(1)} %constant_dynamic-update-slice_fusion.25), channel_id=1, source_target_pairs={{0,4},{4,0},{8,12},{12,8},{16,20},{20,16},{24,28},{28,24},{1,5},{5... | collective-permute-start | bytes 1572872 | tf_op jit(solution)/shard_map/ppermute | solution.py:405
  145.6 88.1 %collective-permute-start.36 = (bf16[352,1024]{1,0:T(8,128)(2,1)S(1)}, bf16[352,1024]{1,0:T(8,128)(2,1)}, u32[]{:S(2)}, u32[]{:S(2)}) collective-permute-start(bf16[352,1024]{1,0:T(8,128)(2,1)S(1)} %constant_dynamic-update-slice_fusion.9), channel_id=1, source_target_pairs={{0,4},{4,0},{8,12},{12,8},{16,20},{20,16},{24,28},{28,24},{1,5},{5... | collective-permute-start | bytes 2162696 | tf_op jit(solution)/shard_map/ppermute | solution.py:405
  146.2 110.5 %collective-permute-start.23 = (bf16[128,5632]{1,0:T(8,128)(2,1)}, bf16[128,5632]{1,0:T(8,128)(2,1)}, u32[]{:S(2)}, u32[]{:S(2)}) collective-permute-start(bf16[128,5632]{1,0:T(8,128)(2,1)} %constant_dynamic-update-slice_fusion.21), channel_id=1, source_target_pairs={{0,16},{4,20},{8,24},{12,28},{16,0},{20,4},{24,8},{28,12},{1,17},{... | collective-permute-start | bytes 4325384 | tf_op jit(solution)/shard_map/ppermute | solution.py:405
  154.0 74.0 %collective-permute-start.15 = (bf16[128,2048]{1,0:T(8,128)(2,1)}, bf16[128,2048]{1,0:T(8,128)(2,1)}, u32[]{:S(2)}, u32[]{:S(2)}) collective-permute-start(bf16[128,2048]{1,0:T(8,128)(2,1)} %collective-permute-done.13), channel_id=1, source_target_pairs={{0,16},{4,20},{8,24},{12,28},{16,0},{20,4},{24,8},{28,12},{1,17},{... | collective-permute-start | bytes 1572872 | tf_op jit(solution)/shard_map/ppermute | solution.py:405
  156.2 77.7 %collective-permute-start.17 = (bf16[128,2048]{1,0:T(8,128)(2,1)}, bf16[128,2048]{1,0:T(8,128)(2,1)}, u32[]{:S(2)}, u32[]{:S(2)}) collective-permute-start(bf16[128,2048]{1,0:T(8,128)(2,1)} %collective-permute-done.13), channel_id=1, source_target_pairs={{0,4},{4,0},{8,12},{12,8},{16,20},{20,16},{24,28},{28,24},{1,5},{5... | collective-permute-start | bytes 1572872 | tf_op jit(solution)/shard_map/ppermute | solution.py:405
  222.1 64.6 %all-to-all-start.1 = ((bf16[4,256,256]{1,2,0:T(8,128)(2,1)}), bf16[4,256,256]{1,2,0:T(8,128)(2,1)}, u32[]{:S(2)}, u32[]{:S(2)}) async-start(bf16[4,256,256]{1,2,0:T(8,128)(2,1)} %copy.327), calls=%async_computation.1 | async-start | bytes 1048576 | tf_op jit(solution)/shard_map/all_to_all | solution.py:581
  228.0 8.0 %collective-permute-start.18 = (bf16[128,2048]{1,0:T(8,128)(2,1)}, bf16[128,2048]{1,0:T(8,128)(2,1)S(1)}, u32[]{:S(2)}, u32[]{:S(2)}) collective-permute-start(bf16[128,2048]{1,0:T(8,128)(2,1)} %collective-permute-done.14), channel_id=1, source_target_pairs={{0,4},{4,0},{8,12},{12,8},{16,20},{20,16},{24,28},{28,24},{1,5},{5... | collective-permute-start | bytes 1572872 | tf_op jit(solution)/shard_map/ppermute | solution.py:405
  230.5 18.0 %collective-permute-start.35 = (bf16[352,1024]{1,0:T(8,128)(2,1)}, bf16[352,1024]{1,0:T(8,128)(2,1)}, u32[]{:S(2)}, u32[]{:S(2)}) collective-permute-start(bf16[352,1024]{1,0:T(8,128)(2,1)} %collective-permute-done.33), channel_id=1, source_target_pairs={{0,16},{4,20},{8,24},{12,28},{16,0},{20,4},{24,8},{28,12},{1,17},{... | collective-permute-start | bytes 2162696 | tf_op jit(solution)/shard_map/ppermute | solution.py:405
  233.6 19.3 %collective-permute-start.37 = (bf16[352,1024]{1,0:T(8,128)(2,1)}, bf16[352,1024]{1,0:T(8,128)(2,1)S(1)}, u32[]{:S(2)}, u32[]{:S(2)}) collective-permute-start(bf16[352,1024]{1,0:T(8,128)(2,1)} %collective-permute-done.33), channel_id=1, source_target_pairs={{0,4},{4,0},{8,12},{12,8},{16,20},{20,16},{24,28},{28,24},{1,5},{5... | collective-permute-start | bytes 2162696 | tf_op jit(solution)/shard_map/ppermute | solution.py:405
  233.9 21.0 %collective-permute-start.38 = (bf16[352,1024]{1,0:T(8,128)(2,1)}, bf16[352,1024]{1,0:T(8,128)(2,1)S(1)}, u32[]{:S(2)}, u32[]{:S(2)}) collective-permute-start(bf16[352,1024]{1,0:T(8,128)(2,1)} %collective-permute-done.34), channel_id=1, source_target_pairs={{0,4},{4,0},{8,12},{12,8},{16,20},{20,16},{24,28},{28,24},{1,5},{5... | collective-permute-start | bytes 2162696 | tf_op jit(solution)/shard_map/ppermute | solution.py:405
  236.0 19.8 %collective-permute-start.19 = (bf16[128,2048]{1,0:T(8,128)(2,1)}, bf16[128,2048]{1,0:T(8,128)(2,1)S(1)}, u32[]{:S(2)}, u32[]{:S(2)}) collective-permute-start(bf16[128,2048]{1,0:T(8,128)(2,1)} %collective-permute-done.15), channel_id=1, source_target_pairs={{0,4},{4,0},{8,12},{12,8},{16,20},{20,16},{24,28},{28,24},{1,5},{5... | collective-permute-start | bytes 1572872 | tf_op jit(solution)/shard_map/ppermute | solution.py:405
  248.5 32.6 %collective-permute-start.24 = (bf16[128,5632]{1,0:T(8,128)(2,1)}, bf16[128,5632]{1,0:T(8,128)(2,1)}, u32[]{:S(2)}, u32[]{:S(2)}) collective-permute-start(bf16[128,5632]{1,0:T(8,128)(2,1)} %constant_dynamic-update-slice_fusion.21), channel_id=1, source_target_pairs={{0,8},{4,12},{8,0},{12,4},{16,24},{20,28},{24,16},{28,20},{1,9},{5... | collective-permute-start | bytes 4325384 | tf_op jit(solution)/shard_map/ppermute | solution.py:405
  252.9 62.3 %collective-permute-start.26 = (bf16[128,5632]{1,0:T(8,128)(2,1)}, bf16[128,5632]{1,0:T(8,128)(2,1)}, u32[]{:S(2)}, u32[]{:S(2)}) collective-permute-start(bf16[128,5632]{1,0:T(8,128)(2,1)} %constant_dynamic-update-slice_fusion.21), channel_id=1, source_target_pairs={{0,4},{4,0},{8,12},{12,8},{16,20},{20,16},{24,28},{28,24},{1,5},{5... | collective-permute-start | bytes 4325384 | tf_op jit(solution)/shard_map/ppermute | solution.py:405
  254.9 42.6 %collective-permute-start.39 = (bf16[352,1024]{1,0:T(8,128)(2,1)}, bf16[352,1024]{1,0:T(8,128)(2,1)}, u32[]{:S(2)}, u32[]{:S(2)}) collective-permute-start(bf16[352,1024]{1,0:T(8,128)(2,1)} %collective-permute-done.35), channel_id=1, source_target_pairs={{0,4},{4,0},{8,12},{12,8},{16,20},{20,16},{24,28},{28,24},{1,5},{5... | collective-permute-start | bytes 2162696 | tf_op jit(solution)/shard_map/ppermute | solution.py:405
  256.7 55.3 %collective-permute-start.25 = (bf16[128,5632]{1,0:T(8,128)(2,1)}, bf16[128,5632]{1,0:T(8,128)(2,1)}, u32[]{:S(2)}, u32[]{:S(2)}) collective-permute-start(bf16[128,5632]{1,0:T(8,128)(2,1)} %collective-permute-done.23), channel_id=1, source_target_pairs={{0,8},{4,12},{8,0},{12,4},{16,24},{20,28},{24,16},{28,20},{1,9},{5... | collective-permute-start | bytes 4325384 | tf_op jit(solution)/shard_map/ppermute | solution.py:405
  257.9 58.9 %collective-permute-start.27 = (bf16[128,5632]{1,0:T(8,128)(2,1)}, bf16[128,5632]{1,0:T(8,128)(2,1)}, u32[]{:S(2)}, u32[]{:S(2)}) collective-permute-start(bf16[128,5632]{1,0:T(8,128)(2,1)} %collective-permute-done.23), channel_id=1, source_target_pairs={{0,4},{4,0},{8,12},{12,8},{16,20},{20,16},{24,28},{28,24},{1,5},{5... | collective-permute-start | bytes 4325384 | tf_op jit(solution)/shard_map/ppermute | solution.py:405
  281.1 37.2 %collective-permute-start.28 = (bf16[128,5632]{1,0:T(8,128)(2,1)}, bf16[128,5632]{1,0:T(8,128)(2,1)}, u32[]{:S(2)}, u32[]{:S(2)}) collective-permute-start(bf16[128,5632]{1,0:T(8,128)(2,1)} %collective-permute-done.24), channel_id=1, source_target_pairs={{0,4},{4,0},{8,12},{12,8},{16,20},{20,16},{24,28},{28,24},{1,5},{5... | collective-permute-start | bytes 4325384 | tf_op jit(solution)/shard_map/ppermute | solution.py:405
  355.3 15.9 %all-to-all-start.2 = ((bf16[256,4,256]{2,0,1:T(8,128)(2,1)}), bf16[256,4,256]{2,0,1:T(8,128)(2,1)S(1)}, u32[]{:S(2)}, u32[]{:S(2)}) async-start(bf16[256,4,256]{2,0,1:T(8,128)(2,1)} %bitcast.222), calls=%async_computation.2 | async-start | bytes 1048576 | tf_op jit(solution)/shard_map/all_to_all | solution.py:605
  416.4 14.4 %collective-permute-start.40 = (bf16[256,1024]{1,0:T(8,128)(2,1)}, bf16[256,1024]{1,0:T(8,128)(2,1)S(1)}, u32[]{:S(2)}, u32[]{:S(2)}) collective-permute-start(bf16[256,1024]{1,0:T(8,128)(2,1)} %get-tuple-element.66), channel_id=1, source_target_pairs={{0,1},{1,2},{2,3},{3,0},{4,5},{5,6},{6,7},{7,4},{8,9},{9,10},{10,1... | collective-permute-start | bytes 1572872 | tf_op jit(solution)/shard_map/ppermute | solution.py:409
  417.6 44.1 %collective-permute-start.41 = (bf16[256,1024]{1,0:T(8,128)(2,1)}, bf16[256,1024]{1,0:T(8,128)(2,1)S(1)}, u32[]{:S(2)}, u32[]{:S(2)}) collective-permute-start(bf16[256,1024]{1,0:T(8,128)(2,1)} %get-tuple-element.67), channel_id=1, source_target_pairs={{0,2},{1,3},{2,0},{3,1},{4,6},{5,7},{6,4},{7,5},{8,10},{9,11},{10,... | collective-permute-start | bytes 1572872 | tf_op jit(solution)/shard_map/ppermute | solution.py:409
  421.5 44.6 %collective-permute-start.42 = (bf16[256,1024]{1,0:T(8,128)(2,1)S(1)}, bf16[256,1024]{1,0:T(8,128)(2,1)}, u32[]{:S(2)}, u32[]{:S(2)}) collective-permute-start(bf16[256,1024]{1,0:T(8,128)(2,1)S(1)} %get-tuple-element.68), channel_id=1, source_target_pairs={{0,3},{1,0},{2,1},{3,2},{4,7},{5,4},{6,5},{7,6},{8,11},{9,8},{10,9... | collective-permute-start | bytes 1572872 | tf_op jit(solution)/shard_map/ppermute | solution.py:409
  479.7 41.2 %collective-permute-start.58 = (bf16[512,5632]{1,0:T(8,128)(2,1)}, bf16[512,5632]{1,0:T(8,128)(2,1)}, u32[]{:S(2)}, u32[]{:S(2)}) collective-permute-start(bf16[512,5632]{1,0:T(8,128)(2,1)} %convolution_convert_fusion), channel_id=1, source_target_pairs={{0,4},{4,0},{8,12},{12,8},{16,20},{20,16},{24,28},{28,24},{1,5},{5... | collective-permute-start | bytes 17301512 | tf_op jit(solution)/shard_map/ppermute | solution.py:405
  487.0 47.1 %collective-permute-start.64 = (bf16[1408,1024]{1,0:T(8,128)(2,1)}, bf16[1408,1024]{1,0:T(8,128)(2,1)}, u32[]{:S(2)}, u32[]{:S(2)}) collective-permute-start(bf16[1408,1024]{1,0:T(8,128)(2,1)} %convolution_convert_fusion.1), channel_id=1, source_target_pairs={{0,4},{4,0},{8,12},{12,8},{16,20},{20,16},{24,28},{28,24},{1,5},{5... | collective-permute-start | bytes 8650760 | tf_op jit(solution)/shard_map/ppermute | solution.py:405
  500.9 25.6 %collective-permute-start.52 = (bf16[512,1024]{1,0:T(8,128)(2,1)}, bf16[512,1024]{1,0:T(8,128)(2,1)}, u32[]{:S(2)}, u32[]{:S(2)}) collective-permute-start(bf16[512,1024]{1,0:T(8,128)(2,1)} %convolution_convert_fusion.3), channel_id=1, source_target_pairs={{0,4},{4,0},{8,12},{12,8},{16,20},{20,16},{24,28},{28,24},{1,5},{5... | collective-permute-start | bytes 3145736 | tf_op jit(solution)/shard_map/ppermute | solution.py:405
  504.8 24.4 %collective-permute-start.46 = (bf16[512,1024]{1,0:T(8,128)(2,1)}, bf16[512,1024]{1,0:T(8,128)(2,1)}, u32[]{:S(2)}, u32[]{:S(2)}) collective-permute-start(bf16[512,1024]{1,0:T(8,128)(2,1)} %convolution_convert_fusion.4), channel_id=1, source_target_pairs={{0,4},{4,0},{8,12},{12,8},{16,20},{20,16},{24,28},{28,24},{1,5},{5... | collective-permute-start | bytes 3145736 | tf_op jit(solution)/shard_map/ppermute | solution.py:405
  520.4 12.2 %collective-permute-start.44 = (bf16[2,128,896]{2,1,0:T(8,128)(2,1)S(1)}, bf16[2,128,896]{2,1,0:T(8,128)(2,1)S(1)}, u32[]{:S(2)}, u32[]{:S(2)}) collective-permute-start(bf16[2,128,896]{2,1,0:T(8,128)(2,1)S(1)} %slice.385), channel_id=1, source_target_pairs={{0,8},{4,12},{8,0},{12,4},{16,24},{20,28},{24,16},{28,20},{1,9},{5... | collective-permute-start | bytes 1376264 | tf_op jit(solution)/shard_map/ppermute | solution.py:405
  525.4 90.8 %collective-permute-start.59 = (bf16[256,5632]{1,0:T(8,128)(2,1)}, bf16[256,5632]{1,0:T(8,128)(2,1)}, u32[]{:S(2)}, u32[]{:S(2)}) collective-permute-start(bf16[256,5632]{1,0:T(8,128)(2,1)} %add_convert_fusion), channel_id=1, source_target_pairs={{0,8},{4,12},{8,0},{12,4},{16,24},{20,28},{24,16},{28,20},{1,9},{5... | collective-permute-start | bytes 8650760 | tf_op jit(solution)/shard_map/ppermute | solution.py:405
  527.8 13.1 %collective-permute-start.53 = (bf16[256,1024]{1,0:T(8,128)(2,1)S(1)}, bf16[256,1024]{1,0:T(8,128)(2,1)S(1)}, u32[]{:S(2)}, u32[]{:S(2)}) collective-permute-start(bf16[256,1024]{1,0:T(8,128)(2,1)S(1)} %add_convert_fusion.4), channel_id=1, source_target_pairs={{0,16},{4,20},{8,24},{12,28},{16,0},{20,4},{24,8},{28,12},{1,17},{... | collective-permute-start | bytes 1572872 | tf_op jit(solution)/shard_map/ppermute | solution.py:405
  530.6 21.5 %collective-permute-start.47 = (bf16[256,1024]{1,0:T(8,128)(2,1)S(1)}, bf16[256,1024]{1,0:T(8,128)(2,1)S(1)}, u32[]{:S(2)}, u32[]{:S(2)}) collective-permute-start(bf16[256,1024]{1,0:T(8,128)(2,1)S(1)} %add_convert_fusion.5), channel_id=1, source_target_pairs={{0,16},{4,20},{8,24},{12,28},{16,0},{20,4},{24,8},{28,12},{1,17},{... | collective-permute-start | bytes 1572872 | tf_op jit(solution)/shard_map/ppermute | solution.py:405
  532.8 24.3 %collective-permute-start.45 = (bf16[1,128,896]{2,1,0:T(8,128)(2,1)S(1)}, bf16[1,128,896]{2,1,0:T(8,128)(2,1)S(1)}, u32[]{:S(2)}, u32[]{:S(2)}) collective-permute-start(bf16[1,128,896]{2,1,0:T(8,128)(2,1)S(1)} %slice.386), channel_id=1, source_target_pairs={{0,16},{4,20},{8,24},{12,28},{16,0},{20,4},{24,8},{28,12},{1,17},{... | collective-permute-start | bytes 688136 | tf_op jit(solution)/shard_map/ppermute | solution.py:405
  537.2 84.0 %collective-permute-start.65 = (bf16[704,1024]{1,0:T(8,128)(2,1)}, bf16[704,1024]{1,0:T(8,128)(2,1)}, u32[]{:S(2)}, u32[]{:S(2)}) collective-permute-start(bf16[704,1024]{1,0:T(8,128)(2,1)} %add_convert_fusion.1), channel_id=1, source_target_pairs={{0,16},{4,20},{8,24},{12,28},{16,0},{20,4},{24,8},{28,12},{1,17},{... | collective-permute-start | bytes 4325384 | tf_op jit(solution)/shard_map/ppermute | solution.py:405
  543.0 57.2 %collective-permute-start.54 = (bf16[128,1024]{1,0:T(8,128)(2,1)}, bf16[128,1024]{1,0:T(8,128)(2,1)}, u32[]{:S(2)}, u32[]{:S(2)}) collective-permute-start(bf16[128,1024]{1,0:T(8,128)(2,1)} %add_convert_fusion.6), channel_id=1, source_target_pairs={{0,8},{4,12},{8,0},{12,4},{16,24},{20,28},{24,16},{28,20},{1,9},{5... | collective-permute-start | bytes 786440 | tf_op jit(solution)/shard_map/ppermute | solution.py:405
  554.2 51.6 %collective-permute-start.48 = (bf16[128,1024]{1,0:T(8,128)(2,1)}, bf16[128,1024]{1,0:T(8,128)(2,1)}, u32[]{:S(2)}, u32[]{:S(2)}) collective-permute-start(bf16[128,1024]{1,0:T(8,128)(2,1)} %add_convert_fusion.7), channel_id=1, source_target_pairs={{0,8},{4,12},{8,0},{12,4},{16,24},{20,28},{24,16},{28,20},{1,9},{5... | collective-permute-start | bytes 786440 | tf_op jit(solution)/shard_map/ppermute | solution.py:405
  557.9 66.2 %all-to-all-start.3 = ((f32[4,32,896]{2,1,0:T(8,128)}), f32[4,32,896]{2,1,0:T(8,128)S(1)}, u32[]{:S(2)}, u32[]{:S(2)}) async-start(f32[4,32,896]{2,1,0:T(8,128)} %bitcast.258), calls=%async_computation.3 | async-start | bytes 917504 | tf_op jit(solution)/shard_map/all_to_all | solution.py:641
  619.9 31.9 %collective-permute-start.60 = (bf16[128,5632]{1,0:T(8,128)(2,1)}, bf16[128,5632]{1,0:T(8,128)(2,1)}, u32[]{:S(2)}, u32[]{:S(2)}) collective-permute-start(bf16[128,5632]{1,0:T(8,128)(2,1)} %add_convert_fusion.2), channel_id=1, source_target_pairs={{0,16},{4,20},{8,24},{12,28},{16,0},{20,4},{24,8},{28,12},{1,17},{... | collective-permute-start | bytes 4325384 | tf_op jit(solution)/shard_map/ppermute | solution.py:405
  623.9 16.3 %collective-permute-start.66 = (bf16[352,1024]{1,0:T(8,128)(2,1)}, bf16[352,1024]{1,0:T(8,128)(2,1)}, u32[]{:S(2)}, u32[]{:S(2)}) collective-permute-start(bf16[352,1024]{1,0:T(8,128)(2,1)} %add_convert_fusion.3), channel_id=1, source_target_pairs={{0,8},{4,12},{8,0},{12,4},{16,24},{20,28},{24,16},{28,20},{1,9},{5... | collective-permute-start | bytes 2162696 | tf_op jit(solution)/shard_map/ppermute | solution.py:405
  643.5 14.1 %collective-permute-start.67 = (bf16[88,1024]{1,0:T(8,128)(2,1)S(1)}, bf16[88,1024]{1,0:T(8,128)(2,1)S(1)}, u32[]{:S(2)}, u32[]{:S(2)}) collective-permute-start(bf16[88,1024]{1,0:T(8,128)(2,1)S(1)} %get-tuple-element.81), channel_id=1, source_target_pairs={{0,1},{1,2},{2,3},{3,0},{4,5},{5,6},{6,7},{7,4},{8,9},{9,10},{10,1... | collective-permute-start | bytes 540680 | tf_op jit(solution)/shard_map/ppermute | solution.py:409
  643.5 20.2 %collective-permute-start.68 = (bf16[88,1024]{1,0:T(8,128)(2,1)}, bf16[88,1024]{1,0:T(8,128)(2,1)}, u32[]{:S(2)}, u32[]{:S(2)}) collective-permute-start(bf16[88,1024]{1,0:T(8,128)(2,1)} %get-tuple-element.83), channel_id=1, source_target_pairs={{0,2},{1,3},{2,0},{3,1},{4,6},{5,7},{6,4},{7,5},{8,10},{9,11},{10,... | collective-permute-start | bytes 540680 | tf_op jit(solution)/shard_map/ppermute | solution.py:409
  644.3 30.1 %collective-permute-start.69 = (bf16[88,1024]{1,0:T(8,128)(2,1)S(1)}, bf16[88,1024]{1,0:T(8,128)(2,1)}, u32[]{:S(2)}, u32[]{:S(2)}) collective-permute-start(bf16[88,1024]{1,0:T(8,128)(2,1)S(1)} %get-tuple-element.82), channel_id=1, source_target_pairs={{0,3},{1,0},{2,1},{3,2},{4,7},{5,4},{6,5},{7,6},{8,11},{9,8},{10,9... | collective-permute-start | bytes 540680 | tf_op jit(solution)/shard_map/ppermute | solution.py:409
  656.4 20.0 %collective-permute-start.61 = (bf16[32,5632]{1,0:T(8,128)(2,1)S(1)}, bf16[32,5632]{1,0:T(8,128)(2,1)S(1)}, u32[]{:S(2)}, u32[]{:S(2)}) collective-permute-start(bf16[32,5632]{1,0:T(8,128)(2,1)S(1)} %get-tuple-element.78), channel_id=1, source_target_pairs={{0,1},{1,2},{2,3},{3,0},{4,5},{5,6},{6,7},{7,4},{8,9},{9,10},{10,1... | collective-permute-start | bytes 1081352 | tf_op jit(solution)/shard_map/ppermute | solution.py:409
  656.5 31.5 %collective-permute-start.62 = (bf16[32,5632]{1,0:T(8,128)(2,1)S(1)}, bf16[32,5632]{1,0:T(8,128)(2,1)S(1)}, u32[]{:S(2)}, u32[]{:S(2)}) collective-permute-start(bf16[32,5632]{1,0:T(8,128)(2,1)S(1)} %get-tuple-element.80), channel_id=1, source_target_pairs={{0,2},{1,3},{2,0},{3,1},{4,6},{5,7},{6,4},{7,5},{8,10},{9,11},{10,... | collective-permute-start | bytes 1081352 | tf_op jit(solution)/shard_map/ppermute | solution.py:409
  657.6 33.7 %collective-permute-start.63 = (bf16[32,5632]{1,0:T(8,128)(2,1)S(1)}, bf16[32,5632]{1,0:T(8,128)(2,1)S(1)}, u32[]{:S(2)}, u32[]{:S(2)}) collective-permute-start(bf16[32,5632]{1,0:T(8,128)(2,1)S(1)} %get-tuple-element.79), channel_id=1, source_target_pairs={{0,3},{1,0},{2,1},{3,2},{4,7},{5,4},{6,5},{7,6},{8,11},{9,8},{10,9... | collective-permute-start | bytes 1081352 | tf_op jit(solution)/shard_map/ppermute | solution.py:409
  (92 other events, 777.8 us)

commit v2 on v1

v2 whole, which is shorter than its diff:
```python
import functools

import jax
import jax.numpy as jnp
from jax import lax
from jax.experimental import pallas as pl
from jax.experimental.pallas import tpu as pltpu
from jax.sharding import PartitionSpec as P

CHUNK = 128
TP = 4
PER_STEP = 4
BACK_STEP = 2
ENTER = 256
HALO = 8
norm_eps = 1e-05
unit_eps = 1e-06
NARROW = jnp.bfloat16
WIDE = jnp.float32


def halves(value):
    top = value.astype(NARROW)
    return top, (value - top.astype(WIDE)).astype(NARROW)


def product(left, right, left_dim=1, right_dim=0):
    dims = (((left_dim,), (right_dim,)), ((), ()))

    def one(a, b):
        return lax.dot_general(a, b, dims, preferred_element_type=WIDE)

    if PASSES == 1:
        return one(left[0], right[0])
    return one(left[0], right[0]) + (one(left[0], right[1]) + one(left[1], right[0]))


PASSES = 3


def turned(value):
    return halves(value.T)


def chunk_masks(seg_col, seg_row, before, after):
    size = seg_col.shape[0]
    down = lax.broadcasted_iota(jnp.int32, (size, size), 0)
    across = lax.broadcasted_iota(jnp.int32, (size, size), 1)
    same = seg_col == seg_row
    strict = same & (down > across)
    inclusive = same & (down >= across)
    carried = jnp.where(seg_col == before, 1.0, 0.0).astype(WIDE)
    last = jnp.where(seg_col == after, 1.0, 0.0).astype(WIDE)
    return strict, inclusive, carried, last


def unit_lower_inverses(systems):
    size = systems[0].shape[0]
    down = lax.broadcasted_iota(jnp.int32, (size, size), 0)
    across = lax.broadcasted_iota(jnp.int32, (size, size), 1)
    gap = jnp.where(down > across, down ^ across, 0)
    eye = jnp.where(down == across, 1.0, 0.0)
    results = [eye - jnp.where(gap == 1, system, 0.0) for system in systems]
    step = 2
    while step < size:
        picked = (gap >= step) & (gap < 2 * step)
        parts = [halves(jnp.where(picked, system, 0.0)) for system in systems]
        done = [halves(result) for result in results]
        inner = [halves(product(part, own)) for part, own in zip(parts, done)]
        results = [result - product(own, side) for result, own, side in zip(results, done, inner)]
        step *= 2
    return results


def conv_rows(pad_ref, taps, pos, start, column, width):
    window = pad_ref[pl.ds(start, CHUNK + HALO), pl.ds(column, width)]
    count = taps.shape[0]
    result = taps[count - 1 : count] * window[HALO : HALO + CHUNK]
    moved = []
    for offset in range(1, count):
        rows = jnp.where(pos >= offset, window[HALO - offset : HALO - offset + CHUNK], 0.0)
        moved.append(rows)
        result = result + taps[count - 1 - offset : count - offset] * rows
    return result, window[HALO : HALO + CHUNK], moved


def fill_padded(raw_ref, pad_ref, width):
    pad_ref[0:HALO, :] = jnp.zeros((HALO, width), WIDE)
    total = raw_ref.shape[0]

    def copy(index, _):
        start = pl.multiple_of(index * CHUNK, CHUNK)
        pad_ref[pl.ds(start + HALO, CHUNK), :] = raw_ref[pl.ds(start, CHUNK), 0:width].astype(NARROW).astype(WIDE)
        return 0

    lax.fori_loop(0, total // CHUNK, copy, 0)


def one_hot(first, second, offset):
    return jnp.where(first - offset == second, 1.0, 0.0).astype(NARROW)


def plain_dot(left, right, left_dim=1, right_dim=0):
    return lax.dot_general(left, right, (((left_dim,), (right_dim,)), ((), ())), preferred_element_type=WIDE)


def pack_rows(near_col, pieces):
    size = pieces[0].shape[0]
    lane = lax.broadcasted_iota(jnp.int32, (near_col.shape[0], size), 1)
    total = plain_dot(one_hot(near_col, lane, 0), pieces[0][...])
    for k in range(1, len(pieces)):
        total = total + plain_dot(one_hot(near_col, lane, k * size), pieces[k][...])
    return total


def unpack_rows(far_row, packed, k, size):
    down = lax.broadcasted_iota(jnp.int32, (size, far_row.shape[1]), 0)
    return plain_dot(one_hot(far_row, down, k * size), packed).astype(NARROW)


def beta_of(raw_ref, rows, lane):
    return jax.nn.sigmoid(raw_ref[rows, lane:lane + 1].astype(NARROW).astype(WIDE))


def forward_kernel(heads, width, n_fs, *refs):
    pieces, refs = refs[:n_fs], refs[n_fs:]
    (win_ref, gmix_ref, near_ref, far_ref, taps_ref, gain_ref, segcol_ref, poscol_ref, segrow_ref, edges_ref,
     *refs) = refs
    blocks, refs = refs[:n_fs], refs[n_fs:]
    (hidden_ref, packed_ref, raw_ref, out_ref, q_ref, k_ref, inv_ref, score_ref, dots_ref, upd_ref, state_ref,
     move_ref, pad_ref, base_ref, w_ref, normed_ref) = refs
    total = raw_ref.shape[0]
    count = total // CHUNK
    span = heads * width

    def enter(index, _):
        rows = pl.ds(pl.multiple_of(index * ENTER, ENTER), ENTER)
        packed = pack_rows(near_ref[rows, :], pieces)
        packed_ref[rows, :] = packed.astype(NARROW)
        scale = lax.rsqrt(jnp.mean(packed * packed, axis=-1, keepdims=True) + norm_eps)
        hidden = (packed * scale * gmix_ref[...]).astype(NARROW)
        hidden_ref[rows, :] = hidden
        raw_ref[rows, :] = plain_dot(hidden, win_ref[...])
        return 0

    lax.fori_loop(0, total // ENTER, enter, 0)
    fill_padded(raw_ref, pad_ref, 3 * span)

    def first(group, _):
        work = []
        for sub in range(PER_STEP):
            index = group * PER_STEP + sub
            start = pl.multiple_of(index * CHUNK, CHUNK)
            rows = pl.ds(start, CHUNK)
            pos = poscol_ref[rows, :]
            before, after = edges_ref[index, 0], edges_ref[index, 1]
            strict, inclusive, carried, last = chunk_masks(
                segcol_ref[rows, :], segrow_ref[pl.ds(index, 1), :], before, after)
            keep = jnp.where(before == after, 1.0, 0.0).astype(WIDE)
            for head in range(heads):
                cols = pl.ds(head * width, width)
                parts = []
                for which in range(3):
                    column = which * span + head * width
                    value = conv_rows(pad_ref, taps_ref[which, :, head * width:(head + 1) * width], pos,
                                      start, column, width)[0]
                    parts.append(value * jax.nn.sigmoid(value))
                query, key, value = parts
                query = query * lax.rsqrt(jnp.sum(query * query, axis=-1, keepdims=True) + unit_eps)
                key = key * lax.rsqrt(jnp.sum(key * key, axis=-1, keepdims=True) + unit_eps)
                q_ref[rows, cols] = query
                k_ref[rows, cols] = key
                beta = beta_of(raw_ref, rows, 4 * span + head)
                key_h, query_h = halves(key), halves(query)
                dots = product(key_h, key_h, 1, 1)
                score = jnp.where(inclusive, product(query_h, key_h, 1, 1), 0.0)
                at = index * heads + head
                dots_ref[at] = dots
                score_ref[at] = score
                work.append((at, rows, cols, keep, jnp.where(strict, beta * dots, 0.0),
                             beta * value, (beta * carried) * key, last * key))
        inverses = unit_lower_inverses([item[4] for item in work])
        for inverse, (at, rows, cols, keep, _, right, carry_in, tail_in) in zip(inverses, work):
            inv_h = halves(inverse)
            base = product(inv_h, halves(right))
            carry = product(inv_h, halves(carry_in))
            tail = turned(tail_in)
            eye = jnp.where(lax.broadcasted_iota(jnp.int32, (width, width), 0)
                            == lax.broadcasted_iota(jnp.int32, (width, width), 1), keep, 0.0)
            inv_ref[at] = inverse
            base_ref[rows, cols] = base
            w_ref[rows, cols] = carry
            move_ref[at] = eye - product(tail, halves(carry))
            state_ref[at] = product(tail, halves(base))
        return 0

    lax.fori_loop(0, count // PER_STEP, first, 0)

    def second(index, states):
        result = []
        for head in range(heads):
            at = index * heads + head
            added = state_ref[at]
            state_ref[at] = states[head]
            result.append(product(halves(move_ref[at]), halves(states[head])) + added)
        return tuple(result)

    lax.fori_loop(0, count, second, tuple(jnp.zeros((width, width), WIDE) for _ in range(heads)))

    def third(index, _):
        rows = pl.ds(pl.multiple_of(index * CHUNK, CHUNK), CHUNK)
        carried = jnp.where(segcol_ref[rows, :] == edges_ref[index, 0], 1.0, 0.0).astype(WIDE)
        for head in range(heads):
            cols = pl.ds(head * width, width)
            at = index * heads + head
            state = halves(state_ref[at])
            update = base_ref[rows, cols] - product(halves(w_ref[rows, cols]), state)
            upd_ref[rows, cols] = update
            out = carried * product(halves(q_ref[rows, cols]), state)
            out = out + product(halves(score_ref[at]), halves(update))
            mixed = out.astype(NARROW)
            out_ref[rows, cols] = mixed
            mixed = mixed.astype(WIDE)
            scale = lax.rsqrt(jnp.mean(mixed * mixed, axis=-1, keepdims=True) + norm_eps)
            gate = raw_ref[rows, pl.ds(3 * span + head * width, width)]
            normed = mixed * scale * gain_ref[...] * (gate * jax.nn.sigmoid(gate))
            normed_ref[rows, cols] = normed.astype(NARROW)
        return 0

    lax.fori_loop(0, count, third, 0)
    for k, block in enumerate(blocks):
        block[...] = unpack_rows(far_ref[...], normed_ref[...], k, total // n_fs)


def backward_kernel(heads, width, n_fs, *refs):
    pieces, refs = refs[:n_fs], refs[n_fs:]
    (win_ref, near_ref, far_ref, taps_ref, gain_ref, segcol_ref, poscol_ref, segrow_ref, edges_ref,
     packed_ref, raw_ref, mixed_ref, q_ref, k_ref, inv_ref, score_ref, dots_ref, upd_ref, state_ref, move_ref,
     *refs) = refs
    blocks, refs = refs[:n_fs], refs[n_fs:]
    (draw_ref, dtaps_ref, dgain_ref, dgmix_ref,
     pad_ref, grad_ref, pdo_ref, dconv_ref, dout_ref, dnormed_ref, dhid_ref) = refs
    total = raw_ref.shape[0]

    def enter(index, _):
        rows = pl.ds(pl.multiple_of(index * ENTER, ENTER), ENTER)
        dnormed_ref[rows, :] = pack_rows(near_ref[rows, :], pieces).astype(NARROW)
        return 0

    lax.fori_loop(0, total // ENTER, enter, 0)
    count = total // CHUNK
    span = heads * width
    fill_padded(raw_ref, pad_ref, 3 * span)

    def first(group, dgain):
        for sub in range(BACK_STEP):
            index = group * BACK_STEP + sub
            rows = pl.ds(pl.multiple_of(index * CHUNK, CHUNK), CHUNK)
            carried = jnp.where(segcol_ref[rows, :] == edges_ref[index, 0], 1.0, 0.0).astype(WIDE)
            for head in range(heads):
                cols = pl.ds(head * width, width)
                at = index * heads + head
                mixed = mixed_ref[rows, cols].astype(WIDE)
                scale = lax.rsqrt(jnp.mean(mixed * mixed, axis=-1, keepdims=True) + norm_eps)
                gate_cols = pl.ds(3 * span + head * width, width)
                gate = raw_ref[rows, gate_cols]
                sig = jax.nn.sigmoid(gate)
                given = dnormed_ref[rows, cols].astype(WIDE)
                unit = mixed * scale
                dgate = given * unit * gain_ref[...] * (sig * (1.0 + gate * (1.0 - sig)))
                draw_ref[rows, gate_cols] = dgate.astype(NARROW)
                given = given * (gate * sig)
                dgain = dgain + jnp.sum(given * unit, axis=0, keepdims=True)
                given = given * gain_ref[...]
                dout = scale * (given - unit * jnp.mean(unit * given, axis=-1, keepdims=True))
                dout = dout.astype(NARROW)
                dout_ref[rows, cols] = dout
                score_t = turned(score_ref[at])
                back = product_exact(score_t, dout)
                pdo_ref[rows, cols] = back
                inv_t = turned(inv_ref[at])
                back = product(inv_t, halves(back))
                query_t = turned(carried * q_ref[rows, cols])
                key_t = turned((beta_of(raw_ref, rows, 4 * span + head) * carried) * k_ref[rows, cols])
                grad_ref[at] = product_exact(query_t, dout) - product(key_t, halves(back))
        return dgain

    dgain_ref[...] = lax.fori_loop(0, count // BACK_STEP, first, jnp.zeros((1, width), WIDE))

    def second(step, grads):
        index = count - 1 - step
        result = []
        for head in range(heads):
            at = index * heads + head
            added = grad_ref[at]
            grad_ref[at] = grads[head]
            result.append(product(turned(move_ref[at]), halves(grads[head])) + added)
        return tuple(result)

    lax.fori_loop(0, count, second, tuple(jnp.zeros((width, width), WIDE) for _ in range(heads)))
    dconv_ref[total:total + HALO, :] = jnp.zeros((HALO, 3 * span), WIDE)

    def third(group, tap_sums):
        for sub in range(BACK_STEP):
            index = group * BACK_STEP + sub
            start = pl.multiple_of(index * CHUNK, CHUNK)
            rows = pl.ds(start, CHUNK)
            pos = poscol_ref[rows, :]
            strict, inclusive, carried, last = chunk_masks(
                segcol_ref[rows, :], segrow_ref[pl.ds(index, 1), :], edges_ref[index, 0], edges_ref[index, 1])
            new_sums = []
            dbetas = []
            for head in range(heads):
                cols = pl.ds(head * width, width)
                at = index * heads + head
                beta = beta_of(raw_ref, rows, 4 * span + head)
                query, key, update = q_ref[rows, cols], k_ref[rows, cols], upd_ref[rows, cols]
                query_h, key_h, update_h = halves(query), halves(key), halves(update)
                dout = dout_ref[rows, cols]
                state, grad = halves(state_ref[at]), halves(grad_ref[at])
                convs = []
                for which in range(3):
                    column = which * span + head * width
                    convs.append(conv_rows(pad_ref, taps_ref[which, :, head * width:(head + 1) * width], pos,
                                           start, column, width))
                gates = [jax.nn.sigmoid(c[0]) for c in convs]
                value = convs[2][0] * gates[2]
                dupdate = pdo_ref[rows, cols] + last * product(key_h, grad)
                dright = product(turned(inv_ref[at]), halves(dupdate))
                dright_h = halves(dright)
                dscore = jnp.where(inclusive, product_exact(update_h, dout, 1, 1, flip=True), 0.0)
                dsystem = jnp.where(strict, product(dright_h, update_h, 1, 1), 0.0)
                dscore_h = halves(dscore)
                dquery = carried * product_exact(state, dout, 1, 1, flip=True) + product(dscore_h, key_h)
                weighted = beta * dsystem
                scaled = beta * carried
                dkey = product(turned(dscore), query_h) + last * product(update_h, grad, 1, 1)
                dkey = dkey - product(halves(weighted + weighted.T), key_h)
                dkey = dkey - scaled * product(dright_h, state, 1, 1)
                dvalue = beta * dright
                seen = carried * product(key_h, state)
                dbeta = jnp.sum(dright * (value - seen), axis=-1, keepdims=True) - jnp.sum(
                    dsystem * dots_ref[at], axis=-1, keepdims=True)
                dbetas.append(dbeta * beta * (1.0 - beta))
                sides = []
                for grads, unit, conv, gate in ((dquery, query, convs[0][0], gates[0]), (dkey, key, convs[1][0], gates[1])):
                    plain = conv * gate
                    inv_norm = lax.rsqrt(jnp.sum(plain * plain, axis=-1, keepdims=True) + unit_eps)
                    sides.append(inv_norm * (grads - unit * jnp.sum(unit * grads, axis=-1, keepdims=True)))
                sides.append(dvalue)
                for which in range(3):
                    conv, plain, moved = convs[which]
                    gate = gates[which]
                    dconv = sides[which] * gate * (1.0 + conv * (1.0 - gate))
                    column = which * span + head * width
                    dconv_ref[rows, pl.ds(column, width)] = dconv
                    sums = [jnp.sum(dconv * plain, axis=0, keepdims=True)]
                    for shifted in moved:
                        sums.append(jnp.sum(dconv * shifted, axis=0, keepdims=True))
                    new_sums.append(jnp.concatenate(sums[::-1], axis=0))
            lane = lax.broadcasted_iota(jnp.int32, (CHUNK, draw_ref.shape[1] - 4 * span), 1)
            packed = jnp.zeros(lane.shape, WIDE)
            for head in range(heads):
                packed = jnp.where(lane == head, dbetas[head], packed)
            draw_ref[rows, pl.ds(4 * span, lane.shape[1])] = packed.astype(draw_ref.dtype)
            tap_sums = tuple(old + new for old, new in zip(tap_sums, new_sums))
        return tap_sums

    zero = tuple(jnp.zeros((taps_ref.shape[1], width), WIDE) for _ in range(3 * heads))
    sums = lax.fori_loop(0, count // BACK_STEP, third, zero)
    for head in range(heads):
        for which in range(3):
            dtaps_ref[which, :, head * width:(head + 1) * width] = sums[head * 3 + which]
    taps_count = taps_ref.shape[1]

    def fourth(index, _):
        start = pl.multiple_of(index * CHUNK, CHUNK)
        pos_window = poscol_ref[pl.ds(start, CHUNK + HALO), :]
        for which in range(3):
            columns = pl.ds(which * span, span)
            window = dconv_ref[pl.ds(start, CHUNK + HALO), columns]
            result = taps_ref[which, taps_count - 1:taps_count, :] * window[0:CHUNK]
            for offset in range(1, taps_count):
                part = jnp.where(pos_window >= offset, window, 0.0)[offset:offset + CHUNK]
                result = result + taps_ref[which, taps_count - 1 - offset:taps_count - offset, :] * part
            draw_ref[pl.ds(start, CHUNK), columns] = result.astype(draw_ref.dtype)
        return 0

    lax.fori_loop(0, count, fourth, 0)

    def leave(index, sums):
        rows = pl.ds(pl.multiple_of(index * ENTER, ENTER), ENTER)
        dhidden = plain_dot(draw_ref[rows, :], win_ref[...], 1, 1)
        dhid_ref[rows, :] = dhidden.astype(NARROW)
        packed = packed_ref[rows, :].astype(WIDE)
        scale = lax.rsqrt(jnp.mean(packed * packed, axis=-1, keepdims=True) + norm_eps)
        return sums + jnp.sum(dhidden * (packed * scale), axis=0, keepdims=True)

    dgmix_ref[...] = lax.fori_loop(0, total // ENTER, leave, jnp.zeros(dgmix_ref.shape, WIDE))
    for k, block in enumerate(blocks):
        block[...] = unpack_rows(far_ref[...], dhid_ref[...], k, total // n_fs)


def weigh_kernel(heads, width, shard_rows, z_ref, hidden_ref, draw_ref, dtaps_ref, dgain_ref, dgmix_ref, dgffn_ref,
                 out_ref, gradin_ref, small_ref):
    total = hidden_ref.shape[0]
    span = heads * width
    taps_count = dtaps_ref.shape[1]

    def weigh(index, _):
        rows = pl.ds(pl.multiple_of(index * ENTER, ENTER), ENTER)
        gradin_ref[...] += plain_dot(hidden_ref[rows, :], draw_ref[rows, :], 0, 0)
        return 0

    gradin_ref[...] = jnp.zeros(gradin_ref.shape, WIDE)
    lax.fori_loop(0, total // ENTER, weigh, 0)
    features = small_ref.shape[1]
    small_ref[...] = jnp.zeros(small_ref.shape, WIDE)
    small_ref[heads:heads + 1, :] = dgmix_ref[...]
    small_ref[heads + 1:heads + 2, :] = dgffn_ref[...]
    own = pl.ds(pl.multiple_of(z_ref[0] * span, span), span)
    for which in range(3):
        first_row = heads + 2 + which * taps_count
        small_ref[first_row:first_row + taps_count, own] = dtaps_ref[which]
    unit, each = shard_rows
    value = lax.broadcasted_iota(jnp.int32, (width, features), 0)
    lane = lax.broadcasted_iota(jnp.int32, (width, features), 1)
    chosen = (lane // unit == value // each) & (lane % unit == value % each)
    chosen = jnp.where(chosen, 1.0, 0.0).astype(NARROW)
    last_row = heads + 2 + 3 * taps_count
    small_ref[last_row:last_row + 1, :] = product_exact(halves(jnp.broadcast_to(dgain_ref[...], (8, width))), chosen)[0:1]
    side = pl.ds(4 * span, small_ref.shape[0])
    gradin_ref[:, side] += small_ref[...].T
    out_ref[...] = gradin_ref[...].astype(NARROW)


def product_exact(left, exact, left_dim=1, right_dim=0, flip=False):
    def one(a):
        if flip:
            return lax.dot_general(exact, a, (((right_dim,), (left_dim,)), ((), ())), preferred_element_type=WIDE)
        return lax.dot_general(a, exact, (((left_dim,), (right_dim,)), ((), ())), preferred_element_type=WIDE)

    if PASSES == 1:
        return one(left[0])
    return one(left[0]) + one(left[1])


def cost(flops, size):
    return pl.CostEstimate(flops=flops, bytes_accessed=size, transcendentals=0)


def specs(count):
    return [pl.BlockSpec(memory_space=pltpu.VMEM)] * count


def in_scalars():
    return pl.BlockSpec(memory_space=pltpu.SMEM)


def delta_forward(pieces, w_in, gmix, near, far, taps, gain, segcol, poscol, segrow, edges, heads, width):
    n_fs = len(pieces)
    total = near.shape[0]
    features, lanes = w_in.shape
    count = total // CHUNK
    span = heads * width
    thin = jax.ShapeDtypeStruct((total, span), NARROW)
    rows = jax.ShapeDtypeStruct((total, span), WIDE)
    full = jax.ShapeDtypeStruct((total, features), NARROW)
    square = jax.ShapeDtypeStruct((count * heads, CHUNK, CHUNK), WIDE)
    state = jax.ShapeDtypeStruct((count * heads, width, width), WIDE)
    block = jax.ShapeDtypeStruct((total // n_fs, span), NARROW)
    raw = jax.ShapeDtypeStruct((total, lanes), WIDE)
    result = pl.pallas_call(
        functools.partial(forward_kernel, heads, width, n_fs),
        out_shape=(block,) * n_fs
        + (full, full, raw, thin, rows, rows, square, square, square, rows, state, state),
        in_specs=specs(n_fs + 9) + [in_scalars()],
        out_specs=tuple(specs(n_fs + 12)),
        scratch_shapes=[
            pltpu.VMEM((total + HALO, 3 * span), WIDE),
            pltpu.VMEM((total, span), WIDE),
            pltpu.VMEM((total, span), WIDE),
            pltpu.VMEM((total, span), NARROW),
        ],
        compiler_params=pltpu.CompilerParams(vmem_limit_bytes=52 << 20),
        cost_estimate=cost(30_000_000_000, 16 << 20),
        name="delta_forward",
    )(*pieces, w_in, gmix, near, far, taps, gain, segcol, poscol, segrow, edges)
    return result[:n_fs], result[n_fs], result[n_fs + 1 :]


def delta_backward(pieces, w_in, near, far, taps, gain, segcol, poscol, segrow, edges, kept, heads, width):
    n_fs = len(pieces)
    total = near.shape[0]
    features, lanes = w_in.shape
    count = total // CHUNK
    span = heads * width
    poscol = jnp.pad(poscol, ((0, HALO), (0, 0)))
    block = jax.ShapeDtypeStruct((total // n_fs, features), NARROW)
    result = pl.pallas_call(
        functools.partial(backward_kernel, heads, width, n_fs),
        out_shape=(block,) * n_fs
        + (
            jax.ShapeDtypeStruct((total, lanes), NARROW),
            jax.ShapeDtypeStruct(taps.shape, WIDE),
            jax.ShapeDtypeStruct(gain.shape, WIDE),
            jax.ShapeDtypeStruct((1, features), WIDE),
        ),
        in_specs=specs(n_fs + 8) + [in_scalars()] + specs(11),
        out_specs=tuple(specs(n_fs + 4)),
        scratch_shapes=[
            pltpu.VMEM((total + HALO, 3 * span), WIDE),
            pltpu.VMEM((count * heads, width, width), WIDE),
            pltpu.VMEM((total, span), WIDE),
            pltpu.VMEM((total + HALO, 3 * span), WIDE),
            pltpu.VMEM((total, span), NARROW),
            pltpu.VMEM((total, span), NARROW),
            pltpu.VMEM((total, features), NARROW),
        ],
        compiler_params=pltpu.CompilerParams(vmem_limit_bytes=52 << 20),
        cost_estimate=cost(40_000_000_000, 16 << 20),
        name="delta_backward",
    )(*pieces, w_in, near, far, taps, gain, segcol, poscol, segrow, edges, *kept)
    return (result[:n_fs],) + tuple(result[n_fs:])


def weigh_inputs(z, hidden, d_raw, dtaps, dgain, dgmix, dgffn, heads, width, shard_rows):
    features, lanes = hidden.shape[1], d_raw.shape[1]
    return pl.pallas_call(
        functools.partial(weigh_kernel, heads, width, shard_rows),
        out_shape=jax.ShapeDtypeStruct((features, lanes), NARROW),
        in_specs=[in_scalars()] + specs(6),
        out_specs=specs(1)[0],
        scratch_shapes=[pltpu.VMEM((features, lanes), WIDE), pltpu.VMEM((128, features), WIDE)],
        compiler_params=pltpu.CompilerParams(vmem_limit_bytes=40 << 20),
        cost_estimate=cost(60_000_000_000, 8 << 20),
        name="weigh_inputs",
    )(z, hidden, d_raw, dtaps, dgain, dgmix, dgffn)


def mix_out_kernel(n_fs, z_ref, *refs):
    pieces, refs = refs[:n_fs], refs[n_fs:]
    wout_ref, tokens_ref, gain_ref, middle_ref, ffn_ref, normed_ref = refs
    span = pieces[0].shape[1]
    middle = tokens_ref[...].astype(WIDE)
    for k, piece in enumerate(pieces):
        place = pl.ds(pl.multiple_of(lax.rem(z_ref[0] + n_fs - k, n_fs) * span, span), span)
        normed_ref[:, place] = piece[...]
        middle = middle + plain_dot(piece[...], wout_ref[place, :])
    middle_ref[...] = middle
    scale = lax.rsqrt(jnp.mean(middle * middle, axis=-1, keepdims=True) + norm_eps)
    ffn_ref[...] = (middle * scale * gain_ref[...]).astype(NARROW)


def mix_out(z, pieces, w_out, tokens, gain):
    n_fs = len(pieces)
    shape = tokens.shape
    return pl.pallas_call(
        functools.partial(mix_out_kernel, n_fs),
        out_shape=(
            jax.ShapeDtypeStruct(shape, WIDE),
            jax.ShapeDtypeStruct(shape, NARROW),
            jax.ShapeDtypeStruct(shape, NARROW),
        ),
        in_specs=[in_scalars()] + specs(n_fs + 3),
        out_specs=tuple(specs(3)),
        compiler_params=pltpu.CompilerParams(vmem_limit_bytes=40 << 20),
        cost_estimate=cost(2_000_000_000, 6 << 20),
        name="mix_out",
    )(z, *pieces, w_out, tokens, gain)


def mix_back_kernel(n_fs, z_ref, dffn_ref, middle_ref, gain_ref, cot_ref, wout_ref, *refs):
    blocks, (dmiddle_ref, dbranch_ref, dgain_ref) = refs[:n_fs], refs[n_fs:]
    middle, given = middle_ref[...], dffn_ref[...]
    scale = lax.rsqrt(jnp.mean(middle * middle, axis=-1, keepdims=True) + norm_eps)
    unit = middle * scale
    dgain_ref[...] = jnp.sum(given * unit, axis=0, keepdims=True)
    given = given * gain_ref[...]
    dmiddle = cot_ref[...].astype(WIDE) + scale * (given - unit * jnp.mean(unit * given, axis=-1, keepdims=True))
    dmiddle_ref[...] = dmiddle
    dbranch = dmiddle.astype(NARROW)
    dbranch_ref[...] = dbranch
    span = blocks[0].shape[1]
    for k, block in enumerate(blocks):
        place = pl.ds(pl.multiple_of(lax.rem(z_ref[0] + k, n_fs) * span, span), span)
        block[...] = plain_dot(dbranch, wout_ref[place, :], 1, 1).astype(NARROW)


def mix_back(z, dffn, middle, gain, cotangent, w_out, n_fs):
    count, features = middle.shape
    block = jax.ShapeDtypeStruct((count, features // n_fs), NARROW)
    result = pl.pallas_call(
        functools.partial(mix_back_kernel, n_fs),
        out_shape=(block,) * n_fs
        + (
            jax.ShapeDtypeStruct(middle.shape, WIDE),
            jax.ShapeDtypeStruct(middle.shape, NARROW),
            jax.ShapeDtypeStruct(gain.shape, WIDE),
        ),
        in_specs=[in_scalars()] + specs(5),
        out_specs=tuple(specs(n_fs + 3)),
        compiler_params=pltpu.CompilerParams(vmem_limit_bytes=40 << 20),
        cost_estimate=cost(2_000_000_000, 6 << 20),
        name="mix_back",
    )(z, dffn, middle, gain, cotangent, w_out)
    return (result[:n_fs],) + tuple(result[n_fs:])


def rms_scale(values, gain):
    return values * lax.rsqrt(jnp.mean(values * values, axis=-1, keepdims=True) + norm_eps) * gain


def swiglu(gate_proj, up_proj):
    return jax.nn.silu(gate_proj) * up_proj


def sequence_layout(lengths_row, total):
    ends = jnp.cumsum(lengths_row)
    index = jnp.arange(total, dtype=jnp.int32)
    before = index[:, None] >= ends[None, :]
    segment = jnp.sum(before.astype(jnp.int32), axis=1)
    start = jnp.sum(jnp.where(before, lengths_row[None, :], 0), axis=1)
    return (segment, index - start)


def project(left, right):
    return jnp.dot(left, right, preferred_element_type=WIDE)


def project_back(left, right):
    return lax.dot_general(left, right, (((1,), (1,)), ((), ())), preferred_element_type=WIDE)


def weight_grad(left, right):
    return lax.dot_general(left, right, (((0,), (0,)), ((), ())), preferred_element_type=WIDE)


def flip(value, bit, n_dp):
    return lax.ppermute(value, "dp", [(i, i ^ bit) for i in range(n_dp)])


def shift(value, by, n_fs):
    return lax.ppermute(value, "fsdp", [(i, (i + by) % n_fs) for i in range(n_fs)])


def line_pieces(shard, n_fs):
    return [shard] + [shift(shard, by, n_fs) for by in range(1, n_fs)]


def line_order(pieces, z):
    n_fs = len(pieces)
    shape = pieces[0].shape
    whole = jnp.zeros((shape[0], n_fs) + shape[1:], pieces[0].dtype)
    for by, piece in enumerate(pieces):
        whole = lax.dynamic_update_slice_in_dim(whole, piece[:, None], lax.rem(z + n_fs - by, n_fs), 1)
    return whole


def gather_cube(piece, order, n_dp):
    pieces = {0: piece}
    for bit in order:
        for key in list(pieces):
            pieces[key ^ bit] = flip(pieces[key], bit, n_dp)
    return pieces


def in_order(pieces, me):
    rows = pieces[0].shape[0]
    whole = jnp.zeros((len(pieces) * rows,) + pieces[0].shape[1:], pieces[0].dtype)
    unit = max(pieces).bit_length()
    step = (1 << unit) // len(pieces)
    for key, piece in pieces.items():
        whole = lax.dynamic_update_slice_in_dim(whole, piece, lax.bitwise_xor(me, key // step) * rows, 0)
    return whole


def per_device(
    n_dp,
    n_fs,
    tokens,
    lengths,
    packing,
    w_query,
    w_key,
    w_value,
    w_gate,
    w_beta,
    conv_taps,
    w_out,
    gain_mix,
    gain_head,
    gain_ffn,
    w_ffn_gate,
    w_ffn_up,
    w_ffn_down,
    cotangent,
):
    me = lax.axis_index("dp")
    z = lax.axis_index("fsdp")
    bits = [1 << k for k in range(n_dp.bit_length() - 1)]
    first_order = bits[:1] + bits[1:]
    second_order = bits[:1] + bits[1:][::-1]
    packing_row = packing[0]
    lengths_row = lengths[0]
    own_rows, features = tokens.shape
    total = own_rows * n_fs
    rows = w_query.shape[0]
    heads_all = w_beta.shape[1]
    heads = heads_all // n_fs
    span = features // n_fs
    width = span // heads
    hidden_ffn = w_ffn_gate.shape[1]
    head_rows = gain_head.shape[0]
    n_taps = conv_taps.shape[1]

    def by_owner(matrix):
        return jnp.swapaxes(matrix.reshape(rows, n_fs, -1), 0, 1)

    small = jnp.concatenate(
        [
            gain_mix[:, None],
            gain_ffn[:, None],
            conv_taps.reshape(3 * n_taps, rows).T,
            jnp.pad(gain_head, (0, rows - head_rows))[:, None],
        ],
        axis=1,
    )
    n_small = small.shape[1]
    side = jnp.concatenate(
        [by_owner(w_beta), jnp.broadcast_to(small[None], (n_fs, rows, n_small))], axis=2
    )
    side = jnp.pad(side, ((0, 0), (0, 0), (0, 128 - heads - n_small)))
    packet = jnp.concatenate(
        [by_owner(w_query), by_owner(w_key), by_owner(w_value), by_owner(w_gate), side], axis=2
    )
    member = lax.rem(me, TP)
    block = me // TP
    n_rest = n_dp // TP
    ff_block = hidden_ffn // n_dp
    ff_own = n_rest * ff_block
    ff_pad = -(-ff_own // 128) * 128
    tp_bits = [bit for bit in bits if bit < TP]
    rest_bits = [bit for bit in bits if bit >= TP]

    def by_member(matrix):
        split = matrix.reshape(rows, n_rest, TP, ff_block)
        split = jnp.transpose(split, (2, 0, 1, 3)).reshape(TP, rows, ff_own)
        return jnp.pad(split, ((0, 0), (0, 0), (0, ff_pad - ff_own)))

    def hand_out(blocks):
        pieces = [lax.dynamic_index_in_dim(blocks, z, 0)]
        for by in range(1, n_fs):
            pieces.append(shift(lax.dynamic_index_in_dim(blocks, lax.rem(z + by, n_fs), 0), by, n_fs))
        return pieces

    packet = line_order(hand_out(packet), z).reshape(n_fs * rows, 4 * span + 128)
    w_in = lax.all_gather(packet, "dp", axis=0, tiled=True)
    full_out = lax.all_gather(w_out, ("dp", "fsdp"), axis=0, tiled=True)
    side_rows = w_in[:, 4 * span :].astype(WIDE).T
    full_gmix = side_rows[heads]
    full_gffn = side_rows[heads + 1]
    local_taps = lax.dynamic_slice_in_dim(
        side_rows[heads + 2 : heads + 2 + 3 * n_taps], z * span, span, 1
    ).reshape(3, n_taps, span)
    full_ghead = side_rows[heads + 2 + 3 * n_taps].reshape(-1, rows)[:, :head_rows].reshape(-1)

    owner, place = packing_row // own_rows, lax.rem(packing_row, own_rows)
    near = (lax.rem(z + n_fs - owner, n_fs) * own_rows + place)[:, None]
    far = (lax.rem(owner + n_fs - z, n_fs) * own_rows + place)[None]
    segment, position = sequence_layout(lengths_row, total)
    seg_rows = segment.reshape(-1, CHUNK)
    ends = seg_rows[:, -1]
    edges = jnp.stack([jnp.concatenate([jnp.full((1,), -1, jnp.int32), ends[:-1]]), ends], axis=1)
    layout = (near, far, local_taps, full_ghead[None], segment[:, None], position[:, None], seg_rows, edges)
    token_pieces = [tokens] + [shift(tokens, by, n_fs) for by in range(1, n_fs)]
    own_gate, own_up, own_cotangent, _ = lax.optimization_barrier(
        (w_ffn_gate, w_ffn_up, cotangent, token_pieces[1])
    )
    both_sends = jnp.concatenate([by_member(own_gate), by_member(own_up)], axis=2)
    blocks, hidden_p, kept = delta_forward(token_pieces, w_in, full_gmix[None], *layout, heads, width)

    both_pieces = {
        key: flip(lax.dynamic_index_in_dim(both_sends, member ^ key, 0, keepdims=False), key, n_dp)
        if key
        else lax.dynamic_index_in_dim(both_sends, member, 0, keepdims=False)
        for key in range(TP)
    }
    both_rows, _ = lax.optimization_barrier((in_order(both_pieces, member), token_pieces))
    both_line = line_pieces(both_rows.reshape(TP, rows, 2 * ff_pad), n_fs)
    both_line, blocks = lax.optimization_barrier((both_line, blocks))
    both_rows = line_order(both_line, z).reshape(-1, 2 * ff_pad)
    w_both = in_order(gather_cube(both_rows, rest_bits, n_dp), block)
    tp_order = sorted(range(TP), key=lambda key: tuple((key & bit) != 0 for bit in tp_bits))

    def spread(value):
        pieces = gather_cube(value, tp_bits[::-1], n_dp)
        return jnp.concatenate([pieces[key] for key in tp_order], axis=0)

    cotangent_near = spread(own_cotangent)

    def collect(left, right, dims):
        arrived = []
        keep = TP

        def term(lo, hi):
            value = lax.dot_general(
                left[lo * own_rows : hi * own_rows], right, (dims, ((), ())), preferred_element_type=WIDE
            )
            for earlier in arrived:
                value = value + earlier[lo * own_rows : hi * own_rows].astype(WIDE)
            return value

        for bit in tp_bits:
            keep //= 2
            arrived.append(flip(term(keep, 2 * keep).astype(NARROW), bit, n_dp))
        return term(0, 1)

    def halve(value, index, some_bits):
        unit = some_bits[0] if some_bits else 1
        for bit in some_bits[::-1]:
            half = value.shape[0] // 2
            mine = (index // (bit // unit)) % 2
            sent = lax.dynamic_slice_in_dim(value, (1 - mine) * half, half, 0)
            value = lax.dynamic_slice_in_dim(value, mine * half, half, 0)
            value = value.astype(WIDE) + flip(sent.astype(NARROW), bit, n_dp).astype(WIDE)
        return value

    def sum_up(pieces, whole):
        total = lax.dynamic_index_in_dim(whole, z, 0, keepdims=False).astype(WIDE)
        for piece in pieces[1:]:
            total = total + piece[0].astype(WIDE)
        return total

    def pass_on(parts):
        return [parts[0]] + [shift(part, by, n_fs) for by, part in enumerate(parts) if by]

    z_ref = z.reshape(1)
    mixed_pieces = pass_on(blocks)
    own_down, _ = lax.optimization_barrier((w_ffn_down, mixed_pieces))
    down_line = line_pieces(own_down[None], n_fs)
    middle, ffn_in, normed_b = mix_out(z_ref, mixed_pieces, full_out, tokens, full_gffn[None])
    down_rows = line_order(down_line, z).reshape(-1, features)
    w_down = in_order(gather_cube(down_rows, rest_bits, n_dp), block)
    w_down = jnp.pad(w_down, ((0, ff_pad - ff_own), (0, 0)))
    ffn_near = spread(ffn_in)
    both = project(ffn_near, w_both)
    active, active_back = jax.vjp(swiglu, both[:, :ff_pad], both[:, ff_pad:])
    active_b = active.astype(NARROW)
    down_terms = weight_grad(active_b, cotangent_near)[:ff_own].reshape(n_rest, -1, features)
    down_sum = halve(down_terms, block, rest_bits).reshape(n_fs, -1, features)
    d_active = project_back(cotangent_near, w_down)
    d_fgate, d_fup = active_back(d_active)
    d_both = jnp.concatenate([d_fgate.astype(NARROW), d_fup.astype(NARROW)], axis=1)
    both_terms = weight_grad(ffn_near, d_both).astype(NARROW)
    both_sum = lax.psum_scatter(
        both_terms.reshape(n_dp, n_fs * rows, 2 * ff_pad), "fsdp", scatter_dimension=1, tiled=True
    )
    d_ffn_in = collect(d_both, w_both, ((1,), (1,)))
    d_ffn_in, both_terms = lax.optimization_barrier((d_ffn_in, both_terms))

    d_blocks, d_middle, d_branch, d_gffn = mix_back(
        z_ref, d_ffn_in, middle, full_gffn[None], cotangent, full_out, n_fs
    )
    d_blocks, down_sum = lax.optimization_barrier((d_blocks, down_sum))
    d_pieces = pass_on(d_blocks)
    grad_fdown = sum_up(hand_out(down_sum.astype(NARROW)), down_sum)
    sum_out = lax.psum_scatter(
        weight_grad(normed_b, d_branch).astype(NARROW), "dp", scatter_dimension=0, tiled=True
    )
    layer_out = (middle + collect(active_b, w_down, ((1,), (0,)))).astype(NARROW)
    d_blocks, d_raw, d_taps, d_ghead, d_gmix = delta_backward(d_pieces, w_in, *layout, kept, heads, width)
    d_blocks = pass_on(d_blocks)
    grad_in = weigh_inputs(
        z_ref, hidden_p, d_raw, d_taps, d_ghead, d_gmix, d_gffn, heads, width, (rows, head_rows)
    )
    grad_in, both_sum, layer_out, grad_fdown = lax.optimization_barrier((grad_in, both_sum, layer_out, grad_fdown))
    part = lax.psum_scatter(grad_in, "dp", scatter_dimension=0, tiled=True)
    d_blocks, both_sum = lax.optimization_barrier((d_blocks, both_sum))
    both_sum = halve(both_sum, block, rest_bits)
    both_pieces = {
        key: flip(lax.dynamic_index_in_dim(both_sum, member ^ key, 0, keepdims=False), key, n_dp)
        if key
        else lax.dynamic_index_in_dim(both_sum, member, 0, keepdims=False)
        for key in range(TP)
    }
    both_mine = in_order({key: piece[None] for key, piece in both_pieces.items()}, member)
    d_hidden = d_blocks[0].astype(WIDE)
    for block_of in d_blocks[1:]:
        d_hidden = d_hidden + block_of.astype(WIDE)

    def units_of(which):
        part = both_mine[:, :, which * ff_pad : which * ff_pad + ff_own].reshape(TP, rows, n_rest, ff_block)
        return jnp.transpose(part, (1, 2, 0, 3)).reshape(rows, hidden_ffn)

    _, norm_mix_back = jax.vjp(rms_scale, tokens.astype(WIDE), full_gmix)
    d_inputs_norm, _ = norm_mix_back(d_hidden)
    grad_tokens = d_middle + d_inputs_norm

    lanes = part.shape[1]
    joint = jnp.concatenate([part, sum_out], axis=1).reshape(n_fs, rows, -1)
    arrived = [piece[0] for piece in hand_out(joint)]
    part = line_order([piece[None, :, :lanes] for piece in arrived], z)[0].astype(WIDE)
    grad_wout = jnp.zeros((rows, features), WIDE)
    for piece in arrived:
        grad_wout = grad_wout + piece[:, lanes:].astype(WIDE)

    def columns_of(which):
        return jnp.swapaxes(part[:, :, which * span : (which + 1) * span], 0, 1).reshape(rows, features)

    grad_beta = jnp.swapaxes(part[:, :, 4 * span : 4 * span + heads], 0, 1).reshape(rows, heads_all)
    small_sum = jnp.sum(part[:, :, 4 * span + heads : 4 * span + heads + n_small], axis=0)
    grad_taps = small_sum[:, 2 : 2 + 3 * n_taps].T.reshape(3, n_taps, rows)
    return (
        layer_out,
        grad_tokens,
        columns_of(0),
        columns_of(1),
        columns_of(2),
        columns_of(3),
        grad_beta,
        grad_taps,
        grad_wout,
        small_sum[:, 0],
        small_sum[:head_rows, 2 + 3 * n_taps],
        small_sum[:, 1],
        units_of(0),
        units_of(1),
        grad_fdown,
    )


def solution(mesh):
    both = ("dp", "fsdp")
    rows = P(both, None)
    group = P("dp", None)
    taps = P(None, None, both)
    line = P(both)
    in_specs = (rows, group, group) + (rows,) * 5 + (taps, rows, line, line, line) + (rows,) * 4
    out_specs = (rows,) * 7 + (taps, rows, line, line, line) + (rows,) * 3
    return jax.shard_map(
        functools.partial(per_device, mesh.shape["dp"], mesh.shape["fsdp"]),
        mesh=mesh,
        in_specs=in_specs,
        out_specs=out_specs,
        check_vma=False,
    )
```

time: 700 us -> 433 us (0.62)
  waiting for transfers between devices: 276 us -> 173 us
  local copies, waits for them, and re-layouts: 134 us -> 47.1 us
  matrix products: 101 us -> 39.7 us
  starting transfers between devices: 71.1 us -> 54.8 us
  between operations: 2.96 us -> 15 us
  other arithmetic: 25.5 us -> 14.2 us
    ppermute x43 -> x20, waiting for transfers between devices: 134 us -> 61.6 us  [flip(): return lax.ppermute(value, 'dp', [(i, i ^ bit) for i in range(n_dp)])]
    dynamic_update_slice x46 -> x27, local copies, waits for them, and re-layouts: 53 us -> 11.2 us  [the longest x16 6.2 us: line_order(): lax.dynamic_update_slice_in_dim(whole, piece[:, None], lax.rem(z + n_fs -...]
    dot_general x19 -> x3, matrix products: 43 us -> 11.3 us  [weight_grad(): lax.dot_general(left, right, (((0,), (0,)), ((), ())), preferred_element_...]
    dot_general x7 -> x1, matrix products: 29.1 us -> 3.53 us  [project(): return jnp.dot(left, right, preferred_element_type=WIDE)]
    dot_general x5 -> x1, matrix products: 28.9 us -> 5.6 us  [project_back(): lax.dot_general(left, right, (((1,), (1,)), ((), ())), preferred_element_...]
    ppermute x27, waiting for transfers between devices: 131 us -> 111 us  [shift(): lax.ppermute(value, 'fsdp', [(i, (i + by) % n_fs) for i in range(n_fs)])]
    dot_general x0 -> x6, matrix products: none -> 19.2 us  [term(): lax.dot_general(left[lo * own_rows:hi * own_rows], right, (dims, ((), ())...]
    all_to_all x4 -> x0, starting transfers between devices: 17.1 us -> none  [the longest x1 5.72 us: per_device(): lax.all_to_all(mixed_arrived, 'fsdp', split_axis=0, concat_axis=1, tiled=...]
  transfers between devices with their start and end apart: 74 -> 52, of which waited for: 28 -> 23; matrix products, arithmetic and copies ran while one was open for 26% -> 15% of each run, Pallas kernels for 8% -> 20%
where the time goes in v2:
time: 433 us; the launch traced here: 427 us
  waiting for transfers between devices  173 us (40%)
  Pallas kernels  83.5 us (19%)
  starting transfers between devices  54.8 us (13%)
  local copies, waits for them, and re-layouts  47.1 us (11%)
  matrix products  39.7 us (9%)
  between operations  15 us (3%)
  other arithmetic  14.2 us (3%)
    ppermute x27, waiting for transfers between devices, shift(): lax.ppermute(value, 'fsdp', [(i, (i + by) % n_fs) for i in range(n_fs)])  111 us
    ppermute x20, waiting for transfers between devices, flip(): return lax.ppermute(value, 'dp', [(i, i ^ bit) for i in range(n_dp)])  61.6 us
    pallas_call x1, Pallas kernels, delta_backward(): pl.pallas_call(functools.partial(backward_kernel, heads, width, n_fs), ou...  40.9 us
    pallas_call x1, Pallas kernels, delta_forward(): pl.pallas_call(functools.partial(forward_kernel, heads, width, n_fs), out...  34.2 us
    ppermute x27, starting transfers between devices, shift(): lax.ppermute(value, 'fsdp', [(i, (i + by) % n_fs) for i in range(n_fs)])  27.4 us
    ppermute x20, starting transfers between devices, flip(): return lax.ppermute(value, 'dp', [(i, i ^ bit) for i in range(n_dp)])  26.8 us
    dot_general x6, matrix products, term(): lax.dot_general(left[lo * own_rows:hi * own_rows], right, (dims, ((), ())...  19.2 us
    unnamed x81, local copies, waits for them, and re-layouts  13 us
  transfers between devices with their start and end apart: 52, of which 23 were waited for; matrix products, arithmetic and copies ran while one was open for 15% of the time, Pallas kernels for 20%

profile of v2, /device:TPU:9, one launch (start us, length us, event | category | flops | bytes accessed | tf_op | source)
XLA Modules:
  0.0 427.3 jit_solution(4812339731448343475)
XLA Ops:
  16.2 1.4 collective-permute-start.5
  17.7 1.9 collective-permute-done.4
  19.6 4.0 collective-permute-done.5
  24.5 1.7 collective-permute-start.1
  29.3 1.4 fusion.37
  30.7 6.9 %collective-permute-done.refs_1_ = bf16[256,1024]{1,0:T(8,128)(2,1)} collective-permute-done((bf16[256,1024]{1,0:T(8,128)(2,1)S(1)}, bf16[256,1024]{1,0:T(8,128)(2,1)}, u32[]{:S(2)}, u32[]{:S(2)}) %collective-permute-start) | collective-permute-done | bytes 524320 | tf_op jit(solution)/shard_map/ppermute | solution.py:644
  38.4 3.0 collective-permute-start.7
  46.0 9.4 %collective-permute-done.10 = bf16[32,1536]{1,0:T(8,128)(2,1)S(1)} collective-permute-done((bf16[32,1536]{1,0:T(8,128)(2,1)S(1)}, bf16[32,1536]{1,0:T(8,128)(2,1)S(1)}, u32[]{:S(2)}, u32[]{:S(2)}) %collective-permute-start.10) | collective-permute-done | bytes 98336 | tf_op jit(solution)/shard_map/ppermute | solution.py:640
  55.4 5.7 %collective-permute-start.11 = (bf16[32,1536]{1,0:T(8,128)(2,1)S(1)}, bf16[32,1536]{1,0:T(8,128)(2,1)S(1)}, u32[]{:S(2)}, u32[]{:S(2)}) collective-permute-start(bf16[32,1536]{1,0:T(8,128)(2,1)S(1)} %get-tuple-element.184), channel_id=1, source_target_pairs={{0,12},{4,8},{8,4},{12,0},{16,28},{20,24},{24,20},{28,16},{1,13},{... | collective-permute-start | bytes 294920 | tf_op jit(solution)/shard_map/ppermute | solution.py:640
  61.7 2.8 collective-permute-done.11
  65.2 3.8 collective-permute-done.1.refs_2_
  69.0 3.5 collective-permute-done.2.refs_3_
  72.5 1.7 collective-permute-start.14
  81.2 34.2 %delta_forward.1 = (bf16[256,256]{1,0:T(8,128)(2,1)S(1)}, bf16[256,256]{1,0:T(8,128)(2,1)S(1)}, bf16[256,256]{1,0:T(8,128)(2,1)S(1)}, bf16[256,256]{1,0:T(8,128)...) custom-call(bf16[256,1024]{1,0:T(8,128)(2,1)S(1)} %copy-done, ...), custom_call_target="tpu_custom_call" | custom-call | flops 30000001024 | bytes 16777216 | tf_op jit(solution)/shard_map/delta_forward/pallas_call | solution.py:473
  116.8 3.0 collective-permute-start.16
  126.5 6.8 %collective-permute-done.16.refs_2_ = bf16[256,256]{1,0:T(8,128)(2,1)S(1)} collective-permute-done((bf16[256,256]{1,0:T(8,128)(2,1)S(1)}, bf16[256,256]{1,0:T(8,128)(2,1)S(1)}, u32[]{:S(2)}, u32[]{:S(2)}) %collective-permute-start.16) | collective-permute-done | bytes 131104 | tf_op jit(solution)/shard_map/ppermute | solution.py:644
  133.4 1.8 collective-permute-done.17.refs_3_
  136.6 1.6 collective-permute-start.20
  138.2 1.6 copy-done.4
  140.7 1.4 collective-permute-start.22
  142.2 1.9 collective-permute-start.23
  145.0 4.9 %collective-permute-done.19 = bf16[1,88,1024]{2,1,0:T(8,128)(2,1)} collective-permute-done((bf16[1,88,1024]{2,1,0:T(8,128)(2,1)S(1)}, bf16[1,88,1024]{2,1,0:T(8,128)(2,1)}, u32[]{:S(2)}, u32[]{:S(2)}) %collective-permute-start.19) | collective-permute-done | bytes 180256 | tf_op jit(solution)/shard_map/ppermute | solution.py:644
  150.8 2.3 collective-permute-done.20
  153.2 1.4 collective-permute-start.21
  156.1 19.0 %collective-permute-done.21 = bf16[352,1024]{1,0:T(8,128)(2,1)S(1)} collective-permute-done((bf16[352,1024]{1,0:T(8,128)(2,1)S(1)}, bf16[352,1024]{1,0:T(8,128)(2,1)S(1)}, u32[]{:S(2)}, u32[]{:S(2)}) %collective-permute-start.21) | collective-permute-done | bytes 720928 | tf_op jit(solution)/shard_map/ppermute | solution.py:640
  175.3 2.0 constant_dynamic-update-slice_fusion.8
  177.4 3.5 fusion.68
  180.9 5.6 %multiply_convert_fusion.1 = (bf16[1024,768]{0,1:T(8,128)(2,1)S(1)}, bf16[1024,768]{0,1:T(8,128)(2,1)S(1)}, bf16[1024,768]{0,1:T(8,128)(2,1)}) fusion(f32[1024,1536]{0,1:T(8,128)S(1)} %fusion.68, bf16[1024,1024]{1,0:T(8,128)(2,1)} %constant_dynamic-update-slice_fusion, bf16[704,1024]{1,0:T(8,128)(2,1)S(1)} %constant_dynamic-update-slice_fusion.10), kind=kOutput, calls=%fused_computation.11 | convolution fusion | flops 1623195648 | bytes 14548992 | tf_op jit(solution)/shard_map/dot_general | solution.py:632
  186.5 5.9 %convolution_convert_fusion = bf16[1024,1536]{1,0:T(8,128)(2,1)} fusion(bf16[1024,1024]{1,0:T(8,128)(2,1)S(1)} %constant_dynamic-update-slice_fusion.4, bf16[1024,768]{0,1:T(8,128)(2,1)S(1)} %get-tuple-element.162, bf16[1024,768]{0,1:T(8,128)(2,1)S(1)} %get-tuple-element.163), kind=kOutput, calls=%fused_computation.6 | convolution fusion | flops 3229089792 | bytes 8388608 | tf_op jit(solution)/shard_map/dot_general | solution.py:636
  193.0 5.3 %fusion.7 = bf16[512,1024]{1,0:T(8,128)(2,1)} fusion(bf16[1024,1536]{1,0:T(8,128)(2,1)} %copy-done.11, bf16[1024,768]{0,1:T(8,128)(2,1)} %copy-done.16, bf16[1024,768]{0,1:T(8,128)(2,1)} %copy-done.14), kind=kOutput, calls=%fused_computation.22 | convolution fusion | flops 1614282752 | bytes 7340032 | tf_op jit(solution)/shard_map/dot_general | solution.py:807
  198.3 2.8 collective-permute-start.26
  201.1 2.0 convolution_convert_fusion.2
  203.1 3.3 fusion.10
  206.4 1.6 copy-done.24
  210.9 3.5 fusion.17
  215.7 10.9 %collective-permute-done.28 = bf16[1,352,1024]{2,1,0:T(8,128)(2,1)} collective-permute-done((bf16[1,352,1024]{2,1,0:T(8,128)(2,1)}, bf16[1,352,1024]{2,1,0:T(8,128)(2,1)}, u32[]{:S(2)}, u32[]{:S(2)}) %collective-permute-start.28) | collective-permute-done | bytes 720928 | tf_op jit(solution)/shard_map/ppermute | solution.py:640
  226.6 1.5 convert_add_fusion
  228.2 3.1 fusion.16
  232.3 2.1 fusion.14.dffn_ref
  234.4 1.7 mix_back.1
  237.0 1.5 collective-permute-start.34
  238.5 1.8 collective-permute-start.35
  240.3 1.5 collective-permute-start.30
  241.8 2.1 convolution_convert_fusion.1
  244.9 3.2 fusion.15
  248.1 26.9 %collective-permute-done.29.refs_1_ = bf16[256,256]{1,0:T(8,128)(2,1)S(1)} collective-permute-done((bf16[256,256]{1,0:T(8,128)(2,1)}, bf16[256,256]{1,0:T(8,128)(2,1)S(1)}, u32[]{:S(2)}, u32[]{:S(2)}) %collective-permute-start.29) | collective-permute-done | bytes 131104 | tf_op jit(solution)/shard_map/ppermute | solution.py:644
  275.1 2.5 collective-permute-done.30.refs_2_
  277.7 40.9 %delta_backward.1 = (bf16[256,1024]{1,0:T(8,128)(2,1)S(1)}, bf16[256,1024]{1,0:T(8,128)(2,1)S(1)}, bf16[256,1024]{1,0:T(8,128)(2,1)}, bf16[256,1024]{1,0:T(8,128...) custom-call(bf16[256,256]{1,0:T(8,128)(2,1)S(1)} %copy-done.7, ...), custom_call_target="tpu_custom_call" | custom-call | flops 40000000000 | bytes 16777216 | tf_op jit(solution)/shard_map/delta_backward/pallas_call | solution.py:500
  318.6 3.4 collective-permute-start.38
  322.0 1.6 collective-permute-start.39
  323.6 1.7 copy-done.9
  325.3 5.9 %weigh_inputs.1 = bf16[1024,1152]{1,0:T(8,128)(2,1)} custom-call(s32[1]{0:T(128)} %bitcast.z_ref, bf16[1024,1024]{1,0:T(8,128)(2,1)S(1)} %copy-done.8, bf16[1024,1152]{1,0:T(8,128)(2,1)S(1)} %copy-done.9, f32[3,4,256]{2,1,0:T(4,128)S(1)} %get-tuple-element.118.dtaps_ref, f32[1,128]{1,0:T(1,128)S(1)} %get-tuple-element.119.dgain_ref, ...), custom_call_target="tpu_custom_call" | custom-call | flops 60000002048 | bytes 8388608 | tf_op jit(solution)/shard_map/weigh_inputs/pallas_call | solution.py:529
  331.2 2.1 add_bitcast_fusion
  333.3 29.0 %collective-permute-done.38 = bf16[256,1024]{1,0:T(8,128)(2,1)} collective-permute-done((bf16[256,1024]{1,0:T(8,128)(2,1)}, bf16[256,1024]{1,0:T(8,128)(2,1)}, u32[]{:S(2)}, u32[]{:S(2)}) %collective-permute-start.38) | collective-permute-done | bytes 524320 | tf_op jit(solution)/shard_map/ppermute | solution.py:644
  362.3 5.9 %collective-permute-done.39 = bf16[256,1024]{1,0:T(8,128)(2,1)} collective-permute-done((bf16[256,1024]{1,0:T(8,128)(2,1)}, bf16[256,1024]{1,0:T(8,128)(2,1)}, u32[]{:S(2)}, u32[]{:S(2)}) %collective-permute-start.39) | collective-permute-done | bytes 524320 | tf_op jit(solution)/shard_map/ppermute | solution.py:644
  369.5 2.0 fusion.23
  371.5 10.1 %collective-permute-done.43 = bf16[4,32,1536]{2,1,0:T(8,128)(2,1)S(1)} collective-permute-done((bf16[4,32,1536]{2,1,0:T(8,128)(2,1)S(1)}, bf16[4,32,1536]{2,1,0:T(8,128)(2,1)S(1)}, u32[]{:S(2)}, u32[]{:S(2)}) %collective-permute-start.43) | collective-permute-done | bytes 393248 | tf_op jit(solution)/shard_map/ppermute | solution.py:640
  381.9 1.4 collective-permute-start.44
  383.3 2.8 fusion.25
  386.1 1.6 collective-permute-start.45
  387.8 5.1 %collective-permute-done.45 = f32[32,1536]{1,0:T(8,128)S(1)} collective-permute-done((f32[32,1536]{1,0:T(8,128)S(1)}, f32[32,1536]{1,0:T(8,128)S(1)}, u32[]{:S(2)}, u32[]{:S(2)}) %collective-permute-start.45) | collective-permute-done | bytes 196640 | tf_op jit(solution)/shard_map/ppermute | solution.py:640
  392.9 4.2 collective-permute-done.46
  403.1 3.4 collective-permute-done.40
  406.4 7.1 %collective-permute-done.41 = bf16[1,32,2176]{2,1,0:T(8,128)(2,1)S(1)} collective-permute-done((bf16[1,32,2176]{2,1,0:T(8,128)(2,1)S(1)}, bf16[1,32,2176]{2,1,0:T(8,128)(2,1)S(1)}, u32[]{:S(2)}, u32[]{:S(2)}) %collective-permute-start.41) | collective-permute-done | bytes 139296 | tf_op jit(solution)/shard_map/ppermute | solution.py:644
  (252 shorter events, 62.7 us)
Async XLA Ops:
  7.2 17.3 %copy-start = (bf16[256,1024]{1,0:T(8,128)(2,1)S(1)}, bf16[256,1024]{1,0:T(8,128)(2,1)}, u32[]{:S(2)}) copy-start(bf16[256,1024]{1,0:T(8,128)(2,1)} %refs_5_.1) | copy-start | bytes 1572868
  7.2 19.8 %copy-start.34 = (s32[1,4]{1,0:T(1,128)S(1)}, s32[1,4]{1,0:T(1,128)}, u32[]{:S(2)}) copy-start(s32[1,4]{1,0:T(1,128)} %param.18) | copy-start | bytes 52
  7.2 20.8 %copy-start.33 = (s32[1,1024]{1,0:T(1,128)S(1)}, s32[1,1024]{1,0:T(1,128)}, u32[]{:S(2)}) copy-start(s32[1,1024]{1,0:T(1,128)} %param.19) | copy-start | bytes 12292
  7.2 69.4 %all-gather.3.cloned.1.call-start = ((), (), s32[]{:S(2)}) async-start(), calls=%async_computation.3 | async-start | bytes 2654208 | tf_op jit(solution)/shard_map/all_gather | solution.py:758
  13.8 3.9 collective-permute-start.3
  15.1 4.4 %collective-permute-start.4 = (bf16[1,32,1152]{2,1,0:T(8,128)(2,1)S(1)}, bf16[1,32,1152]{2,1,0:T(8,128)(2,1)S(1)}, u32[]{:S(2)}, u32[]{:S(2)}) collective-permute-start(bf16[1,32,1152]{2,1,0:T(8,128)(2,1)S(1)} %get-tuple-element.188), channel_id=1, source_target_pairs={{0,2},{1,3},{2,0},{3,1},{4,6},{5,7},{6,4},{7,5},{8,10},{9,11},{10,... | collective-permute-start | bytes 221192 | tf_op jit(solution)/shard_map/ppermute | solution.py:644
  16.2 7.4 %collective-permute-start.5 = (bf16[1,32,1152]{2,1,0:T(8,128)(2,1)S(1)}, bf16[1,32,1152]{2,1,0:T(8,128)(2,1)S(1)}, u32[]{:S(2)}, u32[]{:S(2)}) collective-permute-start(bf16[1,32,1152]{2,1,0:T(8,128)(2,1)S(1)} %get-tuple-element.187), channel_id=1, source_target_pairs={{0,3},{1,0},{2,1},{3,2},{4,7},{5,4},{6,5},{7,6},{8,11},{9,8},{10,9... | collective-permute-start | bytes 221192 | tf_op jit(solution)/shard_map/ppermute | solution.py:644
  23.7 17.7 %copy-start.28 = (bf16[32,2816]{1,0:T(8,128)(2,1)S(1)}, bf16[32,2816]{1,0:T(8,128)(2,1)}, u32[]{:S(2)}) copy-start(bf16[32,2816]{1,0:T(8,128)(2,1)} %param.30) | copy-start | bytes 540676
  24.4 113.8 %all-gather.5.cloned.1.call-start = ((), (), s32[]{:S(2)}) async-start(), calls=%async_computation.4 | async-start | bytes 2162688 | tf_op jit(solution)/shard_map/all_gather | solution.py:759
  24.4 13.2 %collective-permute-start = (bf16[256,1024]{1,0:T(8,128)(2,1)S(1)}, bf16[256,1024]{1,0:T(8,128)(2,1)}, u32[]{:S(2)}, u32[]{:S(2)}) collective-permute-start(bf16[256,1024]{1,0:T(8,128)(2,1)S(1)} %copy-done), channel_id=1, source_target_pairs={{0,1},{1,2},{2,3},{3,0},{4,5},{5,6},{6,7},{7,4},{8,9},{9,10},{10,1... | collective-permute-start | bytes 1572872 | tf_op jit(solution)/shard_map/ppermute | solution.py:644
  24.5 44.5 %collective-permute-start.1 = (bf16[256,1024]{1,0:T(8,128)(2,1)S(1)}, bf16[256,1024]{1,0:T(8,128)(2,1)}, u32[]{:S(2)}, u32[]{:S(2)}) collective-permute-start(bf16[256,1024]{1,0:T(8,128)(2,1)S(1)} %copy-done), channel_id=1, source_target_pairs={{0,2},{1,3},{2,0},{3,1},{4,6},{5,7},{6,4},{7,5},{8,10},{9,11},{10,... | collective-permute-start | bytes 1572872 | tf_op jit(solution)/shard_map/ppermute | solution.py:644
  26.2 46.2 %collective-permute-start.2 = (bf16[256,1024]{1,0:T(8,128)(2,1)S(1)}, bf16[256,1024]{1,0:T(8,128)(2,1)}, u32[]{:S(2)}, u32[]{:S(2)}) collective-permute-start(bf16[256,1024]{1,0:T(8,128)(2,1)S(1)} %copy-done), channel_id=1, source_target_pairs={{0,3},{1,0},{2,1},{3,2},{4,7},{5,4},{6,5},{7,6},{8,11},{9,8},{10,9... | collective-permute-start | bytes 1572872 | tf_op jit(solution)/shard_map/ppermute | solution.py:644
  26.9 306.4 %reduce-scatter.4.cloned.1.call-start = ((), (), s32[]{:S(2)}) async-start(), calls=%async_computation.5 | async-start | bytes 3932160 | tf_op jit(solution)/shard_map/reduce_scatter | solution.py:856
  37.6 23.5 %collective-permute-start.6 = (bf16[256,1024]{1,0:T(8,128)(2,1)S(1)}, bf16[256,1024]{1,0:T(8,128)(2,1)S(1)}, u32[]{:S(2)}, u32[]{:S(2)}) collective-permute-start(bf16[256,1024]{1,0:T(8,128)(2,1)S(1)} %copy-done.1), channel_id=1, source_target_pairs={{0,8},{4,12},{8,0},{12,4},{16,24},{20,28},{24,16},{28,20},{1,9},{5... | collective-permute-start | bytes 1572872 | tf_op jit(solution)/shard_map/ppermute | solution.py:640
  38.4 36.5 %collective-permute-start.7 = (bf16[256,1024]{1,0:T(8,128)(2,1)S(1)}, bf16[256,1024]{1,0:T(8,128)(2,1)S(1)}, u32[]{:S(2)}, u32[]{:S(2)}) collective-permute-start(bf16[256,1024]{1,0:T(8,128)(2,1)S(1)} %copy-done.1), channel_id=1, source_target_pairs={{0,4},{4,0},{8,12},{12,8},{16,20},{20,16},{24,28},{28,24},{1,5},{5... | collective-permute-start | bytes 1572872 | tf_op jit(solution)/shard_map/ppermute | solution.py:640
  42.7 2.4 collective-permute-start.9
  45.1 10.3 %collective-permute-start.10 = (bf16[32,1536]{1,0:T(8,128)(2,1)S(1)}, bf16[32,1536]{1,0:T(8,128)(2,1)S(1)}, u32[]{:S(2)}, u32[]{:S(2)}) collective-permute-start(bf16[32,1536]{1,0:T(8,128)(2,1)S(1)} %get-tuple-element.185), channel_id=1, source_target_pairs={{0,8},{4,12},{8,0},{12,4},{16,24},{20,28},{24,16},{28,20},{1,9},{5... | collective-permute-start | bytes 294920 | tf_op jit(solution)/shard_map/ppermute | solution.py:640
  55.4 9.1 %collective-permute-start.11 = (bf16[32,1536]{1,0:T(8,128)(2,1)S(1)}, bf16[32,1536]{1,0:T(8,128)(2,1)S(1)}, u32[]{:S(2)}, u32[]{:S(2)}) collective-permute-start(bf16[32,1536]{1,0:T(8,128)(2,1)S(1)} %get-tuple-element.184), channel_id=1, source_target_pairs={{0,12},{4,8},{8,4},{12,0},{16,28},{20,24},{24,20},{28,16},{1,13},{... | collective-permute-start | bytes 294920 | tf_op jit(solution)/shard_map/ppermute | solution.py:640
  61.1 14.7 %collective-permute-start.8 = (bf16[256,1024]{1,0:T(8,128)(2,1)S(1)}, bf16[256,1024]{1,0:T(8,128)(2,1)S(1)}, u32[]{:S(2)}, u32[]{:S(2)}) collective-permute-start(bf16[256,1024]{1,0:T(8,128)(2,1)S(1)} %collective-permute-done.6), channel_id=1, source_target_pairs={{0,4},{4,0},{8,12},{12,8},{16,20},{20,16},{24,28},{28,24},{1,5},{5... | collective-permute-start | bytes 1572872 | tf_op jit(solution)/shard_map/ppermute | solution.py:640
  72.4 43.0 %collective-permute-start.12 = (bf16[4,32,1536]{2,1,0:T(8,128)(2,1)}, bf16[4,32,1536]{2,1,0:T(8,128)(2,1)}, u32[]{:S(2)}, u32[]{:S(2)}) collective-permute-start(bf16[4,32,1536]{2,1,0:T(8,128)(2,1)} %bitcast.31), channel_id=1, source_target_pairs={{0,1},{1,2},{2,3},{3,0},{4,5},{5,6},{6,7},{7,4},{8,9},{9,10},{10,1... | collective-permute-start | bytes 1179656 | tf_op jit(solution)/shard_map/ppermute | solution.py:644
  72.4 43.0 %collective-permute-start.13 = (bf16[4,32,1536]{2,1,0:T(8,128)(2,1)}, bf16[4,32,1536]{2,1,0:T(8,128)(2,1)}, u32[]{:S(2)}, u32[]{:S(2)}) collective-permute-start(bf16[4,32,1536]{2,1,0:T(8,128)(2,1)} %bitcast.31), channel_id=1, source_target_pairs={{0,2},{1,3},{2,0},{3,1},{4,6},{5,7},{6,4},{7,5},{8,10},{9,11},{10,... | collective-permute-start | bytes 1179656 | tf_op jit(solution)/shard_map/ppermute | solution.py:644
  72.5 43.0 %collective-permute-start.14 = (bf16[4,32,1536]{2,1,0:T(8,128)(2,1)}, bf16[4,32,1536]{2,1,0:T(8,128)(2,1)}, u32[]{:S(2)}, u32[]{:S(2)}) collective-permute-start(bf16[4,32,1536]{2,1,0:T(8,128)(2,1)} %bitcast.31), channel_id=1, source_target_pairs={{0,3},{1,0},{2,1},{3,2},{4,7},{5,4},{6,5},{7,6},{8,11},{9,8},{10,9... | collective-permute-start | bytes 1179656 | tf_op jit(solution)/shard_map/ppermute | solution.py:644
  115.5 11.0 %collective-permute-start.15 = (bf16[256,256]{1,0:T(8,128)(2,1)S(1)}, bf16[256,256]{1,0:T(8,128)(2,1)S(1)}, u32[]{:S(2)}, u32[]{:S(2)}) collective-permute-start(bf16[256,256]{1,0:T(8,128)(2,1)S(1)} %get-tuple-element.87), channel_id=1, source_target_pairs={{0,1},{1,2},{2,3},{3,0},{4,5},{5,6},{6,7},{7,4},{8,9},{9,10},{10,1... | collective-permute-start | bytes 393224 | tf_op jit(solution)/shard_map/ppermute | solution.py:644
  116.8 16.6 %collective-permute-start.16 = (bf16[256,256]{1,0:T(8,128)(2,1)S(1)}, bf16[256,256]{1,0:T(8,128)(2,1)S(1)}, u32[]{:S(2)}, u32[]{:S(2)}) collective-permute-start(bf16[256,256]{1,0:T(8,128)(2,1)S(1)} %get-tuple-element.88), channel_id=1, source_target_pairs={{0,2},{1,3},{2,0},{3,1},{4,6},{5,7},{6,4},{7,5},{8,10},{9,11},{10,... | collective-permute-start | bytes 393224 | tf_op jit(solution)/shard_map/ppermute | solution.py:644
  119.7 15.5 %collective-permute-start.17 = (bf16[256,256]{1,0:T(8,128)(2,1)S(1)}, bf16[256,256]{1,0:T(8,128)(2,1)S(1)}, u32[]{:S(2)}, u32[]{:S(2)}) collective-permute-start(bf16[256,256]{1,0:T(8,128)(2,1)S(1)} %get-tuple-element.89), channel_id=1, source_target_pairs={{0,3},{1,0},{2,1},{3,2},{4,7},{5,4},{6,5},{7,6},{8,11},{9,8},{10,9... | collective-permute-start | bytes 393224 | tf_op jit(solution)/shard_map/ppermute | solution.py:644
  119.9 15.3 %copy-start.30 = (bf16[88,1024]{1,0:T(8,128)(2,1)S(1)}, bf16[88,1024]{1,0:T(8,128)(2,1)}, u32[]{:S(2)}) copy-start(bf16[88,1024]{1,0:T(8,128)(2,1)} %param.32) | copy-start | bytes 540676
  125.5 49.9 %collective-permute-start.25 = (bf16[512,1536]{1,0:T(8,128)(2,1)}, bf16[512,1536]{1,0:T(8,128)(2,1)}, u32[]{:S(2)}, u32[]{:S(2)}) collective-permute-start(bf16[512,1536]{1,0:T(8,128)(2,1)} %bitcast.184), channel_id=1, source_target_pairs={{0,16},{4,20},{8,24},{12,28},{16,0},{20,4},{24,8},{28,12},{1,17},{... | collective-permute-start | bytes 4718600 | tf_op jit(solution)/shard_map/ppermute | solution.py:640
  135.2 7.0 %collective-permute-start.18 = (bf16[1,88,1024]{2,1,0:T(8,128)(2,1)S(1)}, bf16[1,88,1024]{2,1,0:T(8,128)(2,1)}, u32[]{:S(2)}, u32[]{:S(2)}) collective-permute-start(bf16[1,88,1024]{2,1,0:T(8,128)(2,1)S(1)} %bitcast.197), channel_id=1, source_target_pairs={{0,1},{1,2},{2,3},{3,0},{4,5},{5,6},{6,7},{7,4},{8,9},{9,10},{10,1... | collective-permute-start | bytes 540680 | tf_op jit(solution)/shard_map/ppermute | solution.py:644
  135.2 14.7 %collective-permute-start.19 = (bf16[1,88,1024]{2,1,0:T(8,128)(2,1)S(1)}, bf16[1,88,1024]{2,1,0:T(8,128)(2,1)}, u32[]{:S(2)}, u32[]{:S(2)}) collective-permute-start(bf16[1,88,1024]{2,1,0:T(8,128)(2,1)S(1)} %bitcast.198), channel_id=1, source_target_pairs={{0,2},{1,3},{2,0},{3,1},{4,6},{5,7},{6,4},{7,5},{8,10},{9,11},{10,... | collective-permute-start | bytes 540680 | tf_op jit(solution)/shard_map/ppermute | solution.py:644
  136.6 16.6 %collective-permute-start.20 = (bf16[1,88,1024]{2,1,0:T(8,128)(2,1)S(1)}, bf16[1,88,1024]{2,1,0:T(8,128)(2,1)S(1)}, u32[]{:S(2)}, u32[]{:S(2)}) collective-permute-start(bf16[1,88,1024]{2,1,0:T(8,128)(2,1)S(1)} %bitcast.199), channel_id=1, source_target_pairs={{0,3},{1,0},{2,1},{3,2},{4,7},{5,4},{6,5},{7,6},{8,11},{9,8},{10,9... | collective-permute-start | bytes 540680 | tf_op jit(solution)/shard_map/ppermute | solution.py:644
  140.7 14.2 %copy-start.2 = (bf16[256,1024]{1,0:T(8,128)(2,1)}, bf16[256,1024]{1,0:T(8,128)(2,1)S(1)}, u32[]{:S(2)}) copy-start(bf16[256,1024]{1,0:T(8,128)(2,1)S(1)} %get-tuple-element.135) | copy-start | bytes 1572868
  140.7 14.4 %collective-permute-start.22 = (bf16[256,1024]{1,0:T(8,128)(2,1)S(1)}, bf16[256,1024]{1,0:T(8,128)(2,1)S(1)}, u32[]{:S(2)}, u32[]{:S(2)}) collective-permute-start(bf16[256,1024]{1,0:T(8,128)(2,1)S(1)} %get-tuple-element.91), channel_id=1, source_target_pairs={{0,8},{4,12},{8,0},{12,4},{16,24},{20,28},{24,16},{28,20},{1,9},{5... | collective-permute-start | bytes 1572872 | tf_op jit(solution)/shard_map/ppermute | solution.py:640
  142.2 13.9 %collective-permute-start.23 = (bf16[256,1024]{1,0:T(8,128)(2,1)S(1)}, bf16[256,1024]{1,0:T(8,128)(2,1)S(1)}, u32[]{:S(2)}, u32[]{:S(2)}) collective-permute-start(bf16[256,1024]{1,0:T(8,128)(2,1)S(1)} %get-tuple-element.91), channel_id=1, source_target_pairs={{0,4},{4,0},{8,12},{12,8},{16,20},{20,16},{24,28},{28,24},{1,5},{5... | collective-permute-start | bytes 1572872 | tf_op jit(solution)/shard_map/ppermute | solution.py:640
  153.2 22.0 %collective-permute-start.21 = (bf16[352,1024]{1,0:T(8,128)(2,1)S(1)}, bf16[352,1024]{1,0:T(8,128)(2,1)S(1)}, u32[]{:S(2)}, u32[]{:S(2)}) collective-permute-start(bf16[352,1024]{1,0:T(8,128)(2,1)S(1)} %bitcast.187), channel_id=1, source_target_pairs={{0,16},{4,20},{8,24},{12,28},{16,0},{20,4},{24,8},{28,12},{1,17},{... | collective-permute-start | bytes 2162696 | tf_op jit(solution)/shard_map/ppermute | solution.py:640
  155.0 20.2 %collective-permute-start.24 = (bf16[256,1024]{1,0:T(8,128)(2,1)S(1)}, bf16[256,1024]{1,0:T(8,128)(2,1)S(1)}, u32[]{:S(2)}, u32[]{:S(2)}) collective-permute-start(bf16[256,1024]{1,0:T(8,128)(2,1)S(1)} %collective-permute-done.22), channel_id=1, source_target_pairs={{0,4},{4,0},{8,12},{12,8},{16,20},{20,16},{24,28},{28,24},{1,5},{5... | collective-permute-start | bytes 1572872 | tf_op jit(solution)/shard_map/ppermute | solution.py:640
  192.5 207.9 %reduce-scatter.8.cloned.1.call-start = ((), (), s32[]{:S(2)}) async-start(), calls=%async_computation.7 | async-start | bytes 2359296 | tf_op jit(solution)/shard_map/reduce_scatter | solution.py:868
  198.3 12.6 %collective-permute-start.26 = (bf16[512,1024]{1,0:T(8,128)(2,1)}, bf16[512,1024]{1,0:T(8,128)(2,1)}, u32[]{:S(2)}, u32[]{:S(2)}) collective-permute-start(bf16[512,1024]{1,0:T(8,128)(2,1)} %fusion.7), channel_id=1, source_target_pairs={{0,4},{4,0},{8,12},{12,8},{16,20},{20,16},{24,28},{28,24},{1,5},{5... | collective-permute-start | bytes 3145736 | tf_op jit(solution)/shard_map/ppermute | solution.py:640
  203.1 25.1 %collective-permute-start.32 = (bf16[512,1024]{1,0:T(8,128)(2,1)}, bf16[512,1024]{1,0:T(8,128)(2,1)}, u32[]{:S(2)}, u32[]{:S(2)}) collective-permute-start(bf16[512,1024]{1,0:T(8,128)(2,1)} %convolution_convert_fusion.2), channel_id=1, source_target_pairs={{0,4},{4,0},{8,12},{12,8},{16,20},{20,16},{24,28},{28,24},{1,5},{5... | collective-permute-start | bytes 3145736 | tf_op jit(solution)/shard_map/ppermute | solution.py:640
  209.0 17.6 %collective-permute-start.28 = (bf16[1,352,1024]{2,1,0:T(8,128)(2,1)}, bf16[1,352,1024]{2,1,0:T(8,128)(2,1)}, u32[]{:S(2)}, u32[]{:S(2)}) collective-permute-start(bf16[1,352,1024]{2,1,0:T(8,128)(2,1)} %dynamic-slice_convert_fusion), channel_id=1, source_target_pairs={{0,16},{4,20},{8,24},{12,28},{16,0},{20,4},{24,8},{28,12},{1,17},{... | collective-permute-start | bytes 2162696 | tf_op jit(solution)/shard_map/ppermute | solution.py:640
  210.9 15.7 %copy-start.25 = (f32[704,1024]{1,0:T(8,128)S(1)}, f32[704,1024]{1,0:T(8,128)}, u32[]{:S(2)}) copy-start(f32[704,1024]{1,0:T(8,128)} %copy-done.24) | copy-start | bytes 8650756
  210.9 17.2 %copy-start.22 = (bf16[704,1024]{1,0:T(8,128)(2,1)S(1)}, bf16[704,1024]{1,0:T(8,128)(2,1)}, u32[]{:S(2)}) copy-start(bf16[704,1024]{1,0:T(8,128)(2,1)} %copy-done.20) | copy-start | bytes 4325380
  214.4 17.9 %collective-permute-start.27 = (bf16[256,1024]{1,0:T(8,128)(2,1)S(1)}, bf16[256,1024]{1,0:T(8,128)(2,1)S(1)}, u32[]{:S(2)}, u32[]{:S(2)}) collective-permute-start(bf16[256,1024]{1,0:T(8,128)(2,1)S(1)} %fusion.17), channel_id=1, source_target_pairs={{0,8},{4,12},{8,0},{12,4},{16,24},{20,28},{24,16},{28,20},{1,9},{5... | collective-permute-start | bytes 1572872 | tf_op jit(solution)/shard_map/ppermute | solution.py:640
  231.3 12.7 %collective-permute-start.33 = (bf16[256,1024]{1,0:T(8,128)(2,1)}, bf16[256,1024]{1,0:T(8,128)(2,1)}, u32[]{:S(2)}, u32[]{:S(2)}) collective-permute-start(bf16[256,1024]{1,0:T(8,128)(2,1)} %fusion.16), channel_id=1, source_target_pairs={{0,8},{4,12},{8,0},{12,4},{16,24},{20,28},{24,16},{28,20},{1,9},{5... | collective-permute-start | bytes 1572872 | tf_op jit(solution)/shard_map/ppermute | solution.py:640
  237.0 85.0 %collective-permute-start.34 = (bf16[1,88,1024]{2,1,0:T(8,128)(2,1)}, bf16[1,88,1024]{2,1,0:T(8,128)(2,1)}, u32[]{:S(2)}, u32[]{:S(2)}) collective-permute-start(bf16[1,88,1024]{2,1,0:T(8,128)(2,1)} %get-tuple-element.171), channel_id=1, source_target_pairs={{0,1},{1,2},{2,3},{3,0},{4,5},{5,6},{6,7},{7,4},{8,9},{9,10},{10,1... | collective-permute-start | bytes 540680 | tf_op jit(solution)/shard_map/ppermute | solution.py:644
  238.5 92.6 %collective-permute-start.35 = (bf16[1,88,1024]{2,1,0:T(8,128)(2,1)}, bf16[1,88,1024]{2,1,0:T(8,128)(2,1)}, u32[]{:S(2)}, u32[]{:S(2)}) collective-permute-start(bf16[1,88,1024]{2,1,0:T(8,128)(2,1)} %get-tuple-element.173), channel_id=1, source_target_pairs={{0,2},{1,3},{2,0},{3,1},{4,6},{5,7},{6,4},{7,5},{8,10},{9,11},{10,... | collective-permute-start | bytes 540680 | tf_op jit(solution)/shard_map/ppermute | solution.py:644
  240.3 34.7 %collective-permute-start.29 = (bf16[256,256]{1,0:T(8,128)(2,1)}, bf16[256,256]{1,0:T(8,128)(2,1)S(1)}, u32[]{:S(2)}, u32[]{:S(2)}) collective-permute-start(bf16[256,256]{1,0:T(8,128)(2,1)} %get-tuple-element.103), channel_id=1, source_target_pairs={{0,1},{1,2},{2,3},{3,0},{4,5},{5,6},{6,7},{7,4},{8,9},{9,10},{10,1... | collective-permute-start | bytes 393224 | tf_op jit(solution)/shard_map/ppermute | solution.py:644
  240.3 37.4 %collective-permute-start.30 = (bf16[256,256]{1,0:T(8,128)(2,1)S(1)}, bf16[256,256]{1,0:T(8,128)(2,1)S(1)}, u32[]{:S(2)}, u32[]{:S(2)}) collective-permute-start(bf16[256,256]{1,0:T(8,128)(2,1)S(1)} %get-tuple-element.104), channel_id=1, source_target_pairs={{0,2},{1,3},{2,0},{3,1},{4,6},{5,7},{6,4},{7,5},{8,10},{9,11},{10,... | collective-permute-start | bytes 393224 | tf_op jit(solution)/shard_map/ppermute | solution.py:644
  244.0 33.7 %copy-start.7 = (bf16[256,256]{1,0:T(8,128)(2,1)S(1)}, bf16[256,256]{1,0:T(8,128)(2,1)}, u32[]{:S(2)}) copy-start(bf16[256,256]{1,0:T(8,128)(2,1)} %copy-done.6) | copy-start | bytes 393220
  244.0 156.4 %reduce-scatter.6.cloned.1.call-start = ((), (), s32[]{:S(2)}) async-start(), calls=%async_computation.6 | async-start | bytes 2654208 | tf_op jit(solution)/shard_map/reduce_scatter | solution.py:878
  244.0 33.7 %collective-permute-start.31 = (bf16[256,256]{1,0:T(8,128)(2,1)S(1)}, bf16[256,256]{1,0:T(8,128)(2,1)S(1)}, u32[]{:S(2)}, u32[]{:S(2)}) collective-permute-start(bf16[256,256]{1,0:T(8,128)(2,1)S(1)} %get-tuple-element.105), channel_id=1, source_target_pairs={{0,3},{1,0},{2,1},{3,2},{4,7},{5,4},{6,5},{7,6},{8,11},{9,8},{10,9... | collective-permute-start | bytes 393224 | tf_op jit(solution)/shard_map/ppermute | solution.py:644
  275.0 56.2 %collective-permute-start.36 = (bf16[1,88,1024]{2,1,0:T(8,128)(2,1)}, bf16[1,88,1024]{2,1,0:T(8,128)(2,1)}, u32[]{:S(2)}, u32[]{:S(2)}) collective-permute-start(bf16[1,88,1024]{2,1,0:T(8,128)(2,1)} %get-tuple-element.172), channel_id=1, source_target_pairs={{0,3},{1,0},{2,1},{3,2},{4,7},{5,4},{6,5},{7,6},{8,11},{9,8},{10,9... | collective-permute-start | bytes 540680 | tf_op jit(solution)/shard_map/ppermute | solution.py:644
  277.7 45.9 %copy-start.8 = (bf16[1024,1024]{1,0:T(8,128)(2,1)S(1)}, bf16[1024,1024]{1,0:T(8,128)(2,1)}, u32[]{:S(2)}) copy-start(bf16[1024,1024]{1,0:T(8,128)(2,1)} %get-tuple-element.77.hidden_ref) | copy-start | bytes 6291460
  318.6 14.7 %collective-permute-start.37 = (bf16[256,1024]{1,0:T(8,128)(2,1)S(1)}, bf16[256,1024]{1,0:T(8,128)(2,1)}, u32[]{:S(2)}, u32[]{:S(2)}) collective-permute-start(bf16[256,1024]{1,0:T(8,128)(2,1)S(1)} %get-tuple-element.126), channel_id=1, source_target_pairs={{0,1},{1,2},{2,3},{3,0},{4,5},{5,6},{6,7},{7,4},{8,9},{9,10},{10,1... | collective-permute-start | bytes 1572872 | tf_op jit(solution)/shard_map/ppermute | solution.py:644
  318.6 43.7 %collective-permute-start.38 = (bf16[256,1024]{1,0:T(8,128)(2,1)}, bf16[256,1024]{1,0:T(8,128)(2,1)}, u32[]{:S(2)}, u32[]{:S(2)}) collective-permute-start(bf16[256,1024]{1,0:T(8,128)(2,1)} %get-tuple-element.127), channel_id=1, source_target_pairs={{0,2},{1,3},{2,0},{3,1},{4,6},{5,7},{6,4},{7,5},{8,10},{9,11},{10,... | collective-permute-start | bytes 1572872 | tf_op jit(solution)/shard_map/ppermute | solution.py:644
  322.0 46.2 %collective-permute-start.39 = (bf16[256,1024]{1,0:T(8,128)(2,1)}, bf16[256,1024]{1,0:T(8,128)(2,1)}, u32[]{:S(2)}, u32[]{:S(2)}) collective-permute-start(bf16[256,1024]{1,0:T(8,128)(2,1)} %get-tuple-element.128), channel_id=1, source_target_pairs={{0,3},{1,0},{2,1},{3,2},{4,7},{5,4},{6,5},{7,6},{8,11},{9,8},{10,9... | collective-permute-start | bytes 1572872 | tf_op jit(solution)/shard_map/ppermute | solution.py:644
  331.2 38.4 %copy-start.32 = (f32[1024]{0:T(1024)S(1)}, f32[1024]{0:T(1024)}, u32[]{:S(2)}) copy-start(f32[1024]{0:T(1024)} %get-tuple-element.156) | copy-start | bytes 12292
  333.2 34.9 %copy-start.27 = (bf16[8,32,1536]{2,1,0:T(8,128)(2,1)S(1)}, bf16[8,32,1536]{2,1,0:T(8,128)(2,1)}, u32[]{:S(2)}) copy-start(bf16[8,32,1536]{2,1,0:T(8,128)(2,1)} %reduce-scatter.4.cloned.1.call-done) | copy-start | bytes 2359300
  368.2 13.4 %collective-permute-start.43 = (bf16[4,32,1536]{2,1,0:T(8,128)(2,1)S(1)}, bf16[4,32,1536]{2,1,0:T(8,128)(2,1)S(1)}, u32[]{:S(2)}, u32[]{:S(2)}) collective-permute-start(bf16[4,32,1536]{2,1,0:T(8,128)(2,1)S(1)} %constant_dynamic-slice_fusion), channel_id=1, source_target_pairs={{0,16},{4,20},{8,24},{12,28},{16,0},{20,4},{24,8},{28,12},{1,17},{... | collective-permute-start | bytes 1179656 | tf_op jit(solution)/shard_map/ppermute | solution.py:640
  381.9 5.9 %collective-permute-start.44 = (f32[32,1536]{1,0:T(8,128)S(1)}, f32[32,1536]{1,0:T(8,128)S(1)}, u32[]{:S(2)}, u32[]{:S(2)}) collective-permute-start(f32[32,1536]{1,0:T(8,128)S(1)} %get-tuple-element.169), channel_id=1, source_target_pairs={{0,4},{4,0},{8,12},{12,8},{16,20},{20,16},{24,28},{28,24},{1,5},{5... | collective-permute-start | bytes 589832 | tf_op jit(solution)/shard_map/ppermute | solution.py:640
  386.1 6.8 %collective-permute-start.45 = (f32[32,1536]{1,0:T(8,128)S(1)}, f32[32,1536]{1,0:T(8,128)S(1)}, u32[]{:S(2)}, u32[]{:S(2)}) collective-permute-start(f32[32,1536]{1,0:T(8,128)S(1)} %get-tuple-element.168), channel_id=1, source_target_pairs={{0,8},{4,12},{8,0},{12,4},{16,24},{20,28},{24,16},{28,20},{1,9},{5... | collective-permute-start | bytes 589832 | tf_op jit(solution)/shard_map/ppermute | solution.py:640
  387.7 9.4 %collective-permute-start.46 = (f32[32,1536]{1,0:T(8,128)S(1)}, f32[32,1536]{1,0:T(8,128)S(1)}, u32[]{:S(2)}, u32[]{:S(2)}) collective-permute-start(f32[32,1536]{1,0:T(8,128)S(1)} %get-tuple-element.167), channel_id=1, source_target_pairs={{0,12},{4,8},{8,4},{12,0},{16,28},{20,24},{24,20},{28,16},{1,13},{... | collective-permute-start | bytes 589832 | tf_op jit(solution)/shard_map/ppermute | solution.py:640
  401.5 4.9 %collective-permute-start.40 = (bf16[1,32,2176]{2,1,0:T(8,128)(2,1)S(1)}, bf16[1,32,2176]{2,1,0:T(8,128)(2,1)S(1)}, u32[]{:S(2)}, u32[]{:S(2)}) collective-permute-start(bf16[1,32,2176]{2,1,0:T(8,128)(2,1)S(1)} %get-tuple-element.180), channel_id=1, source_target_pairs={{0,1},{1,2},{2,3},{3,0},{4,5},{5,6},{6,7},{7,4},{8,9},{9,10},{10,1... | collective-permute-start | bytes 417800 | tf_op jit(solution)/shard_map/ppermute | solution.py:644
  401.6 11.9 %collective-permute-start.41 = (bf16[1,32,2176]{2,1,0:T(8,128)(2,1)S(1)}, bf16[1,32,2176]{2,1,0:T(8,128)(2,1)S(1)}, u32[]{:S(2)}, u32[]{:S(2)}) collective-permute-start(bf16[1,32,2176]{2,1,0:T(8,128)(2,1)S(1)} %get-tuple-element.179), channel_id=1, source_target_pairs={{0,2},{1,3},{2,0},{3,1},{4,6},{5,7},{6,4},{7,5},{8,10},{9,11},{10,... | collective-permute-start | bytes 417800 | tf_op jit(solution)/shard_map/ppermute | solution.py:644
  401.6 12.4 %collective-permute-start.42 = (bf16[1,32,2176]{2,1,0:T(8,128)(2,1)S(1)}, bf16[1,32,2176]{2,1,0:T(8,128)(2,1)S(1)}, u32[]{:S(2)}, u32[]{:S(2)}) collective-permute-start(bf16[1,32,2176]{2,1,0:T(8,128)(2,1)S(1)} %get-tuple-element.178), channel_id=1, source_target_pairs={{0,3},{1,0},{2,1},{3,2},{4,7},{5,4},{6,5},{7,6},{8,11},{9,8},{10,9... | collective-permute-start | bytes 417800 | tf_op jit(solution)/shard_map/ppermute | solution.py:644
  (23 other events, 138.3 us)
Sparse Core Ops, SparseCore 0:
  24.5 35.2 all-gather.2
  62.7 73.1 all-gather.4
  192.6 80.7 reduce-scatter.3
  276.5 41.1 reduce-scatter.7
  333.4 46.2 reduce-scatter.5

commit v3 on v2

--- a/solution.py
+++ b/solution.py
@@ -122,23 +122,39 @@
     return jax.nn.sigmoid(raw_ref[rows, lane:lane + 1].astype(NARROW).astype(WIDE))
 
 
-def forward_kernel(heads, width, n_fs, *refs):
+def shard_places(size, features, shard_rows, turned_round):
+    unit, each = shard_rows
+    shape = (features, size) if turned_round else (size, features)
+    value = lax.broadcasted_iota(jnp.int32, shape, 1 if turned_round else 0)
+    lane = lax.broadcasted_iota(jnp.int32, shape, 0 if turned_round else 1)
+    chosen = (lane // unit == value // each) & (lane % unit == value % each)
+    return jnp.where(chosen, 1.0, 0.0).astype(NARROW)
+
+
+def forward_kernel(heads, width, n_fs, shard_rows, *refs):
     pieces, refs = refs[:n_fs], refs[n_fs:]
-    (win_ref, gmix_ref, near_ref, far_ref, taps_ref, gain_ref, segcol_ref, poscol_ref, segrow_ref, edges_ref,
-     *refs) = refs
+    (win_ref, near_ref, far_ref, segcol_ref, poscol_ref, segrow_ref, edges_ref, z_ref, *refs) = refs
     blocks, refs = refs[:n_fs], refs[n_fs:]
-    (hidden_ref, packed_ref, raw_ref, out_ref, q_ref, k_ref, inv_ref, score_ref, dots_ref, upd_ref, state_ref,
+    (side_ref, taps_ref, gain_ref, hidden_ref, raw_ref, out_ref, q_ref, k_ref, inv_ref, score_ref, dots_ref, upd_ref, state_ref,
      move_ref, pad_ref, base_ref, w_ref, normed_ref) = refs
     total = raw_ref.shape[0]
     count = total // CHUNK
     span = heads * width
+    side_ref[...] = win_ref[:, 4 * span:].astype(WIDE).T
+    taps_count = taps_ref.shape[1]
+    own = pl.ds(pl.multiple_of(z_ref[0] * span, span), span)
+    for which in range(3):
+        first_row = heads + 2 + which * taps_count
+        taps_ref[which] = side_ref[first_row:first_row + taps_count, own]
+    last_row = heads + 2 + 3 * taps_count
+    entries = jnp.broadcast_to(side_ref[last_row:last_row + 1, :], (8, side_ref.shape[1])).astype(NARROW)
+    gain_ref[...] = plain_dot(entries, shard_places(width, side_ref.shape[1], shard_rows, True))[0:1]
 
     def enter(index, _):
         rows = pl.ds(pl.multiple_of(index * ENTER, ENTER), ENTER)
         packed = pack_rows(near_ref[rows, :], pieces)
-        packed_ref[rows, :] = packed.astype(NARROW)
         scale = lax.rsqrt(jnp.mean(packed * packed, axis=-1, keepdims=True) + norm_eps)
-        hidden = (packed * scale * gmix_ref[...]).astype(NARROW)
+        hidden = (packed * scale * side_ref[heads:heads + 1, :]).astype(NARROW)
         hidden_ref[rows, :] = hidden
         raw_ref[rows, :] = plain_dot(hidden, win_ref[...])
         return 0
@@ -232,14 +248,12 @@
         block[...] = unpack_rows(far_ref[...], normed_ref[...], k, total // n_fs)
 
 
-def backward_kernel(heads, width, n_fs, *refs):
+def backward_kernel(heads, width, n_fs, shard_rows, *refs):
     pieces, refs = refs[:n_fs], refs[n_fs:]
-    (win_ref, near_ref, far_ref, taps_ref, gain_ref, segcol_ref, poscol_ref, segrow_ref, edges_ref,
-     packed_ref, raw_ref, mixed_ref, q_ref, k_ref, inv_ref, score_ref, dots_ref, upd_ref, state_ref, move_ref,
-     *refs) = refs
-    blocks, refs = refs[:n_fs], refs[n_fs:]
-    (draw_ref, dtaps_ref, dgain_ref, dgmix_ref,
-     pad_ref, grad_ref, pdo_ref, dconv_ref, dout_ref, dnormed_ref, dhid_ref) = refs
+    (win_ref, near_ref, segcol_ref, poscol_ref, segrow_ref, edges_ref, z_ref, dgffn_ref,
+     taps_ref, gain_ref, hidden_ref, raw_ref, mixed_ref, q_ref, k_ref, inv_ref, score_ref, dots_ref, upd_ref, state_ref,
+     move_ref, draw_ref, gradin_ref,
+     dtaps_ref, sum_ref, small_ref, pad_ref, grad_ref, pdo_ref, dconv_ref, dout_ref, dnormed_ref) = refs
     total = raw_ref.shape[0]
 
     def enter(index, _):
@@ -285,7 +299,7 @@
                 grad_ref[at] = product_exact(query_t, dout) - product(key_t, halves(back))
         return dgain
 
-    dgain_ref[...] = lax.fori_loop(0, count // BACK_STEP, first, jnp.zeros((1, width), WIDE))
+    dgain = lax.fori_loop(0, count // BACK_STEP, first, jnp.zeros((1, width), WIDE))
 
     def second(step, grads):
         index = count - 1 - step
@@ -388,50 +402,44 @@
 
     lax.fori_loop(0, count, fourth, 0)
 
-    def leave(index, sums):
-        rows = pl.ds(pl.multiple_of(index * ENTER, ENTER), ENTER)
-        dhidden = plain_dot(draw_ref[rows, :], win_ref[...], 1, 1)
-        dhid_ref[rows, :] = dhidden.astype(NARROW)
-        packed = packed_ref[rows, :].astype(WIDE)
-        scale = lax.rsqrt(jnp.mean(packed * packed, axis=-1, keepdims=True) + norm_eps)
-        return sums + jnp.sum(dhidden * (packed * scale), axis=0, keepdims=True)
-
-    dgmix_ref[...] = lax.fori_loop(0, total // ENTER, leave, jnp.zeros(dgmix_ref.shape, WIDE))
-    for k, block in enumerate(blocks):
-        block[...] = unpack_rows(far_ref[...], dhid_ref[...], k, total // n_fs)
-
-
-def weigh_kernel(heads, width, shard_rows, z_ref, hidden_ref, draw_ref, dtaps_ref, dgain_ref, dgmix_ref, dgffn_ref,
-                 out_ref, gradin_ref, small_ref):
-    total = hidden_ref.shape[0]
-    span = heads * width
-    taps_count = dtaps_ref.shape[1]
-
     def weigh(index, _):
         rows = pl.ds(pl.multiple_of(index * ENTER, ENTER), ENTER)
-        gradin_ref[...] += plain_dot(hidden_ref[rows, :], draw_ref[rows, :], 0, 0)
+        sum_ref[...] += plain_dot(hidden_ref[rows, :], draw_ref[rows, :], 0, 0)
         return 0
 
-    gradin_ref[...] = jnp.zeros(gradin_ref.shape, WIDE)
+    sum_ref[...] = jnp.zeros(sum_ref.shape, WIDE)
     lax.fori_loop(0, total // ENTER, weigh, 0)
     features = small_ref.shape[1]
     small_ref[...] = jnp.zeros(small_ref.shape, WIDE)
-    small_ref[heads:heads + 1, :] = dgmix_ref[...]
     small_ref[heads + 1:heads + 2, :] = dgffn_ref[...]
     own = pl.ds(pl.multiple_of(z_ref[0] * span, span), span)
     for which in range(3):
         first_row = heads + 2 + which * taps_count
         small_ref[first_row:first_row + taps_count, own] = dtaps_ref[which]
-    unit, each = shard_rows
-    value = lax.broadcasted_iota(jnp.int32, (width, features), 0)
-    lane = lax.broadcasted_iota(jnp.int32, (width, features), 1)
-    chosen = (lane // unit == value // each) & (lane % unit == value % each)
-    chosen = jnp.where(chosen, 1.0, 0.0).astype(NARROW)
     last_row = heads + 2 + 3 * taps_count
-    small_ref[last_row:last_row + 1, :] = product_exact(halves(jnp.broadcast_to(dgain_ref[...], (8, width))), chosen)[0:1]
-    side = pl.ds(4 * span, small_ref.shape[0])
-    gradin_ref[:, side] += small_ref[...].T
-    out_ref[...] = gradin_ref[...].astype(NARROW)
+    small_ref[last_row:last_row + 1, :] = product_exact(
+        halves(jnp.broadcast_to(dgain, (8, width))), shard_places(width, features, shard_rows, False))[0:1]
+    gain = win_ref[:, 4 * span + heads:4 * span + heads + 1].astype(WIDE)
+    across = jnp.sum(sum_ref[...] * win_ref[...].astype(WIDE), axis=-1, keepdims=True) / gain
+    beside = small_ref[...].T
+    lane = lax.broadcasted_iota(jnp.int32, beside.shape, 1)
+    gradin_ref[:, 0:4 * span] = sum_ref[:, 0:4 * span].astype(NARROW)
+    beside = sum_ref[:, 4 * span:] + beside + jnp.where(lane == heads, across, 0.0)
+    gradin_ref[:, 4 * span:] = beside.astype(NARROW)
+
+
+def leave_kernel(n_fs, win_ref, far_ref, draw_ref, *refs):
+    blocks, (dhid_ref,) = refs[:n_fs], refs[n_fs:]
+    total = draw_ref.shape[0]
+
+    def leave(index, _):
+        rows = pl.ds(pl.multiple_of(index * ENTER, ENTER), ENTER)
+        dhid_ref[rows, :] = plain_dot(draw_ref[rows, :], win_ref[...], 1, 1).astype(NARROW)
+        return 0
+
+    lax.fori_loop(0, total // ENTER, leave, 0)
+    for k, block in enumerate(blocks):
+        block[...] = unpack_rows(far_ref[...], dhid_ref[...], k, total // n_fs)
 
 
 def product_exact(left, exact, left_dim=1, right_dim=0, flip=False):
@@ -457,7 +465,7 @@
     return pl.BlockSpec(memory_space=pltpu.SMEM)
 
 
-def delta_forward(pieces, w_in, gmix, near, far, taps, gain, segcol, poscol, segrow, edges, heads, width):
+def delta_forward(pieces, w_in, near, far, segcol, poscol, segrow, edges, z, heads, width, n_taps, shard_rows):
     n_fs = len(pieces)
     total = near.shape[0]
     features, lanes = w_in.shape
@@ -470,12 +478,15 @@
     state = jax.ShapeDtypeStruct((count * heads, width, width), WIDE)
     block = jax.ShapeDtypeStruct((total // n_fs, span), NARROW)
     raw = jax.ShapeDtypeStruct((total, lanes), WIDE)
+    side = jax.ShapeDtypeStruct((lanes - 4 * span, features), WIDE)
+    taps = jax.ShapeDtypeStruct((3, n_taps, span), WIDE)
+    gain = jax.ShapeDtypeStruct((1, width), WIDE)
     result = pl.pallas_call(
-        functools.partial(forward_kernel, heads, width, n_fs),
+        functools.partial(forward_kernel, heads, width, n_fs, shard_rows),
         out_shape=(block,) * n_fs
-        + (full, full, raw, thin, rows, rows, square, square, square, rows, state, state),
-        in_specs=specs(n_fs + 9) + [in_scalars()],
-        out_specs=tuple(specs(n_fs + 12)),
+        + (side, taps, gain, full, raw, thin, rows, rows, square, square, square, rows, state, state),
+        in_specs=specs(n_fs + 6) + [in_scalars()] * 2,
+        out_specs=tuple(specs(n_fs + 14)),
         scratch_shapes=[
             pltpu.VMEM((total + HALO, 3 * span), WIDE),
             pltpu.VMEM((total, span), WIDE),
@@ -485,60 +496,58 @@
         compiler_params=pltpu.CompilerParams(vmem_limit_bytes=52 << 20),
         cost_estimate=cost(30_000_000_000, 16 << 20),
         name="delta_forward",
-    )(*pieces, w_in, gmix, near, far, taps, gain, segcol, poscol, segrow, edges)
+    )(*pieces, w_in, near, far, segcol, poscol, segrow, edges, z)
     return result[:n_fs], result[n_fs], result[n_fs + 1 :]
 
 
-def delta_backward(pieces, w_in, near, far, taps, gain, segcol, poscol, segrow, edges, kept, heads, width):
+def delta_backward(pieces, w_in, near, segcol, poscol, segrow, edges, z, dgffn, kept, heads, width, shard_rows):
     n_fs = len(pieces)
     total = near.shape[0]
     features, lanes = w_in.shape
     count = total // CHUNK
     span = heads * width
-    poscol = jnp.pad(poscol, ((0, HALO), (0, 0)))
-    block = jax.ShapeDtypeStruct((total // n_fs, features), NARROW)
-    result = pl.pallas_call(
-        functools.partial(backward_kernel, heads, width, n_fs),
-        out_shape=(block,) * n_fs
-        + (
+    return pl.pallas_call(
+        functools.partial(backward_kernel, heads, width, n_fs, shard_rows),
+        out_shape=(
             jax.ShapeDtypeStruct((total, lanes), NARROW),
-            jax.ShapeDtypeStruct(taps.shape, WIDE),
-            jax.ShapeDtypeStruct(gain.shape, WIDE),
-            jax.ShapeDtypeStruct((1, features), WIDE),
+            jax.ShapeDtypeStruct((features, lanes), NARROW),
         ),
-        in_specs=specs(n_fs + 8) + [in_scalars()] + specs(11),
-        out_specs=tuple(specs(n_fs + 4)),
+        in_specs=specs(n_fs + 5) + [in_scalars()] * 2 + specs(14),
+        out_specs=tuple(specs(2)),
         scratch_shapes=[
+            pltpu.VMEM(kept[0].shape, WIDE),
+            pltpu.VMEM((features, lanes), WIDE),
+            pltpu.VMEM((lanes - 4 * span, features), WIDE),
             pltpu.VMEM((total + HALO, 3 * span), WIDE),
             pltpu.VMEM((count * heads, width, width), WIDE),
             pltpu.VMEM((total, span), WIDE),
             pltpu.VMEM((total + HALO, 3 * span), WIDE),
             pltpu.VMEM((total, span), NARROW),
             pltpu.VMEM((total, span), NARROW),
-            pltpu.VMEM((total, features), NARROW),
         ],
         compiler_params=pltpu.CompilerParams(vmem_limit_bytes=52 << 20),
         cost_estimate=cost(40_000_000_000, 16 << 20),
         name="delta_backward",
-    )(*pieces, w_in, near, far, taps, gain, segcol, poscol, segrow, edges, *kept)
-    return (result[:n_fs],) + tuple(result[n_fs:])
-
-
-def weigh_inputs(z, hidden, d_raw, dtaps, dgain, dgmix, dgffn, heads, width, shard_rows):
-    features, lanes = hidden.shape[1], d_raw.shape[1]
+    )(*pieces, w_in, near, segcol, poscol, segrow, edges, z, dgffn, *kept)
+
+
+def leave_packed(w_in, far, d_raw, n_fs):
+    total = d_raw.shape[0]
+    features = w_in.shape[0]
+    block = jax.ShapeDtypeStruct((total // n_fs, features), NARROW)
     return pl.pallas_call(
-        functools.partial(weigh_kernel, heads, width, shard_rows),
-        out_shape=jax.ShapeDtypeStruct((features, lanes), NARROW),
-        in_specs=[in_scalars()] + specs(6),
-        out_specs=specs(1)[0],
-        scratch_shapes=[pltpu.VMEM((features, lanes), WIDE), pltpu.VMEM((128, features), WIDE)],
+        functools.partial(leave_kernel, n_fs),
+        out_shape=(block,) * n_fs,
+        in_specs=specs(3),
+        out_specs=tuple(specs(n_fs)),
+        scratch_shapes=[pltpu.VMEM((total, features), NARROW)],
         compiler_params=pltpu.CompilerParams(vmem_limit_bytes=40 << 20),
-        cost_estimate=cost(60_000_000_000, 8 << 20),
-        name="weigh_inputs",
-    )(z, hidden, d_raw, dtaps, dgain, dgmix, dgffn)
-
-
-def mix_out_kernel(n_fs, z_ref, *refs):
+        cost_estimate=cost(1_000_000, 1 << 10),
+        name="leave_packed",
+    )(w_in, far, d_raw)
+
+
+def mix_out_kernel(n_fs, row, z_ref, *refs):
     pieces, refs = refs[:n_fs], refs[n_fs:]
     wout_ref, tokens_ref, gain_ref, middle_ref, ffn_ref, normed_ref = refs
     span = pieces[0].shape[1]
@@ -549,14 +558,14 @@
         middle = middle + plain_dot(piece[...], wout_ref[place, :])
     middle_ref[...] = middle
     scale = lax.rsqrt(jnp.mean(middle * middle, axis=-1, keepdims=True) + norm_eps)
-    ffn_ref[...] = (middle * scale * gain_ref[...]).astype(NARROW)
-
-
-def mix_out(z, pieces, w_out, tokens, gain):
+    ffn_ref[...] = (middle * scale * gain_ref[row:row + 1, :]).astype(NARROW)
+
+
+def mix_out(z, pieces, w_out, tokens, side, row):
     n_fs = len(pieces)
     shape = tokens.shape
     return pl.pallas_call(
-        functools.partial(mix_out_kernel, n_fs),
+        functools.partial(mix_out_kernel, n_fs, row),
         out_shape=(
             jax.ShapeDtypeStruct(shape, WIDE),
             jax.ShapeDtypeStruct(shape, NARROW),
@@ -567,16 +576,84 @@
         compiler_params=pltpu.CompilerParams(vmem_limit_bytes=40 << 20),
         cost_estimate=cost(2_000_000_000, 6 << 20),
         name="mix_out",
-    )(z, *pieces, w_out, tokens, gain)
-
-
-def mix_back_kernel(n_fs, z_ref, dffn_ref, middle_ref, gain_ref, cot_ref, wout_ref, *refs):
+    )(z, *pieces, w_out, tokens, side)
+
+
+def ffn_kernel(keys, unit, block_ref, *refs):
+    count = TP
+    rows_in, refs = refs[:count], refs[count:]
+    cots, refs = refs[:count], refs[count:]
+    weights, refs = refs[:len(keys)], refs[len(keys):]
+    (wdown_ref, active_ref, dboth_ref, sent_ref, later_ref, own_ref, part_ref, *ordered) = refs
+    own_rows = rows_in[0].shape[0]
+    if ordered:
+        for near, far in zip(weights, ordered):
+            n_fs, size = near.shape[:2]
+            for by in range(n_fs):
+                line = lax.rem(block_ref[1] + n_fs - by, n_fs)
+                for at in range(size // unit):
+                    place = pl.ds(pl.multiple_of((at * n_fs + line) * unit, unit), unit)
+                    far[place, :] = near[by, at * unit:(at + 1) * unit, :]
+        weights = ordered
+    depth = weights[0].shape[0]
+    units = wdown_ref.shape[0]
+    spots = [pl.ds(pl.multiple_of((block_ref[0] ^ key) * depth, depth), depth) for key in keys]
+    half = count // 2 * own_rows
+    for at in range(count - 1, -1, -1):
+        rows = slice(at * own_rows, (at + 1) * own_rows)
+        both = plain_dot(rows_in[at][:, spots[0]], weights[0][...])
+        for spot, weight in zip(spots[1:], weights[1:]):
+            both = both + plain_dot(rows_in[at][:, spot], weight[...])
+        gate, up = both[:, :units], both[:, units:]
+        sig = jax.nn.sigmoid(gate)
+        silu = gate * sig
+        active_ref[rows, :] = (silu * up).astype(NARROW)
+        dactive = plain_dot(cots[at][...], wdown_ref[...], 1, 1)
+        dboth_ref[rows, :units] = (dactive * up * (sig * (1.0 + gate * (1.0 - sig)))).astype(NARROW)
+        dboth_ref[rows, units:] = (dactive * silu).astype(NARROW)
+        dboth = dboth_ref[rows, :]
+        for spot, weight in zip(spots, weights):
+            part_ref[:, spot] = plain_dot(dboth, weight[...], 1, 1)
+        if at >= count // 2:
+            place = at * own_rows - half
+            sent_ref[place:place + own_rows, :] = part_ref[...].astype(NARROW)
+        elif at:
+            later_ref[(at - 1) * own_rows:at * own_rows, :] = part_ref[...]
+        else:
+            own_ref[...] = part_ref[...]
+
+
+def ffn_units(block, rows_in, cots, weights, keys, w_down, unit):
+    own_rows, features = rows_in[0].shape
+    units = w_down.shape[0]
+    total = TP * own_rows
+    return pl.pallas_call(
+        functools.partial(ffn_kernel, keys, unit),
+        out_shape=(
+            jax.ShapeDtypeStruct((total, units), NARROW),
+            jax.ShapeDtypeStruct((total, 2 * units), NARROW),
+            jax.ShapeDtypeStruct((total // 2, features), NARROW),
+            jax.ShapeDtypeStruct((total // 2 - own_rows, features), WIDE),
+            jax.ShapeDtypeStruct((own_rows, features), WIDE),
+        ),
+        in_specs=[in_scalars()] + specs(2 * TP + len(weights) + 1),
+        out_specs=tuple(specs(5)),
+        scratch_shapes=[pltpu.VMEM((own_rows, features), WIDE)]
+        + [pltpu.VMEM((features // len(keys), 2 * units), NARROW) for w in weights if w.ndim == 3],
+        compiler_params=pltpu.CompilerParams(vmem_limit_bytes=52 << 20),
+        cost_estimate=cost(8_000_000_000, 16 << 20),
+        name="ffn_units",
+    )(block, *rows_in, *cots, *weights, w_down)
+
+
+def mix_back_kernel(n_fs, row, z_ref, own_ref, core_ref, side_ref, middle_ref, gain_ref, cot_ref, wout_ref, *refs):
     blocks, (dmiddle_ref, dbranch_ref, dgain_ref) = refs[:n_fs], refs[n_fs:]
-    middle, given = middle_ref[...], dffn_ref[...]
+    middle = middle_ref[...]
+    given = own_ref[...] + core_ref[0:own_ref.shape[0], :].astype(WIDE) + side_ref[...].astype(WIDE)
     scale = lax.rsqrt(jnp.mean(middle * middle, axis=-1, keepdims=True) + norm_eps)
     unit = middle * scale
     dgain_ref[...] = jnp.sum(given * unit, axis=0, keepdims=True)
-    given = given * gain_ref[...]
+    given = given * gain_ref[row:row + 1, :]
     dmiddle = cot_ref[...].astype(WIDE) + scale * (given - unit * jnp.mean(unit * given, axis=-1, keepdims=True))
     dmiddle_ref[...] = dmiddle
     dbranch = dmiddle.astype(NARROW)
@@ -587,23 +664,23 @@
         block[...] = plain_dot(dbranch, wout_ref[place, :], 1, 1).astype(NARROW)
 
 
-def mix_back(z, dffn, middle, gain, cotangent, w_out, n_fs):
+def mix_back(z, parts, middle, side, row, cotangent, w_out, n_fs):
     count, features = middle.shape
     block = jax.ShapeDtypeStruct((count, features // n_fs), NARROW)
     result = pl.pallas_call(
-        functools.partial(mix_back_kernel, n_fs),
+        functools.partial(mix_back_kernel, n_fs, row),
         out_shape=(block,) * n_fs
         + (
             jax.ShapeDtypeStruct(middle.shape, WIDE),
             jax.ShapeDtypeStruct(middle.shape, NARROW),
-            jax.ShapeDtypeStruct(gain.shape, WIDE),
+            jax.ShapeDtypeStruct((1, features), WIDE),
         ),
-        in_specs=[in_scalars()] + specs(5),
+        in_specs=[in_scalars()] + specs(7),
         out_specs=tuple(specs(n_fs + 3)),
         compiler_params=pltpu.CompilerParams(vmem_limit_bytes=40 << 20),
         cost_estimate=cost(2_000_000_000, 6 << 20),
         name="mix_back",
-    )(z, dffn, middle, gain, cotangent, w_out)
+    )(z, *parts, middle, side, cotangent, w_out)
     return (result[:n_fs],) + tuple(result[n_fs:])
 
 
@@ -754,16 +831,15 @@
             pieces.append(shift(lax.dynamic_index_in_dim(blocks, lax.rem(z + by, n_fs), 0), by, n_fs))
         return pieces
 
-    packet = line_order(hand_out(packet), z).reshape(n_fs * rows, 4 * span + 128)
-    w_in = lax.all_gather(packet, "dp", axis=0, tiled=True)
-    full_out = lax.all_gather(w_out, ("dp", "fsdp"), axis=0, tiled=True)
-    side_rows = w_in[:, 4 * span :].astype(WIDE).T
-    full_gmix = side_rows[heads]
-    full_gffn = side_rows[heads + 1]
-    local_taps = lax.dynamic_slice_in_dim(
-        side_rows[heads + 2 : heads + 2 + 3 * n_taps], z * span, span, 1
-    ).reshape(3, n_taps, span)
-    full_ghead = side_rows[heads + 2 + 3 * n_taps].reshape(-1, rows)[:, :head_rows].reshape(-1)
+    lanes = 4 * span + 128
+    packet = jnp.concatenate([packet, jnp.broadcast_to(w_out[None], (n_fs,) + w_out.shape)], axis=2)
+    packet = hand_out(packet)
+    token_pieces = [tokens] + [shift(tokens, by, n_fs) for by in range(1, n_fs)]
+    packet, token_pieces[1] = lax.optimization_barrier((packet, token_pieces[1]))
+    packet_in = line_order([piece[:, :, :lanes] for piece in packet], z).reshape(n_fs * rows, lanes)
+    packet_out = line_order([piece[:, :, lanes:] for piece in packet], z).reshape(n_fs * rows, features)
+    w_in = lax.all_gather(packet_in, "dp", axis=0, tiled=True)
+    full_out = lax.all_gather(packet_out, "dp", axis=0, tiled=True)
 
     owner, place = packing_row // own_rows, lax.rem(packing_row, own_rows)
     near = (lax.rem(z + n_fs - owner, n_fs) * own_rows + place)[:, None]
@@ -772,13 +848,15 @@
     seg_rows = segment.reshape(-1, CHUNK)
     ends = seg_rows[:, -1]
     edges = jnp.stack([jnp.concatenate([jnp.full((1,), -1, jnp.int32), ends[:-1]]), ends], axis=1)
-    layout = (near, far, local_taps, full_ghead[None], segment[:, None], position[:, None], seg_rows, edges)
-    token_pieces = [tokens] + [shift(tokens, by, n_fs) for by in range(1, n_fs)]
-    own_gate, own_up, own_cotangent, _ = lax.optimization_barrier(
-        (w_ffn_gate, w_ffn_up, cotangent, token_pieces[1])
+    z_ref = z.reshape(1)
+    layout = (segment[:, None], jnp.pad(position, (0, HALO))[:, None], seg_rows, edges, z_ref)
+    shard_rows = (rows, head_rows)
+    own_gate, own_up, _ = lax.optimization_barrier((w_ffn_gate, w_ffn_up, token_pieces[1]))
+    both_sends = jnp.concatenate([by_member(own_gate), by_member(own_up)], axis=2)
+    blocks, side, kept = delta_forward(
+        token_pieces, w_in, near, far, *layout, heads, width, n_taps, shard_rows
     )
-    both_sends = jnp.concatenate([by_member(own_gate), by_member(own_up)], axis=2)
-    blocks, hidden_p, kept = delta_forward(token_pieces, w_in, full_gmix[None], *layout, heads, width)
+    gain_row = heads + 1
 
     both_pieces = {
         key: flip(lax.dynamic_index_in_dim(both_sends, member ^ key, 0, keepdims=False), key, n_dp)
@@ -786,18 +864,24 @@
         else lax.dynamic_index_in_dim(both_sends, member, 0, keepdims=False)
         for key in range(TP)
     }
-    both_rows, _ = lax.optimization_barrier((in_order(both_pieces, member), token_pieces))
-    both_line = line_pieces(both_rows.reshape(TP, rows, 2 * ff_pad), n_fs)
-    both_line, blocks = lax.optimization_barrier((both_line, blocks))
-    both_rows = line_order(both_line, z).reshape(-1, 2 * ff_pad)
-    w_both = in_order(gather_cube(both_rows, rest_bits, n_dp), block)
+    own_down, _ = lax.optimization_barrier((w_ffn_down, token_pieces[1]))
+    down_rows = in_order(gather_cube(own_down, rest_bits, n_dp), block).reshape(n_rest, -1, features)
+    both_rows = in_order(both_pieces, member).reshape(TP, rows, 2 * ff_pad)
+    own_cotangent, both_rows, down_rows = lax.optimization_barrier((cotangent, both_rows, down_rows))
+    both_rows, down_rows, _ = lax.optimization_barrier((both_rows, down_rows, token_pieces))
+    both_line = line_pieces(both_rows, n_fs)
+    both_line, blocks, down_rows = lax.optimization_barrier((both_line, blocks, down_rows))
+    if rows % 16 == 0:
+        both_rows = jnp.stack([piece.reshape(TP * rows, 2 * ff_pad) for piece in both_line])
+    else:
+        both_rows = line_order(both_line, z).reshape(-1, 2 * ff_pad)
+    both_pieces = gather_cube(both_rows, rest_bits, n_dp)
+    unit = 1 << (TP.bit_length() - 1)
+    rest_keys = [key // unit for key in both_pieces]
     tp_order = sorted(range(TP), key=lambda key: tuple((key & bit) != 0 for bit in tp_bits))
 
-    def spread(value):
-        pieces = gather_cube(value, tp_bits[::-1], n_dp)
-        return jnp.concatenate([pieces[key] for key in tp_order], axis=0)
-
-    cotangent_near = spread(own_cotangent)
+    cot_pieces = gather_cube(own_cotangent, tp_bits[::-1], n_dp)
+    cot_pieces, blocks = lax.optimization_barrier((cot_pieces, blocks))
 
     def collect(left, right, dims):
         arrived = []
@@ -813,8 +897,9 @@
 
         for bit in tp_bits:
             keep //= 2
-            arrived.append(flip(term(keep, 2 * keep).astype(NARROW), bit, n_dp))
-        return term(0, 1)
+            sent = yield term(keep, 2 * keep).astype(NARROW)
+            arrived.append(flip(sent, bit, n_dp))
+        yield term(0, 1)
 
     def halve(value, index, some_bits):
         unit = some_bits[0] if some_bits else 1
@@ -835,49 +920,76 @@
     def pass_on(parts):
         return [parts[0]] + [shift(part, by, n_fs) for by, part in enumerate(parts) if by]
 
-    z_ref = z.reshape(1)
     mixed_pieces = pass_on(blocks)
-    own_down, _ = lax.optimization_barrier((w_ffn_down, mixed_pieces))
-    down_line = line_pieces(own_down[None], n_fs)
-    middle, ffn_in, normed_b = mix_out(z_ref, mixed_pieces, full_out, tokens, full_gffn[None])
-    down_rows = line_order(down_line, z).reshape(-1, features)
-    w_down = in_order(gather_cube(down_rows, rest_bits, n_dp), block)
+    down_line = line_pieces(down_rows, n_fs)
+    middle, ffn_in, normed_b = mix_out(z_ref, mixed_pieces, full_out, tokens, side, gain_row)
+    w_down = line_order(down_line, z).reshape(ff_own, features)
     w_down = jnp.pad(w_down, ((0, ff_pad - ff_own), (0, 0)))
-    ffn_near = spread(ffn_in)
-    both = project(ffn_near, w_both)
-    active, active_back = jax.vjp(swiglu, both[:, :ff_pad], both[:, ff_pad:])
-    active_b = active.astype(NARROW)
-    down_terms = weight_grad(active_b, cotangent_near)[:ff_own].reshape(n_rest, -1, features)
-    down_sum = halve(down_terms, block, rest_bits).reshape(n_fs, -1, features)
-    d_active = project_back(cotangent_near, w_down)
-    d_fgate, d_fup = active_back(d_active)
-    d_both = jnp.concatenate([d_fgate.astype(NARROW), d_fup.astype(NARROW)], axis=1)
-    both_terms = weight_grad(ffn_near, d_both).astype(NARROW)
-    both_sum = lax.psum_scatter(
-        both_terms.reshape(n_dp, n_fs * rows, 2 * ff_pad), "fsdp", scatter_dimension=1, tiled=True
+    ffn_pieces = gather_cube(ffn_in, tp_bits[::-1], n_dp)
+    active_b, d_both, first, second, d_own = ffn_units(
+        jnp.stack([block, z]),
+        [ffn_pieces[key] for key in tp_order],
+        [cot_pieces[key] for key in tp_order],
+        list(both_pieces.values()),
+        rest_keys,
+        w_down,
+        rows,
     )
-    d_ffn_in = collect(d_both, w_both, ((1,), (1,)))
-    d_ffn_in, both_terms = lax.optimization_barrier((d_ffn_in, both_terms))
+    ffn_near = jnp.concatenate([ffn_pieces[key] for key in tp_order], axis=0)
+
+    def both_part(lo, size):
+        part = weight_grad(lax.dynamic_slice_in_dim(ffn_near, lo, size, 1), d_both)
+        return part.reshape(-1, n_fs * rows, 2 * ff_pad)
+
+    split = features // 2 if rest_bits else features
+    top = block // max(n_rest // 2, 1)
+    if rest_bits:
+        both_sent = both_part((1 - top) * split, split).astype(NARROW)
+    else:
+        both_sent = None
+    from_core = flip(first, tp_bits[0], n_dp)
+    second = second + from_core[own_rows:].astype(WIDE)
+    second, both_sent, active_late = lax.optimization_barrier((second.astype(NARROW), both_sent, active_b))
+    from_side = flip(second, tp_bits[1], n_dp)
+    cotangent_near = jnp.concatenate([cot_pieces[key] for key in tp_order], axis=0)
+    down_terms = weight_grad(active_late, cotangent_near)[:ff_own].reshape(n_rest, n_fs, -1, features)
+    down_each = down_terms.shape[2]
+    down_terms = jnp.pad(down_terms, ((0, 0), (0, 0), (0, -down_each % 32), (0, 0)))
+    both_sum = both_part(top * split if rest_bits else 0, split)
+    out_terms = collect(active_late, w_down, ((1,), (0,)))
+    out_first = next(out_terms)
+    down_terms = down_terms.astype(NARROW)
+    down_sum = lax.psum_scatter(
+        down_terms.reshape(n_rest, -1, features), "fsdp", scatter_dimension=1, tiled=True
+    )
+    from_side, down_terms, both_sum, out_first = lax.optimization_barrier(
+        (from_side, down_terms, both_sum, out_first)
+    )
+    if rest_bits:
+        both_sum = both_sum + flip(both_sent, rest_bits[-1], n_dp).astype(WIDE)
+        both_sum = halve(both_sum, block, rest_bits[:-1])
 
     d_blocks, d_middle, d_branch, d_gffn = mix_back(
-        z_ref, d_ffn_in, middle, full_gffn[None], cotangent, full_out, n_fs
+        z_ref, (d_own, from_core, from_side), middle, side, gain_row, cotangent, full_out, n_fs
     )
-    d_blocks, down_sum = lax.optimization_barrier((d_blocks, down_sum))
     d_pieces = pass_on(d_blocks)
-    grad_fdown = sum_up(hand_out(down_sum.astype(NARROW)), down_sum)
-    sum_out = lax.psum_scatter(
-        weight_grad(normed_b, d_branch).astype(NARROW), "dp", scatter_dimension=0, tiled=True
+    out_grad = weight_grad(normed_b, d_branch).astype(NARROW)
+    sum_out = lax.psum_scatter(out_grad, "dp", scatter_dimension=0, tiled=True)
+    both_sum = jnp.swapaxes(both_sum.reshape(TP, n_fs, rows, 2 * ff_pad), 0, 1)
+    layer_out = (middle + out_terms.send(out_terms.send(out_first))).astype(NARROW)
+    both_sum, layer_out, d_pieces, out_grad = lax.optimization_barrier((both_sum, layer_out, d_pieces, out_grad))
+    both_line = hand_out(both_sum.astype(NARROW))
+
+    d_raw, grad_in = delta_backward(
+        d_pieces, w_in, near, *layout, d_gffn, kept, heads, width, shard_rows
     )
-    layer_out = (middle + collect(active_b, w_down, ((1,), (0,)))).astype(NARROW)
-    d_blocks, d_raw, d_taps, d_ghead, d_gmix = delta_backward(d_pieces, w_in, *layout, kept, heads, width)
+    grad_in, both_line, down_sum, sum_out = lax.optimization_barrier((grad_in, both_line, down_sum, sum_out))
+    part = lax.psum_scatter(grad_in, "dp", scatter_dimension=0, tiled=True)
+    d_blocks = leave_packed(w_in, far, d_raw, n_fs)
     d_blocks = pass_on(d_blocks)
-    grad_in = weigh_inputs(
-        z_ref, hidden_p, d_raw, d_taps, d_ghead, d_gmix, d_gffn, heads, width, (rows, head_rows)
-    )
-    grad_in, both_sum, layer_out, grad_fdown = lax.optimization_barrier((grad_in, both_sum, layer_out, grad_fdown))
-    part = lax.psum_scatter(grad_in, "dp", scatter_dimension=0, tiled=True)
-    d_blocks, both_sum = lax.optimization_barrier((d_blocks, both_sum))
-    both_sum = halve(both_sum, block, rest_bits)
+    both_line, d_blocks[1] = lax.optimization_barrier((both_line, d_blocks[1]))
+    both_sum = sum_up(both_line, both_sum)
+    grad_fdown = halve(down_sum[:, :down_each], block, rest_bits)[0].astype(WIDE)
     both_pieces = {
         key: flip(lax.dynamic_index_in_dim(both_sum, member ^ key, 0, keepdims=False), key, n_dp)
         if key
@@ -885,21 +997,25 @@
         for key in range(TP)
     }
     both_mine = in_order({key: piece[None] for key, piece in both_pieces.items()}, member)
+    def units_of(which):
+        part = both_mine[:, :, which * ff_pad : which * ff_pad + ff_own].reshape(TP, rows, n_rest, ff_block)
+        return jnp.transpose(part, (1, 2, 0, 3)).reshape(rows, hidden_ffn)
+
+    lanes = part.shape[1]
+    joint = jnp.concatenate([part, sum_out], axis=1).reshape(n_fs, rows, -1)
+    arrived = [piece[0] for piece in hand_out(joint)]
+    d_blocks, arrived[1] = lax.optimization_barrier((d_blocks, arrived[1]))
     d_hidden = d_blocks[0].astype(WIDE)
     for block_of in d_blocks[1:]:
         d_hidden = d_hidden + block_of.astype(WIDE)
 
-    def units_of(which):
-        part = both_mine[:, :, which * ff_pad : which * ff_pad + ff_own].reshape(TP, rows, n_rest, ff_block)
-        return jnp.transpose(part, (1, 2, 0, 3)).reshape(rows, hidden_ffn)
-
-    _, norm_mix_back = jax.vjp(rms_scale, tokens.astype(WIDE), full_gmix)
+    d_hidden = d_blocks[0].astype(WIDE)
+    for block_of in d_blocks[1:]:
+        d_hidden = d_hidden + block_of.astype(WIDE)
+    _, norm_mix_back = jax.vjp(rms_scale, tokens.astype(WIDE), side[heads])
     d_inputs_norm, _ = norm_mix_back(d_hidden)
     grad_tokens = d_middle + d_inputs_norm
 
-    lanes = part.shape[1]
-    joint = jnp.concatenate([part, sum_out], axis=1).reshape(n_fs, rows, -1)
-    arrived = [piece[0] for piece in hand_out(joint)]
     part = line_order([piece[None, :, :lanes] for piece in arrived], z)[0].astype(WIDE)
     grad_wout = jnp.zeros((rows, features), WIDE)
     for piece in arrived:

time: 433 us -> 393 us (0.908)
  waiting for transfers between devices: 173 us -> 125 us
  matrix products: 39.7 us -> 21.2 us
  starting transfers between devices: 54.8 us -> 70.5 us
  Pallas kernels: 83.5 us -> 97.7 us
  local copies, waits for them, and re-layouts: 47.1 us -> 40.8 us
    ppermute x27, waiting for transfers between devices: 111 us -> 86.6 us  [shift(): lax.ppermute(value, 'fsdp', [(i, (i + by) % n_fs) for i in range(n_fs)])]
    ppermute x20, waiting for transfers between devices: 61.6 us -> 38.7 us  [flip(): return lax.ppermute(value, 'dp', [(i, i ^ bit) for i in range(n_dp)])]
    ppermute x20, starting transfers between devices: 26.8 us -> 44.2 us  [flip(): return lax.ppermute(value, 'dp', [(i, i ^ bit) for i in range(n_dp)])]
    pallas_call x5 -> x6, Pallas kernels: 83.5 us -> 97.7 us  [the longest x1 40 us: delta_backward(): pl.pallas_call(functools.partial(backward_kernel, heads, width, n_fs, sha...]
    dot_general x6 -> x3, matrix products: 19.2 us -> 7.02 us  [term(): lax.dot_general(left[lo * own_rows:hi * own_rows], right, (dims, ((), ())...]
    dot_general x2 -> x0, matrix products: 9.13 us -> none  [the longest x1 5.6 us: project_back(): lax.dot_general(left, right, (((1,), (1,)), ((), ())), preferred_element_...]
    dynamic_update_slice x16, local copies, waits for them, and re-layouts: 6.2 us -> 0.31 us  [line_order(): lax.dynamic_update_slice_in_dim(whole, piece[:, None], lax.rem(z + n_fs -...]
    unnamed x81 -> x100, local copies, waits for them, and re-layouts: 13 us -> 18 us
  transfers between devices with their start and end apart: 52 -> 52, of which waited for: 23 -> 20; matrix products, arithmetic and copies ran while one was open for 15% -> 12% of each run, Pallas kernels for 20% -> 22%
where the time goes in v3:
time: 393 us; the launch traced here: 387 us
  waiting for transfers between devices  125 us (32%)
  Pallas kernels  97.7 us (25%)
  starting transfers between devices  70.5 us (18%)
  local copies, waits for them, and re-layouts  40.8 us (10%)
  matrix products  21.2 us (5%)
  other arithmetic  16.4 us (4%)
  between operations  15 us (4%)
    ppermute x27, waiting for transfers between devices, shift(): lax.ppermute(value, 'fsdp', [(i, (i + by) % n_fs) for i in range(n_fs)])  86.6 us
    ppermute x20, starting transfers between devices, flip(): return lax.ppermute(value, 'dp', [(i, i ^ bit) for i in range(n_dp)])  44.2 us
    pallas_call x1, Pallas kernels, delta_backward(): pl.pallas_call(functools.partial(backward_kernel, heads, width, n_fs, sha...  40 us
    ppermute x20, waiting for transfers between devices, flip(): return lax.ppermute(value, 'dp', [(i, i ^ bit) for i in range(n_dp)])  38.7 us
    pallas_call x1, Pallas kernels, delta_forward(): pl.pallas_call(functools.partial(forward_kernel, heads, width, n_fs, shar...  34 us
    ppermute x27, starting transfers between devices, shift(): lax.ppermute(value, 'fsdp', [(i, (i + by) % n_fs) for i in range(n_fs)])  26 us
    unnamed x100, local copies, waits for them, and re-layouts  18 us
    pallas_call x1, Pallas kernels, ffn_units(): pl.pallas_call(functools.partial(ffn_kernel, keys, unit), out_shape=(jax....  14.3 us
  transfers between devices with their start and end apart: 52, of which 20 were waited for; matrix products, arithmetic and copies ran while one was open for 12% of the time, Pallas kernels for 22%

profile of v3, /device:TPU:9, one launch (start us, length us, event | category | flops | bytes accessed | tf_op | source)
XLA Modules:
  0.0 386.9 jit_solution(3092829642961595856)
XLA Ops:
  7.2 1.3 collective-permute-start.3
  16.0 1.3 collective-permute-start
  18.7 4.6 %collective-permute-done = bf16[1,32,2176]{2,1,0:T(8,128)(2,1)S(1)} collective-permute-done((bf16[1,32,2176]{2,1,0:T(8,128)(2,1)S(1)}, bf16[1,32,2176]{2,1,0:T(8,128)(2,1)S(1)}, u32[]{:S(2)}, u32[]{:S(2)}) %collective-permute-start) | collective-permute-done | bytes 139296 | tf_op jit(solution)/shard_map/ppermute | solution.py:721
  23.3 8.0 %collective-permute-done.1 = bf16[1,32,2176]{2,1,0:T(8,128)(2,1)S(1)} collective-permute-done((bf16[1,32,2176]{2,1,0:T(8,128)(2,1)S(1)}, bf16[1,32,2176]{2,1,0:T(8,128)(2,1)S(1)}, u32[]{:S(2)}, u32[]{:S(2)}) %collective-permute-start.1) | collective-permute-done | bytes 139296 | tf_op jit(solution)/shard_map/ppermute | solution.py:721
  31.3 2.9 collective-permute-done.2
  40.0 1.7 collective-permute-start.4
  43.0 1.2 collective-permute-start.7
  45.3 1.8 collective-permute-done.5
  47.0 4.9 %collective-permute-done.6 = bf16[32,1536]{1,0:T(8,128)(2,1)S(1)} collective-permute-done((bf16[32,1536]{1,0:T(8,128)(2,1)S(1)}, bf16[32,1536]{1,0:T(8,128)(2,1)S(1)}, u32[]{:S(2)}, u32[]{:S(2)}) %collective-permute-start.6) | collective-permute-done | bytes 98336 | tf_op jit(solution)/shard_map/ppermute | solution.py:717
  53.9 1.3 fusion.24.refs_5_
  55.8 13.7 %collective-permute-done.11.refs_2_ = bf16[256,1024]{1,0:T(8,128)(2,1)} collective-permute-done((bf16[256,1024]{1,0:T(8,128)(2,1)S(1)}, bf16[256,1024]{1,0:T(8,128)(2,1)}, u32[]{:S(2)}, u32[]{:S(2)}) %collective-permute-start.11) | collective-permute-done | bytes 524320 | tf_op jit(solution)/shard_map/ppermute | solution.py:721
  69.5 3.2 collective-permute-start.14
  72.7 1.7 collective-permute-start.15
  74.4 1.3 collective-permute-start.10
  75.7 34.0 %delta_forward.1 = (bf16[256,256]{1,0:T(8,128)(2,1)S(1)}, bf16[256,256]{1,0:T(8,128)(2,1)S(1)}, bf16[256,256]{1,0:T(8,128)(2,1)S(1)}, bf16[256,256]{1,0:T(8,128)...) custom-call(bf16[256,1024]{1,0:T(8,128)(2,1)} %refs_5_.1, ...), custom_call_target="tpu_custom_call" | custom-call | flops 30000001024 | bytes 16777216 | tf_op jit(solution)/shard_map/delta_forward/pallas_call | solution.py:484
  110.5 2.7 pad_maximum_fusion.refs_8_
  114.4 1.9 collective-permute-start.17
  116.3 2.9 collective-permute-done.16.refs_1_
  119.2 6.4 %collective-permute-done.17.refs_2_ = bf16[256,256]{1,0:T(8,128)(2,1)S(1)} collective-permute-done((bf16[256,256]{1,0:T(8,128)(2,1)S(1)}, bf16[256,256]{1,0:T(8,128)(2,1)S(1)}, u32[]{:S(2)}, u32[]{:S(2)}) %collective-permute-start.17) | collective-permute-done | bytes 131104 | tf_op jit(solution)/shard_map/ppermute | solution.py:721
  125.7 3.1 collective-permute-done.18.refs_3_
  128.8 1.6 copy-done.12
  131.3 1.3 collective-permute-start.19
  133.0 1.4 collective-permute-start.25
  134.6 7.3 %collective-permute-done.23 = bf16[2,88,1024]{2,1,0:T(8,128)(2,1)S(1)} collective-permute-done((bf16[2,88,1024]{2,1,0:T(8,128)(2,1)S(1)}, bf16[2,88,1024]{2,1,0:T(8,128)(2,1)S(1)}, u32[]{:S(2)}, u32[]{:S(2)}) %collective-permute-start.23) | collective-permute-done | bytes 360480 | tf_op jit(solution)/shard_map/ppermute | solution.py:721
  142.0 2.6 collective-permute-start.20
  145.7 17.4 %collective-permute-done.24 = bf16[2,88,1024]{2,1,0:T(8,128)(2,1)S(1)} collective-permute-done((bf16[2,88,1024]{2,1,0:T(8,128)(2,1)S(1)}, bf16[2,88,1024]{2,1,0:T(8,128)(2,1)S(1)}, u32[]{:S(2)}, u32[]{:S(2)}) %collective-permute-start.24) | collective-permute-done | bytes 360480 | tf_op jit(solution)/shard_map/ppermute | solution.py:721
  163.2 1.8 collective-permute-done.25
  165.0 1.4 pad.33.refs_10_
  167.2 14.3 %ffn_units.1 = (bf16[1024,768]{1,0:T(8,128)(2,1)}, bf16[1024,1536]{1,0:T(8,128)(2,1)}, bf16[512,1024]{1,0:T(8,128)(2,1)}, f32[256,1024]{1,0:T(8,128)}, f32[256,1024]{1,0:T(8,128)}) custom-call(s32[2]{0:T(128)S(1)} %pad_add_fusion.1.block_ref, bf16[256,1024]{1,0:T(8,128)(2,1)S(1)} %get-tuple-element.137.refs_0_, ...), custom_call_target="tpu_custom_call" | custom-call | flops 8000000000 | bytes 16777216 | tf_op jit(solution)/shard_map/ffn_units/pallas_call | solution.py:630
  184.1 3.0 convolution_convert_fusion
  187.1 1.4 add_convert_fusion
  188.8 3.2 fusion
  192.2 1.7 pad.34
  194.3 5.9 %fusion.15 = f32[512,1536]{1,0:T(8,128)} fusion(bf16[1024,1536]{1,0:T(8,128)(2,1)} %get-tuple-element.149, bf16[1024,1024]{1,0:T(8,128)(2,1)} %copy-done.39, s32[]{:T(128)S(6)} %select_n.146), kind=kOutput, calls=%fused_computation.29 | convolution fusion | flops 1610612736 | bytes 7340036 | tf_op jit(solution)/shard_map/dot_general | solution.py:713
  200.5 2.0 convolution_convert_fusion.2
  202.5 5.2 %collective-permute-done.27.side_ref = bf16[256,1024]{1,0:T(8,128)(2,1)S(1)} collective-permute-done((bf16[256,1024]{1,0:T(8,128)(2,1)S(1)}, bf16[256,1024]{1,0:T(8,128)(2,1)S(1)}, u32[]{:S(2)}, u32[]{:S(2)}) %collective-permute-start.27) | collective-permute-done | bytes 524320 | tf_op jit(solution)/shard_map/ppermute | solution.py:717
  208.4 2.6 mix_back.1
  212.0 2.0 collective-permute-start.32
  214.0 1.5 collective-permute-start.33
  215.5 2.1 convolution_convert_fusion.1
  217.6 2.3 fusion.11
  220.3 15.9 %collective-permute-done.28 = bf16[4,128,1536]{2,1,0:T(8,128)(2,1)} collective-permute-done((bf16[4,128,1536]{2,1,0:T(8,128)(2,1)}, bf16[4,128,1536]{2,1,0:T(8,128)(2,1)}, u32[]{:S(2)}, u32[]{:S(2)}) %collective-permute-start.28) | collective-permute-done | bytes 1572896 | tf_op jit(solution)/shard_map/ppermute | solution.py:717
  236.2 2.0 convert_add_fusion
  238.4 1.4 copy-done.23
  239.8 2.7 fusion.10
  242.9 2.0 collective-permute-start.35
  244.9 1.5 collective-permute-start.36
  246.5 40.0 %delta_backward.1 = (bf16[1024,1152]{1,0:T(8,128)(2,1)}, bf16[1024,1152]{1,0:T(8,128)(2,1)}) custom-call(bf16[256,256]{1,0:T(8,128)(2,1)S(1)} %get-tuple-element.167.refs_0_, bf16[256,256]{1,0:T(8,128)(2,1)S(1)} %collective-permute-done.31.refs_1_, bf16[256,256]{1,0:T(8,128)(2,1)S(1)} %collective-permute-done.32.refs_2_, ...), custom_call_target="tpu_custom_call" | custom-call | flops 40000000000 | bytes 16777216 | tf_op jit(solution)/shard_map/delta_backward/pallas_call | solution.py:509
  288.4 1.7 copy-done.1
  290.1 6.0 %leave_packed.1 = (bf16[256,1024]{1,0:T(8,128)(2,1)S(1)}, bf16[256,1024]{1,0:T(8,128)(2,1)}, bf16[256,1024]{1,0:T(8,128)(2,1)S(1)}, bf16[256,1024]{1,0:T(8,128)(2,1)S(1)}) custom-call(bf16[1024,1152]{1,0:T(8,128)(2,1)S(1)} %copy-done, s32[1,1024]{1,0:T(1,128)S(1)} %fusion.45.refs_6_.far_ref, bf16[1024,1152]{1,0:T(8,128)(2,1)S(1)} %copy-done.1), custom_call_target="tpu_custom_call" | custom-call | flops 1000000 | bytes 1024 | tf_op jit(solution)/shard_map/leave_packed/pallas_call | solution.py:538
  298.6 2.2 collective-permute-start.38
  301.0 8.4 %collective-permute-done.37 = bf16[256,1024]{1,0:T(8,128)(2,1)S(1)} collective-permute-done((bf16[256,1024]{1,0:T(8,128)(2,1)}, bf16[256,1024]{1,0:T(8,128)(2,1)S(1)}, u32[]{:S(2)}, u32[]{:S(2)}) %collective-permute-start.37) | collective-permute-done | bytes 524320 | tf_op jit(solution)/shard_map/ppermute | solution.py:721
  309.4 1.8 convert_add_fusion.1
  311.2 25.7 %collective-permute-start.43 = (f32[32,1536]{1,0:T(8,128)S(1)}, f32[32,1536]{1,0:T(8,128)S(1)}, u32[]{:S(2)}, u32[]{:S(2)}) collective-permute-start(f32[32,1536]{1,0:T(8,128)S(1)} %get-tuple-element.235), channel_id=1, source_target_pairs={{0,4},{4,0},{8,12},{12,8},{16,20},{20,16},{24,28},{28,24},{1,5},{5... | collective-permute-start | bytes 589832 | tf_op jit(solution)/shard_map/ppermute | solution.py:717
  338.4 5.5 %collective-permute-done.46 = bf16[1,88,1024]{2,1,0:T(8,128)(2,1)S(1)} collective-permute-done((bf16[1,88,1024]{2,1,0:T(8,128)(2,1)S(1)}, bf16[1,88,1024]{2,1,0:T(8,128)(2,1)S(1)}, u32[]{:S(2)}, u32[]{:S(2)}) %collective-permute-start.46) | collective-permute-done | bytes 180256 | tf_op jit(solution)/shard_map/ppermute | solution.py:717
  343.9 1.5 collective-permute-start.45
  346.2 4.8 %collective-permute-done.45 = f32[32,1536]{1,0:T(8,128)S(1)} collective-permute-done((f32[32,1536]{1,0:T(8,128)S(1)}, f32[32,1536]{1,0:T(8,128)S(1)}, u32[]{:S(2)}, u32[]{:S(2)}) %collective-permute-start.45) | collective-permute-done | bytes 196640 | tf_op jit(solution)/shard_map/ppermute | solution.py:717
  353.4 1.3 reshape.323
  357.1 2.1 collective-permute-start.40
  359.3 1.3 collective-permute-start.42
  360.6 1.5 collective-permute-done.40
  362.1 8.5 %collective-permute-done.41 = bf16[1,32,2176]{2,1,0:T(8,128)(2,1)S(1)} collective-permute-done((bf16[1,32,2176]{2,1,0:T(8,128)(2,1)S(1)}, bf16[1,32,2176]{2,1,0:T(8,128)(2,1)S(1)}, u32[]{:S(2)}, u32[]{:S(2)}) %collective-permute-start.41) | collective-permute-done | bytes 139296 | tf_op jit(solution)/shard_map/ppermute | solution.py:721
  377.0 1.6 fusion.12
  378.7 1.5 fusion.14
  (265 shorter events, 49.3 us)
Async XLA Ops:
  7.2 68.5 %all-gather.3.cloned.1.call-start = ((), (), s32[]{:S(2)}) async-start(), calls=%async_computation.3 | async-start | bytes 2654208 | tf_op jit(solution)/shard_map/all_gather | solution.py:841
  7.2 26.9 %collective-permute-start.3 = (bf16[256,1024]{1,0:T(8,128)(2,1)}, bf16[256,1024]{1,0:T(8,128)(2,1)S(1)}, u32[]{:S(2)}, u32[]{:S(2)}) collective-permute-start(bf16[256,1024]{1,0:T(8,128)(2,1)} %refs_5_.1), channel_id=1, source_target_pairs={{0,1},{1,2},{2,3},{3,0},{4,5},{5,6},{6,7},{7,4},{8,9},{9,10},{10,1... | collective-permute-start | bytes 1572872 | tf_op jit(solution)/shard_map/ppermute | solution.py:721
  13.2 21.9 %copy-start.2 = (bf16[256,1024]{1,0:T(8,128)(2,1)S(1)}, bf16[256,1024]{1,0:T(8,128)(2,1)}, u32[]{:S(2)}) copy-start(bf16[256,1024]{1,0:T(8,128)(2,1)} %refs_5_.1) | copy-start | bytes 1572868
  14.1 21.5 %copy-start.42 = (s32[1,1024]{1,0:T(1,128)S(1)}, s32[1,1024]{1,0:T(1,128)}, u32[]{:S(2)}) copy-start(s32[1,1024]{1,0:T(1,128)} %param.19) | copy-start | bytes 12292
  15.9 19.9 %copy-start.43 = (s32[1,4]{1,0:T(1,128)S(1)}, s32[1,4]{1,0:T(1,128)}, u32[]{:S(2)}) copy-start(s32[1,4]{1,0:T(1,128)} %param.18) | copy-start | bytes 52
  16.0 22.7 %copy-start.36 = (bf16[32,2816]{1,0:T(8,128)(2,1)S(1)}, bf16[32,2816]{1,0:T(8,128)(2,1)}, u32[]{:S(2)}) copy-start(bf16[32,2816]{1,0:T(8,128)(2,1)} %param.31) | copy-start | bytes 540676
  16.0 7.2 %collective-permute-start = (bf16[1,32,2176]{2,1,0:T(8,128)(2,1)S(1)}, bf16[1,32,2176]{2,1,0:T(8,128)(2,1)S(1)}, u32[]{:S(2)}, u32[]{:S(2)}) collective-permute-start(bf16[1,32,2176]{2,1,0:T(8,128)(2,1)S(1)} %get-tuple-element.246), channel_id=1, source_target_pairs={{0,1},{1,2},{2,3},{3,0},{4,5},{5,6},{6,7},{7,4},{8,9},{9,10},{10,1... | collective-permute-start | bytes 417800 | tf_op jit(solution)/shard_map/ppermute | solution.py:721
  17.4 13.9 %collective-permute-start.1 = (bf16[1,32,2176]{2,1,0:T(8,128)(2,1)S(1)}, bf16[1,32,2176]{2,1,0:T(8,128)(2,1)S(1)}, u32[]{:S(2)}, u32[]{:S(2)}) collective-permute-start(bf16[1,32,2176]{2,1,0:T(8,128)(2,1)S(1)} %get-tuple-element.245), channel_id=1, source_target_pairs={{0,2},{1,3},{2,0},{3,1},{4,6},{5,7},{6,4},{7,5},{8,10},{9,11},{10,... | collective-permute-start | bytes 417800 | tf_op jit(solution)/shard_map/ppermute | solution.py:721
  18.3 15.8 %collective-permute-start.2 = (bf16[1,32,2176]{2,1,0:T(8,128)(2,1)S(1)}, bf16[1,32,2176]{2,1,0:T(8,128)(2,1)S(1)}, u32[]{:S(2)}, u32[]{:S(2)}) collective-permute-start(bf16[1,32,2176]{2,1,0:T(8,128)(2,1)S(1)} %get-tuple-element.244), channel_id=1, source_target_pairs={{0,3},{1,0},{2,1},{3,2},{4,7},{5,4},{6,5},{7,6},{8,11},{9,8},{10,9... | collective-permute-start | bytes 417800 | tf_op jit(solution)/shard_map/ppermute | solution.py:721
  35.1 81.2 %all-gather.5.cloned.1.call-start = ((), (), s32[]{:S(2)}) async-start(), calls=%async_computation.4 | async-start | bytes 2359296 | tf_op jit(solution)/shard_map/all_gather | solution.py:842
  35.1 34.3 %collective-permute-start.11 = (bf16[256,1024]{1,0:T(8,128)(2,1)S(1)}, bf16[256,1024]{1,0:T(8,128)(2,1)}, u32[]{:S(2)}, u32[]{:S(2)}) collective-permute-start(bf16[256,1024]{1,0:T(8,128)(2,1)S(1)} %copy-done.2), channel_id=1, source_target_pairs={{0,2},{1,3},{2,0},{3,1},{4,6},{5,7},{6,4},{7,5},{8,10},{9,11},{10,... | collective-permute-start | bytes 1572872 | tf_op jit(solution)/shard_map/ppermute | solution.py:721
  35.5 34.0 %collective-permute-start.12 = (bf16[256,1024]{1,0:T(8,128)(2,1)S(1)}, bf16[256,1024]{1,0:T(8,128)(2,1)}, u32[]{:S(2)}, u32[]{:S(2)}) collective-permute-start(bf16[256,1024]{1,0:T(8,128)(2,1)S(1)} %copy-done.2), channel_id=1, source_target_pairs={{0,3},{1,0},{2,1},{3,2},{4,7},{5,4},{6,5},{7,6},{8,11},{9,8},{10,9... | collective-permute-start | bytes 1572872 | tf_op jit(solution)/shard_map/ppermute | solution.py:721
  40.0 12.6 %copy-start.14 = (bf16[256,1024]{1,0:T(8,128)(2,1)S(1)}, bf16[256,1024]{1,0:T(8,128)(2,1)}, u32[]{:S(2)}) copy-start(bf16[256,1024]{1,0:T(8,128)(2,1)} %cot_ref.1) | copy-start | bytes 1572868
  40.0 4.4 %collective-permute-start.4 = (bf16[32,1536]{1,0:T(8,128)(2,1)S(1)}, bf16[32,1536]{1,0:T(8,128)(2,1)S(1)}, u32[]{:S(2)}, u32[]{:S(2)}) collective-permute-start(bf16[32,1536]{1,0:T(8,128)(2,1)S(1)} %get-tuple-element.250), channel_id=1, source_target_pairs={{0,4},{4,0},{8,12},{12,8},{16,20},{20,16},{24,28},{28,24},{1,5},{5... | collective-permute-start | bytes 294920 | tf_op jit(solution)/shard_map/ppermute | solution.py:717
  41.7 5.3 %collective-permute-start.5 = (bf16[32,1536]{1,0:T(8,128)(2,1)S(1)}, bf16[32,1536]{1,0:T(8,128)(2,1)S(1)}, u32[]{:S(2)}, u32[]{:S(2)}) collective-permute-start(bf16[32,1536]{1,0:T(8,128)(2,1)S(1)} %get-tuple-element.249), channel_id=1, source_target_pairs={{0,8},{4,12},{8,0},{12,4},{16,24},{20,28},{24,16},{28,20},{1,9},{5... | collective-permute-start | bytes 294920 | tf_op jit(solution)/shard_map/ppermute | solution.py:717
  43.0 9.6 %collective-permute-start.7 = (bf16[88,1024]{1,0:T(8,128)(2,1)S(1)}, bf16[88,1024]{1,0:T(8,128)(2,1)S(1)}, u32[]{:S(2)}, u32[]{:S(2)}) collective-permute-start(bf16[88,1024]{1,0:T(8,128)(2,1)S(1)} %copy-done.38), channel_id=1, source_target_pairs={{0,16},{4,20},{8,24},{12,28},{16,0},{20,4},{24,8},{28,12},{1,17},{... | collective-permute-start | bytes 540680 | tf_op jit(solution)/shard_map/ppermute | solution.py:717
  44.4 7.5 %collective-permute-start.6 = (bf16[32,1536]{1,0:T(8,128)(2,1)S(1)}, bf16[32,1536]{1,0:T(8,128)(2,1)S(1)}, u32[]{:S(2)}, u32[]{:S(2)}) collective-permute-start(bf16[32,1536]{1,0:T(8,128)(2,1)S(1)} %get-tuple-element.248), channel_id=1, source_target_pairs={{0,12},{4,8},{8,4},{12,0},{16,28},{20,24},{24,20},{28,16},{1,13},{... | collective-permute-start | bytes 294920 | tf_op jit(solution)/shard_map/ppermute | solution.py:717
  52.6 21.8 %collective-permute-start.9 = (bf16[256,1024]{1,0:T(8,128)(2,1)S(1)}, bf16[256,1024]{1,0:T(8,128)(2,1)}, u32[]{:S(2)}, u32[]{:S(2)}) collective-permute-start(bf16[256,1024]{1,0:T(8,128)(2,1)S(1)} %copy-done.14), channel_id=1, source_target_pairs={{0,8},{4,12},{8,0},{12,4},{16,24},{20,28},{24,16},{28,20},{1,9},{5... | collective-permute-start | bytes 1572872 | tf_op jit(solution)/shard_map/ppermute | solution.py:717
  53.8 234.2 %reduce-scatter.4.cloned.1.call-start = ((), (), s32[]{:S(2)}) async-start(), calls=%async_computation.5 | async-start | bytes 1966080 | tf_op jit(solution)/shard_map/reduce_scatter | solution.py:962
  55.2 59.2 %collective-permute-start.8 = (bf16[256,1024]{1,0:T(8,128)(2,1)S(1)}, bf16[256,1024]{1,0:T(8,128)(2,1)}, u32[]{:S(2)}, u32[]{:S(2)}) collective-permute-start(bf16[256,1024]{1,0:T(8,128)(2,1)S(1)} %copy-done.14), channel_id=1, source_target_pairs={{0,4},{4,0},{8,12},{12,8},{16,20},{20,16},{24,28},{28,24},{1,5},{5... | collective-permute-start | bytes 1572872 | tf_op jit(solution)/shard_map/ppermute | solution.py:717
  69.5 40.2 %collective-permute-start.13 = (bf16[4,32,1536]{2,1,0:T(8,128)(2,1)S(1)}, bf16[4,32,1536]{2,1,0:T(8,128)(2,1)S(1)}, u32[]{:S(2)}, u32[]{:S(2)}) collective-permute-start(bf16[4,32,1536]{2,1,0:T(8,128)(2,1)S(1)} %bitcast.195), channel_id=1, source_target_pairs={{0,1},{1,2},{2,3},{3,0},{4,5},{5,6},{6,7},{7,4},{8,9},{9,10},{10,1... | collective-permute-start | bytes 1179656 | tf_op jit(solution)/shard_map/ppermute | solution.py:721
  69.5 40.2 %collective-permute-start.14 = (bf16[4,32,1536]{2,1,0:T(8,128)(2,1)S(1)}, bf16[4,32,1536]{2,1,0:T(8,128)(2,1)}, u32[]{:S(2)}, u32[]{:S(2)}) collective-permute-start(bf16[4,32,1536]{2,1,0:T(8,128)(2,1)S(1)} %bitcast.196), channel_id=1, source_target_pairs={{0,2},{1,3},{2,0},{3,1},{4,6},{5,7},{6,4},{7,5},{8,10},{9,11},{10,... | collective-permute-start | bytes 1179656 | tf_op jit(solution)/shard_map/ppermute | solution.py:721
  72.7 37.0 %collective-permute-start.15 = (bf16[4,32,1536]{2,1,0:T(8,128)(2,1)S(1)}, bf16[4,32,1536]{2,1,0:T(8,128)(2,1)}, u32[]{:S(2)}, u32[]{:S(2)}) collective-permute-start(bf16[4,32,1536]{2,1,0:T(8,128)(2,1)S(1)} %bitcast.197), channel_id=1, source_target_pairs={{0,3},{1,0},{2,1},{3,2},{4,7},{5,4},{6,5},{7,6},{8,11},{9,8},{10,9... | collective-permute-start | bytes 1179656 | tf_op jit(solution)/shard_map/ppermute | solution.py:721
  74.4 40.0 %collective-permute-start.10 = (bf16[256,1024]{1,0:T(8,128)(2,1)}, bf16[256,1024]{1,0:T(8,128)(2,1)}, u32[]{:S(2)}, u32[]{:S(2)}) collective-permute-start(bf16[256,1024]{1,0:T(8,128)(2,1)} %collective-permute-done.9.refs_5_), channel_id=1, source_target_pairs={{0,4},{4,0},{8,12},{12,8},{16,20},{20,16},{24,28},{28,24},{1,5},{5... | collective-permute-start | bytes 1572872 | tf_op jit(solution)/shard_map/ppermute | solution.py:717
  109.7 19.1 %copy-start.10 = (f32[128,1024]{1,0:T(8,128)}, f32[128,1024]{1,0:T(8,128)S(1)}, u32[]{:S(2)}) copy-start(f32[128,1024]{1,0:T(8,128)S(1)} %get-tuple-element.136.refs_6_.gain_ref) | copy-start | bytes 1572868
  110.5 18.3 %copy-start.3 = (bf16[256,1024]{1,0:T(8,128)(2,1)S(1)}, bf16[256,1024]{1,0:T(8,128)(2,1)}, u32[]{:S(2)}) copy-start(bf16[256,1024]{1,0:T(8,128)(2,1)} %refs_5_.1) | copy-start | bytes 1572868
  113.1 53.3 %collective-permute-start.22 = (bf16[4,128,1536]{2,1,0:T(8,128)(2,1)}, bf16[4,128,1536]{2,1,0:T(8,128)(2,1)}, u32[]{:S(2)}, u32[]{:S(2)}) collective-permute-start(bf16[4,128,1536]{2,1,0:T(8,128)(2,1)} %pad_maximum_fusion.refs_8_), channel_id=1, source_target_pairs={{0,16},{4,20},{8,24},{12,28},{16,0},{20,4},{24,8},{28,12},{1,17},{... | collective-permute-start | bytes 4718600 | tf_op jit(solution)/shard_map/ppermute | solution.py:717
  114.4 4.9 %collective-permute-start.16 = (bf16[256,256]{1,0:T(8,128)(2,1)S(1)}, bf16[256,256]{1,0:T(8,128)(2,1)S(1)}, u32[]{:S(2)}, u32[]{:S(2)}) collective-permute-start(bf16[256,256]{1,0:T(8,128)(2,1)S(1)} %get-tuple-element.133), channel_id=1, source_target_pairs={{0,1},{1,2},{2,3},{3,0},{4,5},{5,6},{6,7},{7,4},{8,9},{9,10},{10,1... | collective-permute-start | bytes 393224 | tf_op jit(solution)/shard_map/ppermute | solution.py:721
  114.4 11.3 %collective-permute-start.17 = (bf16[256,256]{1,0:T(8,128)(2,1)S(1)}, bf16[256,256]{1,0:T(8,128)(2,1)S(1)}, u32[]{:S(2)}, u32[]{:S(2)}) collective-permute-start(bf16[256,256]{1,0:T(8,128)(2,1)S(1)} %get-tuple-element.134), channel_id=1, source_target_pairs={{0,2},{1,3},{2,0},{3,1},{4,6},{5,7},{6,4},{7,5},{8,10},{9,11},{10,... | collective-permute-start | bytes 393224 | tf_op jit(solution)/shard_map/ppermute | solution.py:721
  116.3 12.5 %collective-permute-start.18 = (bf16[256,256]{1,0:T(8,128)(2,1)S(1)}, bf16[256,256]{1,0:T(8,128)(2,1)S(1)}, u32[]{:S(2)}, u32[]{:S(2)}) collective-permute-start(bf16[256,256]{1,0:T(8,128)(2,1)S(1)} %get-tuple-element.135), channel_id=1, source_target_pairs={{0,3},{1,0},{2,1},{3,2},{4,7},{5,4},{6,5},{7,6},{8,11},{9,8},{10,9... | collective-permute-start | bytes 393224 | tf_op jit(solution)/shard_map/ppermute | solution.py:721
  131.3 31.9 %copy-start.8 = (bf16[256,1024]{1,0:T(8,128)(2,1)}, bf16[256,1024]{1,0:T(8,128)(2,1)S(1)}, u32[]{:S(2)}) copy-start(bf16[256,1024]{1,0:T(8,128)(2,1)S(1)} %get-tuple-element.163) | copy-start | bytes 1572868
  131.3 13.3 %collective-permute-start.19 = (bf16[256,1024]{1,0:T(8,128)(2,1)S(1)}, bf16[256,1024]{1,0:T(8,128)(2,1)S(1)}, u32[]{:S(2)}, u32[]{:S(2)}) collective-permute-start(bf16[256,1024]{1,0:T(8,128)(2,1)S(1)} %get-tuple-element.137.refs_0_), channel_id=1, source_target_pairs={{0,8},{4,12},{8,0},{12,4},{16,24},{20,28},{24,16},{28,20},{1,9},{5... | collective-permute-start | bytes 1572872 | tf_op jit(solution)/shard_map/ppermute | solution.py:717
  132.6 9.4 %collective-permute-start.23 = (bf16[2,88,1024]{2,1,0:T(8,128)(2,1)S(1)}, bf16[2,88,1024]{2,1,0:T(8,128)(2,1)S(1)}, u32[]{:S(2)}, u32[]{:S(2)}) collective-permute-start(bf16[2,88,1024]{2,1,0:T(8,128)(2,1)S(1)} %bitcast.201), channel_id=1, source_target_pairs={{0,1},{1,2},{2,3},{3,0},{4,5},{5,6},{6,7},{7,4},{8,9},{9,10},{10,1... | collective-permute-start | bytes 1081352 | tf_op jit(solution)/shard_map/ppermute | solution.py:721
  132.6 30.5 %collective-permute-start.24 = (bf16[2,88,1024]{2,1,0:T(8,128)(2,1)S(1)}, bf16[2,88,1024]{2,1,0:T(8,128)(2,1)S(1)}, u32[]{:S(2)}, u32[]{:S(2)}) collective-permute-start(bf16[2,88,1024]{2,1,0:T(8,128)(2,1)S(1)} %bitcast.202), channel_id=1, source_target_pairs={{0,2},{1,3},{2,0},{3,1},{4,6},{5,7},{6,4},{7,5},{8,10},{9,11},{10,... | collective-permute-start | bytes 1081352 | tf_op jit(solution)/shard_map/ppermute | solution.py:721
  133.0 32.0 %collective-permute-start.25 = (bf16[2,88,1024]{2,1,0:T(8,128)(2,1)S(1)}, bf16[2,88,1024]{2,1,0:T(8,128)(2,1)S(1)}, u32[]{:S(2)}, u32[]{:S(2)}) collective-permute-start(bf16[2,88,1024]{2,1,0:T(8,128)(2,1)S(1)} %bitcast.203), channel_id=1, source_target_pairs={{0,3},{1,0},{2,1},{3,2},{4,7},{5,4},{6,5},{7,6},{8,11},{9,8},{10,9... | collective-permute-start | bytes 1081352 | tf_op jit(solution)/shard_map/ppermute | solution.py:721
  142.0 24.5 %collective-permute-start.20 = (bf16[256,1024]{1,0:T(8,128)(2,1)S(1)}, bf16[256,1024]{1,0:T(8,128)(2,1)S(1)}, u32[]{:S(2)}, u32[]{:S(2)}) collective-permute-start(bf16[256,1024]{1,0:T(8,128)(2,1)S(1)} %get-tuple-element.137.refs_0_), channel_id=1, source_target_pairs={{0,4},{4,0},{8,12},{12,8},{16,20},{20,16},{24,28},{28,24},{1,5},{5... | collective-permute-start | bytes 1572872 | tf_op jit(solution)/shard_map/ppermute | solution.py:717
  144.6 21.9 %collective-permute-start.21 = (bf16[256,1024]{1,0:T(8,128)(2,1)S(1)}, bf16[256,1024]{1,0:T(8,128)(2,1)S(1)}, u32[]{:S(2)}, u32[]{:S(2)}) collective-permute-start(bf16[256,1024]{1,0:T(8,128)(2,1)S(1)} %collective-permute-done.19.refs_1_), channel_id=1, source_target_pairs={{0,4},{4,0},{8,12},{12,8},{16,20},{20,16},{24,28},{28,24},{1,5},{5... | collective-permute-start | bytes 1572872 | tf_op jit(solution)/shard_map/ppermute | solution.py:717
  165.0 16.5 %copy-start.21 = (bf16[2,4,88,1024]{3,2,1,0:T(8,128)(2,1)}, bf16[2,4,88,1024]{3,2,1,0:T(8,128)(2,1)S(1)}, u32[]{:S(2)}) copy-start(bf16[2,4,88,1024]{3,2,1,0:T(8,128)(2,1)S(1)} %bitcast_dynamic-update-slice_fusion.3) | copy-start | bytes 4325380
  181.5 5.6 %collective-permute-start.26 = (bf16[512,1024]{1,0:T(8,128)(2,1)}, bf16[512,1024]{1,0:T(8,128)(2,1)}, u32[]{:S(2)}, u32[]{:S(2)}) collective-permute-start(bf16[512,1024]{1,0:T(8,128)(2,1)} %get-tuple-element.148), channel_id=1, source_target_pairs={{0,4},{4,0},{8,12},{12,8},{16,20},{20,16},{24,28},{28,24},{1,5},{5... | collective-permute-start | bytes 3145736 | tf_op jit(solution)/shard_map/ppermute | solution.py:717
  193.9 94.1 %reduce-scatter.6.cloned.1.call-start = ((), (), s32[]{:S(2)}) async-start(), calls=%async_computation.6 | async-start | bytes 2359296 | tf_op jit(solution)/shard_map/reduce_scatter | solution.py:977
  194.0 13.7 %collective-permute-start.27 = (bf16[256,1024]{1,0:T(8,128)(2,1)S(1)}, bf16[256,1024]{1,0:T(8,128)(2,1)S(1)}, u32[]{:S(2)}, u32[]{:S(2)}) collective-permute-start(bf16[256,1024]{1,0:T(8,128)(2,1)S(1)} %add_convert_fusion), channel_id=1, source_target_pairs={{0,8},{4,12},{8,0},{12,4},{16,24},{20,28},{24,16},{28,20},{1,9},{5... | collective-permute-start | bytes 1572872 | tf_op jit(solution)/shard_map/ppermute | solution.py:717
  200.3 35.9 %collective-permute-start.28 = (bf16[4,128,1536]{2,1,0:T(8,128)(2,1)}, bf16[4,128,1536]{2,1,0:T(8,128)(2,1)}, u32[]{:S(2)}, u32[]{:S(2)}) collective-permute-start(bf16[4,128,1536]{2,1,0:T(8,128)(2,1)} %bitcast.49), channel_id=1, source_target_pairs={{0,16},{4,20},{8,24},{12,28},{16,0},{20,4},{24,8},{28,12},{1,17},{... | collective-permute-start | bytes 4718600 | tf_op jit(solution)/shard_map/ppermute | solution.py:717
  207.7 9.9 %collective-permute-start.29 = (bf16[512,1024]{1,0:T(8,128)(2,1)}, bf16[512,1024]{1,0:T(8,128)(2,1)}, u32[]{:S(2)}, u32[]{:S(2)}) collective-permute-start(bf16[512,1024]{1,0:T(8,128)(2,1)} %convolution_convert_fusion.2), channel_id=1, source_target_pairs={{0,4},{4,0},{8,12},{12,8},{16,20},{20,16},{24,28},{28,24},{1,5},{5... | collective-permute-start | bytes 3145736 | tf_op jit(solution)/shard_map/ppermute | solution.py:717
  212.0 30.5 %collective-permute-start.31 = (bf16[256,256]{1,0:T(8,128)(2,1)S(1)}, bf16[256,256]{1,0:T(8,128)(2,1)S(1)}, u32[]{:S(2)}, u32[]{:S(2)}) collective-permute-start(bf16[256,256]{1,0:T(8,128)(2,1)S(1)} %get-tuple-element.160), channel_id=1, source_target_pairs={{0,1},{1,2},{2,3},{3,0},{4,5},{5,6},{6,7},{7,4},{8,9},{9,10},{10,1... | collective-permute-start | bytes 393224 | tf_op jit(solution)/shard_map/ppermute | solution.py:721
  212.0 30.5 %collective-permute-start.32 = (bf16[256,256]{1,0:T(8,128)(2,1)S(1)}, bf16[256,256]{1,0:T(8,128)(2,1)S(1)}, u32[]{:S(2)}, u32[]{:S(2)}) collective-permute-start(bf16[256,256]{1,0:T(8,128)(2,1)S(1)} %get-tuple-element.161), channel_id=1, source_target_pairs={{0,2},{1,3},{2,0},{3,1},{4,6},{5,7},{6,4},{7,5},{8,10},{9,11},{10,... | collective-permute-start | bytes 393224 | tf_op jit(solution)/shard_map/ppermute | solution.py:721
  214.0 28.5 %collective-permute-start.33 = (bf16[256,256]{1,0:T(8,128)(2,1)S(1)}, bf16[256,256]{1,0:T(8,128)(2,1)S(1)}, u32[]{:S(2)}, u32[]{:S(2)}) collective-permute-start(bf16[256,256]{1,0:T(8,128)(2,1)S(1)} %get-tuple-element.162), channel_id=1, source_target_pairs={{0,3},{1,0},{2,1},{3,2},{4,7},{5,4},{6,5},{7,6},{8,11},{9,8},{10,9... | collective-permute-start | bytes 393224 | tf_op jit(solution)/shard_map/ppermute | solution.py:721
  217.6 138.4 %reduce-scatter.8.cloned.1.call-start = ((), (), s32[]{:S(2)}) async-start(), calls=%async_computation.7 | async-start | bytes 2654208 | tf_op jit(solution)/shard_map/reduce_scatter | solution.py:987
  217.6 18.5 %copy-start.24 = (f32[512,1536]{1,0:T(8,128)S(1)}, f32[512,1536]{1,0:T(8,128)}, u32[]{:S(2)}) copy-start(f32[512,1536]{1,0:T(8,128)} %fusion.15) | copy-start | bytes 9437188
  220.0 18.4 %collective-permute-start.30 = (bf16[256,1024]{1,0:T(8,128)(2,1)S(1)}, bf16[256,1024]{1,0:T(8,128)(2,1)S(1)}, u32[]{:S(2)}, u32[]{:S(2)}) collective-permute-start(bf16[256,1024]{1,0:T(8,128)(2,1)S(1)} %fusion.11), channel_id=1, source_target_pairs={{0,8},{4,12},{8,0},{12,4},{16,24},{20,28},{24,16},{28,20},{1,9},{5... | collective-permute-start | bytes 1572872 | tf_op jit(solution)/shard_map/ppermute | solution.py:717
  242.8 43.7 %collective-permute-start.34 = (bf16[1,4,32,1536]{3,2,1,0:T(8,128)(2,1)S(1)}, bf16[1,4,32,1536]{3,2,1,0:T(8,128)(2,1)S(1)}, u32[]{:S(2)}, u32[]{:S(2)}) collective-permute-start(bf16[1,4,32,1536]{3,2,1,0:T(8,128)(2,1)S(1)} %get-tuple-element.230), channel_id=1, source_target_pairs={{0,1},{1,2},{2,3},{3,0},{4,5},{5,6},{6,7},{7,4},{8,9},{9,10},{10,1... | collective-permute-start | bytes 1179656 | tf_op jit(solution)/shard_map/ppermute | solution.py:721
  242.9 43.6 %collective-permute-start.35 = (bf16[1,4,32,1536]{3,2,1,0:T(8,128)(2,1)S(1)}, bf16[1,4,32,1536]{3,2,1,0:T(8,128)(2,1)S(1)}, u32[]{:S(2)}, u32[]{:S(2)}) collective-permute-start(bf16[1,4,32,1536]{3,2,1,0:T(8,128)(2,1)S(1)} %get-tuple-element.229), channel_id=1, source_target_pairs={{0,2},{1,3},{2,0},{3,1},{4,6},{5,7},{6,4},{7,5},{8,10},{9,11},{10,... | collective-permute-start | bytes 1179656 | tf_op jit(solution)/shard_map/ppermute | solution.py:721
  244.9 43.1 %collective-permute-start.36 = (bf16[1,4,32,1536]{3,2,1,0:T(8,128)(2,1)S(1)}, bf16[1,4,32,1536]{3,2,1,0:T(8,128)(2,1)}, u32[]{:S(2)}, u32[]{:S(2)}) collective-permute-start(bf16[1,4,32,1536]{3,2,1,0:T(8,128)(2,1)S(1)} %get-tuple-element.228), channel_id=1, source_target_pairs={{0,3},{1,0},{2,1},{3,2},{4,7},{5,4},{6,5},{7,6},{8,11},{9,8},{10,9... | collective-permute-start | bytes 1179656 | tf_op jit(solution)/shard_map/ppermute | solution.py:721
  297.7 11.6 %collective-permute-start.37 = (bf16[256,1024]{1,0:T(8,128)(2,1)}, bf16[256,1024]{1,0:T(8,128)(2,1)S(1)}, u32[]{:S(2)}, u32[]{:S(2)}) collective-permute-start(bf16[256,1024]{1,0:T(8,128)(2,1)} %get-tuple-element.192), channel_id=1, source_target_pairs={{0,1},{1,2},{2,3},{3,0},{4,5},{5,6},{6,7},{7,4},{8,9},{9,10},{10,1... | collective-permute-start | bytes 1572872 | tf_op jit(solution)/shard_map/ppermute | solution.py:721
  298.6 62.0 %collective-permute-start.38 = (bf16[256,1024]{1,0:T(8,128)(2,1)}, bf16[256,1024]{1,0:T(8,128)(2,1)S(1)}, u32[]{:S(2)}, u32[]{:S(2)}) collective-permute-start(bf16[256,1024]{1,0:T(8,128)(2,1)} %copy-done.17), channel_id=1, source_target_pairs={{0,2},{1,3},{2,0},{3,1},{4,6},{5,7},{6,4},{7,5},{8,10},{9,11},{10,... | collective-permute-start | bytes 1572872 | tf_op jit(solution)/shard_map/ppermute | solution.py:721
  300.8 37.2 %copy-start.35 = (bf16[2,96,1024]{2,1,0:T(8,128)(2,1)S(1)}, bf16[2,96,1024]{2,1,0:T(8,128)(2,1)}, u32[]{:S(2)}) copy-start(bf16[2,96,1024]{2,1,0:T(8,128)(2,1)} %reduce-scatter.4.cloned.1.call-done) | copy-start | bytes 1179652
  300.8 59.8 %collective-permute-start.39 = (bf16[256,1024]{1,0:T(8,128)(2,1)}, bf16[256,1024]{1,0:T(8,128)(2,1)S(1)}, u32[]{:S(2)}, u32[]{:S(2)}) collective-permute-start(bf16[256,1024]{1,0:T(8,128)(2,1)} %copy-done.16), channel_id=1, source_target_pairs={{0,3},{1,0},{2,1},{3,2},{4,7},{5,4},{6,5},{7,6},{8,11},{9,8},{10,9... | collective-permute-start | bytes 1572872 | tf_op jit(solution)/shard_map/ppermute | solution.py:721
  311.2 35.0 %collective-permute-start.43 = (f32[32,1536]{1,0:T(8,128)S(1)}, f32[32,1536]{1,0:T(8,128)S(1)}, u32[]{:S(2)}, u32[]{:S(2)}) collective-permute-start(f32[32,1536]{1,0:T(8,128)S(1)} %get-tuple-element.235), channel_id=1, source_target_pairs={{0,4},{4,0},{8,12},{12,8},{16,20},{20,16},{24,28},{28,24},{1,5},{5... | collective-permute-start | bytes 589832 | tf_op jit(solution)/shard_map/ppermute | solution.py:717
  336.9 9.3 %collective-permute-start.44 = (f32[32,1536]{1,0:T(8,128)S(1)}, f32[32,1536]{1,0:T(8,128)S(1)}, u32[]{:S(2)}, u32[]{:S(2)}) collective-permute-start(f32[32,1536]{1,0:T(8,128)S(1)} %get-tuple-element.234), channel_id=1, source_target_pairs={{0,8},{4,12},{8,0},{12,4},{16,24},{20,28},{24,16},{28,20},{1,9},{5... | collective-permute-start | bytes 589832 | tf_op jit(solution)/shard_map/ppermute | solution.py:717
  338.0 5.9 %collective-permute-start.46 = (bf16[1,88,1024]{2,1,0:T(8,128)(2,1)S(1)}, bf16[1,88,1024]{2,1,0:T(8,128)(2,1)S(1)}, u32[]{:S(2)}, u32[]{:S(2)}) collective-permute-start(bf16[1,88,1024]{2,1,0:T(8,128)(2,1)S(1)} %constant_dynamic-slice_fusion), channel_id=1, source_target_pairs={{0,16},{4,20},{8,24},{12,28},{16,0},{20,4},{24,8},{28,12},{1,17},{... | collective-permute-start | bytes 540680 | tf_op jit(solution)/shard_map/ppermute | solution.py:717
  343.9 7.1 %collective-permute-start.45 = (f32[32,1536]{1,0:T(8,128)S(1)}, f32[32,1536]{1,0:T(8,128)S(1)}, u32[]{:S(2)}, u32[]{:S(2)}) collective-permute-start(f32[32,1536]{1,0:T(8,128)S(1)} %get-tuple-element.233), channel_id=1, source_target_pairs={{0,12},{4,8},{8,4},{12,0},{16,28},{20,24},{24,20},{28,16},{1,13},{... | collective-permute-start | bytes 589832 | tf_op jit(solution)/shard_map/ppermute | solution.py:717
  357.1 4.9 %collective-permute-start.40 = (bf16[1,32,2176]{2,1,0:T(8,128)(2,1)S(1)}, bf16[1,32,2176]{2,1,0:T(8,128)(2,1)S(1)}, u32[]{:S(2)}, u32[]{:S(2)}) collective-permute-start(bf16[1,32,2176]{2,1,0:T(8,128)(2,1)S(1)} %get-tuple-element.243), channel_id=1, source_target_pairs={{0,1},{1,2},{2,3},{3,0},{4,5},{5,6},{6,7},{7,4},{8,9},{9,10},{10,1... | collective-permute-start | bytes 417800 | tf_op jit(solution)/shard_map/ppermute | solution.py:721
  359.2 11.3 %collective-permute-start.41 = (bf16[1,32,2176]{2,1,0:T(8,128)(2,1)S(1)}, bf16[1,32,2176]{2,1,0:T(8,128)(2,1)S(1)}, u32[]{:S(2)}, u32[]{:S(2)}) collective-permute-start(bf16[1,32,2176]{2,1,0:T(8,128)(2,1)S(1)} %get-tuple-element.241), channel_id=1, source_target_pairs={{0,2},{1,3},{2,0},{3,1},{4,6},{5,7},{6,4},{7,5},{8,10},{9,11},{10,... | collective-permute-start | bytes 417800 | tf_op jit(solution)/shard_map/ppermute | solution.py:721
  359.3 11.3 %collective-permute-start.42 = (bf16[1,32,2176]{2,1,0:T(8,128)(2,1)S(1)}, bf16[1,32,2176]{2,1,0:T(8,128)(2,1)S(1)}, u32[]{:S(2)}, u32[]{:S(2)}) collective-permute-start(bf16[1,32,2176]{2,1,0:T(8,128)(2,1)S(1)} %get-tuple-element.240), channel_id=1, source_target_pairs={{0,3},{1,0},{2,1},{3,2},{4,7},{5,4},{6,5},{7,6},{8,11},{9,8},{10,9... | collective-permute-start | bytes 417800 | tf_op jit(solution)/shard_map/ppermute | solution.py:721
  360.6 13.1 %copy-start.25 = (bf16[256,1024]{1,0:T(8,128)(2,1)}, bf16[256,1024]{1,0:T(8,128)(2,1)S(1)}, u32[]{:S(2)}) copy-start(bf16[256,1024]{1,0:T(8,128)(2,1)S(1)} %collective-permute-done.39) | copy-start | bytes 1572868
  (34 other events, 106.1 us)
Sparse Core Ops, SparseCore 0:
  35.2 38.3 all-gather.2
  76.1 27.8 all-gather.4
  194.1 43.1 reduce-scatter.3
  240.4 41.1 reduce-scatter.5
  288.2 43.4 reduce-scatter.7

commit v4 on v3

--- a/solution.py
+++ b/solution.py
@@ -64,11 +64,15 @@
     step = 2
     while step < size:
         picked = (gap >= step) & (gap < 2 * step)
-        parts = [halves(jnp.where(picked, system, 0.0)) for system in systems]
-        done = [halves(result) for result in results]
-        inner = [halves(product(part, own)) for part, own in zip(parts, done)]
-        results = [result - product(own, side) for result, own, side in zip(results, done, inner)]
+        parts = [jnp.where(picked, system, 0.0).astype(NARROW) for system in systems]
+        done = [result.astype(NARROW) for result in results]
+        inner = [plain_dot(part, own).astype(NARROW) for part, own in zip(parts, done)]
+        results = [result - plain_dot(own, side) for result, own, side in zip(results, done, inner)]
         step *= 2
+    left = [eye - result - product(halves(system), halves(result)) for system, result in zip(systems, results)]
+    results = [
+        result + plain_dot(result.astype(NARROW), rest.astype(NARROW)) for result, rest in zip(results, left)
+    ]
     return results
 
 
@@ -250,10 +254,11 @@
 
 def backward_kernel(heads, width, n_fs, shard_rows, *refs):
     pieces, refs = refs[:n_fs], refs[n_fs:]
-    (win_ref, near_ref, segcol_ref, poscol_ref, segrow_ref, edges_ref, z_ref, dgffn_ref,
+    (win_ref, near_ref, far_ref, segcol_ref, poscol_ref, segrow_ref, edges_ref, z_ref, dgffn_ref,
      taps_ref, gain_ref, hidden_ref, raw_ref, mixed_ref, q_ref, k_ref, inv_ref, score_ref, dots_ref, upd_ref, state_ref,
-     move_ref, draw_ref, gradin_ref,
-     dtaps_ref, sum_ref, small_ref, pad_ref, grad_ref, pdo_ref, dconv_ref, dout_ref, dnormed_ref) = refs
+     move_ref, gradin_ref, *refs) = refs
+    blocks, refs = refs[:n_fs], refs[n_fs:]
+    (draw_ref, dhid_ref, dtaps_ref, sum_ref, small_ref, pad_ref, grad_ref, pdo_ref, dconv_ref, dout_ref, dnormed_ref) = refs
     total = raw_ref.shape[0]
 
     def enter(index, _):
@@ -427,11 +432,6 @@
     beside = sum_ref[:, 4 * span:] + beside + jnp.where(lane == heads, across, 0.0)
     gradin_ref[:, 4 * span:] = beside.astype(NARROW)
 
-
-def leave_kernel(n_fs, win_ref, far_ref, draw_ref, *refs):
-    blocks, (dhid_ref,) = refs[:n_fs], refs[n_fs:]
-    total = draw_ref.shape[0]
-
     def leave(index, _):
         rows = pl.ds(pl.multiple_of(index * ENTER, ENTER), ENTER)
         dhid_ref[rows, :] = plain_dot(draw_ref[rows, :], win_ref[...], 1, 1).astype(NARROW)
@@ -459,6 +459,10 @@
 
 def specs(count):
     return [pl.BlockSpec(memory_space=pltpu.VMEM)] * count
+
+
+def anywhere():
+    return pl.BlockSpec(memory_space=pl.ANY)
 
 
 def in_scalars():
@@ -500,21 +504,21 @@
     return result[:n_fs], result[n_fs], result[n_fs + 1 :]
 
 
-def delta_backward(pieces, w_in, near, segcol, poscol, segrow, edges, z, dgffn, kept, heads, width, shard_rows):
+def delta_backward(pieces, w_in, near, far, segcol, poscol, segrow, edges, z, dgffn, kept, heads, width, shard_rows):
     n_fs = len(pieces)
     total = near.shape[0]
     features, lanes = w_in.shape
     count = total // CHUNK
     span = heads * width
-    return pl.pallas_call(
+    block = jax.ShapeDtypeStruct((total // n_fs, features), NARROW)
+    result = pl.pallas_call(
         functools.partial(backward_kernel, heads, width, n_fs, shard_rows),
-        out_shape=(
-            jax.ShapeDtypeStruct((total, lanes), NARROW),
-            jax.ShapeDtypeStruct((features, lanes), NARROW),
-        ),
-        in_specs=specs(n_fs + 5) + [in_scalars()] * 2 + specs(14),
-        out_specs=tuple(specs(2)),
+        out_shape=(jax.ShapeDtypeStruct((features, lanes), NARROW),) + (block,) * n_fs,
+        in_specs=specs(n_fs + 6) + [in_scalars()] * 2 + specs(14),
+        out_specs=tuple(specs(n_fs + 1)),
         scratch_shapes=[
+            pltpu.VMEM((total, lanes), NARROW),
+            pltpu.VMEM((total, features), NARROW),
             pltpu.VMEM(kept[0].shape, WIDE),
             pltpu.VMEM((features, lanes), WIDE),
             pltpu.VMEM((lanes - 4 * span, features), WIDE),
@@ -528,23 +532,60 @@
         compiler_params=pltpu.CompilerParams(vmem_limit_bytes=52 << 20),
         cost_estimate=cost(40_000_000_000, 16 << 20),
         name="delta_backward",
-    )(*pieces, w_in, near, segcol, poscol, segrow, edges, z, dgffn, *kept)
-
-
-def leave_packed(w_in, far, d_raw, n_fs):
-    total = d_raw.shape[0]
-    features = w_in.shape[0]
-    block = jax.ShapeDtypeStruct((total // n_fs, features), NARROW)
+    )(*pieces, w_in, near, far, segcol, poscol, segrow, edges, z, dgffn, *kept)
+    return result[0], list(result[1:])
+
+
+def finish_kernel(heads, span, n_taps, z_ref, *refs):
+    n_fs = len(refs) - 10
+    pieces, refs = refs[:n_fs], refs[n_fs:]
+    (*grads, wout_ref, beta_ref, taps_ref, gmix_ref, gffn_ref, ghead_ref) = refs
+    side = pl.ds(4 * span, 128)
+    lane = lax.broadcasted_iota(jnp.int32, (128, beta_ref.shape[1]), 0)
+    column = lax.broadcasted_iota(jnp.int32, (128, beta_ref.shape[1]), 1)
+    wout = jnp.zeros(wout_ref.shape, WIDE)
+    small = jnp.zeros((wout_ref.shape[0], 128), WIDE)
+    beta = jnp.zeros(beta_ref.shape, WIDE)
+    for k, piece in enumerate(pieces):
+        line = lax.rem(z_ref[0] + n_fs - k, n_fs)
+        place = pl.ds(pl.multiple_of(line * span, span), span)
+        for which, grad in enumerate(grads):
+            grad[:, place] = piece[:, which * span:(which + 1) * span].astype(WIDE)
+        wout = wout + piece[:, 4 * span + 128:].astype(WIDE)
+        beside = piece[:, side]
+        small = small + beside.astype(WIDE)
+        chosen = jnp.where((lane < heads) & (column == line * heads + lane), 1.0, 0.0)
+        beta = beta + plain_dot(beside, chosen.astype(NARROW))
+    wout_ref[...] = wout
+    beta_ref[...] = beta
+    small = small.T
+    gmix_ref[...] = small[heads:heads + 1]
+    gffn_ref[...] = small[heads + 1:heads + 2]
+    last_row = heads + 2 + 3 * n_taps
+    taps_ref[...] = small[heads + 2:last_row]
+    ghead_ref[...] = small[last_row:last_row + 1]
+
+
+def finish(z, pieces, heads, span, n_taps):
+    rows = pieces[0].shape[0]
+    n_fs = len(pieces)
+    full = jax.ShapeDtypeStruct((rows, n_fs * span), WIDE)
+    line = jax.ShapeDtypeStruct((1, rows), WIDE)
     return pl.pallas_call(
-        functools.partial(leave_kernel, n_fs),
-        out_shape=(block,) * n_fs,
-        in_specs=specs(3),
-        out_specs=tuple(specs(n_fs)),
-        scratch_shapes=[pltpu.VMEM((total, features), NARROW)],
-        compiler_params=pltpu.CompilerParams(vmem_limit_bytes=40 << 20),
-        cost_estimate=cost(1_000_000, 1 << 10),
-        name="leave_packed",
-    )(w_in, far, d_raw)
+        functools.partial(finish_kernel, heads, span, n_taps),
+        out_shape=(full,) * 5
+        + (
+            jax.ShapeDtypeStruct((rows, n_fs * heads), WIDE),
+            jax.ShapeDtypeStruct((3 * n_taps, rows), WIDE),
+            line,
+            line,
+            line,
+        ),
+        in_specs=[in_scalars()] + specs(n_fs),
+        out_specs=tuple(specs(10)),
+        cost_estimate=cost(1_000_000, 1 << 20),
+        name="finish_inputs",
+    )(z, *pieces)
 
 
 def mix_out_kernel(n_fs, row, z_ref, *refs):
@@ -646,8 +687,22 @@
     )(block, *rows_in, *cots, *weights, w_down)
 
 
-def mix_back_kernel(n_fs, row, z_ref, own_ref, core_ref, side_ref, middle_ref, gain_ref, cot_ref, wout_ref, *refs):
-    blocks, (dmiddle_ref, dbranch_ref, dgain_ref) = refs[:n_fs], refs[n_fs:]
+def mix_back_kernel(n_fs, row, z_ref, *refs):
+    sources, refs = refs[:6], refs[6:]
+    gain_ref, refs = refs[0], refs[1:]
+    blocks, refs = refs[:n_fs], refs[n_fs:]
+    (dmiddle_ref, dbranch_ref, dgain_ref, *places, sems) = refs
+    fetches = [pltpu.make_async_copy(source, place, sems.at[k]) for k, (source, place) in enumerate(zip(sources, places))]
+    quarter = places[5].shape[0] // 4
+    parts = [pl.ds(k * quarter, quarter) for k in range(4)]
+    fetches[5:] = [
+        pltpu.make_async_copy(sources[5].at[part], places[5].at[part], sems.at[5 + k]) for k, part in enumerate(parts)
+    ]
+    for fetch in fetches:
+        fetch.start()
+    own_ref, core_ref, side_ref, middle_ref, cot_ref, wout_ref = places
+    for fetch in fetches[:5]:
+        fetch.wait()
     middle = middle_ref[...]
     given = own_ref[...] + core_ref[0:own_ref.shape[0], :].astype(WIDE) + side_ref[...].astype(WIDE)
     scale = lax.rsqrt(jnp.mean(middle * middle, axis=-1, keepdims=True) + norm_eps)
@@ -659,6 +714,8 @@
     dbranch = dmiddle.astype(NARROW)
     dbranch_ref[...] = dbranch
     span = blocks[0].shape[1]
+    for fetch in fetches[5:]:
+        fetch.wait()
     for k, block in enumerate(blocks):
         place = pl.ds(pl.multiple_of(lax.rem(z_ref[0] + k, n_fs) * span, span), span)
         block[...] = plain_dot(dbranch, wout_ref[place, :], 1, 1).astype(NARROW)
@@ -667,6 +724,7 @@
 def mix_back(z, parts, middle, side, row, cotangent, w_out, n_fs):
     count, features = middle.shape
     block = jax.ShapeDtypeStruct((count, features // n_fs), NARROW)
+    sources = (*parts, middle, cotangent, w_out)
     result = pl.pallas_call(
         functools.partial(mix_back_kernel, n_fs, row),
         out_shape=(block,) * n_fs
@@ -675,12 +733,13 @@
             jax.ShapeDtypeStruct(middle.shape, NARROW),
             jax.ShapeDtypeStruct((1, features), WIDE),
         ),
-        in_specs=[in_scalars()] + specs(7),
+        in_specs=[in_scalars()] + [anywhere()] * 6 + specs(1),
         out_specs=tuple(specs(n_fs + 3)),
-        compiler_params=pltpu.CompilerParams(vmem_limit_bytes=40 << 20),
+        scratch_shapes=[pltpu.VMEM(part.shape, part.dtype) for part in sources] + [pltpu.SemaphoreType.DMA((9,))],
+        compiler_params=pltpu.CompilerParams(vmem_limit_bytes=60 << 20),
         cost_estimate=cost(2_000_000_000, 6 << 20),
         name="mix_back",
-    )(z, *parts, middle, side, cotangent, w_out)
+    )(z, *sources, side)
     return (result[:n_fs],) + tuple(result[n_fs:])
 
 
@@ -815,15 +874,18 @@
     block = me // TP
     n_rest = n_dp // TP
     ff_block = hidden_ffn // n_dp
-    ff_own = n_rest * ff_block
-    ff_pad = -(-ff_own // 128) * 128
+    ff_line = ff_block // n_fs
+    ff_unit = -(-ff_line // 8) * 8
+    while n_rest * n_fs * ff_unit % 128:
+        ff_unit += 8
+    ff_pad = n_rest * n_fs * ff_unit
     tp_bits = [bit for bit in bits if bit < TP]
     rest_bits = [bit for bit in bits if bit >= TP]
 
     def by_member(matrix):
-        split = matrix.reshape(rows, n_rest, TP, ff_block)
-        split = jnp.transpose(split, (2, 0, 1, 3)).reshape(TP, rows, ff_own)
-        return jnp.pad(split, ((0, 0), (0, 0), (0, ff_pad - ff_own)))
+        split = matrix.reshape(rows, n_rest, TP, n_fs, ff_line)
+        split = jnp.pad(split, ((0, 0),) * 4 + ((0, ff_unit - ff_line),))
+        return jnp.transpose(split, (2, 0, 1, 3, 4)).reshape(TP, rows, ff_pad)
 
     def hand_out(blocks):
         pieces = [lax.dynamic_index_in_dim(blocks, z, 0)]
@@ -865,6 +927,7 @@
         for key in range(TP)
     }
     own_down, _ = lax.optimization_barrier((w_ffn_down, token_pieces[1]))
+    own_down = jnp.pad(own_down, ((0, ff_unit - ff_line), (0, 0)))
     down_rows = in_order(gather_cube(own_down, rest_bits, n_dp), block).reshape(n_rest, -1, features)
     both_rows = in_order(both_pieces, member).reshape(TP, rows, 2 * ff_pad)
     own_cotangent, both_rows, down_rows = lax.optimization_barrier((cotangent, both_rows, down_rows))
@@ -923,8 +986,7 @@
     mixed_pieces = pass_on(blocks)
     down_line = line_pieces(down_rows, n_fs)
     middle, ffn_in, normed_b = mix_out(z_ref, mixed_pieces, full_out, tokens, side, gain_row)
-    w_down = line_order(down_line, z).reshape(ff_own, features)
-    w_down = jnp.pad(w_down, ((0, ff_pad - ff_own), (0, 0)))
+    w_down = line_order(down_line, z).reshape(ff_pad, features)
     ffn_pieces = gather_cube(ffn_in, tp_bits[::-1], n_dp)
     active_b, d_both, first, second, d_own = ffn_units(
         jnp.stack([block, z]),
@@ -952,19 +1014,14 @@
     second, both_sent, active_late = lax.optimization_barrier((second.astype(NARROW), both_sent, active_b))
     from_side = flip(second, tp_bits[1], n_dp)
     cotangent_near = jnp.concatenate([cot_pieces[key] for key in tp_order], axis=0)
-    down_terms = weight_grad(active_late, cotangent_near)[:ff_own].reshape(n_rest, n_fs, -1, features)
-    down_each = down_terms.shape[2]
-    down_terms = jnp.pad(down_terms, ((0, 0), (0, 0), (0, -down_each % 32), (0, 0)))
-    both_sum = both_part(top * split if rest_bits else 0, split)
-    out_terms = collect(active_late, w_down, ((1,), (0,)))
-    out_first = next(out_terms)
-    down_terms = down_terms.astype(NARROW)
+    down_terms = weight_grad(active_late, cotangent_near).astype(NARROW)
     down_sum = lax.psum_scatter(
         down_terms.reshape(n_rest, -1, features), "fsdp", scatter_dimension=1, tiled=True
     )
-    from_side, down_terms, both_sum, out_first = lax.optimization_barrier(
-        (from_side, down_terms, both_sum, out_first)
+    from_side, down_terms, ffn_near, active_late = lax.optimization_barrier(
+        (from_side, down_terms, ffn_near, active_late)
     )
+    both_sum = both_part(top * split if rest_bits else 0, split)
     if rest_bits:
         both_sum = both_sum + flip(both_sent, rest_bits[-1], n_dp).astype(WIDE)
         both_sum = halve(both_sum, block, rest_bits[:-1])
@@ -976,20 +1033,20 @@
     out_grad = weight_grad(normed_b, d_branch).astype(NARROW)
     sum_out = lax.psum_scatter(out_grad, "dp", scatter_dimension=0, tiled=True)
     both_sum = jnp.swapaxes(both_sum.reshape(TP, n_fs, rows, 2 * ff_pad), 0, 1)
-    layer_out = (middle + out_terms.send(out_terms.send(out_first))).astype(NARROW)
-    both_sum, layer_out, d_pieces, out_grad = lax.optimization_barrier((both_sum, layer_out, d_pieces, out_grad))
+    both_sum, d_pieces, out_grad = lax.optimization_barrier((both_sum, d_pieces, out_grad))
     both_line = hand_out(both_sum.astype(NARROW))
 
-    d_raw, grad_in = delta_backward(
-        d_pieces, w_in, near, *layout, d_gffn, kept, heads, width, shard_rows
+    grad_in, d_blocks = delta_backward(
+        d_pieces, w_in, near, far, *layout, d_gffn, kept, heads, width, shard_rows
     )
     grad_in, both_line, down_sum, sum_out = lax.optimization_barrier((grad_in, both_line, down_sum, sum_out))
     part = lax.psum_scatter(grad_in, "dp", scatter_dimension=0, tiled=True)
-    d_blocks = leave_packed(w_in, far, d_raw, n_fs)
+    d_blocks, both_line, active_late = lax.optimization_barrier((d_blocks, both_line, active_late))
     d_blocks = pass_on(d_blocks)
-    both_line, d_blocks[1] = lax.optimization_barrier((both_line, d_blocks[1]))
+    out_terms = collect(active_late, w_down, ((1,), (0,)))
+    layer_out = (middle + out_terms.send(out_terms.send(next(out_terms)))).astype(NARROW)
     both_sum = sum_up(both_line, both_sum)
-    grad_fdown = halve(down_sum[:, :down_each], block, rest_bits)[0].astype(WIDE)
+    grad_fdown = halve(down_sum, block, rest_bits)[0, :ff_line].astype(WIDE)
     both_pieces = {
         key: flip(lax.dynamic_index_in_dim(both_sum, member ^ key, 0, keepdims=False), key, n_dp)
         if key
@@ -998,13 +1055,14 @@
     }
     both_mine = in_order({key: piece[None] for key, piece in both_pieces.items()}, member)
     def units_of(which):
-        part = both_mine[:, :, which * ff_pad : which * ff_pad + ff_own].reshape(TP, rows, n_rest, ff_block)
-        return jnp.transpose(part, (1, 2, 0, 3)).reshape(rows, hidden_ffn)
+        part = both_mine[:, :, which * ff_pad : (which + 1) * ff_pad]
+        part = part.reshape(TP, rows, n_rest, n_fs, ff_unit)[..., :ff_line]
+        return jnp.transpose(part, (1, 2, 0, 3, 4)).reshape(rows, hidden_ffn)
 
     lanes = part.shape[1]
     joint = jnp.concatenate([part, sum_out], axis=1).reshape(n_fs, rows, -1)
     arrived = [piece[0] for piece in hand_out(joint)]
-    d_blocks, arrived[1] = lax.optimization_barrier((d_blocks, arrived[1]))
+    d_blocks, arrived[0], layer_out = lax.optimization_barrier((d_blocks, arrived[0], layer_out))
     d_hidden = d_blocks[0].astype(WIDE)
     for block_of in d_blocks[1:]:
         d_hidden = d_hidden + block_of.astype(WIDE)
@@ -1016,30 +1074,22 @@
     d_inputs_norm, _ = norm_mix_back(d_hidden)
     grad_tokens = d_middle + d_inputs_norm
 
-    part = line_order([piece[None, :, :lanes] for piece in arrived], z)[0].astype(WIDE)
-    grad_wout = jnp.zeros((rows, features), WIDE)
-    for piece in arrived:
-        grad_wout = grad_wout + piece[:, lanes:].astype(WIDE)
-
-    def columns_of(which):
-        return jnp.swapaxes(part[:, :, which * span : (which + 1) * span], 0, 1).reshape(rows, features)
-
-    grad_beta = jnp.swapaxes(part[:, :, 4 * span : 4 * span + heads], 0, 1).reshape(rows, heads_all)
-    small_sum = jnp.sum(part[:, :, 4 * span + heads : 4 * span + heads + n_small], axis=0)
-    grad_taps = small_sum[:, 2 : 2 + 3 * n_taps].T.reshape(3, n_taps, rows)
+    grads, (grad_wout, grad_beta, grad_taps, grad_gmix, grad_gffn, grad_ghead) = (
+        lambda outs: (outs[:4], outs[4:])
+    )(finish(z_ref, arrived, heads, span, n_taps))
     return (
         layer_out,
         grad_tokens,
-        columns_of(0),
-        columns_of(1),
-        columns_of(2),
-        columns_of(3),
+        grads[0],
+        grads[1],
+        grads[2],
+        grads[3],
         grad_beta,
-        grad_taps,
+        grad_taps.reshape(3, n_taps, rows),
         grad_wout,
-        small_sum[:, 0],
-        small_sum[:head_rows, 2 + 3 * n_taps],
-        small_sum[:, 1],
+        grad_gmix[0],
+        grad_ghead[0, :head_rows],
+        grad_gffn[0],
         units_of(0),
         units_of(1),
         grad_fdown,

time: 393 us -> 376 us (0.957)
  starting transfers between devices: 70.5 us -> 58.8 us
  waiting for transfers between devices: 125 us -> 117 us
    ppermute x20, starting transfers between devices: 44.2 us -> 20.8 us  [flip(): return lax.ppermute(value, 'dp', [(i, i ^ bit) for i in range(n_dp)])]
    ppermute x27, waiting for transfers between devices: 86.6 us -> 71.3 us  [shift(): lax.ppermute(value, 'fsdp', [(i, (i + by) % n_fs) for i in range(n_fs)])]
    reduce_scatter x1, starting transfers between devices: 0.04 us -> 10.6 us  [per_device(): sum_out = lax.psum_scatter(out_grad, 'dp', scatter_dimension=0, tiled=True)]
    pallas_call x1, Pallas kernels: 40 us -> 44.8 us  [delta_backward(): pl.pallas_call(functools.partial(backward_kernel, heads, width, n_fs, sha...]
    ppermute x20, waiting for transfers between devices: 38.7 us -> 43.5 us  [flip(): return lax.ppermute(value, 'dp', [(i, i ^ bit) for i in range(n_dp)])]
    pallas_call x1, Pallas kernels: 6.01 us -> 1.99 us  [finish(): pl.pallas_call(functools.partial(finish_kernel, heads, span, n_taps), out...]
    reshape x15 -> x9, local copies, waits for them, and re-layouts: 8.01 us -> 9.06 us  [the longest x2 3.71 us: units_of(): part = part.reshape(TP, rows, n_rest, n_fs, ff_unit)[..., :ff_line]]
    unnamed x100 -> x87, local copies, waits for them, and re-layouts: 18 us -> 17.2 us
  transfers between devices with their start and end apart: 52 -> 52, of which waited for: 20 -> 21; matrix products, arithmetic and copies ran while one was open for 12% -> 16% of each run, Pallas kernels for 22% -> 23%
where the time goes in v4:
time: 376 us; the launch traced here: 373 us
  waiting for transfers between devices  117 us (31%)
  Pallas kernels  100 us (27%)
  starting transfers between devices  58.8 us (16%)
  local copies, waits for them, and re-layouts  40 us (11%)
  matrix products  23.8 us (6%)
  other arithmetic  17.5 us (5%)
  between operations  14.8 us (4%)
    ppermute x27, waiting for transfers between devices, shift(): lax.ppermute(value, 'fsdp', [(i, (i + by) % n_fs) for i in range(n_fs)])  71.3 us
    pallas_call x1, Pallas kernels, delta_backward(): pl.pallas_call(functools.partial(backward_kernel, heads, width, n_fs, sha...  44.8 us
    ppermute x20, waiting for transfers between devices, flip(): return lax.ppermute(value, 'dp', [(i, i ^ bit) for i in range(n_dp)])  43.5 us
    pallas_call x1, Pallas kernels, delta_forward(): pl.pallas_call(functools.partial(forward_kernel, heads, width, n_fs, shar...  32.7 us
    ppermute x27, starting transfers between devices, shift(): lax.ppermute(value, 'fsdp', [(i, (i + by) % n_fs) for i in range(n_fs)])  27.3 us
    ppermute x20, starting transfers between devices, flip(): return lax.ppermute(value, 'dp', [(i, i ^ bit) for i in range(n_dp)])  20.8 us
    unnamed x87, local copies, waits for them, and re-layouts  17.2 us
    dot_general x4, matrix products, weight_grad(): lax.dot_general(left, right, (((0,), (0,)), ((), ())), preferred_element_...  14.7 us
  transfers between devices with their start and end apart: 52, of which 21 were waited for; matrix products, arithmetic and copies ran while one was open for 16% of the time, Pallas kernels for 23%

profile of v4, /device:TPU:9, one launch (start us, length us, event | category | flops | bytes accessed | tf_op | source)
XLA Modules:
  0.0 372.8 jit_solution(17394576000619589328)
XLA Ops:
  7.3 1.3 collective-permute-start.3
  16.0 1.3 collective-permute-start
  18.6 4.7 %collective-permute-done = bf16[1,32,2176]{2,1,0:T(8,128)(2,1)S(1)} collective-permute-done((bf16[1,32,2176]{2,1,0:T(8,128)(2,1)S(1)}, bf16[1,32,2176]{2,1,0:T(8,128)(2,1)S(1)}, u32[]{:S(2)}, u32[]{:S(2)}) %collective-permute-start) | collective-permute-done | bytes 139296 | tf_op jit(solution)/shard_map/ppermute | solution.py:780
  23.3 8.0 %collective-permute-done.1 = bf16[1,32,2176]{2,1,0:T(8,128)(2,1)S(1)} collective-permute-done((bf16[1,32,2176]{2,1,0:T(8,128)(2,1)S(1)}, bf16[1,32,2176]{2,1,0:T(8,128)(2,1)S(1)}, u32[]{:S(2)}, u32[]{:S(2)}) %collective-permute-start.1) | collective-permute-done | bytes 139296 | tf_op jit(solution)/shard_map/ppermute | solution.py:780
  31.3 2.9 collective-permute-done.2
  40.8 1.7 collective-permute-start.4
  47.2 1.4 collective-permute-done.5
  48.6 4.1 %collective-permute-done.6 = bf16[32,1536]{1,0:T(8,128)(2,1)S(1)} collective-permute-done((bf16[32,1536]{1,0:T(8,128)(2,1)S(1)}, bf16[32,1536]{1,0:T(8,128)(2,1)S(1)}, u32[]{:S(2)}, u32[]{:S(2)}) %collective-permute-start.6) | collective-permute-done | bytes 98336 | tf_op jit(solution)/shard_map/ppermute | solution.py:776
  57.8 11.7 %collective-permute-done.11.refs_2_ = bf16[256,1024]{1,0:T(8,128)(2,1)} collective-permute-done((bf16[256,1024]{1,0:T(8,128)(2,1)S(1)}, bf16[256,1024]{1,0:T(8,128)(2,1)}, u32[]{:S(2)}, u32[]{:S(2)}) %collective-permute-start.11) | collective-permute-done | bytes 524320 | tf_op jit(solution)/shard_map/ppermute | solution.py:780
  69.5 3.2 collective-permute-start.14
  72.7 1.7 collective-permute-start.15
  74.4 1.3 collective-permute-start.10
  75.7 32.7 %delta_forward.1 = (bf16[256,256]{1,0:T(8,128)(2,1)S(1)}, bf16[256,256]{1,0:T(8,128)(2,1)S(1)}, bf16[256,256]{1,0:T(8,128)(2,1)S(1)}, bf16[256,256]{1,0:T(8,128)...) custom-call(bf16[256,1024]{1,0:T(8,128)(2,1)} %refs_5_.1, ...), custom_call_target="tpu_custom_call" | custom-call | flops 30000001024 | bytes 16777216 | tf_op jit(solution)/shard_map/delta_forward/pallas_call | solution.py:488
  110.3 2.7 collective-permute-start.17
  113.0 2.4 pad_maximum_fusion.refs_8_
  116.7 5.0 %collective-permute-done.17.refs_2_ = bf16[256,256]{1,0:T(8,128)(2,1)S(1)} collective-permute-done((bf16[256,256]{1,0:T(8,128)(2,1)S(1)}, bf16[256,256]{1,0:T(8,128)(2,1)S(1)}, u32[]{:S(2)}, u32[]{:S(2)}) %collective-permute-start.17) | collective-permute-done | bytes 131104 | tf_op jit(solution)/shard_map/ppermute | solution.py:780
  121.6 3.3 collective-permute-done.18.refs_3_
  124.9 1.6 copy-done.5
  127.4 1.3 collective-permute-start.19
  129.1 1.5 collective-permute-start.25
  131.8 6.9 %collective-permute-done.23 = bf16[2,96,1024]{2,1,0:T(8,128)(2,1)S(1)} collective-permute-done((bf16[2,96,1024]{2,1,0:T(8,128)(2,1)}, bf16[2,96,1024]{2,1,0:T(8,128)(2,1)S(1)}, u32[]{:S(2)}, u32[]{:S(2)}) %collective-permute-start.23) | collective-permute-done | bytes 393248 | tf_op jit(solution)/shard_map/ppermute | solution.py:780
  138.7 3.2 collective-permute-start.20
  141.9 20.2 %collective-permute-done.24 = bf16[2,96,1024]{2,1,0:T(8,128)(2,1)S(1)} collective-permute-done((bf16[2,96,1024]{2,1,0:T(8,128)(2,1)}, bf16[2,96,1024]{2,1,0:T(8,128)(2,1)S(1)}, u32[]{:S(2)}, u32[]{:S(2)}) %collective-permute-start.24) | collective-permute-done | bytes 393248 | tf_op jit(solution)/shard_map/ppermute | solution.py:780
  162.1 2.0 collective-permute-done.25
  165.5 14.3 %ffn_units.1 = (bf16[1024,768]{1,0:T(8,128)(2,1)}, bf16[1024,1536]{1,0:T(8,128)(2,1)}, bf16[512,1024]{1,0:T(8,128)(2,1)}, f32[256,1024]{1,0:T(8,128)}, f32[256,1024]{1,0:T(8,128)}) custom-call(s32[2]{0:T(128)S(1)} %pad_add_fusion.1.block_ref, bf16[256,1024]{1,0:T(8,128)(2,1)S(1)} %get-tuple-element.150.refs_0_, ...), custom_call_target="tpu_custom_call" | custom-call | flops 8000000000 | bytes 16777216 | tf_op jit(solution)/shard_map/ffn_units/pallas_call | solution.py:671
  182.3 3.0 convolution_convert_fusion
  185.3 1.3 add_convert_fusion
  186.9 4.6 %fusion.8 = bf16[768,1024]{1,0:T(8,128)(2,1)} fusion(bf16[1024,768]{1,0:T(8,128)(2,1)S(1)} %copy-done.33, bf16[256,1024]{1,0:T(8,128)(2,1)} %collective-permute-done.10.refs_7_, bf16[256,1024]{1,0:T(8,128)(2,1)} %collective-permute-done.8.refs_6_, bf16[256,1024]{1,0:T(8,128)(2,1)} %collective-permute-done.9.refs_5_, bf16[256,1024]{1,0:T(8,128)(2,1)} %refs_4_.2), kind=kOutput, calls=%fused_computation.12 | convolution fusion | flops 1619787776 | bytes 5242880 | tf_op jit(solution)/shard_map/dot_general | solution.py:772
  191.5 10.6 %reduce-scatter.6.cloned.1.call-start = ((), (), s32[]{:S(2)}) async-start(), calls=%async_computation.6 | async-start | bytes 2359296 | tf_op jit(solution)/shard_map/reduce_scatter | solution.py:1034
  202.1 1.3 collective-permute-start.28
  203.7 13.0 %collective-permute-done.27.refs_2_ = bf16[256,1024]{1,0:T(8,128)(2,1)S(1)} collective-permute-done((bf16[256,1024]{1,0:T(8,128)(2,1)S(1)}, bf16[256,1024]{1,0:T(8,128)(2,1)S(1)}, u32[]{:S(2)}, u32[]{:S(2)}) %collective-permute-start.27) | collective-permute-done | bytes 524320 | tf_op jit(solution)/shard_map/ppermute | solution.py:776
  217.5 5.8 %mix_back.1 = (bf16[256,256]{1,0:T(8,128)(2,1)}, bf16[256,256]{1,0:T(8,128)(2,1)}, bf16[256,256]{1,0:T(8,128)(2,1)}, bf16[256,256]{1,0:T(8,128)(2,1)}, f32[256,1...) custom-call(s32[1]{0:T(128)} %bitcast.1.refs_11_.z_ref, f32[256,1024]{1,0:T(8,128)} %get-tuple-element.168.refs_0_, ...), custom_call_target="tpu_custom_call" | custom-call | flops 2000000000 | bytes 6291456 | tf_op jit(solution)/shard_map/mix_back/pallas_call | solution.py:728
  223.4 2.1 collective-permute-start.30
  225.5 1.4 collective-permute-start.31
  226.9 3.1 convolution_convert_fusion.1
  230.1 4.1 %fusion.18 = f32[512,1536]{1,0:T(8,128)S(1)} fusion(bf16[1024,1536]{1,0:T(8,128)(2,1)} %get-tuple-element.162, bf16[1024,1024]{1,0:T(8,128)(2,1)} %copy-done.32, s32[]{:T(128)S(6)} %select_n.142), kind=kOutput, calls=%fused_computation.29 | convolution fusion | flops 1610612736 | bytes 7340036 | tf_op jit(solution)/shard_map/dot_general | solution.py:772
  234.1 4.3 %collective-permute-done.28 = bf16[4,128,1536]{2,1,0:T(8,128)(2,1)} collective-permute-done((bf16[4,128,1536]{2,1,0:T(8,128)(2,1)}, bf16[4,128,1536]{2,1,0:T(8,128)(2,1)}, u32[]{:S(2)}, u32[]{:S(2)}) %collective-permute-start.28) | collective-permute-done | bytes 1572896 | tf_op jit(solution)/shard_map/ppermute | solution.py:776
  238.5 2.0 convert_add_fusion
  241.0 1.4 copy-done.9
  242.6 2.1 collective-permute-start.33
  244.7 1.4 collective-permute-start.34
  246.1 44.8 %delta_backward.1 = (bf16[1024,1152]{1,0:T(8,128)(2,1)}, bf16[256,1024]{1,0:T(8,128)(2,1)S(1)}, bf16[256,1024]{1,0:T(8,128)(2,1)S(1)}, bf16[256,1024]{1,0:T(8,128)(2,1)}, bf16[256,1024]{1,0:T(8,128)(2,1)}) custom-call(bf16[256,256]{1,0:T(8,128)(2,1)S(1)} %copy-done.6, bf16[256,256]{1,0:T(8,128)(2,1)S(1)} %collective-permute-done.29.refs_1_, ...), custom_call_target="tpu_custom_call" | custom-call | flops 40000000000 | bytes 16777216 | tf_op jit(solution)/shard_map/delta_backward/pallas_call | solution.py:514
  292.5 2.1 collective-permute-start.36
  294.9 3.2 convolution_convert_fusion.2
  298.1 2.1 collective-permute-start.38
  300.1 1.4 convert_add_fusion.1
  301.9 1.4 collective-permute-done.43
  303.3 6.4 %collective-permute-done.44 = f32[32,1536]{1,0:T(8,128)S(1)} collective-permute-done((f32[32,1536]{1,0:T(8,128)S(1)}, f32[32,1536]{1,0:T(8,128)S(1)}, u32[]{:S(2)}, u32[]{:S(2)}) %collective-permute-start.44) | collective-permute-done | bytes 196640 | tf_op jit(solution)/shard_map/ppermute | solution.py:776
  310.5 6.6 %collective-permute-done.45 = f32[32,1536]{1,0:T(8,128)S(1)} collective-permute-done((f32[32,1536]{1,0:T(8,128)S(1)}, f32[32,1536]{1,0:T(8,128)S(1)}, u32[]{:S(2)}, u32[]{:S(2)}) %collective-permute-start.45) | collective-permute-done | bytes 196640 | tf_op jit(solution)/shard_map/ppermute | solution.py:776
  319.1 2.2 reshape.284
  321.3 2.6 fusion.14
  326.1 1.5 reshape.286
  329.0 1.8 add_bitcast_fusion
  330.8 6.1 %collective-permute-done.39 = bf16[256,1024]{1,0:T(8,128)(2,1)} collective-permute-done((bf16[256,1024]{1,0:T(8,128)(2,1)}, bf16[256,1024]{1,0:T(8,128)(2,1)}, u32[]{:S(2)}, u32[]{:S(2)}) %collective-permute-start.39) | collective-permute-done | bytes 524320 | tf_op jit(solution)/shard_map/ppermute | solution.py:776
  336.9 3.3 fusion.13
  340.2 2.6 reduce-scatter.8.cloned.1.call-done
  345.8 2.1 collective-permute-start.41
  348.1 1.9 fusion.15
  350.0 2.8 fusion.17
  352.9 4.4 %collective-permute-done.41 = bf16[1,32,2176]{2,1,0:T(8,128)(2,1)S(1)} collective-permute-done((bf16[1,32,2176]{2,1,0:T(8,128)(2,1)S(1)}, bf16[1,32,2176]{2,1,0:T(8,128)(2,1)S(1)}, u32[]{:S(2)}, u32[]{:S(2)}) %collective-permute-start.41) | collective-permute-done | bytes 139296 | tf_op jit(solution)/shard_map/ppermute | solution.py:780
  357.3 2.3 collective-permute-done.42
  360.2 2.0 finish_inputs.1
  362.2 1.4 copy.138
  363.6 1.3 reshape.283
  (233 shorter events, 50.0 us)
Async XLA Ops:
  7.2 27.9 %copy-start = (bf16[256,1024]{1,0:T(8,128)(2,1)S(1)}, bf16[256,1024]{1,0:T(8,128)(2,1)}, u32[]{:S(2)}) copy-start(bf16[256,1024]{1,0:T(8,128)(2,1)} %refs_5_.1) | copy-start | bytes 1572868
  7.2 28.5 %copy-start.34 = (s32[1,1024]{1,0:T(1,128)S(1)}, s32[1,1024]{1,0:T(1,128)}, u32[]{:S(2)}) copy-start(s32[1,1024]{1,0:T(1,128)} %param.19) | copy-start | bytes 12292
  7.2 28.7 %copy-start.35 = (s32[1,4]{1,0:T(1,128)S(1)}, s32[1,4]{1,0:T(1,128)}, u32[]{:S(2)}) copy-start(s32[1,4]{1,0:T(1,128)} %param.18) | copy-start | bytes 52
  7.2 68.5 %all-gather.3.cloned.1.call-start = ((), (), s32[]{:S(2)}) async-start(), calls=%async_computation.3 | async-start | bytes 2654208 | tf_op jit(solution)/shard_map/all_gather | solution.py:903
  7.3 26.9 %collective-permute-start.3 = (bf16[256,1024]{1,0:T(8,128)(2,1)}, bf16[256,1024]{1,0:T(8,128)(2,1)S(1)}, u32[]{:S(2)}, u32[]{:S(2)}) collective-permute-start(bf16[256,1024]{1,0:T(8,128)(2,1)} %refs_5_.1), channel_id=1, source_target_pairs={{0,1},{1,2},{2,3},{3,0},{4,5},{5,6},{6,7},{7,4},{8,9},{9,10},{10,1... | collective-permute-start | bytes 1572872 | tf_op jit(solution)/shard_map/ppermute | solution.py:780
  15.9 22.9 %copy-start.26 = (bf16[32,2816]{1,0:T(8,128)(2,1)S(1)}, bf16[32,2816]{1,0:T(8,128)(2,1)}, u32[]{:S(2)}) copy-start(bf16[32,2816]{1,0:T(8,128)(2,1)} %param.30) | copy-start | bytes 540676
  16.0 7.3 %collective-permute-start = (bf16[1,32,2176]{2,1,0:T(8,128)(2,1)S(1)}, bf16[1,32,2176]{2,1,0:T(8,128)(2,1)S(1)}, u32[]{:S(2)}, u32[]{:S(2)}) collective-permute-start(bf16[1,32,2176]{2,1,0:T(8,128)(2,1)S(1)} %get-tuple-element.326), channel_id=1, source_target_pairs={{0,1},{1,2},{2,3},{3,0},{4,5},{5,6},{6,7},{7,4},{8,9},{9,10},{10,1... | collective-permute-start | bytes 417800 | tf_op jit(solution)/shard_map/ppermute | solution.py:780
  17.3 14.0 %collective-permute-start.1 = (bf16[1,32,2176]{2,1,0:T(8,128)(2,1)S(1)}, bf16[1,32,2176]{2,1,0:T(8,128)(2,1)S(1)}, u32[]{:S(2)}, u32[]{:S(2)}) collective-permute-start(bf16[1,32,2176]{2,1,0:T(8,128)(2,1)S(1)} %get-tuple-element.325), channel_id=1, source_target_pairs={{0,2},{1,3},{2,0},{3,1},{4,6},{5,7},{6,4},{7,5},{8,10},{9,11},{10,... | collective-permute-start | bytes 417800 | tf_op jit(solution)/shard_map/ppermute | solution.py:780
  18.3 15.9 %collective-permute-start.2 = (bf16[1,32,2176]{2,1,0:T(8,128)(2,1)S(1)}, bf16[1,32,2176]{2,1,0:T(8,128)(2,1)S(1)}, u32[]{:S(2)}, u32[]{:S(2)}) collective-permute-start(bf16[1,32,2176]{2,1,0:T(8,128)(2,1)S(1)} %get-tuple-element.324), channel_id=1, source_target_pairs={{0,3},{1,0},{2,1},{3,2},{4,7},{5,4},{6,5},{7,6},{8,11},{9,8},{10,9... | collective-permute-start | bytes 417800 | tf_op jit(solution)/shard_map/ppermute | solution.py:780
  34.2 5.6 %copy-start.36 = (bf16[256,1024]{1,0:T(8,128)(2,1)}, bf16[256,1024]{1,0:T(8,128)(2,1)S(1)}, u32[]{:S(2)}) copy-start(bf16[256,1024]{1,0:T(8,128)(2,1)S(1)} %collective-permute-done.3.refs_1_) | copy-start | bytes 1572868
  35.1 81.6 %all-gather.5.cloned.1.call-start = ((), (), s32[]{:S(2)}) async-start(), calls=%async_computation.4 | async-start | bytes 2359296 | tf_op jit(solution)/shard_map/all_gather | solution.py:904
  35.1 34.3 %collective-permute-start.11 = (bf16[256,1024]{1,0:T(8,128)(2,1)S(1)}, bf16[256,1024]{1,0:T(8,128)(2,1)}, u32[]{:S(2)}, u32[]{:S(2)}) collective-permute-start(bf16[256,1024]{1,0:T(8,128)(2,1)S(1)} %copy-done), channel_id=1, source_target_pairs={{0,2},{1,3},{2,0},{3,1},{4,6},{5,7},{6,4},{7,5},{8,10},{9,11},{10,... | collective-permute-start | bytes 1572872 | tf_op jit(solution)/shard_map/ppermute | solution.py:780
  35.5 34.0 %collective-permute-start.12 = (bf16[256,1024]{1,0:T(8,128)(2,1)S(1)}, bf16[256,1024]{1,0:T(8,128)(2,1)}, u32[]{:S(2)}, u32[]{:S(2)}) collective-permute-start(bf16[256,1024]{1,0:T(8,128)(2,1)S(1)} %copy-done), channel_id=1, source_target_pairs={{0,3},{1,0},{2,1},{3,2},{4,7},{5,4},{6,5},{7,6},{8,11},{9,8},{10,9... | collective-permute-start | bytes 1572872 | tf_op jit(solution)/shard_map/ppermute | solution.py:780
  40.8 5.1 %collective-permute-start.4 = (bf16[32,1536]{1,0:T(8,128)(2,1)S(1)}, bf16[32,1536]{1,0:T(8,128)(2,1)S(1)}, u32[]{:S(2)}, u32[]{:S(2)}) collective-permute-start(bf16[32,1536]{1,0:T(8,128)(2,1)S(1)} %get-tuple-element.330), channel_id=1, source_target_pairs={{0,4},{4,0},{8,12},{12,8},{16,20},{20,16},{24,28},{28,24},{1,5},{5... | collective-permute-start | bytes 294920 | tf_op jit(solution)/shard_map/ppermute | solution.py:776
  42.5 6.0 %collective-permute-start.5 = (bf16[32,1536]{1,0:T(8,128)(2,1)S(1)}, bf16[32,1536]{1,0:T(8,128)(2,1)S(1)}, u32[]{:S(2)}, u32[]{:S(2)}) collective-permute-start(bf16[32,1536]{1,0:T(8,128)(2,1)S(1)} %get-tuple-element.329), channel_id=1, source_target_pairs={{0,8},{4,12},{8,0},{12,4},{16,24},{20,28},{24,16},{28,20},{1,9},{5... | collective-permute-start | bytes 294920 | tf_op jit(solution)/shard_map/ppermute | solution.py:776
  43.8 8.9 %collective-permute-start.6 = (bf16[32,1536]{1,0:T(8,128)(2,1)S(1)}, bf16[32,1536]{1,0:T(8,128)(2,1)S(1)}, u32[]{:S(2)}, u32[]{:S(2)}) collective-permute-start(bf16[32,1536]{1,0:T(8,128)(2,1)S(1)} %get-tuple-element.328), channel_id=1, source_target_pairs={{0,12},{4,8},{8,4},{12,0},{16,28},{20,24},{24,20},{28,16},{1,13},{... | collective-permute-start | bytes 294920 | tf_op jit(solution)/shard_map/ppermute | solution.py:776
  45.9 6.9 %collective-permute-start.7 = (bf16[96,1024]{1,0:T(8,128)(2,1)S(1)}, bf16[96,1024]{1,0:T(8,128)(2,1)S(1)}, u32[]{:S(2)}, u32[]{:S(2)}) collective-permute-start(bf16[96,1024]{1,0:T(8,128)(2,1)S(1)} %get-tuple-element.331), channel_id=1, source_target_pairs={{0,16},{4,20},{8,24},{12,28},{16,0},{20,4},{24,8},{28,12},{1,17},{... | collective-permute-start | bytes 589832 | tf_op jit(solution)/shard_map/ppermute | solution.py:776
  53.5 20.8 %collective-permute-start.9 = (bf16[256,1024]{1,0:T(8,128)(2,1)}, bf16[256,1024]{1,0:T(8,128)(2,1)}, u32[]{:S(2)}, u32[]{:S(2)}) collective-permute-start(bf16[256,1024]{1,0:T(8,128)(2,1)} %refs_4_.2), channel_id=1, source_target_pairs={{0,8},{4,12},{8,0},{12,4},{16,24},{20,28},{24,16},{28,20},{1,9},{5... | collective-permute-start | bytes 1572872 | tf_op jit(solution)/shard_map/ppermute | solution.py:776
  55.5 237.0 %reduce-scatter.4.cloned.1.call-start = ((), (), s32[]{:S(2)}) async-start(), calls=%async_computation.5 | async-start | bytes 1966080 | tf_op jit(solution)/shard_map/reduce_scatter | solution.py:1018
  56.8 52.5 %collective-permute-start.8 = (bf16[256,1024]{1,0:T(8,128)(2,1)}, bf16[256,1024]{1,0:T(8,128)(2,1)}, u32[]{:S(2)}, u32[]{:S(2)}) collective-permute-start(bf16[256,1024]{1,0:T(8,128)(2,1)} %refs_4_.2), channel_id=1, source_target_pairs={{0,4},{4,0},{8,12},{12,8},{16,20},{20,16},{24,28},{28,24},{1,5},{5... | collective-permute-start | bytes 1572872 | tf_op jit(solution)/shard_map/ppermute | solution.py:776
  69.5 39.8 %collective-permute-start.13 = (bf16[4,32,1536]{2,1,0:T(8,128)(2,1)S(1)}, bf16[4,32,1536]{2,1,0:T(8,128)(2,1)S(1)}, u32[]{:S(2)}, u32[]{:S(2)}) collective-permute-start(bf16[4,32,1536]{2,1,0:T(8,128)(2,1)S(1)} %bitcast.165), channel_id=1, source_target_pairs={{0,1},{1,2},{2,3},{3,0},{4,5},{5,6},{6,7},{7,4},{8,9},{9,10},{10,1... | collective-permute-start | bytes 1179656 | tf_op jit(solution)/shard_map/ppermute | solution.py:780
  69.5 39.8 %collective-permute-start.14 = (bf16[4,32,1536]{2,1,0:T(8,128)(2,1)S(1)}, bf16[4,32,1536]{2,1,0:T(8,128)(2,1)S(1)}, u32[]{:S(2)}, u32[]{:S(2)}) collective-permute-start(bf16[4,32,1536]{2,1,0:T(8,128)(2,1)S(1)} %bitcast.166), channel_id=1, source_target_pairs={{0,2},{1,3},{2,0},{3,1},{4,6},{5,7},{6,4},{7,5},{8,10},{9,11},{10,... | collective-permute-start | bytes 1179656 | tf_op jit(solution)/shard_map/ppermute | solution.py:780
  72.7 36.6 %collective-permute-start.15 = (bf16[4,32,1536]{2,1,0:T(8,128)(2,1)S(1)}, bf16[4,32,1536]{2,1,0:T(8,128)(2,1)S(1)}, u32[]{:S(2)}, u32[]{:S(2)}) collective-permute-start(bf16[4,32,1536]{2,1,0:T(8,128)(2,1)S(1)} %bitcast.167), channel_id=1, source_target_pairs={{0,3},{1,0},{2,1},{3,2},{4,7},{5,4},{6,5},{7,6},{8,11},{9,8},{10,9... | collective-permute-start | bytes 1179656 | tf_op jit(solution)/shard_map/ppermute | solution.py:780
  74.4 35.7 %collective-permute-start.10 = (bf16[256,1024]{1,0:T(8,128)(2,1)}, bf16[256,1024]{1,0:T(8,128)(2,1)}, u32[]{:S(2)}, u32[]{:S(2)}) collective-permute-start(bf16[256,1024]{1,0:T(8,128)(2,1)} %collective-permute-done.9.refs_5_), channel_id=1, source_target_pairs={{0,4},{4,0},{8,12},{12,8},{16,20},{20,16},{24,28},{28,24},{1,5},{5... | collective-permute-start | bytes 1572872 | tf_op jit(solution)/shard_map/ppermute | solution.py:776
  109.2 94.4 %copy-start.4 = (f32[128,1024]{1,0:T(8,128)}, f32[128,1024]{1,0:T(8,128)S(1)}, u32[]{:S(2)}) copy-start(f32[128,1024]{1,0:T(8,128)S(1)} %get-tuple-element.149.refs_6_) | copy-start | bytes 1572868
  109.2 15.7 %copy-start.1 = (bf16[256,1024]{1,0:T(8,128)(2,1)S(1)}, bf16[256,1024]{1,0:T(8,128)(2,1)}, u32[]{:S(2)}) copy-start(bf16[256,1024]{1,0:T(8,128)(2,1)} %refs_5_.1) | copy-start | bytes 1572868
  110.0 6.6 %collective-permute-start.16 = (bf16[256,256]{1,0:T(8,128)(2,1)S(1)}, bf16[256,256]{1,0:T(8,128)(2,1)S(1)}, u32[]{:S(2)}, u32[]{:S(2)}) collective-permute-start(bf16[256,256]{1,0:T(8,128)(2,1)S(1)} %get-tuple-element.146), channel_id=1, source_target_pairs={{0,1},{1,2},{2,3},{3,0},{4,5},{5,6},{6,7},{7,4},{8,9},{9,10},{10,1... | collective-permute-start | bytes 393224 | tf_op jit(solution)/shard_map/ppermute | solution.py:780
  110.3 11.3 %collective-permute-start.17 = (bf16[256,256]{1,0:T(8,128)(2,1)S(1)}, bf16[256,256]{1,0:T(8,128)(2,1)S(1)}, u32[]{:S(2)}, u32[]{:S(2)}) collective-permute-start(bf16[256,256]{1,0:T(8,128)(2,1)S(1)} %get-tuple-element.147), channel_id=1, source_target_pairs={{0,2},{1,3},{2,0},{3,1},{4,6},{5,7},{6,4},{7,5},{8,10},{9,11},{10,... | collective-permute-start | bytes 393224 | tf_op jit(solution)/shard_map/ppermute | solution.py:780
  113.0 11.9 %collective-permute-start.18 = (bf16[256,256]{1,0:T(8,128)(2,1)S(1)}, bf16[256,256]{1,0:T(8,128)(2,1)S(1)}, u32[]{:S(2)}, u32[]{:S(2)}) collective-permute-start(bf16[256,256]{1,0:T(8,128)(2,1)S(1)} %get-tuple-element.148), channel_id=1, source_target_pairs={{0,3},{1,0},{2,1},{3,2},{4,7},{5,4},{6,5},{7,6},{8,11},{9,8},{10,9... | collective-permute-start | bytes 393224 | tf_op jit(solution)/shard_map/ppermute | solution.py:780
  115.4 48.8 %collective-permute-start.22 = (bf16[4,128,1536]{2,1,0:T(8,128)(2,1)}, bf16[4,128,1536]{2,1,0:T(8,128)(2,1)}, u32[]{:S(2)}, u32[]{:S(2)}) collective-permute-start(bf16[4,128,1536]{2,1,0:T(8,128)(2,1)} %pad_maximum_fusion.refs_8_), channel_id=1, source_target_pairs={{0,16},{4,20},{8,24},{12,28},{16,0},{20,4},{24,8},{28,12},{1,17},{... | collective-permute-start | bytes 4718600 | tf_op jit(solution)/shard_map/ppermute | solution.py:776
  127.4 36.8 %copy-start.2 = (f32[256,1024]{1,0:T(8,128)}, f32[256,1024]{1,0:T(8,128)S(1)}, u32[]{:S(2)}) copy-start(f32[256,1024]{1,0:T(8,128)S(1)} %get-tuple-element.170.refs_3_) | copy-start | bytes 3145732
  127.4 14.5 %collective-permute-start.19 = (bf16[256,1024]{1,0:T(8,128)(2,1)S(1)}, bf16[256,1024]{1,0:T(8,128)(2,1)S(1)}, u32[]{:S(2)}, u32[]{:S(2)}) collective-permute-start(bf16[256,1024]{1,0:T(8,128)(2,1)S(1)} %get-tuple-element.150.refs_0_), channel_id=1, source_target_pairs={{0,8},{4,12},{8,0},{12,4},{16,24},{20,28},{24,16},{28,20},{1,9},{5... | collective-permute-start | bytes 1572872 | tf_op jit(solution)/shard_map/ppermute | solution.py:776
  128.7 10.0 %collective-permute-start.23 = (bf16[2,96,1024]{2,1,0:T(8,128)(2,1)}, bf16[2,96,1024]{2,1,0:T(8,128)(2,1)S(1)}, u32[]{:S(2)}, u32[]{:S(2)}) collective-permute-start(bf16[2,96,1024]{2,1,0:T(8,128)(2,1)} %bitcast.19), channel_id=1, source_target_pairs={{0,1},{1,2},{2,3},{3,0},{4,5},{5,6},{6,7},{7,4},{8,9},{9,10},{10,1... | collective-permute-start | bytes 1179656 | tf_op jit(solution)/shard_map/ppermute | solution.py:780
  128.8 33.3 %collective-permute-start.24 = (bf16[2,96,1024]{2,1,0:T(8,128)(2,1)}, bf16[2,96,1024]{2,1,0:T(8,128)(2,1)S(1)}, u32[]{:S(2)}, u32[]{:S(2)}) collective-permute-start(bf16[2,96,1024]{2,1,0:T(8,128)(2,1)} %bitcast.19), channel_id=1, source_target_pairs={{0,2},{1,3},{2,0},{3,1},{4,6},{5,7},{6,4},{7,5},{8,10},{9,11},{10,... | collective-permute-start | bytes 1179656 | tf_op jit(solution)/shard_map/ppermute | solution.py:780
  129.1 35.0 %collective-permute-start.25 = (bf16[2,96,1024]{2,1,0:T(8,128)(2,1)}, bf16[2,96,1024]{2,1,0:T(8,128)(2,1)S(1)}, u32[]{:S(2)}, u32[]{:S(2)}) collective-permute-start(bf16[2,96,1024]{2,1,0:T(8,128)(2,1)} %bitcast.19), channel_id=1, source_target_pairs={{0,3},{1,0},{2,1},{3,2},{4,7},{5,4},{6,5},{7,6},{8,11},{9,8},{10,9... | collective-permute-start | bytes 1179656 | tf_op jit(solution)/shard_map/ppermute | solution.py:780
  138.7 25.5 %collective-permute-start.20 = (bf16[256,1024]{1,0:T(8,128)(2,1)S(1)}, bf16[256,1024]{1,0:T(8,128)(2,1)S(1)}, u32[]{:S(2)}, u32[]{:S(2)}) collective-permute-start(bf16[256,1024]{1,0:T(8,128)(2,1)S(1)} %get-tuple-element.150.refs_0_), channel_id=1, source_target_pairs={{0,4},{4,0},{8,12},{12,8},{16,20},{20,16},{24,28},{28,24},{1,5},{5... | collective-permute-start | bytes 1572872 | tf_op jit(solution)/shard_map/ppermute | solution.py:776
  141.9 22.3 %collective-permute-start.21 = (bf16[256,1024]{1,0:T(8,128)(2,1)S(1)}, bf16[256,1024]{1,0:T(8,128)(2,1)S(1)}, u32[]{:S(2)}, u32[]{:S(2)}) collective-permute-start(bf16[256,1024]{1,0:T(8,128)(2,1)S(1)} %collective-permute-done.19.refs_1_), channel_id=1, source_target_pairs={{0,4},{4,0},{8,12},{12,8},{16,20},{20,16},{24,28},{28,24},{1,5},{5... | collective-permute-start | bytes 1572872 | tf_op jit(solution)/shard_map/ppermute | solution.py:776
  179.8 5.6 %collective-permute-start.26 = (bf16[512,1024]{1,0:T(8,128)(2,1)}, bf16[512,1024]{1,0:T(8,128)(2,1)}, u32[]{:S(2)}, u32[]{:S(2)}) collective-permute-start(bf16[512,1024]{1,0:T(8,128)(2,1)} %get-tuple-element.161), channel_id=1, source_target_pairs={{0,4},{4,0},{8,12},{12,8},{16,20},{20,16},{24,28},{28,24},{1,5},{5... | collective-permute-start | bytes 3145736 | tf_op jit(solution)/shard_map/ppermute | solution.py:776
  191.5 100.9 %reduce-scatter.6.cloned.1.call-start = ((), (), s32[]{:S(2)}) async-start(), calls=%async_computation.6 | async-start | bytes 2359296 | tf_op jit(solution)/shard_map/reduce_scatter | solution.py:1034
  202.1 36.4 %collective-permute-start.28 = (bf16[4,128,1536]{2,1,0:T(8,128)(2,1)}, bf16[4,128,1536]{2,1,0:T(8,128)(2,1)}, u32[]{:S(2)}, u32[]{:S(2)}) collective-permute-start(bf16[4,128,1536]{2,1,0:T(8,128)(2,1)} %bitcast.192), channel_id=1, source_target_pairs={{0,16},{4,20},{8,24},{12,28},{16,0},{20,4},{24,8},{28,12},{1,17},{... | collective-permute-start | bytes 4718600 | tf_op jit(solution)/shard_map/ppermute | solution.py:776
  203.4 13.3 %collective-permute-start.27 = (bf16[256,1024]{1,0:T(8,128)(2,1)S(1)}, bf16[256,1024]{1,0:T(8,128)(2,1)S(1)}, u32[]{:S(2)}, u32[]{:S(2)}) collective-permute-start(bf16[256,1024]{1,0:T(8,128)(2,1)S(1)} %add_convert_fusion), channel_id=1, source_target_pairs={{0,8},{4,12},{8,0},{12,4},{16,24},{20,28},{24,16},{28,20},{1,9},{5... | collective-permute-start | bytes 1572872 | tf_op jit(solution)/shard_map/ppermute | solution.py:776
  223.3 17.5 %collective-permute-start.29 = (bf16[256,256]{1,0:T(8,128)(2,1)}, bf16[256,256]{1,0:T(8,128)(2,1)S(1)}, u32[]{:S(2)}, u32[]{:S(2)}) collective-permute-start(bf16[256,256]{1,0:T(8,128)(2,1)} %get-tuple-element.172), channel_id=1, source_target_pairs={{0,1},{1,2},{2,3},{3,0},{4,5},{5,6},{6,7},{7,4},{8,9},{9,10},{10,1... | collective-permute-start | bytes 393224 | tf_op jit(solution)/shard_map/ppermute | solution.py:780
  223.4 17.5 %collective-permute-start.30 = (bf16[256,256]{1,0:T(8,128)(2,1)}, bf16[256,256]{1,0:T(8,128)(2,1)S(1)}, u32[]{:S(2)}, u32[]{:S(2)}) collective-permute-start(bf16[256,256]{1,0:T(8,128)(2,1)} %get-tuple-element.173), channel_id=1, source_target_pairs={{0,2},{1,3},{2,0},{3,1},{4,6},{5,7},{6,4},{7,5},{8,10},{9,11},{10,... | collective-permute-start | bytes 393224 | tf_op jit(solution)/shard_map/ppermute | solution.py:780
  225.5 15.3 %collective-permute-start.31 = (bf16[256,256]{1,0:T(8,128)(2,1)}, bf16[256,256]{1,0:T(8,128)(2,1)S(1)}, u32[]{:S(2)}, u32[]{:S(2)}) collective-permute-start(bf16[256,256]{1,0:T(8,128)(2,1)} %get-tuple-element.174), channel_id=1, source_target_pairs={{0,3},{1,0},{2,1},{3,2},{4,7},{5,4},{6,5},{7,6},{8,11},{9,8},{10,9... | collective-permute-start | bytes 393224 | tf_op jit(solution)/shard_map/ppermute | solution.py:780
  230.0 112.7 %reduce-scatter.8.cloned.1.call-start = ((), (), s32[]{:S(2)}) async-start(), calls=%async_computation.7 | async-start | bytes 2654208 | tf_op jit(solution)/shard_map/reduce_scatter | solution.py:1043
  242.5 48.4 %collective-permute-start.32 = (bf16[1,4,32,1536]{3,2,1,0:T(8,128)(2,1)S(1)}, bf16[1,4,32,1536]{3,2,1,0:T(8,128)(2,1)S(1)}, u32[]{:S(2)}, u32[]{:S(2)}) collective-permute-start(bf16[1,4,32,1536]{3,2,1,0:T(8,128)(2,1)S(1)} %get-tuple-element.314), channel_id=1, source_target_pairs={{0,1},{1,2},{2,3},{3,0},{4,5},{5,6},{6,7},{7,4},{8,9},{9,10},{10,1... | collective-permute-start | bytes 1179656 | tf_op jit(solution)/shard_map/ppermute | solution.py:780
  242.6 48.4 %collective-permute-start.33 = (bf16[1,4,32,1536]{3,2,1,0:T(8,128)(2,1)S(1)}, bf16[1,4,32,1536]{3,2,1,0:T(8,128)(2,1)S(1)}, u32[]{:S(2)}, u32[]{:S(2)}) collective-permute-start(bf16[1,4,32,1536]{3,2,1,0:T(8,128)(2,1)S(1)} %get-tuple-element.313), channel_id=1, source_target_pairs={{0,2},{1,3},{2,0},{3,1},{4,6},{5,7},{6,4},{7,5},{8,10},{9,11},{10,... | collective-permute-start | bytes 1179656 | tf_op jit(solution)/shard_map/ppermute | solution.py:780
  244.7 47.7 %collective-permute-start.34 = (bf16[1,4,32,1536]{3,2,1,0:T(8,128)(2,1)S(1)}, bf16[1,4,32,1536]{3,2,1,0:T(8,128)(2,1)}, u32[]{:S(2)}, u32[]{:S(2)}) collective-permute-start(bf16[1,4,32,1536]{3,2,1,0:T(8,128)(2,1)S(1)} %get-tuple-element.312), channel_id=1, source_target_pairs={{0,3},{1,0},{2,1},{3,2},{4,7},{5,4},{6,5},{7,6},{8,11},{9,8},{10,9... | collective-permute-start | bytes 1179656 | tf_op jit(solution)/shard_map/ppermute | solution.py:780
  292.4 52.0 %collective-permute-start.35 = (bf16[256,1024]{1,0:T(8,128)(2,1)S(1)}, bf16[256,1024]{1,0:T(8,128)(2,1)}, u32[]{:S(2)}, u32[]{:S(2)}) collective-permute-start(bf16[256,1024]{1,0:T(8,128)(2,1)S(1)} %get-tuple-element.206), channel_id=1, source_target_pairs={{0,1},{1,2},{2,3},{3,0},{4,5},{5,6},{6,7},{7,4},{8,9},{9,10},{10,1... | collective-permute-start | bytes 1572872 | tf_op jit(solution)/shard_map/ppermute | solution.py:780
  292.5 52.0 %collective-permute-start.36 = (bf16[256,1024]{1,0:T(8,128)(2,1)}, bf16[256,1024]{1,0:T(8,128)(2,1)}, u32[]{:S(2)}, u32[]{:S(2)}) collective-permute-start(bf16[256,1024]{1,0:T(8,128)(2,1)} %get-tuple-element.207), channel_id=1, source_target_pairs={{0,2},{1,3},{2,0},{3,1},{4,6},{5,7},{6,4},{7,5},{8,10},{9,11},{10,... | collective-permute-start | bytes 1572872 | tf_op jit(solution)/shard_map/ppermute | solution.py:780
  294.6 49.9 %collective-permute-start.37 = (bf16[256,1024]{1,0:T(8,128)(2,1)}, bf16[256,1024]{1,0:T(8,128)(2,1)}, u32[]{:S(2)}, u32[]{:S(2)}) collective-permute-start(bf16[256,1024]{1,0:T(8,128)(2,1)} %get-tuple-element.208), channel_id=1, source_target_pairs={{0,3},{1,0},{2,1},{3,2},{4,7},{5,4},{6,5},{7,6},{8,11},{9,8},{10,9... | collective-permute-start | bytes 1572872 | tf_op jit(solution)/shard_map/ppermute | solution.py:780
  298.1 23.3 %collective-permute-start.38 = (bf16[512,1024]{1,0:T(8,128)(2,1)}, bf16[512,1024]{1,0:T(8,128)(2,1)}, u32[]{:S(2)}, u32[]{:S(2)}) collective-permute-start(bf16[512,1024]{1,0:T(8,128)(2,1)} %convolution_convert_fusion.2), channel_id=1, source_target_pairs={{0,4},{4,0},{8,12},{12,8},{16,20},{20,16},{24,28},{28,24},{1,5},{5... | collective-permute-start | bytes 3145736 | tf_op jit(solution)/shard_map/ppermute | solution.py:776
  301.6 1.7 collective-permute-start.43
  303.3 6.4 %collective-permute-start.44 = (f32[32,1536]{1,0:T(8,128)S(1)}, f32[32,1536]{1,0:T(8,128)S(1)}, u32[]{:S(2)}, u32[]{:S(2)}) collective-permute-start(f32[32,1536]{1,0:T(8,128)S(1)} %get-tuple-element.318), channel_id=1, source_target_pairs={{0,8},{4,12},{8,0},{12,4},{16,24},{20,28},{24,16},{28,20},{1,9},{5... | collective-permute-start | bytes 589832 | tf_op jit(solution)/shard_map/ppermute | solution.py:776
  309.7 7.4 %collective-permute-start.45 = (f32[32,1536]{1,0:T(8,128)S(1)}, f32[32,1536]{1,0:T(8,128)S(1)}, u32[]{:S(2)}, u32[]{:S(2)}) collective-permute-start(f32[32,1536]{1,0:T(8,128)S(1)} %get-tuple-element.317), channel_id=1, source_target_pairs={{0,12},{4,8},{8,4},{12,0},{16,28},{20,24},{24,20},{28,16},{1,13},{... | collective-permute-start | bytes 589832 | tf_op jit(solution)/shard_map/ppermute | solution.py:776
  317.1 11.9 %collective-permute-start.46 = (bf16[1,96,1024]{2,1,0:T(8,128)(2,1)S(1)}, bf16[1,96,1024]{2,1,0:T(8,128)(2,1)}, u32[]{:S(2)}, u32[]{:S(2)}) collective-permute-start(bf16[1,96,1024]{2,1,0:T(8,128)(2,1)S(1)} %constant_dynamic-slice_fusion), channel_id=1, source_target_pairs={{0,16},{4,20},{8,24},{12,28},{16,0},{20,4},{24,8},{28,12},{1,17},{... | collective-permute-start | bytes 589832 | tf_op jit(solution)/shard_map/ppermute | solution.py:776
  323.9 12.9 %collective-permute-start.39 = (bf16[256,1024]{1,0:T(8,128)(2,1)}, bf16[256,1024]{1,0:T(8,128)(2,1)}, u32[]{:S(2)}, u32[]{:S(2)}) collective-permute-start(bf16[256,1024]{1,0:T(8,128)(2,1)} %fusion.14), channel_id=1, source_target_pairs={{0,8},{4,12},{8,0},{12,4},{16,24},{20,28},{24,16},{28,20},{1,9},{5... | collective-permute-start | bytes 1572872 | tf_op jit(solution)/shard_map/ppermute | solution.py:776
  326.1 10.8 %copy-start.3 = (f32[256,1024]{1,0:T(8,128)S(1)}, f32[256,1024]{1,0:T(8,128)}, u32[]{:S(2)}) copy-start(f32[256,1024]{1,0:T(8,128)} %copy-done.2) | copy-start | bytes 3145732
  330.8 12.0 %copy-start.25 = (bf16[128,1024]{1,0:T(8,128)(2,1)S(1)}, bf16[128,1024]{1,0:T(8,128)(2,1)}, u32[]{:S(2)}) copy-start(bf16[128,1024]{1,0:T(8,128)(2,1)} %reduce-scatter.6.cloned.1.call-done) | copy-start | bytes 786436
  343.8 6.3 %copy-start.14 = (f32[256,1024]{1,0:T(8,128)S(1)}, f32[256,1024]{1,0:T(8,128)}, u32[]{:S(2)}) copy-start(f32[256,1024]{1,0:T(8,128)} %get-tuple-element.213) | copy-start | bytes 3145732
  344.5 8.4 %collective-permute-start.40 = (bf16[1,32,2176]{2,1,0:T(8,128)(2,1)S(1)}, bf16[1,32,2176]{2,1,0:T(8,128)(2,1)S(1)}, u32[]{:S(2)}, u32[]{:S(2)}) collective-permute-start(bf16[1,32,2176]{2,1,0:T(8,128)(2,1)S(1)} %get-tuple-element.322), channel_id=1, source_target_pairs={{0,1},{1,2},{2,3},{3,0},{4,5},{5,6},{6,7},{7,4},{8,9},{9,10},{10,1... | collective-permute-start | bytes 417800 | tf_op jit(solution)/shard_map/ppermute | solution.py:780
  345.8 11.5 %collective-permute-start.41 = (bf16[1,32,2176]{2,1,0:T(8,128)(2,1)S(1)}, bf16[1,32,2176]{2,1,0:T(8,128)(2,1)S(1)}, u32[]{:S(2)}, u32[]{:S(2)}) collective-permute-start(bf16[1,32,2176]{2,1,0:T(8,128)(2,1)S(1)} %get-tuple-element.321), channel_id=1, source_target_pairs={{0,2},{1,3},{2,0},{3,1},{4,6},{5,7},{6,4},{7,5},{8,10},{9,11},{10,... | collective-permute-start | bytes 417800 | tf_op jit(solution)/shard_map/ppermute | solution.py:780
  347.8 11.7 %collective-permute-start.42 = (bf16[1,32,2176]{2,1,0:T(8,128)(2,1)S(1)}, bf16[1,32,2176]{2,1,0:T(8,128)(2,1)S(1)}, u32[]{:S(2)}, u32[]{:S(2)}) collective-permute-start(bf16[1,32,2176]{2,1,0:T(8,128)(2,1)S(1)} %get-tuple-element.320), channel_id=1, source_target_pairs={{0,3},{1,0},{2,1},{3,2},{4,7},{5,4},{6,5},{7,6},{8,11},{9,8},{10,9... | collective-permute-start | bytes 417800 | tf_op jit(solution)/shard_map/ppermute | solution.py:780
  352.9 6.7 %copy-start.29 = (bf16[1,32,2176]{2,1,0:T(8,128)(2,1)}, bf16[1,32,2176]{2,1,0:T(8,128)(2,1)S(1)}, u32[]{:S(2)}) copy-start(bf16[1,32,2176]{2,1,0:T(8,128)(2,1)S(1)} %collective-permute-done.40) | copy-start | bytes 417796
  (27 other events, 64.7 us)
Sparse Core Ops, SparseCore 0:
  35.2 38.7 all-gather.2
  76.4 27.9 all-gather.4
  191.6 32.8 reduce-scatter.3
  230.1 40.0 reduce-scatter.5
  295.0 47.7 reduce-scatter.7

commit v5 on v4

--- a/solution.py
+++ b/solution.py
@@ -135,16 +135,8 @@
     return jnp.where(chosen, 1.0, 0.0).astype(NARROW)
 
 
-def forward_kernel(heads, width, n_fs, shard_rows, *refs):
-    pieces, refs = refs[:n_fs], refs[n_fs:]
-    (win_ref, near_ref, far_ref, segcol_ref, poscol_ref, segrow_ref, edges_ref, z_ref, *refs) = refs
-    blocks, refs = refs[:n_fs], refs[n_fs:]
-    (side_ref, taps_ref, gain_ref, hidden_ref, raw_ref, out_ref, q_ref, k_ref, inv_ref, score_ref, dots_ref, upd_ref, state_ref,
-     move_ref, pad_ref, base_ref, w_ref, normed_ref) = refs
-    total = raw_ref.shape[0]
-    count = total // CHUNK
+def spread_side(heads, width, shard_rows, z_ref, side_ref, taps_ref, gain_ref):
     span = heads * width
-    side_ref[...] = win_ref[:, 4 * span:].astype(WIDE).T
     taps_count = taps_ref.shape[1]
     own = pl.ds(pl.multiple_of(z_ref[0] * span, span), span)
     for which in range(3):
@@ -154,17 +146,34 @@
     entries = jnp.broadcast_to(side_ref[last_row:last_row + 1, :], (8, side_ref.shape[1])).astype(NARROW)
     gain_ref[...] = plain_dot(entries, shard_places(width, side_ref.shape[1], shard_rows, True))[0:1]
 
+
+def forward_kernel(heads, width, n_fs, shard_rows, *refs):
+    pieces, refs = refs[:n_fs], refs[n_fs:]
+    (win_ref, near_ref, far_ref, segcol_ref, poscol_ref, segrow_ref, edges_ref, z_ref, *refs) = refs
+    blocks, refs = refs[:n_fs], refs[n_fs:]
+    (side_ref, hidden_ref, raw_ref, out_ref, q_ref, k_ref, inv_ref, score_ref, dots_ref, upd_ref, state_ref,
+     move_ref, taps_ref, gain_ref, pad_ref, base_ref, w_ref, normed_ref) = refs
+    total = raw_ref.shape[0]
+    count = total // CHUNK
+    span = heads * width
+    side_ref[...] = win_ref[:, 4 * span:].astype(WIDE).T
+    spread_side(heads, width, shard_rows, z_ref, side_ref, taps_ref, gain_ref)
+
+    pad_ref[0:HALO, :] = jnp.zeros((HALO, 3 * span), WIDE)
+
     def enter(index, _):
         rows = pl.ds(pl.multiple_of(index * ENTER, ENTER), ENTER)
         packed = pack_rows(near_ref[rows, :], pieces)
         scale = lax.rsqrt(jnp.mean(packed * packed, axis=-1, keepdims=True) + norm_eps)
         hidden = (packed * scale * side_ref[heads:heads + 1, :]).astype(NARROW)
         hidden_ref[rows, :] = hidden
-        raw_ref[rows, :] = plain_dot(hidden, win_ref[...])
+        raw = plain_dot(hidden, win_ref[...])
+        raw_ref[rows, :] = raw
+        pad_ref[pl.ds(pl.multiple_of(index * ENTER + HALO, HALO), ENTER), :] = (
+            raw[:, 0:3 * span].astype(NARROW).astype(WIDE))
         return 0
 
     lax.fori_loop(0, total // ENTER, enter, 0)
-    fill_padded(raw_ref, pad_ref, 3 * span)
 
     def first(group, _):
         work = []
@@ -255,11 +264,13 @@
 def backward_kernel(heads, width, n_fs, shard_rows, *refs):
     pieces, refs = refs[:n_fs], refs[n_fs:]
     (win_ref, near_ref, far_ref, segcol_ref, poscol_ref, segrow_ref, edges_ref, z_ref, dgffn_ref,
-     taps_ref, gain_ref, hidden_ref, raw_ref, mixed_ref, q_ref, k_ref, inv_ref, score_ref, dots_ref, upd_ref, state_ref,
+     side_ref, hidden_ref, raw_ref, mixed_ref, q_ref, k_ref, inv_ref, score_ref, dots_ref, upd_ref, state_ref,
      move_ref, gradin_ref, *refs) = refs
     blocks, refs = refs[:n_fs], refs[n_fs:]
-    (draw_ref, dhid_ref, dtaps_ref, sum_ref, small_ref, pad_ref, grad_ref, pdo_ref, dconv_ref, dout_ref, dnormed_ref) = refs
+    (taps_ref, gain_ref, draw_ref, dhid_ref, dtaps_ref, sum_ref, small_ref, pad_ref, grad_ref, pdo_ref, dconv_ref, dout_ref, dnormed_ref) = refs
     total = raw_ref.shape[0]
+
+    spread_side(heads, width, shard_rows, z_ref, side_ref, taps_ref, gain_ref)
 
     def enter(index, _):
         rows = pl.ds(pl.multiple_of(index * ENTER, ENTER), ENTER)
@@ -483,28 +494,28 @@
     block = jax.ShapeDtypeStruct((total // n_fs, span), NARROW)
     raw = jax.ShapeDtypeStruct((total, lanes), WIDE)
     side = jax.ShapeDtypeStruct((lanes - 4 * span, features), WIDE)
-    taps = jax.ShapeDtypeStruct((3, n_taps, span), WIDE)
-    gain = jax.ShapeDtypeStruct((1, width), WIDE)
     result = pl.pallas_call(
         functools.partial(forward_kernel, heads, width, n_fs, shard_rows),
         out_shape=(block,) * n_fs
-        + (side, taps, gain, full, raw, thin, rows, rows, square, square, square, rows, state, state),
+        + (side, full, raw, thin, rows, rows, square, square, square, rows, state, state),
         in_specs=specs(n_fs + 6) + [in_scalars()] * 2,
-        out_specs=tuple(specs(n_fs + 14)),
+        out_specs=tuple(specs(n_fs + 12)),
         scratch_shapes=[
+            pltpu.VMEM((3, n_taps, span), WIDE),
+            pltpu.VMEM((1, width), WIDE),
             pltpu.VMEM((total + HALO, 3 * span), WIDE),
             pltpu.VMEM((total, span), WIDE),
             pltpu.VMEM((total, span), WIDE),
             pltpu.VMEM((total, span), NARROW),
         ],
-        compiler_params=pltpu.CompilerParams(vmem_limit_bytes=52 << 20),
+        compiler_params=pltpu.CompilerParams(vmem_limit_bytes=60 << 20),
         cost_estimate=cost(30_000_000_000, 16 << 20),
         name="delta_forward",
     )(*pieces, w_in, near, far, segcol, poscol, segrow, edges, z)
     return result[:n_fs], result[n_fs], result[n_fs + 1 :]
 
 
-def delta_backward(pieces, w_in, near, far, segcol, poscol, segrow, edges, z, dgffn, kept, heads, width, shard_rows):
+def delta_backward(pieces, w_in, near, far, segcol, poscol, segrow, edges, z, dgffn, side, kept, heads, width, n_taps, shard_rows):
     n_fs = len(pieces)
     total = near.shape[0]
     features, lanes = w_in.shape
@@ -514,12 +525,14 @@
     result = pl.pallas_call(
         functools.partial(backward_kernel, heads, width, n_fs, shard_rows),
         out_shape=(jax.ShapeDtypeStruct((features, lanes), NARROW),) + (block,) * n_fs,
-        in_specs=specs(n_fs + 6) + [in_scalars()] * 2 + specs(14),
+        in_specs=specs(n_fs + 6) + [in_scalars()] * 2 + specs(13),
         out_specs=tuple(specs(n_fs + 1)),
         scratch_shapes=[
+            pltpu.VMEM((3, n_taps, span), WIDE),
+            pltpu.VMEM((1, width), WIDE),
             pltpu.VMEM((total, lanes), NARROW),
             pltpu.VMEM((total, features), NARROW),
-            pltpu.VMEM(kept[0].shape, WIDE),
+            pltpu.VMEM((3, n_taps, span), WIDE),
             pltpu.VMEM((features, lanes), WIDE),
             pltpu.VMEM((lanes - 4 * span, features), WIDE),
             pltpu.VMEM((total + HALO, 3 * span), WIDE),
@@ -532,7 +545,7 @@
         compiler_params=pltpu.CompilerParams(vmem_limit_bytes=52 << 20),
         cost_estimate=cost(40_000_000_000, 16 << 20),
         name="delta_backward",
-    )(*pieces, w_in, near, far, segcol, poscol, segrow, edges, z, dgffn, *kept)
+    )(*pieces, w_in, near, far, segcol, poscol, segrow, edges, z, dgffn, side, *kept)
     return result[0], list(result[1:])
 
 
@@ -541,8 +554,8 @@
     pieces, refs = refs[:n_fs], refs[n_fs:]
     (*grads, wout_ref, beta_ref, taps_ref, gmix_ref, gffn_ref, ghead_ref) = refs
     side = pl.ds(4 * span, 128)
-    lane = lax.broadcasted_iota(jnp.int32, (128, beta_ref.shape[1]), 0)
-    column = lax.broadcasted_iota(jnp.int32, (128, beta_ref.shape[1]), 1)
+    lane = lax.broadcasted_iota(jnp.int32, (128, beta_ref.shape[0]), 0)
+    column = lax.broadcasted_iota(jnp.int32, (128, beta_ref.shape[0]), 1)
     wout = jnp.zeros(wout_ref.shape, WIDE)
     small = jnp.zeros((wout_ref.shape[0], 128), WIDE)
     beta = jnp.zeros(beta_ref.shape, WIDE)
@@ -555,18 +568,20 @@
         beside = piece[:, side]
         small = small + beside.astype(WIDE)
         chosen = jnp.where((lane < heads) & (column == line * heads + lane), 1.0, 0.0)
-        beta = beta + plain_dot(beside, chosen.astype(NARROW))
+        beta = beta + plain_dot(chosen.astype(NARROW), beside, 0, 1)
     wout_ref[...] = wout
     beta_ref[...] = beta
     small = small.T
     gmix_ref[...] = small[heads:heads + 1]
     gffn_ref[...] = small[heads + 1:heads + 2]
     last_row = heads + 2 + 3 * n_taps
-    taps_ref[...] = small[heads + 2:last_row]
-    ghead_ref[...] = small[last_row:last_row + 1]
-
-
-def finish(z, pieces, heads, span, n_taps):
+    for which in range(3):
+        first_row = heads + 2 + which * n_taps
+        taps_ref[which] = small[first_row:first_row + n_taps]
+    ghead_ref[...] = small[last_row:last_row + 1, :ghead_ref.shape[1]]
+
+
+def finish(z, pieces, heads, span, n_taps, head_rows):
     rows = pieces[0].shape[0]
     n_fs = len(pieces)
     full = jax.ShapeDtypeStruct((rows, n_fs * span), WIDE)
@@ -575,11 +590,11 @@
         functools.partial(finish_kernel, heads, span, n_taps),
         out_shape=(full,) * 5
         + (
-            jax.ShapeDtypeStruct((rows, n_fs * heads), WIDE),
-            jax.ShapeDtypeStruct((3 * n_taps, rows), WIDE),
+            jax.ShapeDtypeStruct((n_fs * heads, rows), WIDE),
+            jax.ShapeDtypeStruct((3, n_taps, rows), WIDE),
             line,
             line,
-            line,
+            jax.ShapeDtypeStruct((1, head_rows), WIDE),
         ),
         in_specs=[in_scalars()] + specs(n_fs),
         out_specs=tuple(specs(10)),
@@ -692,10 +707,11 @@
     gain_ref, refs = refs[0], refs[1:]
     blocks, refs = refs[:n_fs], refs[n_fs:]
     (dmiddle_ref, dbranch_ref, dgain_ref, *places, sems) = refs
-    fetches = [pltpu.make_async_copy(source, place, sems.at[k]) for k, (source, place) in enumerate(zip(sources, places))]
+    fetches = [pltpu.make_async_copy(source, place, sems.at[k]) for k, (source, place) in enumerate(
+        zip((sources[0], sources[1].at[pl.ds(0, places[1].shape[0])], *sources[2:5]), places))]
     quarter = places[5].shape[0] // 4
     parts = [pl.ds(k * quarter, quarter) for k in range(4)]
-    fetches[5:] = [
+    fetches += [
         pltpu.make_async_copy(sources[5].at[part], places[5].at[part], sems.at[5 + k]) for k, part in enumerate(parts)
     ]
     for fetch in fetches:
@@ -704,7 +720,7 @@
     for fetch in fetches[:5]:
         fetch.wait()
     middle = middle_ref[...]
-    given = own_ref[...] + core_ref[0:own_ref.shape[0], :].astype(WIDE) + side_ref[...].astype(WIDE)
+    given = own_ref[...] + core_ref[...].astype(WIDE) + side_ref[...].astype(WIDE)
     scale = lax.rsqrt(jnp.mean(middle * middle, axis=-1, keepdims=True) + norm_eps)
     unit = middle * scale
     dgain_ref[...] = jnp.sum(given * unit, axis=0, keepdims=True)
@@ -735,7 +751,7 @@
         ),
         in_specs=[in_scalars()] + [anywhere()] * 6 + specs(1),
         out_specs=tuple(specs(n_fs + 3)),
-        scratch_shapes=[pltpu.VMEM(part.shape, part.dtype) for part in sources] + [pltpu.SemaphoreType.DMA((9,))],
+        scratch_shapes=[pltpu.VMEM((min(part.shape[0], count) if k < 5 else part.shape[0], features), part.dtype) for k, part in enumerate(sources)] + [pltpu.SemaphoreType.DMA((9,))],
         compiler_params=pltpu.CompilerParams(vmem_limit_bytes=60 << 20),
         cost_estimate=cost(2_000_000_000, 6 << 20),
         name="mix_back",
@@ -1003,6 +1019,12 @@
         part = weight_grad(lax.dynamic_slice_in_dim(ffn_near, lo, size, 1), d_both)
         return part.reshape(-1, n_fs * rows, 2 * ff_pad)
 
+    cotangent_near = jnp.concatenate([cot_pieces[key] for key in tp_order], axis=0)
+    down_terms = weight_grad(active_b, cotangent_near).astype(NARROW)
+    down_sum = lax.psum_scatter(
+        down_terms.reshape(n_rest, -1, features), "fsdp", scatter_dimension=1, tiled=True
+    )
+    d_both, down_terms = lax.optimization_barrier((d_both, down_terms))
     split = features // 2 if rest_bits else features
     top = block // max(n_rest // 2, 1)
     if rest_bits:
@@ -1013,14 +1035,7 @@
     second = second + from_core[own_rows:].astype(WIDE)
     second, both_sent, active_late = lax.optimization_barrier((second.astype(NARROW), both_sent, active_b))
     from_side = flip(second, tp_bits[1], n_dp)
-    cotangent_near = jnp.concatenate([cot_pieces[key] for key in tp_order], axis=0)
-    down_terms = weight_grad(active_late, cotangent_near).astype(NARROW)
-    down_sum = lax.psum_scatter(
-        down_terms.reshape(n_rest, -1, features), "fsdp", scatter_dimension=1, tiled=True
-    )
-    from_side, down_terms, ffn_near, active_late = lax.optimization_barrier(
-        (from_side, down_terms, ffn_near, active_late)
-    )
+    from_side, ffn_near, active_late = lax.optimization_barrier((from_side, ffn_near, active_late))
     both_sum = both_part(top * split if rest_bits else 0, split)
     if rest_bits:
         both_sum = both_sum + flip(both_sent, rest_bits[-1], n_dp).astype(WIDE)
@@ -1037,7 +1052,7 @@
     both_line = hand_out(both_sum.astype(NARROW))
 
     grad_in, d_blocks = delta_backward(
-        d_pieces, w_in, near, far, *layout, d_gffn, kept, heads, width, shard_rows
+        d_pieces, w_in, near, far, *layout, d_gffn, side, kept, heads, width, n_taps, shard_rows
     )
     grad_in, both_line, down_sum, sum_out = lax.optimization_barrier((grad_in, both_line, down_sum, sum_out))
     part = lax.psum_scatter(grad_in, "dp", scatter_dimension=0, tiled=True)
@@ -1048,7 +1063,9 @@
     both_sum = sum_up(both_line, both_sum)
     grad_fdown = halve(down_sum, block, rest_bits)[0, :ff_line].astype(WIDE)
     both_pieces = {
-        key: flip(lax.dynamic_index_in_dim(both_sum, member ^ key, 0, keepdims=False), key, n_dp)
+        key: flip(
+            lax.dynamic_index_in_dim(both_sum, member ^ key, 0, keepdims=False).astype(NARROW), key, n_dp
+        ).astype(WIDE)
         if key
         else lax.dynamic_index_in_dim(both_sum, member, 0, keepdims=False)
         for key in range(TP)
@@ -1066,17 +1083,13 @@
     d_hidden = d_blocks[0].astype(WIDE)
     for block_of in d_blocks[1:]:
         d_hidden = d_hidden + block_of.astype(WIDE)
-
-    d_hidden = d_blocks[0].astype(WIDE)
-    for block_of in d_blocks[1:]:
-        d_hidden = d_hidden + block_of.astype(WIDE)
     _, norm_mix_back = jax.vjp(rms_scale, tokens.astype(WIDE), side[heads])
     d_inputs_norm, _ = norm_mix_back(d_hidden)
     grad_tokens = d_middle + d_inputs_norm
 
     grads, (grad_wout, grad_beta, grad_taps, grad_gmix, grad_gffn, grad_ghead) = (
         lambda outs: (outs[:4], outs[4:])
-    )(finish(z_ref, arrived, heads, span, n_taps))
+    )(finish(z_ref, arrived, heads, span, n_taps, head_rows))
     return (
         layer_out,
         grad_tokens,
@@ -1084,11 +1097,11 @@
         grads[1],
         grads[2],
         grads[3],
-        grad_beta,
-        grad_taps.reshape(3, n_taps, rows),
+        grad_beta.T,
+        grad_taps,
         grad_wout,
         grad_gmix[0],
-        grad_ghead[0, :head_rows],
+        grad_ghead[0],
         grad_gffn[0],
         units_of(0),
         units_of(1),

time: 376 us -> 365 us (0.971)
  starting transfers between devices: 58.8 us -> 48.4 us
  local copies, waits for them, and re-layouts: 40 us -> 30.3 us
  waiting for transfers between devices: 117 us -> 122 us
    reduce_scatter x1, starting transfers between devices: 10.6 us -> 0.51 us  [per_device(): sum_out = lax.psum_scatter(out_grad, 'dp', scatter_dimension=0, tiled=True)]
    unnamed x87 -> x90, local copies, waits for them, and re-layouts: 17.2 us -> 14.1 us
  transfers between devices with their start and end apart: 52 -> 52, of which waited for: 21 -> 20; matrix products, arithmetic and copies ran while one was open for 16% -> 16% of each run, Pallas kernels for 23% -> 24%
where the time goes in v5:
time: 365 us; the launch traced here: 360 us
  waiting for transfers between devices  122 us (33%)
  Pallas kernels  102 us (28%)
  starting transfers between devices  48.4 us (13%)
  local copies, waits for them, and re-layouts  30.3 us (8%)
  matrix products  24.4 us (7%)
  other arithmetic  17.8 us (5%)
  between operations  14.9 us (4%)
    ppermute x27, waiting for transfers between devices, shift(): lax.ppermute(value, 'fsdp', [(i, (i + by) % n_fs) for i in range(n_fs)])  73.6 us
    pallas_call x1, Pallas kernels, delta_backward(): pl.pallas_call(functools.partial(backward_kernel, heads, width, n_fs, sha...  46.1 us
    ppermute x20, waiting for transfers between devices, flip(): return lax.ppermute(value, 'dp', [(i, i ^ bit) for i in range(n_dp)])  45.2 us
    pallas_call x1, Pallas kernels, delta_forward(): pl.pallas_call(functools.partial(forward_kernel, heads, width, n_fs, shar...  33 us
    ppermute x27, starting transfers between devices, shift(): lax.ppermute(value, 'fsdp', [(i, (i + by) % n_fs) for i in range(n_fs)])  26.5 us
    ppermute x20, starting transfers between devices, flip(): return lax.ppermute(value, 'dp', [(i, i ^ bit) for i in range(n_dp)])  21.3 us
    dot_general x4, matrix products, weight_grad(): lax.dot_general(left, right, (((0,), (0,)), ((), ())), preferred_element_...  15.2 us
    pallas_call x1, Pallas kernels, ffn_units(): pl.pallas_call(functools.partial(ffn_kernel, keys, unit), out_shape=(jax....  14.3 us
  transfers between devices with their start and end apart: 52, of which 20 were waited for; matrix products, arithmetic and copies ran while one was open for 16% of the time, Pallas kernels for 24%

profile of v5, /device:TPU:9, one launch (start us, length us, event | category | flops | bytes accessed | tf_op | source)
XLA Modules:
  0.0 359.8 jit_solution(9232830081395214157)
XLA Ops:
  7.3 1.3 collective-permute-start.3
  16.0 1.3 collective-permute-start
  18.6 4.7 %collective-permute-done = bf16[1,32,2176]{2,1,0:T(8,128)(2,1)S(1)} collective-permute-done((bf16[1,32,2176]{2,1,0:T(8,128)(2,1)S(1)}, bf16[1,32,2176]{2,1,0:T(8,128)(2,1)S(1)}, u32[]{:S(2)}, u32[]{:S(2)}) %collective-permute-start) | collective-permute-done | bytes 139296 | tf_op jit(solution)/shard_map/ppermute | solution.py:796
  23.3 8.0 %collective-permute-done.1 = bf16[1,32,2176]{2,1,0:T(8,128)(2,1)S(1)} collective-permute-done((bf16[1,32,2176]{2,1,0:T(8,128)(2,1)S(1)}, bf16[1,32,2176]{2,1,0:T(8,128)(2,1)S(1)}, u32[]{:S(2)}, u32[]{:S(2)}) %collective-permute-start.1) | collective-permute-done | bytes 139296 | tf_op jit(solution)/shard_map/ppermute | solution.py:796
  31.3 2.9 collective-permute-done.2
  41.4 1.7 collective-permute-start.4
  43.1 1.2 collective-permute-start.5
  45.0 1.3 collective-permute-start.7
  46.4 3.5 collective-permute-done.5
  49.8 3.1 collective-permute-done.6
  55.6 1.2 fusion.25.refs_5_
  57.7 11.7 %collective-permute-done.11.refs_2_ = bf16[256,1024]{1,0:T(8,128)(2,1)} collective-permute-done((bf16[256,1024]{1,0:T(8,128)(2,1)S(1)}, bf16[256,1024]{1,0:T(8,128)(2,1)}, u32[]{:S(2)}, u32[]{:S(2)}) %collective-permute-start.11) | collective-permute-done | bytes 524320 | tf_op jit(solution)/shard_map/ppermute | solution.py:796
  69.5 3.2 collective-permute-start.14
  72.7 1.7 collective-permute-start.15
  74.3 1.3 collective-permute-start.10
  75.7 33.0 %delta_forward.1 = (bf16[256,256]{1,0:T(8,128)(2,1)}, bf16[256,256]{1,0:T(8,128)(2,1)}, bf16[256,256]{1,0:T(8,128)(2,1)}, bf16[256,256]{1,0:T(8,128)(2,1)}, f32[...) custom-call(bf16[256,1024]{1,0:T(8,128)(2,1)} %refs_5_.1, ...), custom_call_target="tpu_custom_call" | custom-call | flops 30000001024 | bytes 16777216 | tf_op jit(solution)/shard_map/delta_forward/pallas_call | solution.py:497
  109.5 1.9 collective-permute-start.17
  111.5 2.3 pad_maximum_fusion.refs_8_
  115.0 6.3 %collective-permute-done.17.refs_2_ = bf16[256,256]{1,0:T(8,128)(2,1)S(1)} collective-permute-done((bf16[256,256]{1,0:T(8,128)(2,1)}, bf16[256,256]{1,0:T(8,128)(2,1)S(1)}, u32[]{:S(2)}, u32[]{:S(2)}) %collective-permute-start.17) | collective-permute-done | bytes 131104 | tf_op jit(solution)/shard_map/ppermute | solution.py:796
  121.3 2.9 collective-permute-done.18.refs_3_
  124.2 1.6 copy-done.9
  126.7 1.3 collective-permute-start.19
  128.4 1.6 collective-permute-start.25
  130.2 7.9 %collective-permute-done.23 = bf16[2,96,1024]{2,1,0:T(8,128)(2,1)S(1)} collective-permute-done((bf16[2,96,1024]{2,1,0:T(8,128)(2,1)S(1)}, bf16[2,96,1024]{2,1,0:T(8,128)(2,1)S(1)}, u32[]{:S(2)}, u32[]{:S(2)}) %collective-permute-start.23) | collective-permute-done | bytes 393248 | tf_op jit(solution)/shard_map/ppermute | solution.py:796
  138.1 2.5 collective-permute-start.20
  141.1 20.2 %collective-permute-done.24 = bf16[2,96,1024]{2,1,0:T(8,128)(2,1)S(1)} collective-permute-done((bf16[2,96,1024]{2,1,0:T(8,128)(2,1)S(1)}, bf16[2,96,1024]{2,1,0:T(8,128)(2,1)S(1)}, u32[]{:S(2)}, u32[]{:S(2)}) %collective-permute-start.24) | collective-permute-done | bytes 393248 | tf_op jit(solution)/shard_map/ppermute | solution.py:796
  161.4 1.8 collective-permute-done.25
  164.6 14.3 %ffn_units.1 = (bf16[1024,768]{1,0:T(8,128)(2,1)}, bf16[1024,1536]{1,0:T(8,128)(2,1)}, bf16[512,1024]{1,0:T(8,128)(2,1)}, f32[256,1024]{1,0:T(8,128)}, f32[256,1024]{1,0:T(8,128)}) custom-call(s32[2]{0:T(128)S(1)} %pad_add_fusion.1.block_ref, bf16[256,1024]{1,0:T(8,128)(2,1)S(1)} %get-tuple-element.149.refs_0_, ...), custom_call_target="tpu_custom_call" | custom-call | flops 8000000000 | bytes 16777216 | tf_op jit(solution)/shard_map/ffn_units/pallas_call | solution.py:686
  178.8 5.0 %fusion.8 = bf16[768,1024]{1,0:T(8,128)(2,1)} fusion(bf16[1024,768]{1,0:T(8,128)(2,1)} %get-tuple-element.209, bf16[256,1024]{1,0:T(8,128)(2,1)} %collective-permute-done.10.refs_7_, bf16[256,1024]{1,0:T(8,128)(2,1)} %collective-permute-done.8.refs_6_, bf16[256,1024]{1,0:T(8,128)(2,1)} %collective-permute-done.9.refs_5_, bf16[256,1024]{1,0:T(8,128)(2,1)} %refs_4_.2), kind=kOutput, calls=%fused_computation.11 | convolution fusion | flops 1619787776 | bytes 5242880 | tf_op jit(solution)/shard_map/dot_general | solution.py:788
  187.0 3.1 convolution_convert_fusion
  190.1 2.0 add_convert_fusion
  192.1 1.3 collective-permute-start.28
  193.6 13.2 %collective-permute-done.27.refs_2_ = bf16[256,1024]{1,0:T(8,128)(2,1)} collective-permute-done((bf16[256,1024]{1,0:T(8,128)(2,1)}, bf16[256,1024]{1,0:T(8,128)(2,1)}, u32[]{:S(2)}, u32[]{:S(2)}) %collective-permute-start.27) | collective-permute-done | bytes 524320 | tf_op jit(solution)/shard_map/ppermute | solution.py:792
  206.9 5.6 %mix_back.1 = (bf16[256,256]{1,0:T(8,128)(2,1)}, bf16[256,256]{1,0:T(8,128)(2,1)}, bf16[256,256]{1,0:T(8,128)(2,1)}, bf16[256,256]{1,0:T(8,128)(2,1)}, f32[256,1...) custom-call(s32[1]{0:T(128)} %bitcast.1.refs_11_.z_ref, f32[256,1024]{1,0:T(8,128)} %get-tuple-element.168.refs_0_, ...), custom_call_target="tpu_custom_call" | custom-call | flops 2000000000 | bytes 6291456 | tf_op jit(solution)/shard_map/mix_back/pallas_call | solution.py:744
  212.5 2.1 collective-permute-start.30
  214.6 1.4 collective-permute-start.31
  216.0 3.1 convolution_convert_fusion.1
  219.2 4.0 %fusion.18 = f32[512,1536]{1,0:T(8,128)S(1)} fusion(bf16[1024,1536]{1,0:T(8,128)(2,1)} %get-tuple-element.163, bf16[1024,1024]{1,0:T(8,128)(2,1)} %copy-done.36, s32[]{:T(128)S(6)} %select_n.142), kind=kOutput, calls=%fused_computation.28 | convolution fusion | flops 1610612736 | bytes 7340036 | tf_op jit(solution)/shard_map/dot_general | solution.py:788
  223.2 5.1 %collective-permute-done.28 = bf16[4,128,1536]{2,1,0:T(8,128)(2,1)S(1)} collective-permute-done((bf16[4,128,1536]{2,1,0:T(8,128)(2,1)}, bf16[4,128,1536]{2,1,0:T(8,128)(2,1)S(1)}, u32[]{:S(2)}, u32[]{:S(2)}) %collective-permute-start.28) | collective-permute-done | bytes 1572896 | tf_op jit(solution)/shard_map/ppermute | solution.py:792
  229.1 1.4 copy-done.13
  230.7 2.1 collective-permute-start.33
  232.8 1.5 collective-permute-start.34
  234.4 46.1 %delta_backward.1 = (bf16[1024,1152]{1,0:T(8,128)(2,1)}, bf16[256,1024]{1,0:T(8,128)(2,1)S(1)}, bf16[256,1024]{1,0:T(8,128)(2,1)S(1)}, bf16[256,1024]{1,0:T(8,128)(2,1)}, bf16[256,1024]{1,0:T(8,128)(2,1)}) custom-call(bf16[256,256]{1,0:T(8,128)(2,1)S(1)} %copy-done.10, bf16[256,256]{1,0:T(8,128)(2,1)S(1)} %collective-permute-done.29.refs_1_, ...), custom_call_target="tpu_custom_call" | custom-call | flops 40000000000 | bytes 16777216 | tf_op jit(solution)/shard_map/delta_backward/pallas_call | solution.py:525
  282.2 1.9 collective-permute-start.36
  284.4 3.2 convolution_convert_fusion.2
  287.5 2.2 collective-permute-start.38
  289.7 1.4 convert_add_fusion.1
  292.9 4.0 %collective-permute-done.44 = bf16[32,1536]{1,0:T(8,128)(2,1)S(1)} collective-permute-done((bf16[32,1536]{1,0:T(8,128)(2,1)S(1)}, bf16[32,1536]{1,0:T(8,128)(2,1)S(1)}, u32[]{:S(2)}, u32[]{:S(2)}) %collective-permute-start.44) | collective-permute-done | bytes 98336 | tf_op jit(solution)/shard_map/ppermute | solution.py:792
  298.0 4.1 %collective-permute-done.45 = bf16[32,1536]{1,0:T(8,128)(2,1)S(1)} collective-permute-done((bf16[32,1536]{1,0:T(8,128)(2,1)S(1)}, bf16[32,1536]{1,0:T(8,128)(2,1)S(1)}, u32[]{:S(2)}, u32[]{:S(2)}) %collective-permute-start.45) | collective-permute-done | bytes 98336 | tf_op jit(solution)/shard_map/ppermute | solution.py:792
  302.2 1.2 collective-permute-start.46
  304.3 2.2 reshape.286
  306.5 2.6 fusion.14
  311.7 1.2 reshape.289
  312.9 1.8 add_bitcast_fusion
  314.7 11.7 %collective-permute-done.39 = bf16[256,1024]{1,0:T(8,128)(2,1)} collective-permute-done((bf16[256,1024]{1,0:T(8,128)(2,1)}, bf16[256,1024]{1,0:T(8,128)(2,1)}, u32[]{:S(2)}, u32[]{:S(2)}) %collective-permute-start.39) | collective-permute-done | bytes 524320 | tf_op jit(solution)/shard_map/ppermute | solution.py:792
  326.5 3.5 fusion.13
  329.9 3.2 reduce-scatter.8.cloned.1.call-done
  334.9 1.3 collective-permute-start.40
  337.3 1.3 collective-permute-start.42
  338.6 1.9 fusion.15
  340.5 2.8 fusion.17
  343.3 4.2 %collective-permute-done.41 = bf16[1,32,2176]{2,1,0:T(8,128)(2,1)S(1)} collective-permute-done((bf16[1,32,2176]{2,1,0:T(8,128)(2,1)S(1)}, bf16[1,32,2176]{2,1,0:T(8,128)(2,1)S(1)}, u32[]{:S(2)}, u32[]{:S(2)}) %collective-permute-start.41) | collective-permute-done | bytes 139296 | tf_op jit(solution)/shard_map/ppermute | solution.py:796
  347.5 2.9 collective-permute-done.42
  351.1 2.0 finish_inputs.1
  (233 shorter events, 41.4 us)
Async XLA Ops:
  7.2 27.9 %copy-start = (bf16[256,1024]{1,0:T(8,128)(2,1)S(1)}, bf16[256,1024]{1,0:T(8,128)(2,1)}, u32[]{:S(2)}) copy-start(bf16[256,1024]{1,0:T(8,128)(2,1)} %refs_5_.1) | copy-start | bytes 1572868
  7.2 28.5 %copy-start.37 = (s32[1,1024]{1,0:T(1,128)S(1)}, s32[1,1024]{1,0:T(1,128)}, u32[]{:S(2)}) copy-start(s32[1,1024]{1,0:T(1,128)} %param.19) | copy-start | bytes 12292
  7.2 28.7 %copy-start.38 = (s32[1,4]{1,0:T(1,128)S(1)}, s32[1,4]{1,0:T(1,128)}, u32[]{:S(2)}) copy-start(s32[1,4]{1,0:T(1,128)} %param.18) | copy-start | bytes 52
  7.2 68.5 %all-gather.3.cloned.1.call-start = ((), (), s32[]{:S(2)}) async-start(), calls=%async_computation.3 | async-start | bytes 2654208 | tf_op jit(solution)/shard_map/all_gather | solution.py:919
  7.3 26.9 %collective-permute-start.3 = (bf16[256,1024]{1,0:T(8,128)(2,1)}, bf16[256,1024]{1,0:T(8,128)(2,1)S(1)}, u32[]{:S(2)}, u32[]{:S(2)}) collective-permute-start(bf16[256,1024]{1,0:T(8,128)(2,1)} %refs_5_.1), channel_id=1, source_target_pairs={{0,1},{1,2},{2,3},{3,0},{4,5},{5,6},{6,7},{7,4},{8,9},{9,10},{10,1... | collective-permute-start | bytes 1572872 | tf_op jit(solution)/shard_map/ppermute | solution.py:796
  15.9 23.4 %copy-start.30 = (bf16[32,2816]{1,0:T(8,128)(2,1)S(1)}, bf16[32,2816]{1,0:T(8,128)(2,1)}, u32[]{:S(2)}) copy-start(bf16[32,2816]{1,0:T(8,128)(2,1)} %param.30) | copy-start | bytes 540676
  16.0 7.3 %collective-permute-start = (bf16[1,32,2176]{2,1,0:T(8,128)(2,1)S(1)}, bf16[1,32,2176]{2,1,0:T(8,128)(2,1)S(1)}, u32[]{:S(2)}, u32[]{:S(2)}) collective-permute-start(bf16[1,32,2176]{2,1,0:T(8,128)(2,1)S(1)} %get-tuple-element.249), channel_id=1, source_target_pairs={{0,1},{1,2},{2,3},{3,0},{4,5},{5,6},{6,7},{7,4},{8,9},{9,10},{10,1... | collective-permute-start | bytes 417800 | tf_op jit(solution)/shard_map/ppermute | solution.py:796
  17.3 14.0 %collective-permute-start.1 = (bf16[1,32,2176]{2,1,0:T(8,128)(2,1)S(1)}, bf16[1,32,2176]{2,1,0:T(8,128)(2,1)S(1)}, u32[]{:S(2)}, u32[]{:S(2)}) collective-permute-start(bf16[1,32,2176]{2,1,0:T(8,128)(2,1)S(1)} %get-tuple-element.248), channel_id=1, source_target_pairs={{0,2},{1,3},{2,0},{3,1},{4,6},{5,7},{6,4},{7,5},{8,10},{9,11},{10,... | collective-permute-start | bytes 417800 | tf_op jit(solution)/shard_map/ppermute | solution.py:796
  18.3 15.9 %collective-permute-start.2 = (bf16[1,32,2176]{2,1,0:T(8,128)(2,1)S(1)}, bf16[1,32,2176]{2,1,0:T(8,128)(2,1)S(1)}, u32[]{:S(2)}, u32[]{:S(2)}) collective-permute-start(bf16[1,32,2176]{2,1,0:T(8,128)(2,1)S(1)} %get-tuple-element.247), channel_id=1, source_target_pairs={{0,3},{1,0},{2,1},{3,2},{4,7},{5,4},{6,5},{7,6},{8,11},{9,8},{10,9... | collective-permute-start | bytes 417800 | tf_op jit(solution)/shard_map/ppermute | solution.py:796
  35.1 79.9 %all-gather.5.cloned.1.call-start = ((), (), s32[]{:S(2)}) async-start(), calls=%async_computation.4 | async-start | bytes 2359296 | tf_op jit(solution)/shard_map/all_gather | solution.py:920
  35.1 34.3 %collective-permute-start.11 = (bf16[256,1024]{1,0:T(8,128)(2,1)S(1)}, bf16[256,1024]{1,0:T(8,128)(2,1)}, u32[]{:S(2)}, u32[]{:S(2)}) collective-permute-start(bf16[256,1024]{1,0:T(8,128)(2,1)S(1)} %copy-done), channel_id=1, source_target_pairs={{0,2},{1,3},{2,0},{3,1},{4,6},{5,7},{6,4},{7,5},{8,10},{9,11},{10,... | collective-permute-start | bytes 1572872 | tf_op jit(solution)/shard_map/ppermute | solution.py:796
  35.5 34.0 %collective-permute-start.12 = (bf16[256,1024]{1,0:T(8,128)(2,1)S(1)}, bf16[256,1024]{1,0:T(8,128)(2,1)}, u32[]{:S(2)}, u32[]{:S(2)}) collective-permute-start(bf16[256,1024]{1,0:T(8,128)(2,1)S(1)} %copy-done), channel_id=1, source_target_pairs={{0,3},{1,0},{2,1},{3,2},{4,7},{5,4},{6,5},{7,6},{8,11},{9,8},{10,9... | collective-permute-start | bytes 1572872 | tf_op jit(solution)/shard_map/ppermute | solution.py:796
  41.4 3.7 %collective-permute-start.4 = (bf16[32,1536]{1,0:T(8,128)(2,1)S(1)}, bf16[32,1536]{1,0:T(8,128)(2,1)S(1)}, u32[]{:S(2)}, u32[]{:S(2)}) collective-permute-start(bf16[32,1536]{1,0:T(8,128)(2,1)S(1)} %get-tuple-element.253), channel_id=1, source_target_pairs={{0,4},{4,0},{8,12},{12,8},{16,20},{20,16},{24,28},{28,24},{1,5},{5... | collective-permute-start | bytes 294920 | tf_op jit(solution)/shard_map/ppermute | solution.py:792
  43.1 6.7 %collective-permute-start.5 = (bf16[32,1536]{1,0:T(8,128)(2,1)S(1)}, bf16[32,1536]{1,0:T(8,128)(2,1)S(1)}, u32[]{:S(2)}, u32[]{:S(2)}) collective-permute-start(bf16[32,1536]{1,0:T(8,128)(2,1)S(1)} %get-tuple-element.252), channel_id=1, source_target_pairs={{0,8},{4,12},{8,0},{12,4},{16,24},{20,28},{24,16},{28,20},{1,9},{5... | collective-permute-start | bytes 294920 | tf_op jit(solution)/shard_map/ppermute | solution.py:792
  44.3 8.7 %collective-permute-start.6 = (bf16[32,1536]{1,0:T(8,128)(2,1)S(1)}, bf16[32,1536]{1,0:T(8,128)(2,1)S(1)}, u32[]{:S(2)}, u32[]{:S(2)}) collective-permute-start(bf16[32,1536]{1,0:T(8,128)(2,1)S(1)} %get-tuple-element.251), channel_id=1, source_target_pairs={{0,12},{4,8},{8,4},{12,0},{16,28},{20,24},{24,20},{28,16},{1,13},{... | collective-permute-start | bytes 294920 | tf_op jit(solution)/shard_map/ppermute | solution.py:792
  45.0 7.9 %collective-permute-start.7 = (bf16[96,1024]{1,0:T(8,128)(2,1)S(1)}, bf16[96,1024]{1,0:T(8,128)(2,1)S(1)}, u32[]{:S(2)}, u32[]{:S(2)}) collective-permute-start(bf16[96,1024]{1,0:T(8,128)(2,1)S(1)} %get-tuple-element.254), channel_id=1, source_target_pairs={{0,16},{4,20},{8,24},{12,28},{16,0},{20,4},{24,8},{28,12},{1,17},{... | collective-permute-start | bytes 589832 | tf_op jit(solution)/shard_map/ppermute | solution.py:792
  53.0 21.3 %collective-permute-start.9 = (bf16[256,1024]{1,0:T(8,128)(2,1)}, bf16[256,1024]{1,0:T(8,128)(2,1)}, u32[]{:S(2)}, u32[]{:S(2)}) collective-permute-start(bf16[256,1024]{1,0:T(8,128)(2,1)} %refs_4_.2), channel_id=1, source_target_pairs={{0,8},{4,12},{8,0},{12,4},{16,24},{20,28},{24,16},{28,20},{1,9},{5... | collective-permute-start | bytes 1572872 | tf_op jit(solution)/shard_map/ppermute | solution.py:792
  54.9 227.0 %reduce-scatter.4.cloned.1.call-start = ((), (), s32[]{:S(2)}) async-start(), calls=%async_computation.5 | async-start | bytes 1966080 | tf_op jit(solution)/shard_map/reduce_scatter | solution.py:1024
  56.9 51.9 %collective-permute-start.8 = (bf16[256,1024]{1,0:T(8,128)(2,1)}, bf16[256,1024]{1,0:T(8,128)(2,1)}, u32[]{:S(2)}, u32[]{:S(2)}) collective-permute-start(bf16[256,1024]{1,0:T(8,128)(2,1)} %refs_4_.2), channel_id=1, source_target_pairs={{0,4},{4,0},{8,12},{12,8},{16,20},{20,16},{24,28},{28,24},{1,5},{5... | collective-permute-start | bytes 1572872 | tf_op jit(solution)/shard_map/ppermute | solution.py:792
  69.5 39.3 %collective-permute-start.13 = (bf16[4,32,1536]{2,1,0:T(8,128)(2,1)S(1)}, bf16[4,32,1536]{2,1,0:T(8,128)(2,1)S(1)}, u32[]{:S(2)}, u32[]{:S(2)}) collective-permute-start(bf16[4,32,1536]{2,1,0:T(8,128)(2,1)S(1)} %bitcast.166), channel_id=1, source_target_pairs={{0,1},{1,2},{2,3},{3,0},{4,5},{5,6},{6,7},{7,4},{8,9},{9,10},{10,1... | collective-permute-start | bytes 1179656 | tf_op jit(solution)/shard_map/ppermute | solution.py:796
  69.5 39.3 %collective-permute-start.14 = (bf16[4,32,1536]{2,1,0:T(8,128)(2,1)S(1)}, bf16[4,32,1536]{2,1,0:T(8,128)(2,1)S(1)}, u32[]{:S(2)}, u32[]{:S(2)}) collective-permute-start(bf16[4,32,1536]{2,1,0:T(8,128)(2,1)S(1)} %bitcast.167), channel_id=1, source_target_pairs={{0,2},{1,3},{2,0},{3,1},{4,6},{5,7},{6,4},{7,5},{8,10},{9,11},{10,... | collective-permute-start | bytes 1179656 | tf_op jit(solution)/shard_map/ppermute | solution.py:796
  72.7 36.1 %collective-permute-start.15 = (bf16[4,32,1536]{2,1,0:T(8,128)(2,1)S(1)}, bf16[4,32,1536]{2,1,0:T(8,128)(2,1)S(1)}, u32[]{:S(2)}, u32[]{:S(2)}) collective-permute-start(bf16[4,32,1536]{2,1,0:T(8,128)(2,1)S(1)} %bitcast.168), channel_id=1, source_target_pairs={{0,3},{1,0},{2,1},{3,2},{4,7},{5,4},{6,5},{7,6},{8,11},{9,8},{10,9... | collective-permute-start | bytes 1179656 | tf_op jit(solution)/shard_map/ppermute | solution.py:796
  74.3 35.2 %collective-permute-start.10 = (bf16[256,1024]{1,0:T(8,128)(2,1)}, bf16[256,1024]{1,0:T(8,128)(2,1)}, u32[]{:S(2)}, u32[]{:S(2)}) collective-permute-start(bf16[256,1024]{1,0:T(8,128)(2,1)} %collective-permute-done.9.refs_5_), channel_id=1, source_target_pairs={{0,4},{4,0},{8,12},{12,8},{16,20},{20,16},{24,28},{28,24},{1,5},{5... | collective-permute-start | bytes 1572872 | tf_op jit(solution)/shard_map/ppermute | solution.py:792
  108.7 15.5 %copy-start.1 = (bf16[256,1024]{1,0:T(8,128)(2,1)S(1)}, bf16[256,1024]{1,0:T(8,128)(2,1)}, u32[]{:S(2)}) copy-start(bf16[256,1024]{1,0:T(8,128)(2,1)} %refs_5_.1) | copy-start | bytes 1572868
  108.7 15.5 %copy-start.8 = (f32[128,1024]{1,0:T(8,128)S(1)}, f32[128,1024]{1,0:T(8,128)}, u32[]{:S(2)}) copy-start(f32[128,1024]{1,0:T(8,128)} %get-tuple-element.148.refs_6_.refs_13_) | copy-start | bytes 1572868
  108.7 15.5 %copy-start.12 = (bf16[256,256]{1,0:T(8,128)(2,1)S(1)}, bf16[256,256]{1,0:T(8,128)(2,1)}, u32[]{:S(2)}) copy-start(bf16[256,256]{1,0:T(8,128)(2,1)} %get-tuple-element.144.refs_0_) | copy-start | bytes 393220
  109.5 5.5 %collective-permute-start.16 = (bf16[256,256]{1,0:T(8,128)(2,1)}, bf16[256,256]{1,0:T(8,128)(2,1)S(1)}, u32[]{:S(2)}, u32[]{:S(2)}) collective-permute-start(bf16[256,256]{1,0:T(8,128)(2,1)} %get-tuple-element.145), channel_id=1, source_target_pairs={{0,1},{1,2},{2,3},{3,0},{4,5},{5,6},{6,7},{7,4},{8,9},{9,10},{10,1... | collective-permute-start | bytes 393224 | tf_op jit(solution)/shard_map/ppermute | solution.py:796
  109.5 11.8 %collective-permute-start.17 = (bf16[256,256]{1,0:T(8,128)(2,1)}, bf16[256,256]{1,0:T(8,128)(2,1)S(1)}, u32[]{:S(2)}, u32[]{:S(2)}) collective-permute-start(bf16[256,256]{1,0:T(8,128)(2,1)} %get-tuple-element.146), channel_id=1, source_target_pairs={{0,2},{1,3},{2,0},{3,1},{4,6},{5,7},{6,4},{7,5},{8,10},{9,11},{10,... | collective-permute-start | bytes 393224 | tf_op jit(solution)/shard_map/ppermute | solution.py:796
  111.4 12.8 %collective-permute-start.18 = (bf16[256,256]{1,0:T(8,128)(2,1)}, bf16[256,256]{1,0:T(8,128)(2,1)S(1)}, u32[]{:S(2)}, u32[]{:S(2)}) collective-permute-start(bf16[256,256]{1,0:T(8,128)(2,1)} %get-tuple-element.147), channel_id=1, source_target_pairs={{0,3},{1,0},{2,1},{3,2},{4,7},{5,4},{6,5},{7,6},{8,11},{9,8},{10,9... | collective-permute-start | bytes 393224 | tf_op jit(solution)/shard_map/ppermute | solution.py:796
  113.8 49.5 %collective-permute-start.22 = (bf16[4,128,1536]{2,1,0:T(8,128)(2,1)}, bf16[4,128,1536]{2,1,0:T(8,128)(2,1)}, u32[]{:S(2)}, u32[]{:S(2)}) collective-permute-start(bf16[4,128,1536]{2,1,0:T(8,128)(2,1)} %pad_maximum_fusion.refs_8_), channel_id=1, source_target_pairs={{0,16},{4,20},{8,24},{12,28},{16,0},{20,4},{24,8},{28,12},{1,17},{... | collective-permute-start | bytes 4718600 | tf_op jit(solution)/shard_map/ppermute | solution.py:792
  126.7 36.6 %copy-start.2 = (f32[256,1024]{1,0:T(8,128)}, f32[256,1024]{1,0:T(8,128)S(1)}, u32[]{:S(2)}) copy-start(f32[256,1024]{1,0:T(8,128)S(1)} %get-tuple-element.170.refs_3_) | copy-start | bytes 3145732
  126.7 13.9 %collective-permute-start.19 = (bf16[256,1024]{1,0:T(8,128)(2,1)S(1)}, bf16[256,1024]{1,0:T(8,128)(2,1)S(1)}, u32[]{:S(2)}, u32[]{:S(2)}) collective-permute-start(bf16[256,1024]{1,0:T(8,128)(2,1)S(1)} %get-tuple-element.149.refs_0_), channel_id=1, source_target_pairs={{0,8},{4,12},{8,0},{12,4},{16,24},{20,28},{24,16},{28,20},{1,9},{5... | collective-permute-start | bytes 1572872 | tf_op jit(solution)/shard_map/ppermute | solution.py:792
  127.9 10.1 %collective-permute-start.23 = (bf16[2,96,1024]{2,1,0:T(8,128)(2,1)S(1)}, bf16[2,96,1024]{2,1,0:T(8,128)(2,1)S(1)}, u32[]{:S(2)}, u32[]{:S(2)}) collective-permute-start(bf16[2,96,1024]{2,1,0:T(8,128)(2,1)S(1)} %bitcast.170), channel_id=1, source_target_pairs={{0,1},{1,2},{2,3},{3,0},{4,5},{5,6},{6,7},{7,4},{8,9},{9,10},{10,1... | collective-permute-start | bytes 1179656 | tf_op jit(solution)/shard_map/ppermute | solution.py:796
  128.0 33.3 %collective-permute-start.24 = (bf16[2,96,1024]{2,1,0:T(8,128)(2,1)S(1)}, bf16[2,96,1024]{2,1,0:T(8,128)(2,1)S(1)}, u32[]{:S(2)}, u32[]{:S(2)}) collective-permute-start(bf16[2,96,1024]{2,1,0:T(8,128)(2,1)S(1)} %bitcast.171), channel_id=1, source_target_pairs={{0,2},{1,3},{2,0},{3,1},{4,6},{5,7},{6,4},{7,5},{8,10},{9,11},{10,... | collective-permute-start | bytes 1179656 | tf_op jit(solution)/shard_map/ppermute | solution.py:796
  128.4 34.8 %collective-permute-start.25 = (bf16[2,96,1024]{2,1,0:T(8,128)(2,1)S(1)}, bf16[2,96,1024]{2,1,0:T(8,128)(2,1)S(1)}, u32[]{:S(2)}, u32[]{:S(2)}) collective-permute-start(bf16[2,96,1024]{2,1,0:T(8,128)(2,1)S(1)} %bitcast.172), channel_id=1, source_target_pairs={{0,3},{1,0},{2,1},{3,2},{4,7},{5,4},{6,5},{7,6},{8,11},{9,8},{10,9... | collective-permute-start | bytes 1179656 | tf_op jit(solution)/shard_map/ppermute | solution.py:796
  138.1 25.2 %collective-permute-start.20 = (bf16[256,1024]{1,0:T(8,128)(2,1)S(1)}, bf16[256,1024]{1,0:T(8,128)(2,1)S(1)}, u32[]{:S(2)}, u32[]{:S(2)}) collective-permute-start(bf16[256,1024]{1,0:T(8,128)(2,1)S(1)} %get-tuple-element.149.refs_0_), channel_id=1, source_target_pairs={{0,4},{4,0},{8,12},{12,8},{16,20},{20,16},{24,28},{28,24},{1,5},{5... | collective-permute-start | bytes 1572872 | tf_op jit(solution)/shard_map/ppermute | solution.py:792
  140.6 22.7 %collective-permute-start.21 = (bf16[256,1024]{1,0:T(8,128)(2,1)S(1)}, bf16[256,1024]{1,0:T(8,128)(2,1)S(1)}, u32[]{:S(2)}, u32[]{:S(2)}) collective-permute-start(bf16[256,1024]{1,0:T(8,128)(2,1)S(1)} %collective-permute-done.19.refs_1_), channel_id=1, source_target_pairs={{0,4},{4,0},{8,12},{12,8},{16,20},{20,16},{24,28},{28,24},{1,5},{5... | collective-permute-start | bytes 1572872 | tf_op jit(solution)/shard_map/ppermute | solution.py:792
  183.9 98.1 %reduce-scatter.6.cloned.1.call-start = ((), (), s32[]{:S(2)}) async-start(), calls=%async_computation.6 | async-start | bytes 2359296 | tf_op jit(solution)/shard_map/reduce_scatter | solution.py:1049
  184.4 5.7 %collective-permute-start.26 = (bf16[512,1024]{1,0:T(8,128)(2,1)}, bf16[512,1024]{1,0:T(8,128)(2,1)}, u32[]{:S(2)}, u32[]{:S(2)}) collective-permute-start(bf16[512,1024]{1,0:T(8,128)(2,1)} %get-tuple-element.160), channel_id=1, source_target_pairs={{0,4},{4,0},{8,12},{12,8},{16,20},{20,16},{24,28},{28,24},{1,5},{5... | collective-permute-start | bytes 3145736 | tf_op jit(solution)/shard_map/ppermute | solution.py:792
  192.1 36.2 %collective-permute-start.28 = (bf16[4,128,1536]{2,1,0:T(8,128)(2,1)}, bf16[4,128,1536]{2,1,0:T(8,128)(2,1)S(1)}, u32[]{:S(2)}, u32[]{:S(2)}) collective-permute-start(bf16[4,128,1536]{2,1,0:T(8,128)(2,1)} %bitcast.49), channel_id=1, source_target_pairs={{0,16},{4,20},{8,24},{12,28},{16,0},{20,4},{24,8},{28,12},{1,17},{... | collective-permute-start | bytes 4718600 | tf_op jit(solution)/shard_map/ppermute | solution.py:792
  193.4 13.5 %collective-permute-start.27 = (bf16[256,1024]{1,0:T(8,128)(2,1)}, bf16[256,1024]{1,0:T(8,128)(2,1)}, u32[]{:S(2)}, u32[]{:S(2)}) collective-permute-start(bf16[256,1024]{1,0:T(8,128)(2,1)} %add_convert_fusion), channel_id=1, source_target_pairs={{0,8},{4,12},{8,0},{12,4},{16,24},{20,28},{24,16},{28,20},{1,9},{5... | collective-permute-start | bytes 1572872 | tf_op jit(solution)/shard_map/ppermute | solution.py:792
  212.4 16.4 %collective-permute-start.29 = (bf16[256,256]{1,0:T(8,128)(2,1)}, bf16[256,256]{1,0:T(8,128)(2,1)S(1)}, u32[]{:S(2)}, u32[]{:S(2)}) collective-permute-start(bf16[256,256]{1,0:T(8,128)(2,1)} %get-tuple-element.172), channel_id=1, source_target_pairs={{0,1},{1,2},{2,3},{3,0},{4,5},{5,6},{6,7},{7,4},{8,9},{9,10},{10,1... | collective-permute-start | bytes 393224 | tf_op jit(solution)/shard_map/ppermute | solution.py:796
  212.5 16.3 %collective-permute-start.30 = (bf16[256,256]{1,0:T(8,128)(2,1)}, bf16[256,256]{1,0:T(8,128)(2,1)S(1)}, u32[]{:S(2)}, u32[]{:S(2)}) collective-permute-start(bf16[256,256]{1,0:T(8,128)(2,1)} %get-tuple-element.173), channel_id=1, source_target_pairs={{0,2},{1,3},{2,0},{3,1},{4,6},{5,7},{6,4},{7,5},{8,10},{9,11},{10,... | collective-permute-start | bytes 393224 | tf_op jit(solution)/shard_map/ppermute | solution.py:796
  214.6 14.2 %collective-permute-start.31 = (bf16[256,256]{1,0:T(8,128)(2,1)}, bf16[256,256]{1,0:T(8,128)(2,1)S(1)}, u32[]{:S(2)}, u32[]{:S(2)}) collective-permute-start(bf16[256,256]{1,0:T(8,128)(2,1)} %get-tuple-element.174), channel_id=1, source_target_pairs={{0,3},{1,0},{2,1},{3,2},{4,7},{5,4},{6,5},{7,6},{8,11},{9,8},{10,9... | collective-permute-start | bytes 393224 | tf_op jit(solution)/shard_map/ppermute | solution.py:796
  219.1 114.0 %reduce-scatter.8.cloned.1.call-start = ((), (), s32[]{:S(2)}) async-start(), calls=%async_computation.7 | async-start | bytes 2654208 | tf_op jit(solution)/shard_map/reduce_scatter | solution.py:1058
  230.6 49.8 %collective-permute-start.32 = (bf16[1,4,32,1536]{3,2,0,1:T(8,128)(2,1)S(1)}, bf16[1,4,32,1536]{3,2,0,1:T(8,128)(2,1)S(1)}, u32[]{:S(2)}, u32[]{:S(2)}) collective-permute-start(bf16[1,4,32,1536]{3,2,0,1:T(8,128)(2,1)S(1)} %get-tuple-element.237), channel_id=1, source_target_pairs={{0,1},{1,2},{2,3},{3,0},{4,5},{5,6},{6,7},{7,4},{8,9},{9,10},{10,1... | collective-permute-start | bytes 1179656 | tf_op jit(solution)/shard_map/ppermute | solution.py:796
  230.7 49.8 %collective-permute-start.33 = (bf16[1,4,32,1536]{3,2,0,1:T(8,128)(2,1)S(1)}, bf16[1,4,32,1536]{3,2,0,1:T(8,128)(2,1)S(1)}, u32[]{:S(2)}, u32[]{:S(2)}) collective-permute-start(bf16[1,4,32,1536]{3,2,0,1:T(8,128)(2,1)S(1)} %get-tuple-element.236), channel_id=1, source_target_pairs={{0,2},{1,3},{2,0},{3,1},{4,6},{5,7},{6,4},{7,5},{8,10},{9,11},{10,... | collective-permute-start | bytes 1179656 | tf_op jit(solution)/shard_map/ppermute | solution.py:796
  232.8 49.1 %collective-permute-start.34 = (bf16[1,4,32,1536]{3,2,0,1:T(8,128)(2,1)S(1)}, bf16[1,4,32,1536]{3,2,0,1:T(8,128)(2,1)}, u32[]{:S(2)}, u32[]{:S(2)}) collective-permute-start(bf16[1,4,32,1536]{3,2,0,1:T(8,128)(2,1)S(1)} %get-tuple-element.235), channel_id=1, source_target_pairs={{0,3},{1,0},{2,1},{3,2},{4,7},{5,4},{6,5},{7,6},{8,11},{9,8},{10,9... | collective-permute-start | bytes 1179656 | tf_op jit(solution)/shard_map/ppermute | solution.py:796
  282.0 53.0 %collective-permute-start.35 = (bf16[256,1024]{1,0:T(8,128)(2,1)S(1)}, bf16[256,1024]{1,0:T(8,128)(2,1)}, u32[]{:S(2)}, u32[]{:S(2)}) collective-permute-start(bf16[256,1024]{1,0:T(8,128)(2,1)S(1)} %get-tuple-element.204), channel_id=1, source_target_pairs={{0,1},{1,2},{2,3},{3,0},{4,5},{5,6},{6,7},{7,4},{8,9},{9,10},{10,1... | collective-permute-start | bytes 1572872 | tf_op jit(solution)/shard_map/ppermute | solution.py:796
  282.2 52.7 %collective-permute-start.36 = (bf16[256,1024]{1,0:T(8,128)(2,1)}, bf16[256,1024]{1,0:T(8,128)(2,1)}, u32[]{:S(2)}, u32[]{:S(2)}) collective-permute-start(bf16[256,1024]{1,0:T(8,128)(2,1)} %get-tuple-element.205), channel_id=1, source_target_pairs={{0,2},{1,3},{2,0},{3,1},{4,6},{5,7},{6,4},{7,5},{8,10},{9,11},{10,... | collective-permute-start | bytes 1572872 | tf_op jit(solution)/shard_map/ppermute | solution.py:796
  284.1 50.8 %collective-permute-start.37 = (bf16[256,1024]{1,0:T(8,128)(2,1)}, bf16[256,1024]{1,0:T(8,128)(2,1)}, u32[]{:S(2)}, u32[]{:S(2)}) collective-permute-start(bf16[256,1024]{1,0:T(8,128)(2,1)} %get-tuple-element.206), channel_id=1, source_target_pairs={{0,3},{1,0},{2,1},{3,2},{4,7},{5,4},{6,5},{7,6},{8,11},{9,8},{10,9... | collective-permute-start | bytes 1572872 | tf_op jit(solution)/shard_map/ppermute | solution.py:796
  287.5 18.9 %collective-permute-start.38 = (bf16[512,1024]{1,0:T(8,128)(2,1)}, bf16[512,1024]{1,0:T(8,128)(2,1)}, u32[]{:S(2)}, u32[]{:S(2)}) collective-permute-start(bf16[512,1024]{1,0:T(8,128)(2,1)} %convolution_convert_fusion.2), channel_id=1, source_target_pairs={{0,4},{4,0},{8,12},{12,8},{16,20},{20,16},{24,28},{28,24},{1,5},{5... | collective-permute-start | bytes 3145736 | tf_op jit(solution)/shard_map/ppermute | solution.py:792
  291.2 1.4 collective-permute-start.43
  292.6 4.3 %collective-permute-start.44 = (bf16[32,1536]{1,0:T(8,128)(2,1)S(1)}, bf16[32,1536]{1,0:T(8,128)(2,1)S(1)}, u32[]{:S(2)}, u32[]{:S(2)}) collective-permute-start(bf16[32,1536]{1,0:T(8,128)(2,1)S(1)} %get-tuple-element.241), channel_id=1, source_target_pairs={{0,8},{4,12},{8,0},{12,4},{16,24},{20,28},{24,16},{28,20},{1,9},{5... | collective-permute-start | bytes 294920 | tf_op jit(solution)/shard_map/ppermute | solution.py:792
  296.9 5.3 %collective-permute-start.45 = (bf16[32,1536]{1,0:T(8,128)(2,1)S(1)}, bf16[32,1536]{1,0:T(8,128)(2,1)S(1)}, u32[]{:S(2)}, u32[]{:S(2)}) collective-permute-start(bf16[32,1536]{1,0:T(8,128)(2,1)S(1)} %get-tuple-element.240), channel_id=1, source_target_pairs={{0,12},{4,8},{8,4},{12,0},{16,28},{20,24},{24,20},{28,16},{1,13},{... | collective-permute-start | bytes 294920 | tf_op jit(solution)/shard_map/ppermute | solution.py:792
  302.2 10.8 %collective-permute-start.46 = (bf16[1,96,1024]{2,1,0:T(8,128)(2,1)}, bf16[1,96,1024]{2,1,0:T(8,128)(2,1)}, u32[]{:S(2)}, u32[]{:S(2)}) collective-permute-start(bf16[1,96,1024]{2,1,0:T(8,128)(2,1)} %constant_dynamic-slice_fusion), channel_id=1, source_target_pairs={{0,16},{4,20},{8,24},{12,28},{16,0},{20,4},{24,8},{28,12},{1,17},{... | collective-permute-start | bytes 589832 | tf_op jit(solution)/shard_map/ppermute | solution.py:792
  309.1 17.4 %collective-permute-start.39 = (bf16[256,1024]{1,0:T(8,128)(2,1)}, bf16[256,1024]{1,0:T(8,128)(2,1)}, u32[]{:S(2)}, u32[]{:S(2)}) collective-permute-start(bf16[256,1024]{1,0:T(8,128)(2,1)} %fusion.14), channel_id=1, source_target_pairs={{0,8},{4,12},{8,0},{12,4},{16,24},{20,28},{24,16},{28,20},{1,9},{5... | collective-permute-start | bytes 1572872 | tf_op jit(solution)/shard_map/ppermute | solution.py:792
  311.1 15.4 %copy-start.3 = (f32[256,1024]{1,0:T(8,128)S(1)}, f32[256,1024]{1,0:T(8,128)}, u32[]{:S(2)}) copy-start(f32[256,1024]{1,0:T(8,128)} %copy-done.2) | copy-start | bytes 3145732
  314.7 18.4 %copy-start.29 = (bf16[128,1024]{1,0:T(8,128)(2,1)S(1)}, bf16[128,1024]{1,0:T(8,128)(2,1)}, u32[]{:S(2)}) copy-start(bf16[128,1024]{1,0:T(8,128)(2,1)} %reduce-scatter.6.cloned.1.call-done) | copy-start | bytes 786436
  334.2 6.3 %copy-start.18 = (f32[256,1024]{1,0:T(8,128)S(1)}, f32[256,1024]{1,0:T(8,128)}, u32[]{:S(2)}) copy-start(f32[256,1024]{1,0:T(8,128)} %get-tuple-element.211) | copy-start | bytes 3145732
  334.9 8.4 %collective-permute-start.40 = (bf16[1,32,2176]{2,1,0:T(8,128)(2,1)S(1)}, bf16[1,32,2176]{2,1,0:T(8,128)(2,1)S(1)}, u32[]{:S(2)}, u32[]{:S(2)}) collective-permute-start(bf16[1,32,2176]{2,1,0:T(8,128)(2,1)S(1)} %get-tuple-element.245), channel_id=1, source_target_pairs={{0,1},{1,2},{2,3},{3,0},{4,5},{5,6},{6,7},{7,4},{8,9},{9,10},{10,1... | collective-permute-start | bytes 417800 | tf_op jit(solution)/shard_map/ppermute | solution.py:796
  336.2 11.3 %collective-permute-start.41 = (bf16[1,32,2176]{2,1,0:T(8,128)(2,1)S(1)}, bf16[1,32,2176]{2,1,0:T(8,128)(2,1)S(1)}, u32[]{:S(2)}, u32[]{:S(2)}) collective-permute-start(bf16[1,32,2176]{2,1,0:T(8,128)(2,1)S(1)} %get-tuple-element.244), channel_id=1, source_target_pairs={{0,2},{1,3},{2,0},{3,1},{4,6},{5,7},{6,4},{7,5},{8,10},{9,11},{10,... | collective-permute-start | bytes 417800 | tf_op jit(solution)/shard_map/ppermute | solution.py:796
  337.3 13.1 %collective-permute-start.42 = (bf16[1,32,2176]{2,1,0:T(8,128)(2,1)S(1)}, bf16[1,32,2176]{2,1,0:T(8,128)(2,1)S(1)}, u32[]{:S(2)}, u32[]{:S(2)}) collective-permute-start(bf16[1,32,2176]{2,1,0:T(8,128)(2,1)S(1)} %get-tuple-element.243), channel_id=1, source_target_pairs={{0,3},{1,0},{2,1},{3,2},{4,7},{5,4},{6,5},{7,6},{8,11},{9,8},{10,9... | collective-permute-start | bytes 417800 | tf_op jit(solution)/shard_map/ppermute | solution.py:796
  343.3 7.1 %copy-start.33 = (bf16[1,32,2176]{2,1,0:T(8,128)(2,1)}, bf16[1,32,2176]{2,1,0:T(8,128)(2,1)S(1)}, u32[]{:S(2)}) copy-start(bf16[1,32,2176]{2,1,0:T(8,128)(2,1)S(1)} %collective-permute-done.40) | copy-start | bytes 417796
  (29 other events, 85.8 us)
Sparse Core Ops, SparseCore 0:
  35.2 38.7 all-gather.2
  76.5 28.0 all-gather.4
  184.0 33.1 reduce-scatter.3
  220.3 47.5 reduce-scatter.5
  284.5 48.6 reduce-scatter.7

commit v6 on v5

--- a/solution.py
+++ b/solution.py
@@ -962,24 +962,6 @@
     cot_pieces = gather_cube(own_cotangent, tp_bits[::-1], n_dp)
     cot_pieces, blocks = lax.optimization_barrier((cot_pieces, blocks))
 
-    def collect(left, right, dims):
-        arrived = []
-        keep = TP
-
-        def term(lo, hi):
-            value = lax.dot_general(
-                left[lo * own_rows : hi * own_rows], right, (dims, ((), ())), preferred_element_type=WIDE
-            )
-            for earlier in arrived:
-                value = value + earlier[lo * own_rows : hi * own_rows].astype(WIDE)
-            return value
-
-        for bit in tp_bits:
-            keep //= 2
-            sent = yield term(keep, 2 * keep).astype(NARROW)
-            arrived.append(flip(sent, bit, n_dp))
-        yield term(0, 1)
-
     def halve(value, index, some_bits):
         unit = some_bits[0] if some_bits else 1
         for bit in some_bits[::-1]:
@@ -1037,14 +1019,23 @@
     from_side = flip(second, tp_bits[1], n_dp)
     from_side, ffn_near, active_late = lax.optimization_barrier((from_side, ffn_near, active_late))
     both_sum = both_part(top * split if rest_bits else 0, split)
-    if rest_bits:
-        both_sum = both_sum + flip(both_sent, rest_bits[-1], n_dp).astype(WIDE)
-        both_sum = halve(both_sum, block, rest_bits[:-1])
 
     d_blocks, d_middle, d_branch, d_gffn = mix_back(
         z_ref, (d_own, from_core, from_side), middle, side, gain_row, cotangent, full_out, n_fs
     )
     d_pieces = pass_on(d_blocks)
+    d_branch, active_late = lax.optimization_barrier((d_branch, active_late))
+
+    def out_term(units, lo):
+        return project(units[lo * own_rows : (lo + 1) * own_rows], w_down)
+
+    out_core = flip(project(active_late[2 * own_rows :], w_down).astype(NARROW), tp_bits[0], n_dp)
+    out_sent = (out_term(active_late, 1) + out_core[own_rows:].astype(WIDE)).astype(NARROW)
+    if rest_bits:
+        both_came, out_sent = lax.optimization_barrier((flip(both_sent, rest_bits[-1], n_dp), out_sent))
+        both_sum = both_sum + both_came.astype(WIDE)
+        both_sum = halve(both_sum, block, rest_bits[:-1])
+    out_side = flip(out_sent, tp_bits[1], n_dp)
     out_grad = weight_grad(normed_b, d_branch).astype(NARROW)
     sum_out = lax.psum_scatter(out_grad, "dp", scatter_dimension=0, tiled=True)
     both_sum = jnp.swapaxes(both_sum.reshape(TP, n_fs, rows, 2 * ff_pad), 0, 1)
@@ -1058,8 +1049,8 @@
     part = lax.psum_scatter(grad_in, "dp", scatter_dimension=0, tiled=True)
     d_blocks, both_line, active_late = lax.optimization_barrier((d_blocks, both_line, active_late))
     d_blocks = pass_on(d_blocks)
-    out_terms = collect(active_late, w_down, ((1,), (0,)))
-    layer_out = (middle + out_terms.send(out_terms.send(next(out_terms)))).astype(NARROW)
+    layer_out = middle + out_term(active_late, 0) + out_core[:own_rows].astype(WIDE) + out_side.astype(WIDE)
+    layer_out = layer_out.astype(NARROW)
     both_sum = sum_up(both_line, both_sum)
     grad_fdown = halve(down_sum, block, rest_bits)[0, :ff_line].astype(WIDE)
     both_pieces = {

time: 365 us -> 363 us (level)
    ppermute x20, waiting for transfers between devices: 45.2 us -> 21.6 us  [flip(): return lax.ppermute(value, 'dp', [(i, i ^ bit) for i in range(n_dp)])]
    reduce_scatter x1, waiting for transfers between devices: 3.24 us -> 25.9 us  [per_device(): part = lax.psum_scatter(grad_in, 'dp', scatter_dimension=0, tiled=True)]
    unnamed x90 -> x86, local copies, waits for them, and re-layouts: 14.1 us -> 14.5 us
  transfers between devices with their start and end apart: 52 -> 52, of which waited for: 20 -> 17; matrix products, arithmetic and copies ran while one was open for 16% -> 15% of each run, Pallas kernels for 24% -> 24%
where the time goes in v6:
time: 363 us; the launch traced here: 357 us
  waiting for transfers between devices  121 us (33%)
  Pallas kernels  102 us (28%)
  starting transfers between devices  49.7 us (14%)
  local copies, waits for them, and re-layouts  28.2 us (8%)
  matrix products  22.8 us (6%)
  other arithmetic  18.6 us (5%)
  between operations  15 us (4%)
    ppermute x27, waiting for transfers between devices, shift(): lax.ppermute(value, 'fsdp', [(i, (i + by) % n_fs) for i in range(n_fs)])  73.8 us
    pallas_call x1, Pallas kernels, delta_backward(): pl.pallas_call(functools.partial(backward_kernel, heads, width, n_fs, sha...  45.6 us
    pallas_call x1, Pallas kernels, delta_forward(): pl.pallas_call(functools.partial(forward_kernel, heads, width, n_fs, shar...  33 us
    reduce_scatter x1, waiting for transfers between devices, per_device(): part = lax.psum_scatter(grad_in, 'dp', scatter_dimension=0, tiled=True)  25.9 us
    ppermute x27, starting transfers between devices, shift(): lax.ppermute(value, 'fsdp', [(i, (i + by) % n_fs) for i in range(n_fs)])  25.7 us
    ppermute x20, starting transfers between devices, flip(): return lax.ppermute(value, 'dp', [(i, i ^ bit) for i in range(n_dp)])  23.3 us
    ppermute x20, waiting for transfers between devices, flip(): return lax.ppermute(value, 'dp', [(i, i ^ bit) for i in range(n_dp)])  21.6 us
    unnamed x86, local copies, waits for them, and re-layouts  14.5 us
  transfers between devices with their start and end apart: 52, of which 17 were waited for; matrix products, arithmetic and copies ran while one was open for 15% of the time, Pallas kernels for 24%

profile of v6, /device:TPU:9, one launch (start us, length us, event | category | flops | bytes accessed | tf_op | source)
XLA Modules:
  0.0 357.4 jit_solution(9969387671720626915)
XLA Ops:
  7.3 1.3 collective-permute-start.3
  16.0 1.3 collective-permute-start
  18.6 4.7 %collective-permute-done = bf16[1,32,2176]{2,1,0:T(8,128)(2,1)S(1)} collective-permute-done((bf16[1,32,2176]{2,1,0:T(8,128)(2,1)S(1)}, bf16[1,32,2176]{2,1,0:T(8,128)(2,1)S(1)}, u32[]{:S(2)}, u32[]{:S(2)}) %collective-permute-start) | collective-permute-done | bytes 139296 | tf_op jit(solution)/shard_map/ppermute | solution.py:796
  23.3 8.0 %collective-permute-done.1 = bf16[1,32,2176]{2,1,0:T(8,128)(2,1)S(1)} collective-permute-done((bf16[1,32,2176]{2,1,0:T(8,128)(2,1)S(1)}, bf16[1,32,2176]{2,1,0:T(8,128)(2,1)S(1)}, u32[]{:S(2)}, u32[]{:S(2)}) %collective-permute-start.1) | collective-permute-done | bytes 139296 | tf_op jit(solution)/shard_map/ppermute | solution.py:796
  31.3 2.9 collective-permute-done.2
  42.2 1.7 collective-permute-start.4
  43.9 1.2 collective-permute-start.5
  45.8 1.3 collective-permute-start.7
  47.1 3.5 collective-permute-done.5
  50.7 3.1 collective-permute-done.6
  53.8 1.2 collective-permute-start.9
  56.4 1.2 fusion.25.refs_5_
  58.5 11.7 %collective-permute-done.11.refs_2_ = bf16[256,1024]{1,0:T(8,128)(2,1)} collective-permute-done((bf16[256,1024]{1,0:T(8,128)(2,1)S(1)}, bf16[256,1024]{1,0:T(8,128)(2,1)}, u32[]{:S(2)}, u32[]{:S(2)}) %collective-permute-start.11) | collective-permute-done | bytes 524320 | tf_op jit(solution)/shard_map/ppermute | solution.py:796
  70.3 3.2 collective-permute-start.14
  73.5 1.7 collective-permute-start.15
  75.1 1.3 collective-permute-start.10
  76.5 33.0 %delta_forward.1 = (bf16[256,256]{1,0:T(8,128)(2,1)}, bf16[256,256]{1,0:T(8,128)(2,1)}, bf16[256,256]{1,0:T(8,128)(2,1)}, bf16[256,256]{1,0:T(8,128)(2,1)}, f32[...) custom-call(bf16[256,1024]{1,0:T(8,128)(2,1)} %refs_5_.1, ...), custom_call_target="tpu_custom_call" | custom-call | flops 30000001024 | bytes 16777216 | tf_op jit(solution)/shard_map/delta_forward/pallas_call | solution.py:497
  109.7 1.9 collective-permute-start.17
  111.6 2.4 pad_maximum_fusion.refs_8_
  114.0 1.2 collective-permute-start.22
  115.2 6.3 %collective-permute-done.17.refs_2_ = bf16[256,256]{1,0:T(8,128)(2,1)S(1)} collective-permute-done((bf16[256,256]{1,0:T(8,128)(2,1)}, bf16[256,256]{1,0:T(8,128)(2,1)S(1)}, u32[]{:S(2)}, u32[]{:S(2)}) %collective-permute-start.17) | collective-permute-done | bytes 131104 | tf_op jit(solution)/shard_map/ppermute | solution.py:796
  121.4 2.9 collective-permute-done.18.refs_3_
  124.3 1.6 copy-done.9
  126.8 1.3 collective-permute-start.19
  128.5 1.5 collective-permute-start.25
  130.3 7.9 %collective-permute-done.23 = bf16[2,96,1024]{2,1,0:T(8,128)(2,1)S(1)} collective-permute-done((bf16[2,96,1024]{2,1,0:T(8,128)(2,1)S(1)}, bf16[2,96,1024]{2,1,0:T(8,128)(2,1)S(1)}, u32[]{:S(2)}, u32[]{:S(2)}) %collective-permute-start.23) | collective-permute-done | bytes 393248 | tf_op jit(solution)/shard_map/ppermute | solution.py:796
  138.2 2.5 collective-permute-start.20
  141.2 20.3 %collective-permute-done.24 = bf16[2,96,1024]{2,1,0:T(8,128)(2,1)S(1)} collective-permute-done((bf16[2,96,1024]{2,1,0:T(8,128)(2,1)S(1)}, bf16[2,96,1024]{2,1,0:T(8,128)(2,1)S(1)}, u32[]{:S(2)}, u32[]{:S(2)}) %collective-permute-start.24) | collective-permute-done | bytes 393248 | tf_op jit(solution)/shard_map/ppermute | solution.py:796
  161.5 1.8 collective-permute-done.25
  164.7 14.4 %ffn_units.1 = (bf16[1024,768]{1,0:T(8,128)(2,1)}, bf16[1024,1536]{1,0:T(8,128)(2,1)}, bf16[512,1024]{1,0:T(8,128)(2,1)}, f32[256,1024]{1,0:T(8,128)}, f32[256,1024]{1,0:T(8,128)}) custom-call(s32[2]{0:T(128)S(1)} %pad_add_fusion.1.block_ref, bf16[256,1024]{1,0:T(8,128)(2,1)S(1)} %get-tuple-element.153.refs_0_, ...), custom_call_target="tpu_custom_call" | custom-call | flops 8000000000 | bytes 16777216 | tf_op jit(solution)/shard_map/ffn_units/pallas_call | solution.py:686
  179.0 5.0 %fusion.8 = bf16[768,1024]{1,0:T(8,128)(2,1)} fusion(bf16[1024,768]{1,0:T(8,128)(2,1)} %get-tuple-element.216, bf16[256,1024]{1,0:T(8,128)(2,1)} %collective-permute-done.10.refs_7_, bf16[256,1024]{1,0:T(8,128)(2,1)} %collective-permute-done.8.refs_6_, bf16[256,1024]{1,0:T(8,128)(2,1)} %collective-permute-done.9.refs_5_, bf16[256,1024]{1,0:T(8,128)(2,1)} %refs_4_.2), kind=kOutput, calls=%fused_computation.11 | convolution fusion | flops 1619787776 | bytes 5242880 | tf_op jit(solution)/shard_map/dot_general | solution.py:788
  185.4 2.5 copy-done.38
  187.8 3.0 convolution_convert_fusion
  190.8 1.2 add_convert_fusion
  192.5 1.2 collective-permute-start.28
  193.7 12.0 %collective-permute-done.27.refs_2_ = bf16[256,1024]{1,0:T(8,128)(2,1)S(1)} collective-permute-done((bf16[256,1024]{1,0:T(8,128)(2,1)S(1)}, bf16[256,1024]{1,0:T(8,128)(2,1)S(1)}, u32[]{:S(2)}, u32[]{:S(2)}) %collective-permute-start.27) | collective-permute-done | bytes 524320 | tf_op jit(solution)/shard_map/ppermute | solution.py:792
  206.5 5.7 %mix_back.1 = (bf16[256,256]{1,0:T(8,128)(2,1)}, bf16[256,256]{1,0:T(8,128)(2,1)}, bf16[256,256]{1,0:T(8,128)(2,1)}, bf16[256,256]{1,0:T(8,128)(2,1)}, f32[256,1...) custom-call(s32[1]{0:T(128)} %bitcast.1.refs_11_.z_ref, f32[256,1024]{1,0:T(8,128)} %get-tuple-element.172.refs_0_, ...), custom_call_target="tpu_custom_call" | custom-call | flops 2000000000 | bytes 6291456 | tf_op jit(solution)/shard_map/mix_back/pallas_call | solution.py:744
  212.2 3.2 convolution_convert_fusion.2
  216.9 2.0 collective-permute-start.31
  219.0 1.5 collective-permute-start.32
  220.4 2.1 convolution_convert_fusion.1
  222.6 4.1 %fusion.18 = f32[512,1536]{1,0:T(8,128)S(1)} fusion(bf16[1024,1536]{1,0:T(8,128)(2,1)} %get-tuple-element.167, bf16[1024,1024]{1,0:T(8,128)(2,1)} %copy-done.33, s32[]{:T(128)S(6)} %select_n.142), kind=kOutput, calls=%fused_computation.28 | convolution fusion | flops 1610612736 | bytes 7340036 | tf_op jit(solution)/shard_map/dot_general | solution.py:788
  226.7 2.7 fusion.13
  229.3 2.0 convert_add_fusion
  231.8 1.2 copy-done.13
  233.2 2.1 collective-permute-start.34
  237.1 45.6 %delta_backward.1 = (bf16[1024,1152]{1,0:T(8,128)(2,1)}, bf16[256,1024]{1,0:T(8,128)(2,1)S(1)}, bf16[256,1024]{1,0:T(8,128)(2,1)S(1)}, bf16[256,1024]{1,0:T(8,128)(2,1)}, bf16[256,1024]{1,0:T(8,128)(2,1)}) custom-call(bf16[256,256]{1,0:T(8,128)(2,1)S(1)} %copy-done.10, bf16[256,256]{1,0:T(8,128)(2,1)S(1)} %collective-permute-done.30.refs_1_, ...), custom_call_target="tpu_custom_call" | custom-call | flops 40000000000 | bytes 16777216 | tf_op jit(solution)/shard_map/delta_backward/pallas_call | solution.py:525
  283.5 2.3 collective-permute-start.37
  286.0 1.6 convert_add_fusion.1
  287.7 2.7 collective-permute-start.43
  291.4 2.8 fusion.14
  295.2 1.3 collective-permute-start.46
  296.5 2.9 collective-permute-done.45
  300.1 1.2 reshape.287
  301.9 1.2 reshape.289
  303.1 1.7 add_bitcast_fusion
  304.8 25.9 %reduce-scatter.8.cloned.1.call-done = bf16[128,1152]{1,0:T(8,128)(2,1)} async-done(((bf16[1024,1152]{1,0:T(8,128)(2,1)}), bf16[128,1152]{1,0:T(8,128)(2,1)}) %reduce-scatter.8.cloned.1.call-update) | async-done | bytes 294928 | tf_op jit(solution)/shard_map/reduce_scatter | solution.py:1049
  332.4 1.3 collective-permute-start.40
  334.8 1.2 collective-permute-start.42
  336.1 1.9 fusion.15
  338.0 2.8 fusion.17
  340.8 4.2 %collective-permute-done.41 = bf16[1,32,2176]{2,1,0:T(8,128)(2,1)S(1)} collective-permute-done((bf16[1,32,2176]{2,1,0:T(8,128)(2,1)S(1)}, bf16[1,32,2176]{2,1,0:T(8,128)(2,1)S(1)}, u32[]{:S(2)}, u32[]{:S(2)}) %collective-permute-start.41) | collective-permute-done | bytes 139296 | tf_op jit(solution)/shard_map/ppermute | solution.py:796
  345.0 2.9 collective-permute-done.42
  348.6 2.0 finish_inputs.1
  (229 shorter events, 37.0 us)
Async XLA Ops:
  7.2 28.7 %copy-start = (bf16[256,1024]{1,0:T(8,128)(2,1)S(1)}, bf16[256,1024]{1,0:T(8,128)(2,1)}, u32[]{:S(2)}) copy-start(bf16[256,1024]{1,0:T(8,128)(2,1)} %refs_5_.1) | copy-start | bytes 1572868
  7.2 29.3 %copy-start.34 = (s32[1,1024]{1,0:T(1,128)S(1)}, s32[1,1024]{1,0:T(1,128)}, u32[]{:S(2)}) copy-start(s32[1,1024]{1,0:T(1,128)} %param.19) | copy-start | bytes 12292
  7.2 29.5 %copy-start.35 = (s32[1,4]{1,0:T(1,128)S(1)}, s32[1,4]{1,0:T(1,128)}, u32[]{:S(2)}) copy-start(s32[1,4]{1,0:T(1,128)} %param.18) | copy-start | bytes 52
  7.2 69.3 %all-gather.3.cloned.1.call-start = ((), (), s32[]{:S(2)}) async-start(), calls=%async_computation.3 | async-start | bytes 2654208 | tf_op jit(solution)/shard_map/all_gather | solution.py:919
  7.3 26.9 %collective-permute-start.3 = (bf16[256,1024]{1,0:T(8,128)(2,1)}, bf16[256,1024]{1,0:T(8,128)(2,1)S(1)}, u32[]{:S(2)}, u32[]{:S(2)}) collective-permute-start(bf16[256,1024]{1,0:T(8,128)(2,1)} %refs_5_.1), channel_id=1, source_target_pairs={{0,1},{1,2},{2,3},{3,0},{4,5},{5,6},{6,7},{7,4},{8,9},{9,10},{10,1... | collective-permute-start | bytes 1572872 | tf_op jit(solution)/shard_map/ppermute | solution.py:796
  15.9 24.2 %copy-start.27 = (bf16[32,2816]{1,0:T(8,128)(2,1)S(1)}, bf16[32,2816]{1,0:T(8,128)(2,1)}, u32[]{:S(2)}) copy-start(bf16[32,2816]{1,0:T(8,128)(2,1)} %param.30) | copy-start | bytes 540676
  16.0 7.3 %collective-permute-start = (bf16[1,32,2176]{2,1,0:T(8,128)(2,1)S(1)}, bf16[1,32,2176]{2,1,0:T(8,128)(2,1)S(1)}, u32[]{:S(2)}, u32[]{:S(2)}) collective-permute-start(bf16[1,32,2176]{2,1,0:T(8,128)(2,1)S(1)} %get-tuple-element.257), channel_id=1, source_target_pairs={{0,1},{1,2},{2,3},{3,0},{4,5},{5,6},{6,7},{7,4},{8,9},{9,10},{10,1... | collective-permute-start | bytes 417800 | tf_op jit(solution)/shard_map/ppermute | solution.py:796
  17.3 14.0 %collective-permute-start.1 = (bf16[1,32,2176]{2,1,0:T(8,128)(2,1)S(1)}, bf16[1,32,2176]{2,1,0:T(8,128)(2,1)S(1)}, u32[]{:S(2)}, u32[]{:S(2)}) collective-permute-start(bf16[1,32,2176]{2,1,0:T(8,128)(2,1)S(1)} %get-tuple-element.256), channel_id=1, source_target_pairs={{0,2},{1,3},{2,0},{3,1},{4,6},{5,7},{6,4},{7,5},{8,10},{9,11},{10,... | collective-permute-start | bytes 417800 | tf_op jit(solution)/shard_map/ppermute | solution.py:796
  18.3 15.9 %collective-permute-start.2 = (bf16[1,32,2176]{2,1,0:T(8,128)(2,1)S(1)}, bf16[1,32,2176]{2,1,0:T(8,128)(2,1)S(1)}, u32[]{:S(2)}, u32[]{:S(2)}) collective-permute-start(bf16[1,32,2176]{2,1,0:T(8,128)(2,1)S(1)} %get-tuple-element.255), channel_id=1, source_target_pairs={{0,3},{1,0},{2,1},{3,2},{4,7},{5,4},{6,5},{7,6},{8,11},{9,8},{10,9... | collective-permute-start | bytes 417800 | tf_op jit(solution)/shard_map/ppermute | solution.py:796
  35.9 79.3 %all-gather.5.cloned.1.call-start = ((), (), s32[]{:S(2)}) async-start(), calls=%async_computation.4 | async-start | bytes 2359296 | tf_op jit(solution)/shard_map/all_gather | solution.py:920
  35.9 34.3 %collective-permute-start.11 = (bf16[256,1024]{1,0:T(8,128)(2,1)S(1)}, bf16[256,1024]{1,0:T(8,128)(2,1)}, u32[]{:S(2)}, u32[]{:S(2)}) collective-permute-start(bf16[256,1024]{1,0:T(8,128)(2,1)S(1)} %copy-done), channel_id=1, source_target_pairs={{0,2},{1,3},{2,0},{3,1},{4,6},{5,7},{6,4},{7,5},{8,10},{9,11},{10,... | collective-permute-start | bytes 1572872 | tf_op jit(solution)/shard_map/ppermute | solution.py:796
  36.2 34.0 %collective-permute-start.12 = (bf16[256,1024]{1,0:T(8,128)(2,1)S(1)}, bf16[256,1024]{1,0:T(8,128)(2,1)}, u32[]{:S(2)}, u32[]{:S(2)}) collective-permute-start(bf16[256,1024]{1,0:T(8,128)(2,1)S(1)} %copy-done), channel_id=1, source_target_pairs={{0,3},{1,0},{2,1},{3,2},{4,7},{5,4},{6,5},{7,6},{8,11},{9,8},{10,9... | collective-permute-start | bytes 1572872 | tf_op jit(solution)/shard_map/ppermute | solution.py:796
  42.2 3.6 %collective-permute-start.4 = (bf16[32,1536]{1,0:T(8,128)(2,1)S(1)}, bf16[32,1536]{1,0:T(8,128)(2,1)S(1)}, u32[]{:S(2)}, u32[]{:S(2)}) collective-permute-start(bf16[32,1536]{1,0:T(8,128)(2,1)S(1)} %get-tuple-element.261), channel_id=1, source_target_pairs={{0,4},{4,0},{8,12},{12,8},{16,20},{20,16},{24,28},{28,24},{1,5},{5... | collective-permute-start | bytes 294920 | tf_op jit(solution)/shard_map/ppermute | solution.py:792
  43.9 6.8 %collective-permute-start.5 = (bf16[32,1536]{1,0:T(8,128)(2,1)S(1)}, bf16[32,1536]{1,0:T(8,128)(2,1)S(1)}, u32[]{:S(2)}, u32[]{:S(2)}) collective-permute-start(bf16[32,1536]{1,0:T(8,128)(2,1)S(1)} %get-tuple-element.260), channel_id=1, source_target_pairs={{0,8},{4,12},{8,0},{12,4},{16,24},{20,28},{24,16},{28,20},{1,9},{5... | collective-permute-start | bytes 294920 | tf_op jit(solution)/shard_map/ppermute | solution.py:792
  45.1 8.7 %collective-permute-start.6 = (bf16[32,1536]{1,0:T(8,128)(2,1)S(1)}, bf16[32,1536]{1,0:T(8,128)(2,1)S(1)}, u32[]{:S(2)}, u32[]{:S(2)}) collective-permute-start(bf16[32,1536]{1,0:T(8,128)(2,1)S(1)} %get-tuple-element.259), channel_id=1, source_target_pairs={{0,12},{4,8},{8,4},{12,0},{16,28},{20,24},{24,20},{28,16},{1,13},{... | collective-permute-start | bytes 294920 | tf_op jit(solution)/shard_map/ppermute | solution.py:792
  45.8 8.0 %collective-permute-start.7 = (bf16[96,1024]{1,0:T(8,128)(2,1)S(1)}, bf16[96,1024]{1,0:T(8,128)(2,1)S(1)}, u32[]{:S(2)}, u32[]{:S(2)}) collective-permute-start(bf16[96,1024]{1,0:T(8,128)(2,1)S(1)} %get-tuple-element.262), channel_id=1, source_target_pairs={{0,16},{4,20},{8,24},{12,28},{16,0},{20,4},{24,8},{28,12},{1,17},{... | collective-permute-start | bytes 589832 | tf_op jit(solution)/shard_map/ppermute | solution.py:792
  53.8 21.3 %collective-permute-start.9 = (bf16[256,1024]{1,0:T(8,128)(2,1)}, bf16[256,1024]{1,0:T(8,128)(2,1)}, u32[]{:S(2)}, u32[]{:S(2)}) collective-permute-start(bf16[256,1024]{1,0:T(8,128)(2,1)} %refs_4_.2), channel_id=1, source_target_pairs={{0,8},{4,12},{8,0},{12,4},{16,24},{20,28},{24,16},{28,20},{1,9},{5... | collective-permute-start | bytes 1572872 | tf_op jit(solution)/shard_map/ppermute | solution.py:792
  55.7 227.7 %reduce-scatter.4.cloned.1.call-start = ((), (), s32[]{:S(2)}) async-start(), calls=%async_computation.5 | async-start | bytes 1966080 | tf_op jit(solution)/shard_map/reduce_scatter | solution.py:1006
  57.7 51.9 %collective-permute-start.8 = (bf16[256,1024]{1,0:T(8,128)(2,1)}, bf16[256,1024]{1,0:T(8,128)(2,1)}, u32[]{:S(2)}, u32[]{:S(2)}) collective-permute-start(bf16[256,1024]{1,0:T(8,128)(2,1)} %refs_4_.2), channel_id=1, source_target_pairs={{0,4},{4,0},{8,12},{12,8},{16,20},{20,16},{24,28},{28,24},{1,5},{5... | collective-permute-start | bytes 1572872 | tf_op jit(solution)/shard_map/ppermute | solution.py:792
  70.3 39.3 %collective-permute-start.13 = (bf16[4,32,1536]{2,1,0:T(8,128)(2,1)S(1)}, bf16[4,32,1536]{2,1,0:T(8,128)(2,1)S(1)}, u32[]{:S(2)}, u32[]{:S(2)}) collective-permute-start(bf16[4,32,1536]{2,1,0:T(8,128)(2,1)S(1)} %bitcast.166), channel_id=1, source_target_pairs={{0,1},{1,2},{2,3},{3,0},{4,5},{5,6},{6,7},{7,4},{8,9},{9,10},{10,1... | collective-permute-start | bytes 1179656 | tf_op jit(solution)/shard_map/ppermute | solution.py:796
  70.3 39.3 %collective-permute-start.14 = (bf16[4,32,1536]{2,1,0:T(8,128)(2,1)S(1)}, bf16[4,32,1536]{2,1,0:T(8,128)(2,1)S(1)}, u32[]{:S(2)}, u32[]{:S(2)}) collective-permute-start(bf16[4,32,1536]{2,1,0:T(8,128)(2,1)S(1)} %bitcast.167), channel_id=1, source_target_pairs={{0,2},{1,3},{2,0},{3,1},{4,6},{5,7},{6,4},{7,5},{8,10},{9,11},{10,... | collective-permute-start | bytes 1179656 | tf_op jit(solution)/shard_map/ppermute | solution.py:796
  73.5 36.1 %collective-permute-start.15 = (bf16[4,32,1536]{2,1,0:T(8,128)(2,1)S(1)}, bf16[4,32,1536]{2,1,0:T(8,128)(2,1)}, u32[]{:S(2)}, u32[]{:S(2)}) collective-permute-start(bf16[4,32,1536]{2,1,0:T(8,128)(2,1)S(1)} %bitcast.168), channel_id=1, source_target_pairs={{0,3},{1,0},{2,1},{3,2},{4,7},{5,4},{6,5},{7,6},{8,11},{9,8},{10,9... | collective-permute-start | bytes 1179656 | tf_op jit(solution)/shard_map/ppermute | solution.py:796
  75.1 34.4 %collective-permute-start.10 = (bf16[256,1024]{1,0:T(8,128)(2,1)}, bf16[256,1024]{1,0:T(8,128)(2,1)}, u32[]{:S(2)}, u32[]{:S(2)}) collective-permute-start(bf16[256,1024]{1,0:T(8,128)(2,1)} %collective-permute-done.9.refs_5_), channel_id=1, source_target_pairs={{0,4},{4,0},{8,12},{12,8},{16,20},{20,16},{24,28},{28,24},{1,5},{5... | collective-permute-start | bytes 1572872 | tf_op jit(solution)/shard_map/ppermute | solution.py:792
  109.5 14.8 %copy-start.1 = (bf16[256,1024]{1,0:T(8,128)(2,1)S(1)}, bf16[256,1024]{1,0:T(8,128)(2,1)}, u32[]{:S(2)}) copy-start(bf16[256,1024]{1,0:T(8,128)(2,1)} %refs_5_.1) | copy-start | bytes 1572868
  109.5 14.8 %copy-start.8 = (f32[128,1024]{1,0:T(8,128)S(1)}, f32[128,1024]{1,0:T(8,128)}, u32[]{:S(2)}) copy-start(f32[128,1024]{1,0:T(8,128)} %get-tuple-element.152.refs_6_.refs_13_) | copy-start | bytes 1572868
  109.5 14.8 %copy-start.12 = (bf16[256,256]{1,0:T(8,128)(2,1)S(1)}, bf16[256,256]{1,0:T(8,128)(2,1)}, u32[]{:S(2)}) copy-start(bf16[256,256]{1,0:T(8,128)(2,1)} %get-tuple-element.148.refs_0_) | copy-start | bytes 393220
  109.6 5.6 %collective-permute-start.16 = (bf16[256,256]{1,0:T(8,128)(2,1)}, bf16[256,256]{1,0:T(8,128)(2,1)S(1)}, u32[]{:S(2)}, u32[]{:S(2)}) collective-permute-start(bf16[256,256]{1,0:T(8,128)(2,1)} %get-tuple-element.149), channel_id=1, source_target_pairs={{0,1},{1,2},{2,3},{3,0},{4,5},{5,6},{6,7},{7,4},{8,9},{9,10},{10,1... | collective-permute-start | bytes 393224 | tf_op jit(solution)/shard_map/ppermute | solution.py:796
  109.7 11.8 %collective-permute-start.17 = (bf16[256,256]{1,0:T(8,128)(2,1)}, bf16[256,256]{1,0:T(8,128)(2,1)S(1)}, u32[]{:S(2)}, u32[]{:S(2)}) collective-permute-start(bf16[256,256]{1,0:T(8,128)(2,1)} %get-tuple-element.150), channel_id=1, source_target_pairs={{0,2},{1,3},{2,0},{3,1},{4,6},{5,7},{6,4},{7,5},{8,10},{9,11},{10,... | collective-permute-start | bytes 393224 | tf_op jit(solution)/shard_map/ppermute | solution.py:796
  111.5 12.8 %collective-permute-start.18 = (bf16[256,256]{1,0:T(8,128)(2,1)}, bf16[256,256]{1,0:T(8,128)(2,1)S(1)}, u32[]{:S(2)}, u32[]{:S(2)}) collective-permute-start(bf16[256,256]{1,0:T(8,128)(2,1)} %get-tuple-element.151), channel_id=1, source_target_pairs={{0,3},{1,0},{2,1},{3,2},{4,7},{5,4},{6,5},{7,6},{8,11},{9,8},{10,9... | collective-permute-start | bytes 393224 | tf_op jit(solution)/shard_map/ppermute | solution.py:796
  114.0 49.4 %collective-permute-start.22 = (bf16[4,128,1536]{2,1,0:T(8,128)(2,1)}, bf16[4,128,1536]{2,1,0:T(8,128)(2,1)}, u32[]{:S(2)}, u32[]{:S(2)}) collective-permute-start(bf16[4,128,1536]{2,1,0:T(8,128)(2,1)} %pad_maximum_fusion.refs_8_), channel_id=1, source_target_pairs={{0,16},{4,20},{8,24},{12,28},{16,0},{20,4},{24,8},{28,12},{1,17},{... | collective-permute-start | bytes 4718600 | tf_op jit(solution)/shard_map/ppermute | solution.py:792
  126.8 36.6 %copy-start.2 = (f32[256,1024]{1,0:T(8,128)}, f32[256,1024]{1,0:T(8,128)S(1)}, u32[]{:S(2)}) copy-start(f32[256,1024]{1,0:T(8,128)S(1)} %get-tuple-element.174.refs_3_) | copy-start | bytes 3145732
  126.8 13.9 %collective-permute-start.19 = (bf16[256,1024]{1,0:T(8,128)(2,1)S(1)}, bf16[256,1024]{1,0:T(8,128)(2,1)S(1)}, u32[]{:S(2)}, u32[]{:S(2)}) collective-permute-start(bf16[256,1024]{1,0:T(8,128)(2,1)S(1)} %get-tuple-element.153.refs_0_), channel_id=1, source_target_pairs={{0,8},{4,12},{8,0},{12,4},{16,24},{20,28},{24,16},{28,20},{1,9},{5... | collective-permute-start | bytes 1572872 | tf_op jit(solution)/shard_map/ppermute | solution.py:792
  128.1 10.1 %collective-permute-start.23 = (bf16[2,96,1024]{2,1,0:T(8,128)(2,1)S(1)}, bf16[2,96,1024]{2,1,0:T(8,128)(2,1)S(1)}, u32[]{:S(2)}, u32[]{:S(2)}) collective-permute-start(bf16[2,96,1024]{2,1,0:T(8,128)(2,1)S(1)} %bitcast.170), channel_id=1, source_target_pairs={{0,1},{1,2},{2,3},{3,0},{4,5},{5,6},{6,7},{7,4},{8,9},{9,10},{10,1... | collective-permute-start | bytes 1179656 | tf_op jit(solution)/shard_map/ppermute | solution.py:796
  128.1 33.3 %collective-permute-start.24 = (bf16[2,96,1024]{2,1,0:T(8,128)(2,1)S(1)}, bf16[2,96,1024]{2,1,0:T(8,128)(2,1)S(1)}, u32[]{:S(2)}, u32[]{:S(2)}) collective-permute-start(bf16[2,96,1024]{2,1,0:T(8,128)(2,1)S(1)} %bitcast.171), channel_id=1, source_target_pairs={{0,2},{1,3},{2,0},{3,1},{4,6},{5,7},{6,4},{7,5},{8,10},{9,11},{10,... | collective-permute-start | bytes 1179656 | tf_op jit(solution)/shard_map/ppermute | solution.py:796
  128.5 34.8 %collective-permute-start.25 = (bf16[2,96,1024]{2,1,0:T(8,128)(2,1)S(1)}, bf16[2,96,1024]{2,1,0:T(8,128)(2,1)S(1)}, u32[]{:S(2)}, u32[]{:S(2)}) collective-permute-start(bf16[2,96,1024]{2,1,0:T(8,128)(2,1)S(1)} %bitcast.172), channel_id=1, source_target_pairs={{0,3},{1,0},{2,1},{3,2},{4,7},{5,4},{6,5},{7,6},{8,11},{9,8},{10,9... | collective-permute-start | bytes 1179656 | tf_op jit(solution)/shard_map/ppermute | solution.py:796
  138.2 25.2 %collective-permute-start.20 = (bf16[256,1024]{1,0:T(8,128)(2,1)S(1)}, bf16[256,1024]{1,0:T(8,128)(2,1)S(1)}, u32[]{:S(2)}, u32[]{:S(2)}) collective-permute-start(bf16[256,1024]{1,0:T(8,128)(2,1)S(1)} %get-tuple-element.153.refs_0_), channel_id=1, source_target_pairs={{0,4},{4,0},{8,12},{12,8},{16,20},{20,16},{24,28},{28,24},{1,5},{5... | collective-permute-start | bytes 1572872 | tf_op jit(solution)/shard_map/ppermute | solution.py:792
  140.7 22.7 %collective-permute-start.21 = (bf16[256,1024]{1,0:T(8,128)(2,1)S(1)}, bf16[256,1024]{1,0:T(8,128)(2,1)S(1)}, u32[]{:S(2)}, u32[]{:S(2)}) collective-permute-start(bf16[256,1024]{1,0:T(8,128)(2,1)S(1)} %collective-permute-done.19.refs_1_), channel_id=1, source_target_pairs={{0,4},{4,0},{8,12},{12,8},{16,20},{20,16},{24,28},{28,24},{1,5},{5... | collective-permute-start | bytes 1572872 | tf_op jit(solution)/shard_map/ppermute | solution.py:792
  184.1 99.3 %reduce-scatter.6.cloned.1.call-start = ((), (), s32[]{:S(2)}) async-start(), calls=%async_computation.6 | async-start | bytes 2359296 | tf_op jit(solution)/shard_map/reduce_scatter | solution.py:1040
  184.6 6.2 %collective-permute-start.26 = (bf16[512,1024]{1,0:T(8,128)(2,1)}, bf16[512,1024]{1,0:T(8,128)(2,1)}, u32[]{:S(2)}, u32[]{:S(2)}) collective-permute-start(bf16[512,1024]{1,0:T(8,128)(2,1)} %get-tuple-element.164), channel_id=1, source_target_pairs={{0,4},{4,0},{8,12},{12,8},{16,20},{20,16},{24,28},{28,24},{1,5},{5... | collective-permute-start | bytes 3145736 | tf_op jit(solution)/shard_map/ppermute | solution.py:792
  192.0 13.7 %collective-permute-start.27 = (bf16[256,1024]{1,0:T(8,128)(2,1)S(1)}, bf16[256,1024]{1,0:T(8,128)(2,1)S(1)}, u32[]{:S(2)}, u32[]{:S(2)}) collective-permute-start(bf16[256,1024]{1,0:T(8,128)(2,1)S(1)} %add_convert_fusion), channel_id=1, source_target_pairs={{0,8},{4,12},{8,0},{12,4},{16,24},{20,28},{24,16},{28,20},{1,9},{5... | collective-permute-start | bytes 1572872 | tf_op jit(solution)/shard_map/ppermute | solution.py:792
  192.5 36.9 %collective-permute-start.28 = (bf16[4,128,1536]{2,1,0:T(8,128)(2,1)}, bf16[4,128,1536]{2,1,0:T(8,128)(2,1)}, u32[]{:S(2)}, u32[]{:S(2)}) collective-permute-start(bf16[4,128,1536]{2,1,0:T(8,128)(2,1)} %bitcast.49), channel_id=1, source_target_pairs={{0,16},{4,20},{8,24},{12,28},{16,0},{20,4},{24,8},{28,12},{1,17},{... | collective-permute-start | bytes 4718600 | tf_op jit(solution)/shard_map/ppermute | solution.py:792
  212.2 8.2 %copy-start.22 = (bf16[256,1024]{1,0:T(8,128)(2,1)S(1)}, bf16[256,1024]{1,0:T(8,128)(2,1)}, u32[]{:S(2)}) copy-start(bf16[256,1024]{1,0:T(8,128)(2,1)} %get-tuple-element.184) | copy-start | bytes 1572868
  215.4 11.2 %collective-permute-start.29 = (bf16[512,1024]{1,0:T(8,128)(2,1)}, bf16[512,1024]{1,0:T(8,128)(2,1)}, u32[]{:S(2)}, u32[]{:S(2)}) collective-permute-start(bf16[512,1024]{1,0:T(8,128)(2,1)} %convolution_convert_fusion.2), channel_id=1, source_target_pairs={{0,4},{4,0},{8,12},{12,8},{16,20},{20,16},{24,28},{28,24},{1,5},{5... | collective-permute-start | bytes 3145736 | tf_op jit(solution)/shard_map/ppermute | solution.py:792
  216.9 14.4 %collective-permute-start.30 = (bf16[256,256]{1,0:T(8,128)(2,1)}, bf16[256,256]{1,0:T(8,128)(2,1)S(1)}, u32[]{:S(2)}, u32[]{:S(2)}) collective-permute-start(bf16[256,256]{1,0:T(8,128)(2,1)} %get-tuple-element.180), channel_id=1, source_target_pairs={{0,1},{1,2},{2,3},{3,0},{4,5},{5,6},{6,7},{7,4},{8,9},{9,10},{10,1... | collective-permute-start | bytes 393224 | tf_op jit(solution)/shard_map/ppermute | solution.py:796
  216.9 14.4 %collective-permute-start.31 = (bf16[256,256]{1,0:T(8,128)(2,1)}, bf16[256,256]{1,0:T(8,128)(2,1)S(1)}, u32[]{:S(2)}, u32[]{:S(2)}) collective-permute-start(bf16[256,256]{1,0:T(8,128)(2,1)} %get-tuple-element.181), channel_id=1, source_target_pairs={{0,2},{1,3},{2,0},{3,1},{4,6},{5,7},{6,4},{7,5},{8,10},{9,11},{10,... | collective-permute-start | bytes 393224 | tf_op jit(solution)/shard_map/ppermute | solution.py:796
  219.0 12.6 %collective-permute-start.32 = (bf16[256,256]{1,0:T(8,128)(2,1)}, bf16[256,256]{1,0:T(8,128)(2,1)S(1)}, u32[]{:S(2)}, u32[]{:S(2)}) collective-permute-start(bf16[256,256]{1,0:T(8,128)(2,1)} %get-tuple-element.182), channel_id=1, source_target_pairs={{0,3},{1,0},{2,1},{3,2},{4,7},{5,4},{6,5},{7,6},{8,11},{9,8},{10,9... | collective-permute-start | bytes 393224 | tf_op jit(solution)/shard_map/ppermute | solution.py:796
  222.5 108.2 %reduce-scatter.8.cloned.1.call-start = ((), (), s32[]{:S(2)}) async-start(), calls=%async_computation.7 | async-start | bytes 2654208 | tf_op jit(solution)/shard_map/reduce_scatter | solution.py:1049
  233.2 49.5 %collective-permute-start.33 = (bf16[1,4,32,1536]{3,2,0,1:T(8,128)(2,1)S(1)}, bf16[1,4,32,1536]{3,2,0,1:T(8,128)(2,1)S(1)}, u32[]{:S(2)}, u32[]{:S(2)}) collective-permute-start(bf16[1,4,32,1536]{3,2,0,1:T(8,128)(2,1)S(1)} %get-tuple-element.245), channel_id=1, source_target_pairs={{0,1},{1,2},{2,3},{3,0},{4,5},{5,6},{6,7},{7,4},{8,9},{9,10},{10,1... | collective-permute-start | bytes 1179656 | tf_op jit(solution)/shard_map/ppermute | solution.py:796
  233.2 49.4 %collective-permute-start.34 = (bf16[1,4,32,1536]{3,2,0,1:T(8,128)(2,1)S(1)}, bf16[1,4,32,1536]{3,2,0,1:T(8,128)(2,1)}, u32[]{:S(2)}, u32[]{:S(2)}) collective-permute-start(bf16[1,4,32,1536]{3,2,0,1:T(8,128)(2,1)S(1)} %get-tuple-element.244), channel_id=1, source_target_pairs={{0,2},{1,3},{2,0},{3,1},{4,6},{5,7},{6,4},{7,5},{8,10},{9,11},{10,... | collective-permute-start | bytes 1179656 | tf_op jit(solution)/shard_map/ppermute | solution.py:796
  235.3 48.1 %collective-permute-start.35 = (bf16[1,4,32,1536]{3,2,0,1:T(8,128)(2,1)S(1)}, bf16[1,4,32,1536]{3,2,0,1:T(8,128)(2,1)}, u32[]{:S(2)}, u32[]{:S(2)}) collective-permute-start(bf16[1,4,32,1536]{3,2,0,1:T(8,128)(2,1)S(1)} %get-tuple-element.243), channel_id=1, source_target_pairs={{0,3},{1,0},{2,1},{3,2},{4,7},{5,4},{6,5},{7,6},{8,11},{9,8},{10,9... | collective-permute-start | bytes 1179656 | tf_op jit(solution)/shard_map/ppermute | solution.py:796
  236.0 54.5 %collective-permute-start.39 = (bf16[256,1024]{1,0:T(8,128)(2,1)}, bf16[256,1024]{1,0:T(8,128)(2,1)}, u32[]{:S(2)}, u32[]{:S(2)}) collective-permute-start(bf16[256,1024]{1,0:T(8,128)(2,1)} %fusion.13), channel_id=1, source_target_pairs={{0,8},{4,12},{8,0},{12,4},{16,24},{20,28},{24,16},{28,20},{1,9},{5... | collective-permute-start | bytes 1572872 | tf_op jit(solution)/shard_map/ppermute | solution.py:792
  283.4 49.0 %collective-permute-start.36 = (bf16[256,1024]{1,0:T(8,128)(2,1)S(1)}, bf16[256,1024]{1,0:T(8,128)(2,1)}, u32[]{:S(2)}, u32[]{:S(2)}) collective-permute-start(bf16[256,1024]{1,0:T(8,128)(2,1)S(1)} %get-tuple-element.211), channel_id=1, source_target_pairs={{0,1},{1,2},{2,3},{3,0},{4,5},{5,6},{6,7},{7,4},{8,9},{9,10},{10,1... | collective-permute-start | bytes 1572872 | tf_op jit(solution)/shard_map/ppermute | solution.py:796
  283.5 48.9 %collective-permute-start.37 = (bf16[256,1024]{1,0:T(8,128)(2,1)}, bf16[256,1024]{1,0:T(8,128)(2,1)}, u32[]{:S(2)}, u32[]{:S(2)}) collective-permute-start(bf16[256,1024]{1,0:T(8,128)(2,1)} %get-tuple-element.212), channel_id=1, source_target_pairs={{0,2},{1,3},{2,0},{3,1},{4,6},{5,7},{6,4},{7,5},{8,10},{9,11},{10,... | collective-permute-start | bytes 1572872 | tf_op jit(solution)/shard_map/ppermute | solution.py:796
  285.8 46.6 %collective-permute-start.38 = (bf16[256,1024]{1,0:T(8,128)(2,1)}, bf16[256,1024]{1,0:T(8,128)(2,1)}, u32[]{:S(2)}, u32[]{:S(2)}) collective-permute-start(bf16[256,1024]{1,0:T(8,128)(2,1)} %get-tuple-element.213), channel_id=1, source_target_pairs={{0,3},{1,0},{2,1},{3,2},{4,7},{5,4},{6,5},{7,6},{8,11},{9,8},{10,9... | collective-permute-start | bytes 1572872 | tf_op jit(solution)/shard_map/ppermute | solution.py:796
  287.7 6.5 %collective-permute-start.43 = (bf16[32,1536]{1,0:T(8,128)(2,1)S(1)}, bf16[32,1536]{1,0:T(8,128)(2,1)S(1)}, u32[]{:S(2)}, u32[]{:S(2)}) collective-permute-start(bf16[32,1536]{1,0:T(8,128)(2,1)S(1)} %get-tuple-element.250), channel_id=1, source_target_pairs={{0,4},{4,0},{8,12},{12,8},{16,20},{20,16},{24,28},{28,24},{1,5},{5... | collective-permute-start | bytes 294920 | tf_op jit(solution)/shard_map/ppermute | solution.py:792
  290.6 4.6 %collective-permute-start.44 = (bf16[32,1536]{1,0:T(8,128)(2,1)S(1)}, bf16[32,1536]{1,0:T(8,128)(2,1)S(1)}, u32[]{:S(2)}, u32[]{:S(2)}) collective-permute-start(bf16[32,1536]{1,0:T(8,128)(2,1)S(1)} %get-tuple-element.249), channel_id=1, source_target_pairs={{0,8},{4,12},{8,0},{12,4},{16,24},{20,28},{24,16},{28,20},{1,9},{5... | collective-permute-start | bytes 294920 | tf_op jit(solution)/shard_map/ppermute | solution.py:792
  294.2 5.2 %collective-permute-start.45 = (bf16[32,1536]{1,0:T(8,128)(2,1)S(1)}, bf16[32,1536]{1,0:T(8,128)(2,1)S(1)}, u32[]{:S(2)}, u32[]{:S(2)}) collective-permute-start(bf16[32,1536]{1,0:T(8,128)(2,1)S(1)} %get-tuple-element.248), channel_id=1, source_target_pairs={{0,12},{4,8},{8,4},{12,0},{16,28},{20,24},{24,20},{28,16},{1,13},{... | collective-permute-start | bytes 294920 | tf_op jit(solution)/shard_map/ppermute | solution.py:792
  295.2 7.9 %collective-permute-start.46 = (bf16[1,96,1024]{2,1,0:T(8,128)(2,1)S(1)}, bf16[1,96,1024]{2,1,0:T(8,128)(2,1)S(1)}, u32[]{:S(2)}, u32[]{:S(2)}) collective-permute-start(bf16[1,96,1024]{2,1,0:T(8,128)(2,1)S(1)} %constant_dynamic-slice_fusion), channel_id=1, source_target_pairs={{0,16},{4,20},{8,24},{12,28},{16,0},{20,4},{24,8},{28,12},{1,17},{... | collective-permute-start | bytes 589832 | tf_op jit(solution)/shard_map/ppermute | solution.py:792
  301.3 29.4 %copy-start.26 = (bf16[128,1024]{1,0:T(8,128)(2,1)S(1)}, bf16[128,1024]{1,0:T(8,128)(2,1)}, u32[]{:S(2)}) copy-start(bf16[128,1024]{1,0:T(8,128)(2,1)} %reduce-scatter.6.cloned.1.call-done) | copy-start | bytes 786436
  331.7 6.3 %copy-start.17 = (f32[256,1024]{1,0:T(8,128)S(1)}, f32[256,1024]{1,0:T(8,128)}, u32[]{:S(2)}) copy-start(f32[256,1024]{1,0:T(8,128)} %get-tuple-element.219) | copy-start | bytes 3145732
  332.4 8.4 %collective-permute-start.40 = (bf16[1,32,2176]{2,1,0:T(8,128)(2,1)S(1)}, bf16[1,32,2176]{2,1,0:T(8,128)(2,1)S(1)}, u32[]{:S(2)}, u32[]{:S(2)}) collective-permute-start(bf16[1,32,2176]{2,1,0:T(8,128)(2,1)S(1)} %get-tuple-element.253), channel_id=1, source_target_pairs={{0,1},{1,2},{2,3},{3,0},{4,5},{5,6},{6,7},{7,4},{8,9},{9,10},{10,1... | collective-permute-start | bytes 417800 | tf_op jit(solution)/shard_map/ppermute | solution.py:796
  333.7 11.3 %collective-permute-start.41 = (bf16[1,32,2176]{2,1,0:T(8,128)(2,1)S(1)}, bf16[1,32,2176]{2,1,0:T(8,128)(2,1)S(1)}, u32[]{:S(2)}, u32[]{:S(2)}) collective-permute-start(bf16[1,32,2176]{2,1,0:T(8,128)(2,1)S(1)} %get-tuple-element.252), channel_id=1, source_target_pairs={{0,2},{1,3},{2,0},{3,1},{4,6},{5,7},{6,4},{7,5},{8,10},{9,11},{10,... | collective-permute-start | bytes 417800 | tf_op jit(solution)/shard_map/ppermute | solution.py:796
  334.8 13.1 %collective-permute-start.42 = (bf16[1,32,2176]{2,1,0:T(8,128)(2,1)S(1)}, bf16[1,32,2176]{2,1,0:T(8,128)(2,1)S(1)}, u32[]{:S(2)}, u32[]{:S(2)}) collective-permute-start(bf16[1,32,2176]{2,1,0:T(8,128)(2,1)S(1)} %get-tuple-element.251), channel_id=1, source_target_pairs={{0,3},{1,0},{2,1},{3,2},{4,7},{5,4},{6,5},{7,6},{8,11},{9,8},{10,9... | collective-permute-start | bytes 417800 | tf_op jit(solution)/shard_map/ppermute | solution.py:796
  340.8 7.1 %copy-start.30 = (bf16[1,32,2176]{2,1,0:T(8,128)(2,1)}, bf16[1,32,2176]{2,1,0:T(8,128)(2,1)S(1)}, u32[]{:S(2)}) copy-start(bf16[1,32,2176]{2,1,0:T(8,128)(2,1)S(1)} %collective-permute-done.40) | copy-start | bytes 417796
  (27 other events, 78.1 us)
Sparse Core Ops, SparseCore 0:
  36.0 38.7 all-gather.2
  77.3 28.0 all-gather.4
  184.2 33.1 reduce-scatter.3
  222.7 43.9 reduce-scatter.5
  286.1 44.5 reduce-scatter.7

commit v7 on v6

--- a/solution.py
+++ b/solution.py
@@ -10,8 +10,8 @@
 CHUNK = 128
 TP = 4
 PER_STEP = 4
-BACK_STEP = 2
-ENTER = 256
+BACK_STEP = 4
+ENTER = 512
 HALO = 8
 norm_eps = 1e-05
 unit_eps = 1e-06

time: 363 us -> 361 us (level)
  transfers between devices with their start and end apart: 52 -> 52, of which waited for: 17 -> 18; matrix products, arithmetic and copies ran while one was open for 15% -> 15% of each run, Pallas kernels for 24% -> 24%
where the time goes in v7:
time: 361 us; the launch traced here: 355 us
  waiting for transfers between devices  121 us (34%)
  Pallas kernels  99.9 us (28%)
  starting transfers between devices  49.5 us (14%)
  local copies, waits for them, and re-layouts  28.2 us (8%)
  matrix products  22.7 us (6%)
  other arithmetic  18.6 us (5%)
  between operations  15 us (4%)
    ppermute x27, waiting for transfers between devices, shift(): lax.ppermute(value, 'fsdp', [(i, (i + by) % n_fs) for i in range(n_fs)])  73.6 us
    pallas_call x1, Pallas kernels, delta_backward(): pl.pallas_call(functools.partial(backward_kernel, heads, width, n_fs, sha...  43.8 us
    pallas_call x1, Pallas kernels, delta_forward(): pl.pallas_call(functools.partial(forward_kernel, heads, width, n_fs, shar...  33.2 us
    ppermute x27, starting transfers between devices, shift(): lax.ppermute(value, 'fsdp', [(i, (i + by) % n_fs) for i in range(n_fs)])  26.1 us
    reduce_scatter x1, waiting for transfers between devices, per_device(): part = lax.psum_scatter(grad_in, 'dp', scatter_dimension=0, tiled=True)  26 us
    ppermute x20, starting transfers between devices, flip(): return lax.ppermute(value, 'dp', [(i, i ^ bit) for i in range(n_dp)])  23 us
    ppermute x20, waiting for transfers between devices, flip(): return lax.ppermute(value, 'dp', [(i, i ^ bit) for i in range(n_dp)])  21.6 us
    unnamed x86, local copies, waits for them, and re-layouts  14.5 us
  transfers between devices with their start and end apart: 52, of which 18 were waited for; matrix products, arithmetic and copies ran while one was open for 15% of the time, Pallas kernels for 24%

profile of v7, /device:TPU:9, one launch (start us, length us, event | category | flops | bytes accessed | tf_op | source)
XLA Modules:
  0.0 355.4 jit_solution(3336909539912778468)
XLA Ops:
  7.3 1.3 collective-permute-start.3
  16.0 1.3 collective-permute-start
  18.6 4.7 %collective-permute-done = bf16[1,32,2176]{2,1,0:T(8,128)(2,1)S(1)} collective-permute-done((bf16[1,32,2176]{2,1,0:T(8,128)(2,1)S(1)}, bf16[1,32,2176]{2,1,0:T(8,128)(2,1)S(1)}, u32[]{:S(2)}, u32[]{:S(2)}) %collective-permute-start) | collective-permute-done | bytes 139296 | tf_op jit(solution)/shard_map/ppermute | solution.py:796
  23.3 8.0 %collective-permute-done.1 = bf16[1,32,2176]{2,1,0:T(8,128)(2,1)S(1)} collective-permute-done((bf16[1,32,2176]{2,1,0:T(8,128)(2,1)S(1)}, bf16[1,32,2176]{2,1,0:T(8,128)(2,1)S(1)}, u32[]{:S(2)}, u32[]{:S(2)}) %collective-permute-start.1) | collective-permute-done | bytes 139296 | tf_op jit(solution)/shard_map/ppermute | solution.py:796
  31.3 2.9 collective-permute-done.2
  42.2 1.7 collective-permute-start.4
  43.9 1.2 collective-permute-start.5
  45.8 1.3 collective-permute-start.7
  47.1 3.5 collective-permute-done.5
  50.7 3.1 collective-permute-done.6
  53.8 1.2 collective-permute-start.9
  56.4 1.2 fusion.25.refs_5_
  58.5 11.7 %collective-permute-done.11.refs_2_ = bf16[256,1024]{1,0:T(8,128)(2,1)} collective-permute-done((bf16[256,1024]{1,0:T(8,128)(2,1)S(1)}, bf16[256,1024]{1,0:T(8,128)(2,1)}, u32[]{:S(2)}, u32[]{:S(2)}) %collective-permute-start.11) | collective-permute-done | bytes 524320 | tf_op jit(solution)/shard_map/ppermute | solution.py:796
  70.3 3.2 collective-permute-start.14
  73.5 1.7 collective-permute-start.15
  75.2 1.3 collective-permute-start.10
  76.6 33.2 %delta_forward.1 = (bf16[256,256]{1,0:T(8,128)(2,1)}, bf16[256,256]{1,0:T(8,128)(2,1)}, bf16[256,256]{1,0:T(8,128)(2,1)}, bf16[256,256]{1,0:T(8,128)(2,1)}, f32[...) custom-call(bf16[256,1024]{1,0:T(8,128)(2,1)} %refs_5_.1, ...), custom_call_target="tpu_custom_call" | custom-call | flops 30000001024 | bytes 16777216 | tf_op jit(solution)/shard_map/delta_forward/pallas_call | solution.py:497
  109.9 1.9 collective-permute-start.17
  111.8 2.4 pad_maximum_fusion.refs_8_
  114.2 1.2 collective-permute-start.22
  115.4 6.3 %collective-permute-done.17.refs_2_ = bf16[256,256]{1,0:T(8,128)(2,1)S(1)} collective-permute-done((bf16[256,256]{1,0:T(8,128)(2,1)}, bf16[256,256]{1,0:T(8,128)(2,1)S(1)}, u32[]{:S(2)}, u32[]{:S(2)}) %collective-permute-start.17) | collective-permute-done | bytes 131104 | tf_op jit(solution)/shard_map/ppermute | solution.py:796
  121.8 2.8 collective-permute-done.18.refs_3_
  124.6 1.6 copy-done.9
  127.0 1.3 collective-permute-start.19
  128.8 1.8 collective-permute-start.25
  130.8 7.6 %collective-permute-done.23 = bf16[2,96,1024]{2,1,0:T(8,128)(2,1)S(1)} collective-permute-done((bf16[2,96,1024]{2,1,0:T(8,128)(2,1)S(1)}, bf16[2,96,1024]{2,1,0:T(8,128)(2,1)S(1)}, u32[]{:S(2)}, u32[]{:S(2)}) %collective-permute-start.23) | collective-permute-done | bytes 393248 | tf_op jit(solution)/shard_map/ppermute | solution.py:796
  138.4 2.5 collective-permute-start.20
  141.5 20.3 %collective-permute-done.24 = bf16[2,96,1024]{2,1,0:T(8,128)(2,1)S(1)} collective-permute-done((bf16[2,96,1024]{2,1,0:T(8,128)(2,1)S(1)}, bf16[2,96,1024]{2,1,0:T(8,128)(2,1)S(1)}, u32[]{:S(2)}, u32[]{:S(2)}) %collective-permute-start.24) | collective-permute-done | bytes 393248 | tf_op jit(solution)/shard_map/ppermute | solution.py:796
  161.8 1.8 collective-permute-done.25
  164.9 14.4 %ffn_units.1 = (bf16[1024,768]{1,0:T(8,128)(2,1)}, bf16[1024,1536]{1,0:T(8,128)(2,1)}, bf16[512,1024]{1,0:T(8,128)(2,1)}, f32[256,1024]{1,0:T(8,128)}, f32[256,1024]{1,0:T(8,128)}) custom-call(s32[2]{0:T(128)S(1)} %pad_add_fusion.1.block_ref, bf16[256,1024]{1,0:T(8,128)(2,1)S(1)} %get-tuple-element.153.refs_0_, ...), custom_call_target="tpu_custom_call" | custom-call | flops 8000000000 | bytes 16777216 | tf_op jit(solution)/shard_map/ffn_units/pallas_call | solution.py:686
  179.3 5.0 %fusion.8 = bf16[768,1024]{1,0:T(8,128)(2,1)} fusion(bf16[1024,768]{1,0:T(8,128)(2,1)} %get-tuple-element.216, bf16[256,1024]{1,0:T(8,128)(2,1)} %collective-permute-done.10.refs_7_, bf16[256,1024]{1,0:T(8,128)(2,1)} %collective-permute-done.8.refs_6_, bf16[256,1024]{1,0:T(8,128)(2,1)} %collective-permute-done.9.refs_5_, bf16[256,1024]{1,0:T(8,128)(2,1)} %refs_4_.2), kind=kOutput, calls=%fused_computation.11 | convolution fusion | flops 1619787776 | bytes 5242880 | tf_op jit(solution)/shard_map/dot_general | solution.py:788
  185.4 2.4 copy-done.38
  187.8 3.0 convolution_convert_fusion
  190.8 1.2 add_convert_fusion
  192.4 1.2 collective-permute-start.28
  193.6 12.3 %collective-permute-done.27.refs_2_ = bf16[256,1024]{1,0:T(8,128)(2,1)S(1)} collective-permute-done((bf16[256,1024]{1,0:T(8,128)(2,1)S(1)}, bf16[256,1024]{1,0:T(8,128)(2,1)S(1)}, u32[]{:S(2)}, u32[]{:S(2)}) %collective-permute-start.27) | collective-permute-done | bytes 524320 | tf_op jit(solution)/shard_map/ppermute | solution.py:792
  206.7 5.7 %mix_back.1 = (bf16[256,256]{1,0:T(8,128)(2,1)}, bf16[256,256]{1,0:T(8,128)(2,1)}, bf16[256,256]{1,0:T(8,128)(2,1)}, bf16[256,256]{1,0:T(8,128)(2,1)}, f32[256,1...) custom-call(s32[1]{0:T(128)} %bitcast.1.refs_11_.z_ref, f32[256,1024]{1,0:T(8,128)} %get-tuple-element.172.refs_0_, ...), custom_call_target="tpu_custom_call" | custom-call | flops 2000000000 | bytes 6291456 | tf_op jit(solution)/shard_map/mix_back/pallas_call | solution.py:744
  212.4 3.2 convolution_convert_fusion.2
  217.0 2.0 collective-permute-start.31
  219.0 1.5 collective-permute-start.32
  220.4 2.1 convolution_convert_fusion.1
  222.6 4.1 %fusion.18 = f32[512,1536]{1,0:T(8,128)S(1)} fusion(bf16[1024,1536]{1,0:T(8,128)(2,1)} %get-tuple-element.167, bf16[1024,1024]{1,0:T(8,128)(2,1)} %copy-done.33, s32[]{:T(128)S(6)} %select_n.142), kind=kOutput, calls=%fused_computation.28 | convolution fusion | flops 1610612736 | bytes 7340036 | tf_op jit(solution)/shard_map/dot_general | solution.py:788
  226.7 2.6 fusion.13
  229.3 2.0 convert_add_fusion
  231.8 1.2 copy-done.13
  233.2 2.2 collective-permute-start.34
  237.3 43.8 %delta_backward.1 = (bf16[1024,1152]{1,0:T(8,128)(2,1)}, bf16[256,1024]{1,0:T(8,128)(2,1)S(1)}, bf16[256,1024]{1,0:T(8,128)(2,1)S(1)}, bf16[256,1024]{1,0:T(8,128)(2,1)}, bf16[256,1024]{1,0:T(8,128)(2,1)}) custom-call(bf16[256,256]{1,0:T(8,128)(2,1)S(1)} %copy-done.10, bf16[256,256]{1,0:T(8,128)(2,1)S(1)} %collective-permute-done.30.refs_1_, ...), custom_call_target="tpu_custom_call" | custom-call | flops 40000000000 | bytes 16777216 | tf_op jit(solution)/shard_map/delta_backward/pallas_call | solution.py:525
  282.0 2.4 collective-permute-start.37
  284.4 1.6 convert_add_fusion.1
  286.1 2.4 collective-permute-start.43
  289.4 2.8 fusion.14
  293.3 1.3 collective-permute-start.46
  294.6 2.7 collective-permute-done.45
  298.0 1.2 reshape.287
  299.8 1.2 reshape.289
  301.0 1.7 add_bitcast_fusion
  302.7 26.0 %reduce-scatter.8.cloned.1.call-done = bf16[128,1152]{1,0:T(8,128)(2,1)} async-done(((bf16[1024,1152]{1,0:T(8,128)(2,1)}), bf16[128,1152]{1,0:T(8,128)(2,1)}) %reduce-scatter.8.cloned.1.call-update) | async-done | bytes 294928 | tf_op jit(solution)/shard_map/reduce_scatter | solution.py:1049
  330.6 1.2 collective-permute-start.40
  332.9 1.3 collective-permute-start.42
  334.2 1.9 fusion.15
  336.1 2.8 fusion.17
  338.9 4.1 %collective-permute-done.41 = bf16[1,32,2176]{2,1,0:T(8,128)(2,1)S(1)} collective-permute-done((bf16[1,32,2176]{2,1,0:T(8,128)(2,1)S(1)}, bf16[1,32,2176]{2,1,0:T(8,128)(2,1)S(1)}, u32[]{:S(2)}, u32[]{:S(2)}) %collective-permute-start.41) | collective-permute-done | bytes 139296 | tf_op jit(solution)/shard_map/ppermute | solution.py:796
  343.0 2.9 collective-permute-done.42
  346.6 2.0 finish_inputs.1
  (229 shorter events, 36.7 us)
Async XLA Ops:
  7.2 28.7 %copy-start = (bf16[256,1024]{1,0:T(8,128)(2,1)S(1)}, bf16[256,1024]{1,0:T(8,128)(2,1)}, u32[]{:S(2)}) copy-start(bf16[256,1024]{1,0:T(8,128)(2,1)} %refs_5_.1) | copy-start | bytes 1572868
  7.2 29.3 %copy-start.34 = (s32[1,1024]{1,0:T(1,128)S(1)}, s32[1,1024]{1,0:T(1,128)}, u32[]{:S(2)}) copy-start(s32[1,1024]{1,0:T(1,128)} %param.19) | copy-start | bytes 12292
  7.2 29.5 %copy-start.35 = (s32[1,4]{1,0:T(1,128)S(1)}, s32[1,4]{1,0:T(1,128)}, u32[]{:S(2)}) copy-start(s32[1,4]{1,0:T(1,128)} %param.18) | copy-start | bytes 52
  7.2 69.3 %all-gather.3.cloned.1.call-start = ((), (), s32[]{:S(2)}) async-start(), calls=%async_computation.3 | async-start | bytes 2654208 | tf_op jit(solution)/shard_map/all_gather | solution.py:919
  7.3 26.9 %collective-permute-start.3 = (bf16[256,1024]{1,0:T(8,128)(2,1)}, bf16[256,1024]{1,0:T(8,128)(2,1)S(1)}, u32[]{:S(2)}, u32[]{:S(2)}) collective-permute-start(bf16[256,1024]{1,0:T(8,128)(2,1)} %refs_5_.1), channel_id=1, source_target_pairs={{0,1},{1,2},{2,3},{3,0},{4,5},{5,6},{6,7},{7,4},{8,9},{9,10},{10,1... | collective-permute-start | bytes 1572872 | tf_op jit(solution)/shard_map/ppermute | solution.py:796
  15.9 24.2 %copy-start.27 = (bf16[32,2816]{1,0:T(8,128)(2,1)S(1)}, bf16[32,2816]{1,0:T(8,128)(2,1)}, u32[]{:S(2)}) copy-start(bf16[32,2816]{1,0:T(8,128)(2,1)} %param.30) | copy-start | bytes 540676
  16.0 7.3 %collective-permute-start = (bf16[1,32,2176]{2,1,0:T(8,128)(2,1)S(1)}, bf16[1,32,2176]{2,1,0:T(8,128)(2,1)S(1)}, u32[]{:S(2)}, u32[]{:S(2)}) collective-permute-start(bf16[1,32,2176]{2,1,0:T(8,128)(2,1)S(1)} %get-tuple-element.257), channel_id=1, source_target_pairs={{0,1},{1,2},{2,3},{3,0},{4,5},{5,6},{6,7},{7,4},{8,9},{9,10},{10,1... | collective-permute-start | bytes 417800 | tf_op jit(solution)/shard_map/ppermute | solution.py:796
  17.3 14.0 %collective-permute-start.1 = (bf16[1,32,2176]{2,1,0:T(8,128)(2,1)S(1)}, bf16[1,32,2176]{2,1,0:T(8,128)(2,1)S(1)}, u32[]{:S(2)}, u32[]{:S(2)}) collective-permute-start(bf16[1,32,2176]{2,1,0:T(8,128)(2,1)S(1)} %get-tuple-element.256), channel_id=1, source_target_pairs={{0,2},{1,3},{2,0},{3,1},{4,6},{5,7},{6,4},{7,5},{8,10},{9,11},{10,... | collective-permute-start | bytes 417800 | tf_op jit(solution)/shard_map/ppermute | solution.py:796
  18.3 15.9 %collective-permute-start.2 = (bf16[1,32,2176]{2,1,0:T(8,128)(2,1)S(1)}, bf16[1,32,2176]{2,1,0:T(8,128)(2,1)S(1)}, u32[]{:S(2)}, u32[]{:S(2)}) collective-permute-start(bf16[1,32,2176]{2,1,0:T(8,128)(2,1)S(1)} %get-tuple-element.255), channel_id=1, source_target_pairs={{0,3},{1,0},{2,1},{3,2},{4,7},{5,4},{6,5},{7,6},{8,11},{9,8},{10,9... | collective-permute-start | bytes 417800 | tf_op jit(solution)/shard_map/ppermute | solution.py:796
  35.9 79.5 %all-gather.5.cloned.1.call-start = ((), (), s32[]{:S(2)}) async-start(), calls=%async_computation.4 | async-start | bytes 2359296 | tf_op jit(solution)/shard_map/all_gather | solution.py:920
  35.9 34.3 %collective-permute-start.11 = (bf16[256,1024]{1,0:T(8,128)(2,1)S(1)}, bf16[256,1024]{1,0:T(8,128)(2,1)}, u32[]{:S(2)}, u32[]{:S(2)}) collective-permute-start(bf16[256,1024]{1,0:T(8,128)(2,1)S(1)} %copy-done), channel_id=1, source_target_pairs={{0,2},{1,3},{2,0},{3,1},{4,6},{5,7},{6,4},{7,5},{8,10},{9,11},{10,... | collective-permute-start | bytes 1572872 | tf_op jit(solution)/shard_map/ppermute | solution.py:796
  36.2 34.0 %collective-permute-start.12 = (bf16[256,1024]{1,0:T(8,128)(2,1)S(1)}, bf16[256,1024]{1,0:T(8,128)(2,1)}, u32[]{:S(2)}, u32[]{:S(2)}) collective-permute-start(bf16[256,1024]{1,0:T(8,128)(2,1)S(1)} %copy-done), channel_id=1, source_target_pairs={{0,3},{1,0},{2,1},{3,2},{4,7},{5,4},{6,5},{7,6},{8,11},{9,8},{10,9... | collective-permute-start | bytes 1572872 | tf_op jit(solution)/shard_map/ppermute | solution.py:796
  42.2 3.6 %collective-permute-start.4 = (bf16[32,1536]{1,0:T(8,128)(2,1)S(1)}, bf16[32,1536]{1,0:T(8,128)(2,1)S(1)}, u32[]{:S(2)}, u32[]{:S(2)}) collective-permute-start(bf16[32,1536]{1,0:T(8,128)(2,1)S(1)} %get-tuple-element.261), channel_id=1, source_target_pairs={{0,4},{4,0},{8,12},{12,8},{16,20},{20,16},{24,28},{28,24},{1,5},{5... | collective-permute-start | bytes 294920 | tf_op jit(solution)/shard_map/ppermute | solution.py:792
  43.9 6.8 %collective-permute-start.5 = (bf16[32,1536]{1,0:T(8,128)(2,1)S(1)}, bf16[32,1536]{1,0:T(8,128)(2,1)S(1)}, u32[]{:S(2)}, u32[]{:S(2)}) collective-permute-start(bf16[32,1536]{1,0:T(8,128)(2,1)S(1)} %get-tuple-element.260), channel_id=1, source_target_pairs={{0,8},{4,12},{8,0},{12,4},{16,24},{20,28},{24,16},{28,20},{1,9},{5... | collective-permute-start | bytes 294920 | tf_op jit(solution)/shard_map/ppermute | solution.py:792
  45.1 8.7 %collective-permute-start.6 = (bf16[32,1536]{1,0:T(8,128)(2,1)S(1)}, bf16[32,1536]{1,0:T(8,128)(2,1)S(1)}, u32[]{:S(2)}, u32[]{:S(2)}) collective-permute-start(bf16[32,1536]{1,0:T(8,128)(2,1)S(1)} %get-tuple-element.259), channel_id=1, source_target_pairs={{0,12},{4,8},{8,4},{12,0},{16,28},{20,24},{24,20},{28,16},{1,13},{... | collective-permute-start | bytes 294920 | tf_op jit(solution)/shard_map/ppermute | solution.py:792
  45.8 8.0 %collective-permute-start.7 = (bf16[96,1024]{1,0:T(8,128)(2,1)S(1)}, bf16[96,1024]{1,0:T(8,128)(2,1)S(1)}, u32[]{:S(2)}, u32[]{:S(2)}) collective-permute-start(bf16[96,1024]{1,0:T(8,128)(2,1)S(1)} %get-tuple-element.262), channel_id=1, source_target_pairs={{0,16},{4,20},{8,24},{12,28},{16,0},{20,4},{24,8},{28,12},{1,17},{... | collective-permute-start | bytes 589832 | tf_op jit(solution)/shard_map/ppermute | solution.py:792
  53.8 21.4 %collective-permute-start.9 = (bf16[256,1024]{1,0:T(8,128)(2,1)}, bf16[256,1024]{1,0:T(8,128)(2,1)}, u32[]{:S(2)}, u32[]{:S(2)}) collective-permute-start(bf16[256,1024]{1,0:T(8,128)(2,1)} %refs_4_.2), channel_id=1, source_target_pairs={{0,8},{4,12},{8,0},{12,4},{16,24},{20,28},{24,16},{28,20},{1,9},{5... | collective-permute-start | bytes 1572872 | tf_op jit(solution)/shard_map/ppermute | solution.py:792
  55.7 226.1 %reduce-scatter.4.cloned.1.call-start = ((), (), s32[]{:S(2)}) async-start(), calls=%async_computation.5 | async-start | bytes 1966080 | tf_op jit(solution)/shard_map/reduce_scatter | solution.py:1006
  57.7 52.2 %collective-permute-start.8 = (bf16[256,1024]{1,0:T(8,128)(2,1)}, bf16[256,1024]{1,0:T(8,128)(2,1)}, u32[]{:S(2)}, u32[]{:S(2)}) collective-permute-start(bf16[256,1024]{1,0:T(8,128)(2,1)} %refs_4_.2), channel_id=1, source_target_pairs={{0,4},{4,0},{8,12},{12,8},{16,20},{20,16},{24,28},{28,24},{1,5},{5... | collective-permute-start | bytes 1572872 | tf_op jit(solution)/shard_map/ppermute | solution.py:792
  70.3 39.5 %collective-permute-start.13 = (bf16[4,32,1536]{2,1,0:T(8,128)(2,1)S(1)}, bf16[4,32,1536]{2,1,0:T(8,128)(2,1)S(1)}, u32[]{:S(2)}, u32[]{:S(2)}) collective-permute-start(bf16[4,32,1536]{2,1,0:T(8,128)(2,1)S(1)} %bitcast.166), channel_id=1, source_target_pairs={{0,1},{1,2},{2,3},{3,0},{4,5},{5,6},{6,7},{7,4},{8,9},{9,10},{10,1... | collective-permute-start | bytes 1179656 | tf_op jit(solution)/shard_map/ppermute | solution.py:796
  70.3 39.5 %collective-permute-start.14 = (bf16[4,32,1536]{2,1,0:T(8,128)(2,1)S(1)}, bf16[4,32,1536]{2,1,0:T(8,128)(2,1)S(1)}, u32[]{:S(2)}, u32[]{:S(2)}) collective-permute-start(bf16[4,32,1536]{2,1,0:T(8,128)(2,1)S(1)} %bitcast.167), channel_id=1, source_target_pairs={{0,2},{1,3},{2,0},{3,1},{4,6},{5,7},{6,4},{7,5},{8,10},{9,11},{10,... | collective-permute-start | bytes 1179656 | tf_op jit(solution)/shard_map/ppermute | solution.py:796
  73.5 36.4 %collective-permute-start.15 = (bf16[4,32,1536]{2,1,0:T(8,128)(2,1)S(1)}, bf16[4,32,1536]{2,1,0:T(8,128)(2,1)}, u32[]{:S(2)}, u32[]{:S(2)}) collective-permute-start(bf16[4,32,1536]{2,1,0:T(8,128)(2,1)S(1)} %bitcast.168), channel_id=1, source_target_pairs={{0,3},{1,0},{2,1},{3,2},{4,7},{5,4},{6,5},{7,6},{8,11},{9,8},{10,9... | collective-permute-start | bytes 1179656 | tf_op jit(solution)/shard_map/ppermute | solution.py:796
  75.2 34.6 %collective-permute-start.10 = (bf16[256,1024]{1,0:T(8,128)(2,1)}, bf16[256,1024]{1,0:T(8,128)(2,1)}, u32[]{:S(2)}, u32[]{:S(2)}) collective-permute-start(bf16[256,1024]{1,0:T(8,128)(2,1)} %collective-permute-done.9.refs_5_), channel_id=1, source_target_pairs={{0,4},{4,0},{8,12},{12,8},{16,20},{20,16},{24,28},{28,24},{1,5},{5... | collective-permute-start | bytes 1572872 | tf_op jit(solution)/shard_map/ppermute | solution.py:792
  109.8 14.8 %copy-start.1 = (bf16[256,1024]{1,0:T(8,128)(2,1)S(1)}, bf16[256,1024]{1,0:T(8,128)(2,1)}, u32[]{:S(2)}) copy-start(bf16[256,1024]{1,0:T(8,128)(2,1)} %refs_5_.1) | copy-start | bytes 1572868
  109.8 14.8 %copy-start.8 = (f32[128,1024]{1,0:T(8,128)S(1)}, f32[128,1024]{1,0:T(8,128)}, u32[]{:S(2)}) copy-start(f32[128,1024]{1,0:T(8,128)} %get-tuple-element.152.refs_6_.refs_13_) | copy-start | bytes 1572868
  109.8 14.8 %copy-start.12 = (bf16[256,256]{1,0:T(8,128)(2,1)S(1)}, bf16[256,256]{1,0:T(8,128)(2,1)}, u32[]{:S(2)}) copy-start(bf16[256,256]{1,0:T(8,128)(2,1)} %get-tuple-element.148.refs_0_) | copy-start | bytes 393220
  109.9 5.6 %collective-permute-start.16 = (bf16[256,256]{1,0:T(8,128)(2,1)}, bf16[256,256]{1,0:T(8,128)(2,1)S(1)}, u32[]{:S(2)}, u32[]{:S(2)}) collective-permute-start(bf16[256,256]{1,0:T(8,128)(2,1)} %get-tuple-element.149), channel_id=1, source_target_pairs={{0,1},{1,2},{2,3},{3,0},{4,5},{5,6},{6,7},{7,4},{8,9},{9,10},{10,1... | collective-permute-start | bytes 393224 | tf_op jit(solution)/shard_map/ppermute | solution.py:796
  109.9 11.8 %collective-permute-start.17 = (bf16[256,256]{1,0:T(8,128)(2,1)}, bf16[256,256]{1,0:T(8,128)(2,1)S(1)}, u32[]{:S(2)}, u32[]{:S(2)}) collective-permute-start(bf16[256,256]{1,0:T(8,128)(2,1)} %get-tuple-element.150), channel_id=1, source_target_pairs={{0,2},{1,3},{2,0},{3,1},{4,6},{5,7},{6,4},{7,5},{8,10},{9,11},{10,... | collective-permute-start | bytes 393224 | tf_op jit(solution)/shard_map/ppermute | solution.py:796
  111.8 12.8 %collective-permute-start.18 = (bf16[256,256]{1,0:T(8,128)(2,1)}, bf16[256,256]{1,0:T(8,128)(2,1)S(1)}, u32[]{:S(2)}, u32[]{:S(2)}) collective-permute-start(bf16[256,256]{1,0:T(8,128)(2,1)} %get-tuple-element.151), channel_id=1, source_target_pairs={{0,3},{1,0},{2,1},{3,2},{4,7},{5,4},{6,5},{7,6},{8,11},{9,8},{10,9... | collective-permute-start | bytes 393224 | tf_op jit(solution)/shard_map/ppermute | solution.py:796
  114.2 49.5 %collective-permute-start.22 = (bf16[4,128,1536]{2,1,0:T(8,128)(2,1)}, bf16[4,128,1536]{2,1,0:T(8,128)(2,1)}, u32[]{:S(2)}, u32[]{:S(2)}) collective-permute-start(bf16[4,128,1536]{2,1,0:T(8,128)(2,1)} %pad_maximum_fusion.refs_8_), channel_id=1, source_target_pairs={{0,16},{4,20},{8,24},{12,28},{16,0},{20,4},{24,8},{28,12},{1,17},{... | collective-permute-start | bytes 4718600 | tf_op jit(solution)/shard_map/ppermute | solution.py:792
  127.0 36.6 %copy-start.2 = (f32[256,1024]{1,0:T(8,128)}, f32[256,1024]{1,0:T(8,128)S(1)}, u32[]{:S(2)}) copy-start(f32[256,1024]{1,0:T(8,128)S(1)} %get-tuple-element.174.refs_3_) | copy-start | bytes 3145732
  127.0 13.9 %collective-permute-start.19 = (bf16[256,1024]{1,0:T(8,128)(2,1)S(1)}, bf16[256,1024]{1,0:T(8,128)(2,1)S(1)}, u32[]{:S(2)}, u32[]{:S(2)}) collective-permute-start(bf16[256,1024]{1,0:T(8,128)(2,1)S(1)} %get-tuple-element.153.refs_0_), channel_id=1, source_target_pairs={{0,8},{4,12},{8,0},{12,4},{16,24},{20,28},{24,16},{28,20},{1,9},{5... | collective-permute-start | bytes 1572872 | tf_op jit(solution)/shard_map/ppermute | solution.py:792
  128.3 10.1 %collective-permute-start.23 = (bf16[2,96,1024]{2,1,0:T(8,128)(2,1)S(1)}, bf16[2,96,1024]{2,1,0:T(8,128)(2,1)S(1)}, u32[]{:S(2)}, u32[]{:S(2)}) collective-permute-start(bf16[2,96,1024]{2,1,0:T(8,128)(2,1)S(1)} %bitcast.170), channel_id=1, source_target_pairs={{0,1},{1,2},{2,3},{3,0},{4,5},{5,6},{6,7},{7,4},{8,9},{9,10},{10,1... | collective-permute-start | bytes 1179656 | tf_op jit(solution)/shard_map/ppermute | solution.py:796
  128.4 33.3 %collective-permute-start.24 = (bf16[2,96,1024]{2,1,0:T(8,128)(2,1)S(1)}, bf16[2,96,1024]{2,1,0:T(8,128)(2,1)S(1)}, u32[]{:S(2)}, u32[]{:S(2)}) collective-permute-start(bf16[2,96,1024]{2,1,0:T(8,128)(2,1)S(1)} %bitcast.171), channel_id=1, source_target_pairs={{0,2},{1,3},{2,0},{3,1},{4,6},{5,7},{6,4},{7,5},{8,10},{9,11},{10,... | collective-permute-start | bytes 1179656 | tf_op jit(solution)/shard_map/ppermute | solution.py:796
  128.8 34.8 %collective-permute-start.25 = (bf16[2,96,1024]{2,1,0:T(8,128)(2,1)S(1)}, bf16[2,96,1024]{2,1,0:T(8,128)(2,1)S(1)}, u32[]{:S(2)}, u32[]{:S(2)}) collective-permute-start(bf16[2,96,1024]{2,1,0:T(8,128)(2,1)S(1)} %bitcast.172), channel_id=1, source_target_pairs={{0,3},{1,0},{2,1},{3,2},{4,7},{5,4},{6,5},{7,6},{8,11},{9,8},{10,9... | collective-permute-start | bytes 1179656 | tf_op jit(solution)/shard_map/ppermute | solution.py:796
  138.4 25.2 %collective-permute-start.20 = (bf16[256,1024]{1,0:T(8,128)(2,1)S(1)}, bf16[256,1024]{1,0:T(8,128)(2,1)S(1)}, u32[]{:S(2)}, u32[]{:S(2)}) collective-permute-start(bf16[256,1024]{1,0:T(8,128)(2,1)S(1)} %get-tuple-element.153.refs_0_), channel_id=1, source_target_pairs={{0,4},{4,0},{8,12},{12,8},{16,20},{20,16},{24,28},{28,24},{1,5},{5... | collective-permute-start | bytes 1572872 | tf_op jit(solution)/shard_map/ppermute | solution.py:792
  141.0 22.7 %collective-permute-start.21 = (bf16[256,1024]{1,0:T(8,128)(2,1)S(1)}, bf16[256,1024]{1,0:T(8,128)(2,1)S(1)}, u32[]{:S(2)}, u32[]{:S(2)}) collective-permute-start(bf16[256,1024]{1,0:T(8,128)(2,1)S(1)} %collective-permute-done.19.refs_1_), channel_id=1, source_target_pairs={{0,4},{4,0},{8,12},{12,8},{16,20},{20,16},{24,28},{28,24},{1,5},{5... | collective-permute-start | bytes 1572872 | tf_op jit(solution)/shard_map/ppermute | solution.py:792
  184.4 97.5 %reduce-scatter.6.cloned.1.call-start = ((), (), s32[]{:S(2)}) async-start(), calls=%async_computation.6 | async-start | bytes 2359296 | tf_op jit(solution)/shard_map/reduce_scatter | solution.py:1040
  184.6 6.3 %collective-permute-start.26 = (bf16[512,1024]{1,0:T(8,128)(2,1)}, bf16[512,1024]{1,0:T(8,128)(2,1)}, u32[]{:S(2)}, u32[]{:S(2)}) collective-permute-start(bf16[512,1024]{1,0:T(8,128)(2,1)} %get-tuple-element.164), channel_id=1, source_target_pairs={{0,4},{4,0},{8,12},{12,8},{16,20},{20,16},{24,28},{28,24},{1,5},{5... | collective-permute-start | bytes 3145736 | tf_op jit(solution)/shard_map/ppermute | solution.py:792
  192.1 13.8 %collective-permute-start.27 = (bf16[256,1024]{1,0:T(8,128)(2,1)S(1)}, bf16[256,1024]{1,0:T(8,128)(2,1)S(1)}, u32[]{:S(2)}, u32[]{:S(2)}) collective-permute-start(bf16[256,1024]{1,0:T(8,128)(2,1)S(1)} %add_convert_fusion), channel_id=1, source_target_pairs={{0,8},{4,12},{8,0},{12,4},{16,24},{20,28},{24,16},{28,20},{1,9},{5... | collective-permute-start | bytes 1572872 | tf_op jit(solution)/shard_map/ppermute | solution.py:792
  192.4 36.9 %collective-permute-start.28 = (bf16[4,128,1536]{2,1,0:T(8,128)(2,1)}, bf16[4,128,1536]{2,1,0:T(8,128)(2,1)}, u32[]{:S(2)}, u32[]{:S(2)}) collective-permute-start(bf16[4,128,1536]{2,1,0:T(8,128)(2,1)} %bitcast.49), channel_id=1, source_target_pairs={{0,16},{4,20},{8,24},{12,28},{16,0},{20,4},{24,8},{28,12},{1,17},{... | collective-permute-start | bytes 4718600 | tf_op jit(solution)/shard_map/ppermute | solution.py:792
  212.4 8.0 %copy-start.22 = (bf16[256,1024]{1,0:T(8,128)(2,1)S(1)}, bf16[256,1024]{1,0:T(8,128)(2,1)}, u32[]{:S(2)}) copy-start(bf16[256,1024]{1,0:T(8,128)(2,1)} %get-tuple-element.184) | copy-start | bytes 1572868
  215.6 11.1 %collective-permute-start.29 = (bf16[512,1024]{1,0:T(8,128)(2,1)}, bf16[512,1024]{1,0:T(8,128)(2,1)}, u32[]{:S(2)}, u32[]{:S(2)}) collective-permute-start(bf16[512,1024]{1,0:T(8,128)(2,1)} %convolution_convert_fusion.2), channel_id=1, source_target_pairs={{0,4},{4,0},{8,12},{12,8},{16,20},{20,16},{24,28},{28,24},{1,5},{5... | collective-permute-start | bytes 3145736 | tf_op jit(solution)/shard_map/ppermute | solution.py:792
  217.0 14.3 %collective-permute-start.30 = (bf16[256,256]{1,0:T(8,128)(2,1)}, bf16[256,256]{1,0:T(8,128)(2,1)S(1)}, u32[]{:S(2)}, u32[]{:S(2)}) collective-permute-start(bf16[256,256]{1,0:T(8,128)(2,1)} %get-tuple-element.180), channel_id=1, source_target_pairs={{0,1},{1,2},{2,3},{3,0},{4,5},{5,6},{6,7},{7,4},{8,9},{9,10},{10,1... | collective-permute-start | bytes 393224 | tf_op jit(solution)/shard_map/ppermute | solution.py:796
  217.0 14.3 %collective-permute-start.31 = (bf16[256,256]{1,0:T(8,128)(2,1)}, bf16[256,256]{1,0:T(8,128)(2,1)S(1)}, u32[]{:S(2)}, u32[]{:S(2)}) collective-permute-start(bf16[256,256]{1,0:T(8,128)(2,1)} %get-tuple-element.181), channel_id=1, source_target_pairs={{0,2},{1,3},{2,0},{3,1},{4,6},{5,7},{6,4},{7,5},{8,10},{9,11},{10,... | collective-permute-start | bytes 393224 | tf_op jit(solution)/shard_map/ppermute | solution.py:796
  219.0 12.6 %collective-permute-start.32 = (bf16[256,256]{1,0:T(8,128)(2,1)}, bf16[256,256]{1,0:T(8,128)(2,1)S(1)}, u32[]{:S(2)}, u32[]{:S(2)}) collective-permute-start(bf16[256,256]{1,0:T(8,128)(2,1)} %get-tuple-element.182), channel_id=1, source_target_pairs={{0,3},{1,0},{2,1},{3,2},{4,7},{5,4},{6,5},{7,6},{8,11},{9,8},{10,9... | collective-permute-start | bytes 393224 | tf_op jit(solution)/shard_map/ppermute | solution.py:796
  222.5 106.2 %reduce-scatter.8.cloned.1.call-start = ((), (), s32[]{:S(2)}) async-start(), calls=%async_computation.7 | async-start | bytes 2654208 | tf_op jit(solution)/shard_map/reduce_scatter | solution.py:1049
  233.1 48.0 %collective-permute-start.33 = (bf16[1,4,32,1536]{3,2,0,1:T(8,128)(2,1)S(1)}, bf16[1,4,32,1536]{3,2,0,1:T(8,128)(2,1)S(1)}, u32[]{:S(2)}, u32[]{:S(2)}) collective-permute-start(bf16[1,4,32,1536]{3,2,0,1:T(8,128)(2,1)S(1)} %get-tuple-element.245), channel_id=1, source_target_pairs={{0,1},{1,2},{2,3},{3,0},{4,5},{5,6},{6,7},{7,4},{8,9},{9,10},{10,1... | collective-permute-start | bytes 1179656 | tf_op jit(solution)/shard_map/ppermute | solution.py:796
  233.2 48.0 %collective-permute-start.34 = (bf16[1,4,32,1536]{3,2,0,1:T(8,128)(2,1)S(1)}, bf16[1,4,32,1536]{3,2,0,1:T(8,128)(2,1)}, u32[]{:S(2)}, u32[]{:S(2)}) collective-permute-start(bf16[1,4,32,1536]{3,2,0,1:T(8,128)(2,1)S(1)} %get-tuple-element.244), channel_id=1, source_target_pairs={{0,2},{1,3},{2,0},{3,1},{4,6},{5,7},{6,4},{7,5},{8,10},{9,11},{10,... | collective-permute-start | bytes 1179656 | tf_op jit(solution)/shard_map/ppermute | solution.py:796
  235.4 46.5 %collective-permute-start.35 = (bf16[1,4,32,1536]{3,2,0,1:T(8,128)(2,1)S(1)}, bf16[1,4,32,1536]{3,2,0,1:T(8,128)(2,1)}, u32[]{:S(2)}, u32[]{:S(2)}) collective-permute-start(bf16[1,4,32,1536]{3,2,0,1:T(8,128)(2,1)S(1)} %get-tuple-element.243), channel_id=1, source_target_pairs={{0,3},{1,0},{2,1},{3,2},{4,7},{5,4},{6,5},{7,6},{8,11},{9,8},{10,9... | collective-permute-start | bytes 1179656 | tf_op jit(solution)/shard_map/ppermute | solution.py:796
  236.2 52.4 %collective-permute-start.39 = (bf16[256,1024]{1,0:T(8,128)(2,1)}, bf16[256,1024]{1,0:T(8,128)(2,1)}, u32[]{:S(2)}, u32[]{:S(2)}) collective-permute-start(bf16[256,1024]{1,0:T(8,128)(2,1)} %fusion.13), channel_id=1, source_target_pairs={{0,8},{4,12},{8,0},{12,4},{16,24},{20,28},{24,16},{28,20},{1,9},{5... | collective-permute-start | bytes 1572872 | tf_op jit(solution)/shard_map/ppermute | solution.py:792
  281.9 48.6 %collective-permute-start.36 = (bf16[256,1024]{1,0:T(8,128)(2,1)S(1)}, bf16[256,1024]{1,0:T(8,128)(2,1)}, u32[]{:S(2)}, u32[]{:S(2)}) collective-permute-start(bf16[256,1024]{1,0:T(8,128)(2,1)S(1)} %get-tuple-element.211), channel_id=1, source_target_pairs={{0,1},{1,2},{2,3},{3,0},{4,5},{5,6},{6,7},{7,4},{8,9},{9,10},{10,1... | collective-permute-start | bytes 1572872 | tf_op jit(solution)/shard_map/ppermute | solution.py:796
  282.0 48.5 %collective-permute-start.37 = (bf16[256,1024]{1,0:T(8,128)(2,1)}, bf16[256,1024]{1,0:T(8,128)(2,1)}, u32[]{:S(2)}, u32[]{:S(2)}) collective-permute-start(bf16[256,1024]{1,0:T(8,128)(2,1)} %get-tuple-element.212), channel_id=1, source_target_pairs={{0,2},{1,3},{2,0},{3,1},{4,6},{5,7},{6,4},{7,5},{8,10},{9,11},{10,... | collective-permute-start | bytes 1572872 | tf_op jit(solution)/shard_map/ppermute | solution.py:796
  284.3 46.2 %collective-permute-start.38 = (bf16[256,1024]{1,0:T(8,128)(2,1)}, bf16[256,1024]{1,0:T(8,128)(2,1)}, u32[]{:S(2)}, u32[]{:S(2)}) collective-permute-start(bf16[256,1024]{1,0:T(8,128)(2,1)} %get-tuple-element.213), channel_id=1, source_target_pairs={{0,3},{1,0},{2,1},{3,2},{4,7},{5,4},{6,5},{7,6},{8,11},{9,8},{10,9... | collective-permute-start | bytes 1572872 | tf_op jit(solution)/shard_map/ppermute | solution.py:796
  286.1 6.1 %collective-permute-start.43 = (bf16[32,1536]{1,0:T(8,128)(2,1)S(1)}, bf16[32,1536]{1,0:T(8,128)(2,1)S(1)}, u32[]{:S(2)}, u32[]{:S(2)}) collective-permute-start(bf16[32,1536]{1,0:T(8,128)(2,1)S(1)} %get-tuple-element.250), channel_id=1, source_target_pairs={{0,4},{4,0},{8,12},{12,8},{16,20},{20,16},{24,28},{28,24},{1,5},{5... | collective-permute-start | bytes 294920 | tf_op jit(solution)/shard_map/ppermute | solution.py:792
  288.6 4.6 %collective-permute-start.44 = (bf16[32,1536]{1,0:T(8,128)(2,1)S(1)}, bf16[32,1536]{1,0:T(8,128)(2,1)S(1)}, u32[]{:S(2)}, u32[]{:S(2)}) collective-permute-start(bf16[32,1536]{1,0:T(8,128)(2,1)S(1)} %get-tuple-element.249), channel_id=1, source_target_pairs={{0,8},{4,12},{8,0},{12,4},{16,24},{20,28},{24,16},{28,20},{1,9},{5... | collective-permute-start | bytes 294920 | tf_op jit(solution)/shard_map/ppermute | solution.py:792
  292.2 5.2 %collective-permute-start.45 = (bf16[32,1536]{1,0:T(8,128)(2,1)S(1)}, bf16[32,1536]{1,0:T(8,128)(2,1)S(1)}, u32[]{:S(2)}, u32[]{:S(2)}) collective-permute-start(bf16[32,1536]{1,0:T(8,128)(2,1)S(1)} %get-tuple-element.248), channel_id=1, source_target_pairs={{0,12},{4,8},{8,4},{12,0},{16,28},{20,24},{24,20},{28,16},{1,13},{... | collective-permute-start | bytes 294920 | tf_op jit(solution)/shard_map/ppermute | solution.py:792
  293.3 7.8 %collective-permute-start.46 = (bf16[1,96,1024]{2,1,0:T(8,128)(2,1)S(1)}, bf16[1,96,1024]{2,1,0:T(8,128)(2,1)S(1)}, u32[]{:S(2)}, u32[]{:S(2)}) collective-permute-start(bf16[1,96,1024]{2,1,0:T(8,128)(2,1)S(1)} %constant_dynamic-slice_fusion), channel_id=1, source_target_pairs={{0,16},{4,20},{8,24},{12,28},{16,0},{20,4},{24,8},{28,12},{1,17},{... | collective-permute-start | bytes 589832 | tf_op jit(solution)/shard_map/ppermute | solution.py:792
  299.2 29.5 %copy-start.26 = (bf16[128,1024]{1,0:T(8,128)(2,1)S(1)}, bf16[128,1024]{1,0:T(8,128)(2,1)}, u32[]{:S(2)}) copy-start(bf16[128,1024]{1,0:T(8,128)(2,1)} %reduce-scatter.6.cloned.1.call-done) | copy-start | bytes 786436
  329.8 6.3 %copy-start.17 = (f32[256,1024]{1,0:T(8,128)S(1)}, f32[256,1024]{1,0:T(8,128)}, u32[]{:S(2)}) copy-start(f32[256,1024]{1,0:T(8,128)} %get-tuple-element.219) | copy-start | bytes 3145732
  330.6 8.3 %collective-permute-start.40 = (bf16[1,32,2176]{2,1,0:T(8,128)(2,1)S(1)}, bf16[1,32,2176]{2,1,0:T(8,128)(2,1)S(1)}, u32[]{:S(2)}, u32[]{:S(2)}) collective-permute-start(bf16[1,32,2176]{2,1,0:T(8,128)(2,1)S(1)} %get-tuple-element.253), channel_id=1, source_target_pairs={{0,1},{1,2},{2,3},{3,0},{4,5},{5,6},{6,7},{7,4},{8,9},{9,10},{10,1... | collective-permute-start | bytes 417800 | tf_op jit(solution)/shard_map/ppermute | solution.py:796
  331.7 11.3 %collective-permute-start.41 = (bf16[1,32,2176]{2,1,0:T(8,128)(2,1)S(1)}, bf16[1,32,2176]{2,1,0:T(8,128)(2,1)S(1)}, u32[]{:S(2)}, u32[]{:S(2)}) collective-permute-start(bf16[1,32,2176]{2,1,0:T(8,128)(2,1)S(1)} %get-tuple-element.252), channel_id=1, source_target_pairs={{0,2},{1,3},{2,0},{3,1},{4,6},{5,7},{6,4},{7,5},{8,10},{9,11},{10,... | collective-permute-start | bytes 417800 | tf_op jit(solution)/shard_map/ppermute | solution.py:796
  332.9 13.1 %collective-permute-start.42 = (bf16[1,32,2176]{2,1,0:T(8,128)(2,1)S(1)}, bf16[1,32,2176]{2,1,0:T(8,128)(2,1)S(1)}, u32[]{:S(2)}, u32[]{:S(2)}) collective-permute-start(bf16[1,32,2176]{2,1,0:T(8,128)(2,1)S(1)} %get-tuple-element.251), channel_id=1, source_target_pairs={{0,3},{1,0},{2,1},{3,2},{4,7},{5,4},{6,5},{7,6},{8,11},{9,8},{10,9... | collective-permute-start | bytes 417800 | tf_op jit(solution)/shard_map/ppermute | solution.py:796
  338.9 7.1 %copy-start.30 = (bf16[1,32,2176]{2,1,0:T(8,128)(2,1)}, bf16[1,32,2176]{2,1,0:T(8,128)(2,1)S(1)}, u32[]{:S(2)}) copy-start(bf16[1,32,2176]{2,1,0:T(8,128)(2,1)S(1)} %collective-permute-done.40) | copy-start | bytes 417796
  (27 other events, 78.9 us)
Sparse Core Ops, SparseCore 0:
  36.0 38.7 all-gather.2
  77.3 27.9 all-gather.4
  184.5 33.1 reduce-scatter.3
  222.7 44.1 reduce-scatter.5
  284.5 44.2 reduce-scatter.7

commit v8 on v7

--- a/solution.py
+++ b/solution.py
@@ -234,7 +234,9 @@
             result.append(product(halves(move_ref[at]), halves(states[head])) + added)
         return tuple(result)
 
-    lax.fori_loop(0, count, second, tuple(jnp.zeros((width, width), WIDE) for _ in range(heads)))
+    lax.fori_loop(
+        0, count, second, tuple(jnp.zeros((width, width), WIDE) for _ in range(heads)), unroll=True
+    )
 
     def third(index, _):
         rows = pl.ds(pl.multiple_of(index * CHUNK, CHUNK), CHUNK)
@@ -327,7 +329,9 @@
             result.append(product(turned(move_ref[at]), halves(grads[head])) + added)
         return tuple(result)
 
-    lax.fori_loop(0, count, second, tuple(jnp.zeros((width, width), WIDE) for _ in range(heads)))
+    lax.fori_loop(
+        0, count, second, tuple(jnp.zeros((width, width), WIDE) for _ in range(heads)), unroll=True
+    )
     dconv_ref[total:total + HALO, :] = jnp.zeros((HALO, 3 * span), WIDE)
 
     def third(group, tap_sums):

time: 361 us -> 359 us (level)
  transfers between devices with their start and end apart: 52 -> 52, of which waited for: 18 -> 17; matrix products, arithmetic and copies ran while one was open for 15% -> 15% of each run, Pallas kernels for 24% -> 23%
where the time goes in v8:
time: 359 us; the launch traced here: 354 us
  waiting for transfers between devices  121 us (34%)
  Pallas kernels  98.8 us (28%)
  starting transfers between devices  49.5 us (14%)
  local copies, waits for them, and re-layouts  28.3 us (8%)
  matrix products  22.8 us (6%)
  other arithmetic  18.7 us (5%)
  between operations  15 us (4%)
    ppermute x27, waiting for transfers between devices, shift(): lax.ppermute(value, 'fsdp', [(i, (i + by) % n_fs) for i in range(n_fs)])  73.8 us
    pallas_call x1, Pallas kernels, delta_backward(): pl.pallas_call(functools.partial(backward_kernel, heads, width, n_fs, sha...  42.9 us
    pallas_call x1, Pallas kernels, delta_forward(): pl.pallas_call(functools.partial(forward_kernel, heads, width, n_fs, shar...  32.9 us
    reduce_scatter x1, waiting for transfers between devices, per_device(): part = lax.psum_scatter(grad_in, 'dp', scatter_dimension=0, tiled=True)  25.9 us
    ppermute x27, starting transfers between devices, shift(): lax.ppermute(value, 'fsdp', [(i, (i + by) % n_fs) for i in range(n_fs)])  25.3 us
    ppermute x20, starting transfers between devices, flip(): return lax.ppermute(value, 'dp', [(i, i ^ bit) for i in range(n_dp)])  23.5 us
    ppermute x20, waiting for transfers between devices, flip(): return lax.ppermute(value, 'dp', [(i, i ^ bit) for i in range(n_dp)])  21.6 us
    unnamed x86, local copies, waits for them, and re-layouts  14.6 us
  transfers between devices with their start and end apart: 52, of which 17 were waited for; matrix products, arithmetic and copies ran while one was open for 15% of the time, Pallas kernels for 23%

profile of v8, /device:TPU:9, one launch (start us, length us, event | category | flops | bytes accessed | tf_op | source)
XLA Modules:
  0.0 354.3 jit_solution(2410126036193144227)
XLA Ops:
  7.3 1.3 collective-permute-start.3
  16.0 1.3 collective-permute-start
  18.6 4.7 %collective-permute-done = bf16[1,32,2176]{2,1,0:T(8,128)(2,1)S(1)} collective-permute-done((bf16[1,32,2176]{2,1,0:T(8,128)(2,1)S(1)}, bf16[1,32,2176]{2,1,0:T(8,128)(2,1)S(1)}, u32[]{:S(2)}, u32[]{:S(2)}) %collective-permute-start) | collective-permute-done | bytes 139296 | tf_op jit(solution)/shard_map/ppermute | solution.py:800
  23.3 8.0 %collective-permute-done.1 = bf16[1,32,2176]{2,1,0:T(8,128)(2,1)S(1)} collective-permute-done((bf16[1,32,2176]{2,1,0:T(8,128)(2,1)S(1)}, bf16[1,32,2176]{2,1,0:T(8,128)(2,1)S(1)}, u32[]{:S(2)}, u32[]{:S(2)}) %collective-permute-start.1) | collective-permute-done | bytes 139296 | tf_op jit(solution)/shard_map/ppermute | solution.py:800
  31.3 2.9 collective-permute-done.2
  42.2 1.7 collective-permute-start.4
  43.9 1.2 collective-permute-start.5
  45.8 1.3 collective-permute-start.7
  47.1 3.5 collective-permute-done.5
  50.7 3.1 collective-permute-done.6
  53.8 1.2 collective-permute-start.9
  56.4 1.2 fusion.25.refs_5_
  58.5 11.7 %collective-permute-done.11.refs_2_ = bf16[256,1024]{1,0:T(8,128)(2,1)} collective-permute-done((bf16[256,1024]{1,0:T(8,128)(2,1)S(1)}, bf16[256,1024]{1,0:T(8,128)(2,1)}, u32[]{:S(2)}, u32[]{:S(2)}) %collective-permute-start.11) | collective-permute-done | bytes 524320 | tf_op jit(solution)/shard_map/ppermute | solution.py:800
  70.3 3.2 collective-permute-start.14
  73.5 1.6 collective-permute-start.15
  75.1 1.3 collective-permute-start.10
  76.4 32.9 %delta_forward.1 = (bf16[256,256]{1,0:T(8,128)(2,1)}, bf16[256,256]{1,0:T(8,128)(2,1)}, bf16[256,256]{1,0:T(8,128)(2,1)}, bf16[256,256]{1,0:T(8,128)(2,1)}, f32[...) custom-call(bf16[256,1024]{1,0:T(8,128)(2,1)} %refs_5_.1, ...), custom_call_target="tpu_custom_call" | custom-call | flops 30000001024 | bytes 16777216 | tf_op jit(solution)/shard_map/delta_forward/pallas_call | solution.py:501
  109.5 1.9 collective-permute-start.17
  111.6 2.4 pad_maximum_fusion.refs_8_
  115.0 6.3 %collective-permute-done.17.refs_2_ = bf16[256,256]{1,0:T(8,128)(2,1)S(1)} collective-permute-done((bf16[256,256]{1,0:T(8,128)(2,1)}, bf16[256,256]{1,0:T(8,128)(2,1)S(1)}, u32[]{:S(2)}, u32[]{:S(2)}) %collective-permute-start.17) | collective-permute-done | bytes 131104 | tf_op jit(solution)/shard_map/ppermute | solution.py:800
  121.3 2.8 collective-permute-done.18.refs_3_
  124.2 1.6 copy-done.9
  126.6 1.3 collective-permute-start.19
  128.4 1.5 collective-permute-start.25
  130.1 7.9 %collective-permute-done.23 = bf16[2,96,1024]{2,1,0:T(8,128)(2,1)S(1)} collective-permute-done((bf16[2,96,1024]{2,1,0:T(8,128)(2,1)S(1)}, bf16[2,96,1024]{2,1,0:T(8,128)(2,1)S(1)}, u32[]{:S(2)}, u32[]{:S(2)}) %collective-permute-start.23) | collective-permute-done | bytes 393248 | tf_op jit(solution)/shard_map/ppermute | solution.py:800
  138.1 2.5 collective-permute-start.20
  141.1 20.3 %collective-permute-done.24 = bf16[2,96,1024]{2,1,0:T(8,128)(2,1)S(1)} collective-permute-done((bf16[2,96,1024]{2,1,0:T(8,128)(2,1)S(1)}, bf16[2,96,1024]{2,1,0:T(8,128)(2,1)S(1)}, u32[]{:S(2)}, u32[]{:S(2)}) %collective-permute-start.24) | collective-permute-done | bytes 393248 | tf_op jit(solution)/shard_map/ppermute | solution.py:800
  161.4 1.8 collective-permute-done.25
  164.5 14.4 %ffn_units.1 = (bf16[1024,768]{1,0:T(8,128)(2,1)}, bf16[1024,1536]{1,0:T(8,128)(2,1)}, bf16[512,1024]{1,0:T(8,128)(2,1)}, f32[256,1024]{1,0:T(8,128)}, f32[256,1024]{1,0:T(8,128)}) custom-call(s32[2]{0:T(128)S(1)} %pad_add_fusion.1.block_ref, bf16[256,1024]{1,0:T(8,128)(2,1)S(1)} %get-tuple-element.153.refs_0_, ...), custom_call_target="tpu_custom_call" | custom-call | flops 8000000000 | bytes 16777216 | tf_op jit(solution)/shard_map/ffn_units/pallas_call | solution.py:690
  178.9 5.0 %fusion.8 = bf16[768,1024]{1,0:T(8,128)(2,1)} fusion(bf16[1024,768]{1,0:T(8,128)(2,1)} %get-tuple-element.216, bf16[256,1024]{1,0:T(8,128)(2,1)} %collective-permute-done.10.refs_7_, bf16[256,1024]{1,0:T(8,128)(2,1)} %collective-permute-done.8.refs_6_, bf16[256,1024]{1,0:T(8,128)(2,1)} %collective-permute-done.9.refs_5_, bf16[256,1024]{1,0:T(8,128)(2,1)} %refs_4_.2), kind=kOutput, calls=%fused_computation.11 | convolution fusion | flops 1619787776 | bytes 5242880 | tf_op jit(solution)/shard_map/dot_general | solution.py:792
  185.2 2.5 copy-done.38
  187.6 3.0 convolution_convert_fusion
  190.6 1.2 add_convert_fusion
  192.2 1.3 collective-permute-start.28
  193.5 12.0 %collective-permute-done.27.refs_2_ = bf16[256,1024]{1,0:T(8,128)(2,1)S(1)} collective-permute-done((bf16[256,1024]{1,0:T(8,128)(2,1)S(1)}, bf16[256,1024]{1,0:T(8,128)(2,1)S(1)}, u32[]{:S(2)}, u32[]{:S(2)}) %collective-permute-start.27) | collective-permute-done | bytes 524320 | tf_op jit(solution)/shard_map/ppermute | solution.py:796
  206.3 5.7 %mix_back.1 = (bf16[256,256]{1,0:T(8,128)(2,1)}, bf16[256,256]{1,0:T(8,128)(2,1)}, bf16[256,256]{1,0:T(8,128)(2,1)}, bf16[256,256]{1,0:T(8,128)(2,1)}, f32[256,1...) custom-call(s32[1]{0:T(128)} %bitcast.1.refs_11_.z_ref, f32[256,1024]{1,0:T(8,128)} %get-tuple-element.172.refs_0_, ...), custom_call_target="tpu_custom_call" | custom-call | flops 2000000000 | bytes 6291456 | tf_op jit(solution)/shard_map/mix_back/pallas_call | solution.py:748
  212.0 3.2 convolution_convert_fusion.2
  216.8 2.0 collective-permute-start.31
  218.8 1.5 collective-permute-start.32
  220.3 2.1 convolution_convert_fusion.1
  222.4 4.1 %fusion.18 = f32[512,1536]{1,0:T(8,128)S(1)} fusion(bf16[1024,1536]{1,0:T(8,128)(2,1)} %get-tuple-element.167, bf16[1024,1024]{1,0:T(8,128)(2,1)} %copy-done.33, s32[]{:T(128)S(6)} %select_n.142), kind=kOutput, calls=%fused_computation.28 | convolution fusion | flops 1610612736 | bytes 7340036 | tf_op jit(solution)/shard_map/dot_general | solution.py:792
  226.5 2.7 fusion.13
  229.2 2.0 convert_add_fusion
  231.6 1.3 copy-done.13
  233.1 2.1 collective-permute-start.34
  235.7 1.2 collective-permute-start.39
  236.9 42.9 %delta_backward.1 = (bf16[1024,1152]{1,0:T(8,128)(2,1)}, bf16[256,1024]{1,0:T(8,128)(2,1)S(1)}, bf16[256,1024]{1,0:T(8,128)(2,1)S(1)}, bf16[256,1024]{1,0:T(8,128)(2,1)}, bf16[256,1024]{1,0:T(8,128)(2,1)}) custom-call(bf16[256,256]{1,0:T(8,128)(2,1)S(1)} %copy-done.10, bf16[256,256]{1,0:T(8,128)(2,1)S(1)} %collective-permute-done.30.refs_1_, ...), custom_call_target="tpu_custom_call" | custom-call | flops 40000000000 | bytes 16777216 | tf_op jit(solution)/shard_map/delta_backward/pallas_call | solution.py:529
  280.6 2.2 collective-permute-start.37
  282.9 1.6 convert_add_fusion.1
  284.6 2.8 collective-permute-start.43
  288.4 2.8 fusion.14
  292.2 1.3 collective-permute-start.46
  293.5 2.9 collective-permute-done.45
  297.1 1.2 reshape.287
  298.9 1.2 reshape.289
  300.1 1.7 add_bitcast_fusion
  301.8 25.9 %reduce-scatter.8.cloned.1.call-done = bf16[128,1152]{1,0:T(8,128)(2,1)} async-done(((bf16[1024,1152]{1,0:T(8,128)(2,1)}), bf16[128,1152]{1,0:T(8,128)(2,1)}) %reduce-scatter.8.cloned.1.call-update) | async-done | bytes 294928 | tf_op jit(solution)/shard_map/reduce_scatter | solution.py:1053
  329.4 1.2 collective-permute-start.40
  331.8 1.2 collective-permute-start.42
  333.0 1.9 fusion.15
  334.9 2.8 fusion.17
  337.8 4.1 %collective-permute-done.41 = bf16[1,32,2176]{2,1,0:T(8,128)(2,1)S(1)} collective-permute-done((bf16[1,32,2176]{2,1,0:T(8,128)(2,1)S(1)}, bf16[1,32,2176]{2,1,0:T(8,128)(2,1)S(1)}, u32[]{:S(2)}, u32[]{:S(2)}) %collective-permute-start.41) | collective-permute-done | bytes 139296 | tf_op jit(solution)/shard_map/ppermute | solution.py:800
  341.9 3.0 collective-permute-done.42
  345.5 2.0 finish_inputs.1
  (229 shorter events, 36.7 us)
Async XLA Ops:
  7.2 28.7 %copy-start = (bf16[256,1024]{1,0:T(8,128)(2,1)S(1)}, bf16[256,1024]{1,0:T(8,128)(2,1)}, u32[]{:S(2)}) copy-start(bf16[256,1024]{1,0:T(8,128)(2,1)} %refs_5_.1) | copy-start | bytes 1572868
  7.2 29.3 %copy-start.34 = (s32[1,1024]{1,0:T(1,128)S(1)}, s32[1,1024]{1,0:T(1,128)}, u32[]{:S(2)}) copy-start(s32[1,1024]{1,0:T(1,128)} %param.19) | copy-start | bytes 12292
  7.2 29.5 %copy-start.35 = (s32[1,4]{1,0:T(1,128)S(1)}, s32[1,4]{1,0:T(1,128)}, u32[]{:S(2)}) copy-start(s32[1,4]{1,0:T(1,128)} %param.18) | copy-start | bytes 52
  7.2 69.2 %all-gather.3.cloned.1.call-start = ((), (), s32[]{:S(2)}) async-start(), calls=%async_computation.3 | async-start | bytes 2654208 | tf_op jit(solution)/shard_map/all_gather | solution.py:923
  7.3 26.9 %collective-permute-start.3 = (bf16[256,1024]{1,0:T(8,128)(2,1)}, bf16[256,1024]{1,0:T(8,128)(2,1)S(1)}, u32[]{:S(2)}, u32[]{:S(2)}) collective-permute-start(bf16[256,1024]{1,0:T(8,128)(2,1)} %refs_5_.1), channel_id=1, source_target_pairs={{0,1},{1,2},{2,3},{3,0},{4,5},{5,6},{6,7},{7,4},{8,9},{9,10},{10,1... | collective-permute-start | bytes 1572872 | tf_op jit(solution)/shard_map/ppermute | solution.py:800
  15.9 24.2 %copy-start.27 = (bf16[32,2816]{1,0:T(8,128)(2,1)S(1)}, bf16[32,2816]{1,0:T(8,128)(2,1)}, u32[]{:S(2)}) copy-start(bf16[32,2816]{1,0:T(8,128)(2,1)} %param.30) | copy-start | bytes 540676
  16.0 7.3 %collective-permute-start = (bf16[1,32,2176]{2,1,0:T(8,128)(2,1)S(1)}, bf16[1,32,2176]{2,1,0:T(8,128)(2,1)S(1)}, u32[]{:S(2)}, u32[]{:S(2)}) collective-permute-start(bf16[1,32,2176]{2,1,0:T(8,128)(2,1)S(1)} %get-tuple-element.257), channel_id=1, source_target_pairs={{0,1},{1,2},{2,3},{3,0},{4,5},{5,6},{6,7},{7,4},{8,9},{9,10},{10,1... | collective-permute-start | bytes 417800 | tf_op jit(solution)/shard_map/ppermute | solution.py:800
  17.3 14.0 %collective-permute-start.1 = (bf16[1,32,2176]{2,1,0:T(8,128)(2,1)S(1)}, bf16[1,32,2176]{2,1,0:T(8,128)(2,1)S(1)}, u32[]{:S(2)}, u32[]{:S(2)}) collective-permute-start(bf16[1,32,2176]{2,1,0:T(8,128)(2,1)S(1)} %get-tuple-element.256), channel_id=1, source_target_pairs={{0,2},{1,3},{2,0},{3,1},{4,6},{5,7},{6,4},{7,5},{8,10},{9,11},{10,... | collective-permute-start | bytes 417800 | tf_op jit(solution)/shard_map/ppermute | solution.py:800
  18.3 15.9 %collective-permute-start.2 = (bf16[1,32,2176]{2,1,0:T(8,128)(2,1)S(1)}, bf16[1,32,2176]{2,1,0:T(8,128)(2,1)S(1)}, u32[]{:S(2)}, u32[]{:S(2)}) collective-permute-start(bf16[1,32,2176]{2,1,0:T(8,128)(2,1)S(1)} %get-tuple-element.255), channel_id=1, source_target_pairs={{0,3},{1,0},{2,1},{3,2},{4,7},{5,4},{6,5},{7,6},{8,11},{9,8},{10,9... | collective-permute-start | bytes 417800 | tf_op jit(solution)/shard_map/ppermute | solution.py:800
  35.9 79.2 %all-gather.5.cloned.1.call-start = ((), (), s32[]{:S(2)}) async-start(), calls=%async_computation.4 | async-start | bytes 2359296 | tf_op jit(solution)/shard_map/all_gather | solution.py:924
  35.9 34.3 %collective-permute-start.11 = (bf16[256,1024]{1,0:T(8,128)(2,1)S(1)}, bf16[256,1024]{1,0:T(8,128)(2,1)}, u32[]{:S(2)}, u32[]{:S(2)}) collective-permute-start(bf16[256,1024]{1,0:T(8,128)(2,1)S(1)} %copy-done), channel_id=1, source_target_pairs={{0,2},{1,3},{2,0},{3,1},{4,6},{5,7},{6,4},{7,5},{8,10},{9,11},{10,... | collective-permute-start | bytes 1572872 | tf_op jit(solution)/shard_map/ppermute | solution.py:800
  36.2 34.0 %collective-permute-start.12 = (bf16[256,1024]{1,0:T(8,128)(2,1)S(1)}, bf16[256,1024]{1,0:T(8,128)(2,1)}, u32[]{:S(2)}, u32[]{:S(2)}) collective-permute-start(bf16[256,1024]{1,0:T(8,128)(2,1)S(1)} %copy-done), channel_id=1, source_target_pairs={{0,3},{1,0},{2,1},{3,2},{4,7},{5,4},{6,5},{7,6},{8,11},{9,8},{10,9... | collective-permute-start | bytes 1572872 | tf_op jit(solution)/shard_map/ppermute | solution.py:800
  42.2 3.6 %collective-permute-start.4 = (bf16[32,1536]{1,0:T(8,128)(2,1)S(1)}, bf16[32,1536]{1,0:T(8,128)(2,1)S(1)}, u32[]{:S(2)}, u32[]{:S(2)}) collective-permute-start(bf16[32,1536]{1,0:T(8,128)(2,1)S(1)} %get-tuple-element.261), channel_id=1, source_target_pairs={{0,4},{4,0},{8,12},{12,8},{16,20},{20,16},{24,28},{28,24},{1,5},{5... | collective-permute-start | bytes 294920 | tf_op jit(solution)/shard_map/ppermute | solution.py:796
  43.9 6.8 %collective-permute-start.5 = (bf16[32,1536]{1,0:T(8,128)(2,1)S(1)}, bf16[32,1536]{1,0:T(8,128)(2,1)S(1)}, u32[]{:S(2)}, u32[]{:S(2)}) collective-permute-start(bf16[32,1536]{1,0:T(8,128)(2,1)S(1)} %get-tuple-element.260), channel_id=1, source_target_pairs={{0,8},{4,12},{8,0},{12,4},{16,24},{20,28},{24,16},{28,20},{1,9},{5... | collective-permute-start | bytes 294920 | tf_op jit(solution)/shard_map/ppermute | solution.py:796
  45.1 8.7 %collective-permute-start.6 = (bf16[32,1536]{1,0:T(8,128)(2,1)S(1)}, bf16[32,1536]{1,0:T(8,128)(2,1)S(1)}, u32[]{:S(2)}, u32[]{:S(2)}) collective-permute-start(bf16[32,1536]{1,0:T(8,128)(2,1)S(1)} %get-tuple-element.259), channel_id=1, source_target_pairs={{0,12},{4,8},{8,4},{12,0},{16,28},{20,24},{24,20},{28,16},{1,13},{... | collective-permute-start | bytes 294920 | tf_op jit(solution)/shard_map/ppermute | solution.py:796
  45.8 8.0 %collective-permute-start.7 = (bf16[96,1024]{1,0:T(8,128)(2,1)S(1)}, bf16[96,1024]{1,0:T(8,128)(2,1)S(1)}, u32[]{:S(2)}, u32[]{:S(2)}) collective-permute-start(bf16[96,1024]{1,0:T(8,128)(2,1)S(1)} %get-tuple-element.262), channel_id=1, source_target_pairs={{0,16},{4,20},{8,24},{12,28},{16,0},{20,4},{24,8},{28,12},{1,17},{... | collective-permute-start | bytes 589832 | tf_op jit(solution)/shard_map/ppermute | solution.py:796
  53.8 21.3 %collective-permute-start.9 = (bf16[256,1024]{1,0:T(8,128)(2,1)}, bf16[256,1024]{1,0:T(8,128)(2,1)}, u32[]{:S(2)}, u32[]{:S(2)}) collective-permute-start(bf16[256,1024]{1,0:T(8,128)(2,1)} %refs_4_.2), channel_id=1, source_target_pairs={{0,8},{4,12},{8,0},{12,4},{16,24},{20,28},{24,16},{28,20},{1,9},{5... | collective-permute-start | bytes 1572872 | tf_op jit(solution)/shard_map/ppermute | solution.py:796
  55.7 224.8 %reduce-scatter.4.cloned.1.call-start = ((), (), s32[]{:S(2)}) async-start(), calls=%async_computation.5 | async-start | bytes 1966080 | tf_op jit(solution)/shard_map/reduce_scatter | solution.py:1010
  57.7 51.8 %collective-permute-start.8 = (bf16[256,1024]{1,0:T(8,128)(2,1)}, bf16[256,1024]{1,0:T(8,128)(2,1)}, u32[]{:S(2)}, u32[]{:S(2)}) collective-permute-start(bf16[256,1024]{1,0:T(8,128)(2,1)} %refs_4_.2), channel_id=1, source_target_pairs={{0,4},{4,0},{8,12},{12,8},{16,20},{20,16},{24,28},{28,24},{1,5},{5... | collective-permute-start | bytes 1572872 | tf_op jit(solution)/shard_map/ppermute | solution.py:796
  70.3 39.1 %collective-permute-start.13 = (bf16[4,32,1536]{2,1,0:T(8,128)(2,1)S(1)}, bf16[4,32,1536]{2,1,0:T(8,128)(2,1)S(1)}, u32[]{:S(2)}, u32[]{:S(2)}) collective-permute-start(bf16[4,32,1536]{2,1,0:T(8,128)(2,1)S(1)} %bitcast.166), channel_id=1, source_target_pairs={{0,1},{1,2},{2,3},{3,0},{4,5},{5,6},{6,7},{7,4},{8,9},{9,10},{10,1... | collective-permute-start | bytes 1179656 | tf_op jit(solution)/shard_map/ppermute | solution.py:800
  70.3 39.1 %collective-permute-start.14 = (bf16[4,32,1536]{2,1,0:T(8,128)(2,1)S(1)}, bf16[4,32,1536]{2,1,0:T(8,128)(2,1)S(1)}, u32[]{:S(2)}, u32[]{:S(2)}) collective-permute-start(bf16[4,32,1536]{2,1,0:T(8,128)(2,1)S(1)} %bitcast.167), channel_id=1, source_target_pairs={{0,2},{1,3},{2,0},{3,1},{4,6},{5,7},{6,4},{7,5},{8,10},{9,11},{10,... | collective-permute-start | bytes 1179656 | tf_op jit(solution)/shard_map/ppermute | solution.py:800
  73.5 35.9 %collective-permute-start.15 = (bf16[4,32,1536]{2,1,0:T(8,128)(2,1)S(1)}, bf16[4,32,1536]{2,1,0:T(8,128)(2,1)}, u32[]{:S(2)}, u32[]{:S(2)}) collective-permute-start(bf16[4,32,1536]{2,1,0:T(8,128)(2,1)S(1)} %bitcast.168), channel_id=1, source_target_pairs={{0,3},{1,0},{2,1},{3,2},{4,7},{5,4},{6,5},{7,6},{8,11},{9,8},{10,9... | collective-permute-start | bytes 1179656 | tf_op jit(solution)/shard_map/ppermute | solution.py:800
  75.1 34.4 %collective-permute-start.10 = (bf16[256,1024]{1,0:T(8,128)(2,1)}, bf16[256,1024]{1,0:T(8,128)(2,1)}, u32[]{:S(2)}, u32[]{:S(2)}) collective-permute-start(bf16[256,1024]{1,0:T(8,128)(2,1)} %collective-permute-done.9.refs_5_), channel_id=1, source_target_pairs={{0,4},{4,0},{8,12},{12,8},{16,20},{20,16},{24,28},{28,24},{1,5},{5... | collective-permute-start | bytes 1572872 | tf_op jit(solution)/shard_map/ppermute | solution.py:796
  109.4 14.8 %copy-start.1 = (bf16[256,1024]{1,0:T(8,128)(2,1)S(1)}, bf16[256,1024]{1,0:T(8,128)(2,1)}, u32[]{:S(2)}) copy-start(bf16[256,1024]{1,0:T(8,128)(2,1)} %refs_5_.1) | copy-start | bytes 1572868
  109.4 14.8 %copy-start.8 = (f32[128,1024]{1,0:T(8,128)S(1)}, f32[128,1024]{1,0:T(8,128)}, u32[]{:S(2)}) copy-start(f32[128,1024]{1,0:T(8,128)} %get-tuple-element.152.refs_6_.refs_13_) | copy-start | bytes 1572868
  109.4 14.8 %copy-start.12 = (bf16[256,256]{1,0:T(8,128)(2,1)S(1)}, bf16[256,256]{1,0:T(8,128)(2,1)}, u32[]{:S(2)}) copy-start(bf16[256,256]{1,0:T(8,128)(2,1)} %get-tuple-element.148.refs_0_) | copy-start | bytes 393220
  109.5 5.6 %collective-permute-start.16 = (bf16[256,256]{1,0:T(8,128)(2,1)}, bf16[256,256]{1,0:T(8,128)(2,1)S(1)}, u32[]{:S(2)}, u32[]{:S(2)}) collective-permute-start(bf16[256,256]{1,0:T(8,128)(2,1)} %get-tuple-element.149), channel_id=1, source_target_pairs={{0,1},{1,2},{2,3},{3,0},{4,5},{5,6},{6,7},{7,4},{8,9},{9,10},{10,1... | collective-permute-start | bytes 393224 | tf_op jit(solution)/shard_map/ppermute | solution.py:800
  109.5 11.8 %collective-permute-start.17 = (bf16[256,256]{1,0:T(8,128)(2,1)}, bf16[256,256]{1,0:T(8,128)(2,1)S(1)}, u32[]{:S(2)}, u32[]{:S(2)}) collective-permute-start(bf16[256,256]{1,0:T(8,128)(2,1)} %get-tuple-element.150), channel_id=1, source_target_pairs={{0,2},{1,3},{2,0},{3,1},{4,6},{5,7},{6,4},{7,5},{8,10},{9,11},{10,... | collective-permute-start | bytes 393224 | tf_op jit(solution)/shard_map/ppermute | solution.py:800
  111.4 12.8 %collective-permute-start.18 = (bf16[256,256]{1,0:T(8,128)(2,1)}, bf16[256,256]{1,0:T(8,128)(2,1)S(1)}, u32[]{:S(2)}, u32[]{:S(2)}) collective-permute-start(bf16[256,256]{1,0:T(8,128)(2,1)} %get-tuple-element.151), channel_id=1, source_target_pairs={{0,3},{1,0},{2,1},{3,2},{4,7},{5,4},{6,5},{7,6},{8,11},{9,8},{10,9... | collective-permute-start | bytes 393224 | tf_op jit(solution)/shard_map/ppermute | solution.py:800
  113.9 49.4 %collective-permute-start.22 = (bf16[4,128,1536]{2,1,0:T(8,128)(2,1)}, bf16[4,128,1536]{2,1,0:T(8,128)(2,1)}, u32[]{:S(2)}, u32[]{:S(2)}) collective-permute-start(bf16[4,128,1536]{2,1,0:T(8,128)(2,1)} %pad_maximum_fusion.refs_8_), channel_id=1, source_target_pairs={{0,16},{4,20},{8,24},{12,28},{16,0},{20,4},{24,8},{28,12},{1,17},{... | collective-permute-start | bytes 4718600 | tf_op jit(solution)/shard_map/ppermute | solution.py:796
  126.6 36.6 %copy-start.2 = (f32[256,1024]{1,0:T(8,128)}, f32[256,1024]{1,0:T(8,128)S(1)}, u32[]{:S(2)}) copy-start(f32[256,1024]{1,0:T(8,128)S(1)} %get-tuple-element.174.refs_3_) | copy-start | bytes 3145732
  126.6 13.9 %collective-permute-start.19 = (bf16[256,1024]{1,0:T(8,128)(2,1)S(1)}, bf16[256,1024]{1,0:T(8,128)(2,1)S(1)}, u32[]{:S(2)}, u32[]{:S(2)}) collective-permute-start(bf16[256,1024]{1,0:T(8,128)(2,1)S(1)} %get-tuple-element.153.refs_0_), channel_id=1, source_target_pairs={{0,8},{4,12},{8,0},{12,4},{16,24},{20,28},{24,16},{28,20},{1,9},{5... | collective-permute-start | bytes 1572872 | tf_op jit(solution)/shard_map/ppermute | solution.py:796
  127.9 10.1 %collective-permute-start.23 = (bf16[2,96,1024]{2,1,0:T(8,128)(2,1)S(1)}, bf16[2,96,1024]{2,1,0:T(8,128)(2,1)S(1)}, u32[]{:S(2)}, u32[]{:S(2)}) collective-permute-start(bf16[2,96,1024]{2,1,0:T(8,128)(2,1)S(1)} %bitcast.170), channel_id=1, source_target_pairs={{0,1},{1,2},{2,3},{3,0},{4,5},{5,6},{6,7},{7,4},{8,9},{9,10},{10,1... | collective-permute-start | bytes 1179656 | tf_op jit(solution)/shard_map/ppermute | solution.py:800
  128.0 33.3 %collective-permute-start.24 = (bf16[2,96,1024]{2,1,0:T(8,128)(2,1)S(1)}, bf16[2,96,1024]{2,1,0:T(8,128)(2,1)S(1)}, u32[]{:S(2)}, u32[]{:S(2)}) collective-permute-start(bf16[2,96,1024]{2,1,0:T(8,128)(2,1)S(1)} %bitcast.171), channel_id=1, source_target_pairs={{0,2},{1,3},{2,0},{3,1},{4,6},{5,7},{6,4},{7,5},{8,10},{9,11},{10,... | collective-permute-start | bytes 1179656 | tf_op jit(solution)/shard_map/ppermute | solution.py:800
  128.4 34.8 %collective-permute-start.25 = (bf16[2,96,1024]{2,1,0:T(8,128)(2,1)S(1)}, bf16[2,96,1024]{2,1,0:T(8,128)(2,1)S(1)}, u32[]{:S(2)}, u32[]{:S(2)}) collective-permute-start(bf16[2,96,1024]{2,1,0:T(8,128)(2,1)S(1)} %bitcast.172), channel_id=1, source_target_pairs={{0,3},{1,0},{2,1},{3,2},{4,7},{5,4},{6,5},{7,6},{8,11},{9,8},{10,9... | collective-permute-start | bytes 1179656 | tf_op jit(solution)/shard_map/ppermute | solution.py:800
  138.1 25.2 %collective-permute-start.20 = (bf16[256,1024]{1,0:T(8,128)(2,1)S(1)}, bf16[256,1024]{1,0:T(8,128)(2,1)S(1)}, u32[]{:S(2)}, u32[]{:S(2)}) collective-permute-start(bf16[256,1024]{1,0:T(8,128)(2,1)S(1)} %get-tuple-element.153.refs_0_), channel_id=1, source_target_pairs={{0,4},{4,0},{8,12},{12,8},{16,20},{20,16},{24,28},{28,24},{1,5},{5... | collective-permute-start | bytes 1572872 | tf_op jit(solution)/shard_map/ppermute | solution.py:796
  140.6 22.7 %collective-permute-start.21 = (bf16[256,1024]{1,0:T(8,128)(2,1)S(1)}, bf16[256,1024]{1,0:T(8,128)(2,1)S(1)}, u32[]{:S(2)}, u32[]{:S(2)}) collective-permute-start(bf16[256,1024]{1,0:T(8,128)(2,1)S(1)} %collective-permute-done.19.refs_1_), channel_id=1, source_target_pairs={{0,4},{4,0},{8,12},{12,8},{16,20},{20,16},{24,28},{28,24},{1,5},{5... | collective-permute-start | bytes 1572872 | tf_op jit(solution)/shard_map/ppermute | solution.py:796
  184.0 96.6 %reduce-scatter.6.cloned.1.call-start = ((), (), s32[]{:S(2)}) async-start(), calls=%async_computation.6 | async-start | bytes 2359296 | tf_op jit(solution)/shard_map/reduce_scatter | solution.py:1044
  184.4 6.2 %collective-permute-start.26 = (bf16[512,1024]{1,0:T(8,128)(2,1)}, bf16[512,1024]{1,0:T(8,128)(2,1)}, u32[]{:S(2)}, u32[]{:S(2)}) collective-permute-start(bf16[512,1024]{1,0:T(8,128)(2,1)} %get-tuple-element.164), channel_id=1, source_target_pairs={{0,4},{4,0},{8,12},{12,8},{16,20},{20,16},{24,28},{28,24},{1,5},{5... | collective-permute-start | bytes 3145736 | tf_op jit(solution)/shard_map/ppermute | solution.py:796
  191.9 13.6 %collective-permute-start.27 = (bf16[256,1024]{1,0:T(8,128)(2,1)S(1)}, bf16[256,1024]{1,0:T(8,128)(2,1)S(1)}, u32[]{:S(2)}, u32[]{:S(2)}) collective-permute-start(bf16[256,1024]{1,0:T(8,128)(2,1)S(1)} %add_convert_fusion), channel_id=1, source_target_pairs={{0,8},{4,12},{8,0},{12,4},{16,24},{20,28},{24,16},{28,20},{1,9},{5... | collective-permute-start | bytes 1572872 | tf_op jit(solution)/shard_map/ppermute | solution.py:796
  192.2 36.9 %collective-permute-start.28 = (bf16[4,128,1536]{2,1,0:T(8,128)(2,1)}, bf16[4,128,1536]{2,1,0:T(8,128)(2,1)}, u32[]{:S(2)}, u32[]{:S(2)}) collective-permute-start(bf16[4,128,1536]{2,1,0:T(8,128)(2,1)} %bitcast.49), channel_id=1, source_target_pairs={{0,16},{4,20},{8,24},{12,28},{16,0},{20,4},{24,8},{28,12},{1,17},{... | collective-permute-start | bytes 4718600 | tf_op jit(solution)/shard_map/ppermute | solution.py:796
  212.0 8.2 %copy-start.22 = (bf16[256,1024]{1,0:T(8,128)(2,1)S(1)}, bf16[256,1024]{1,0:T(8,128)(2,1)}, u32[]{:S(2)}) copy-start(bf16[256,1024]{1,0:T(8,128)(2,1)} %get-tuple-element.184) | copy-start | bytes 1572868
  215.2 11.3 %collective-permute-start.29 = (bf16[512,1024]{1,0:T(8,128)(2,1)}, bf16[512,1024]{1,0:T(8,128)(2,1)}, u32[]{:S(2)}, u32[]{:S(2)}) collective-permute-start(bf16[512,1024]{1,0:T(8,128)(2,1)} %convolution_convert_fusion.2), channel_id=1, source_target_pairs={{0,4},{4,0},{8,12},{12,8},{16,20},{20,16},{24,28},{28,24},{1,5},{5... | collective-permute-start | bytes 3145736 | tf_op jit(solution)/shard_map/ppermute | solution.py:796
  216.7 14.5 %collective-permute-start.30 = (bf16[256,256]{1,0:T(8,128)(2,1)}, bf16[256,256]{1,0:T(8,128)(2,1)S(1)}, u32[]{:S(2)}, u32[]{:S(2)}) collective-permute-start(bf16[256,256]{1,0:T(8,128)(2,1)} %get-tuple-element.180), channel_id=1, source_target_pairs={{0,1},{1,2},{2,3},{3,0},{4,5},{5,6},{6,7},{7,4},{8,9},{9,10},{10,1... | collective-permute-start | bytes 393224 | tf_op jit(solution)/shard_map/ppermute | solution.py:800
  216.8 14.5 %collective-permute-start.31 = (bf16[256,256]{1,0:T(8,128)(2,1)}, bf16[256,256]{1,0:T(8,128)(2,1)S(1)}, u32[]{:S(2)}, u32[]{:S(2)}) collective-permute-start(bf16[256,256]{1,0:T(8,128)(2,1)} %get-tuple-element.181), channel_id=1, source_target_pairs={{0,2},{1,3},{2,0},{3,1},{4,6},{5,7},{6,4},{7,5},{8,10},{9,11},{10,... | collective-permute-start | bytes 393224 | tf_op jit(solution)/shard_map/ppermute | solution.py:800
  218.8 12.6 %collective-permute-start.32 = (bf16[256,256]{1,0:T(8,128)(2,1)}, bf16[256,256]{1,0:T(8,128)(2,1)S(1)}, u32[]{:S(2)}, u32[]{:S(2)}) collective-permute-start(bf16[256,256]{1,0:T(8,128)(2,1)} %get-tuple-element.182), channel_id=1, source_target_pairs={{0,3},{1,0},{2,1},{3,2},{4,7},{5,4},{6,5},{7,6},{8,11},{9,8},{10,9... | collective-permute-start | bytes 393224 | tf_op jit(solution)/shard_map/ppermute | solution.py:800
  222.4 105.3 %reduce-scatter.8.cloned.1.call-start = ((), (), s32[]{:S(2)}) async-start(), calls=%async_computation.7 | async-start | bytes 2654208 | tf_op jit(solution)/shard_map/reduce_scatter | solution.py:1053
  233.0 46.8 %collective-permute-start.33 = (bf16[1,4,32,1536]{3,2,0,1:T(8,128)(2,1)S(1)}, bf16[1,4,32,1536]{3,2,0,1:T(8,128)(2,1)S(1)}, u32[]{:S(2)}, u32[]{:S(2)}) collective-permute-start(bf16[1,4,32,1536]{3,2,0,1:T(8,128)(2,1)S(1)} %get-tuple-element.245), channel_id=1, source_target_pairs={{0,1},{1,2},{2,3},{3,0},{4,5},{5,6},{6,7},{7,4},{8,9},{9,10},{10,1... | collective-permute-start | bytes 1179656 | tf_op jit(solution)/shard_map/ppermute | solution.py:800
  233.1 46.7 %collective-permute-start.34 = (bf16[1,4,32,1536]{3,2,0,1:T(8,128)(2,1)S(1)}, bf16[1,4,32,1536]{3,2,0,1:T(8,128)(2,1)}, u32[]{:S(2)}, u32[]{:S(2)}) collective-permute-start(bf16[1,4,32,1536]{3,2,0,1:T(8,128)(2,1)S(1)} %get-tuple-element.244), channel_id=1, source_target_pairs={{0,2},{1,3},{2,0},{3,1},{4,6},{5,7},{6,4},{7,5},{8,10},{9,11},{10,... | collective-permute-start | bytes 1179656 | tf_op jit(solution)/shard_map/ppermute | solution.py:800
  235.2 45.4 %collective-permute-start.35 = (bf16[1,4,32,1536]{3,2,0,1:T(8,128)(2,1)S(1)}, bf16[1,4,32,1536]{3,2,0,1:T(8,128)(2,1)}, u32[]{:S(2)}, u32[]{:S(2)}) collective-permute-start(bf16[1,4,32,1536]{3,2,0,1:T(8,128)(2,1)S(1)} %get-tuple-element.243), channel_id=1, source_target_pairs={{0,3},{1,0},{2,1},{3,2},{4,7},{5,4},{6,5},{7,6},{8,11},{9,8},{10,9... | collective-permute-start | bytes 1179656 | tf_op jit(solution)/shard_map/ppermute | solution.py:800
  235.7 51.8 %collective-permute-start.39 = (bf16[256,1024]{1,0:T(8,128)(2,1)}, bf16[256,1024]{1,0:T(8,128)(2,1)}, u32[]{:S(2)}, u32[]{:S(2)}) collective-permute-start(bf16[256,1024]{1,0:T(8,128)(2,1)} %fusion.13), channel_id=1, source_target_pairs={{0,8},{4,12},{8,0},{12,4},{16,24},{20,28},{24,16},{28,20},{1,9},{5... | collective-permute-start | bytes 1572872 | tf_op jit(solution)/shard_map/ppermute | solution.py:796
  280.6 48.8 %collective-permute-start.36 = (bf16[256,1024]{1,0:T(8,128)(2,1)S(1)}, bf16[256,1024]{1,0:T(8,128)(2,1)}, u32[]{:S(2)}, u32[]{:S(2)}) collective-permute-start(bf16[256,1024]{1,0:T(8,128)(2,1)S(1)} %get-tuple-element.211), channel_id=1, source_target_pairs={{0,1},{1,2},{2,3},{3,0},{4,5},{5,6},{6,7},{7,4},{8,9},{9,10},{10,1... | collective-permute-start | bytes 1572872 | tf_op jit(solution)/shard_map/ppermute | solution.py:800
  280.6 48.8 %collective-permute-start.37 = (bf16[256,1024]{1,0:T(8,128)(2,1)}, bf16[256,1024]{1,0:T(8,128)(2,1)}, u32[]{:S(2)}, u32[]{:S(2)}) collective-permute-start(bf16[256,1024]{1,0:T(8,128)(2,1)} %get-tuple-element.212), channel_id=1, source_target_pairs={{0,2},{1,3},{2,0},{3,1},{4,6},{5,7},{6,4},{7,5},{8,10},{9,11},{10,... | collective-permute-start | bytes 1572872 | tf_op jit(solution)/shard_map/ppermute | solution.py:800
  282.9 46.5 %collective-permute-start.38 = (bf16[256,1024]{1,0:T(8,128)(2,1)}, bf16[256,1024]{1,0:T(8,128)(2,1)}, u32[]{:S(2)}, u32[]{:S(2)}) collective-permute-start(bf16[256,1024]{1,0:T(8,128)(2,1)} %get-tuple-element.213), channel_id=1, source_target_pairs={{0,3},{1,0},{2,1},{3,2},{4,7},{5,4},{6,5},{7,6},{8,11},{9,8},{10,9... | collective-permute-start | bytes 1572872 | tf_op jit(solution)/shard_map/ppermute | solution.py:800
  284.6 6.6 %collective-permute-start.43 = (bf16[32,1536]{1,0:T(8,128)(2,1)S(1)}, bf16[32,1536]{1,0:T(8,128)(2,1)S(1)}, u32[]{:S(2)}, u32[]{:S(2)}) collective-permute-start(bf16[32,1536]{1,0:T(8,128)(2,1)S(1)} %get-tuple-element.250), channel_id=1, source_target_pairs={{0,4},{4,0},{8,12},{12,8},{16,20},{20,16},{24,28},{28,24},{1,5},{5... | collective-permute-start | bytes 294920 | tf_op jit(solution)/shard_map/ppermute | solution.py:796
  287.5 4.6 %collective-permute-start.44 = (bf16[32,1536]{1,0:T(8,128)(2,1)S(1)}, bf16[32,1536]{1,0:T(8,128)(2,1)S(1)}, u32[]{:S(2)}, u32[]{:S(2)}) collective-permute-start(bf16[32,1536]{1,0:T(8,128)(2,1)S(1)} %get-tuple-element.249), channel_id=1, source_target_pairs={{0,8},{4,12},{8,0},{12,4},{16,24},{20,28},{24,16},{28,20},{1,9},{5... | collective-permute-start | bytes 294920 | tf_op jit(solution)/shard_map/ppermute | solution.py:796
  291.2 5.2 %collective-permute-start.45 = (bf16[32,1536]{1,0:T(8,128)(2,1)S(1)}, bf16[32,1536]{1,0:T(8,128)(2,1)S(1)}, u32[]{:S(2)}, u32[]{:S(2)}) collective-permute-start(bf16[32,1536]{1,0:T(8,128)(2,1)S(1)} %get-tuple-element.248), channel_id=1, source_target_pairs={{0,12},{4,8},{8,4},{12,0},{16,28},{20,24},{24,20},{28,16},{1,13},{... | collective-permute-start | bytes 294920 | tf_op jit(solution)/shard_map/ppermute | solution.py:796
  292.2 7.9 %collective-permute-start.46 = (bf16[1,96,1024]{2,1,0:T(8,128)(2,1)S(1)}, bf16[1,96,1024]{2,1,0:T(8,128)(2,1)S(1)}, u32[]{:S(2)}, u32[]{:S(2)}) collective-permute-start(bf16[1,96,1024]{2,1,0:T(8,128)(2,1)S(1)} %constant_dynamic-slice_fusion), channel_id=1, source_target_pairs={{0,16},{4,20},{8,24},{12,28},{16,0},{20,4},{24,8},{28,12},{1,17},{... | collective-permute-start | bytes 589832 | tf_op jit(solution)/shard_map/ppermute | solution.py:796
  298.3 29.4 %copy-start.26 = (bf16[128,1024]{1,0:T(8,128)(2,1)S(1)}, bf16[128,1024]{1,0:T(8,128)(2,1)}, u32[]{:S(2)}) copy-start(bf16[128,1024]{1,0:T(8,128)(2,1)} %reduce-scatter.6.cloned.1.call-done) | copy-start | bytes 786436
  328.7 6.3 %copy-start.17 = (f32[256,1024]{1,0:T(8,128)S(1)}, f32[256,1024]{1,0:T(8,128)}, u32[]{:S(2)}) copy-start(f32[256,1024]{1,0:T(8,128)} %get-tuple-element.219) | copy-start | bytes 3145732
  329.4 8.4 %collective-permute-start.40 = (bf16[1,32,2176]{2,1,0:T(8,128)(2,1)S(1)}, bf16[1,32,2176]{2,1,0:T(8,128)(2,1)S(1)}, u32[]{:S(2)}, u32[]{:S(2)}) collective-permute-start(bf16[1,32,2176]{2,1,0:T(8,128)(2,1)S(1)} %get-tuple-element.253), channel_id=1, source_target_pairs={{0,1},{1,2},{2,3},{3,0},{4,5},{5,6},{6,7},{7,4},{8,9},{9,10},{10,1... | collective-permute-start | bytes 417800 | tf_op jit(solution)/shard_map/ppermute | solution.py:800
  330.6 11.3 %collective-permute-start.41 = (bf16[1,32,2176]{2,1,0:T(8,128)(2,1)S(1)}, bf16[1,32,2176]{2,1,0:T(8,128)(2,1)S(1)}, u32[]{:S(2)}, u32[]{:S(2)}) collective-permute-start(bf16[1,32,2176]{2,1,0:T(8,128)(2,1)S(1)} %get-tuple-element.252), channel_id=1, source_target_pairs={{0,2},{1,3},{2,0},{3,1},{4,6},{5,7},{6,4},{7,5},{8,10},{9,11},{10,... | collective-permute-start | bytes 417800 | tf_op jit(solution)/shard_map/ppermute | solution.py:800
  331.8 13.1 %collective-permute-start.42 = (bf16[1,32,2176]{2,1,0:T(8,128)(2,1)S(1)}, bf16[1,32,2176]{2,1,0:T(8,128)(2,1)S(1)}, u32[]{:S(2)}, u32[]{:S(2)}) collective-permute-start(bf16[1,32,2176]{2,1,0:T(8,128)(2,1)S(1)} %get-tuple-element.251), channel_id=1, source_target_pairs={{0,3},{1,0},{2,1},{3,2},{4,7},{5,4},{6,5},{7,6},{8,11},{9,8},{10,9... | collective-permute-start | bytes 417800 | tf_op jit(solution)/shard_map/ppermute | solution.py:800
  337.8 7.1 %copy-start.30 = (bf16[1,32,2176]{2,1,0:T(8,128)(2,1)}, bf16[1,32,2176]{2,1,0:T(8,128)(2,1)S(1)}, u32[]{:S(2)}) copy-start(bf16[1,32,2176]{2,1,0:T(8,128)(2,1)S(1)} %collective-permute-done.40) | copy-start | bytes 417796
  (27 other events, 77.7 us)
Sparse Core Ops, SparseCore 0:
  36.0 38.7 all-gather.2
  77.3 27.9 all-gather.4
  184.1 33.1 reduce-scatter.3
  222.5 43.9 reduce-scatter.5
  283.0 44.5 reduce-scatter.7
